TPU v7x, 32 devices: a whole 2x2x4 slice. The times are simulated.
32 devices in a mesh: dp: 4 (over y, core), fsdp: 8 (over z, x).
Axes of the slice: x: 2, y: 2, z: 4, core: 2. Of those that a mesh axis runs over, the one named last changes fastest.
Arguments:
- tokens: bfloat16 [8192, 1024], P(('dp', 'fsdp')), may hold values from -6 to 6
- teacher: bfloat16 [8192, 1024], P(('dp', 'fsdp')), may hold values from -6 to 6
- lengths: int32 [32], P(('dp', 'fsdp')), may hold values from 85 to 256, as said below
- routes: int32 [8192, 8], P(('dp', 'fsdp')), may hold values from 0 to 31, all different within a row; in each aligned block of 256 rows (0 to 255, 256 to 511, ...) at most 96 rows name the same one
- gain_attn: bfloat16 [1024], P(('dp', 'fsdp')), may hold values from 0.5 to 1.5
- w_query: bfloat16 [1024, 1024], P(('dp', 'fsdp')), may hold values from -0.75 to 0.75
- w_key: bfloat16 [1024, 512], P(('dp', 'fsdp')), may hold values from -0.5 to 0.5
- w_value: bfloat16 [1024, 512], P(('dp', 'fsdp')), may hold values from -0.1875 to 0.1875
- w_out: bfloat16 [1024, 1024], P(('dp', 'fsdp')), may hold values from -6 to 6
- gain_ffn: bfloat16 [1024], P(('dp', 'fsdp')), may hold values from 0.5 to 1.5
- w_router: bfloat16 [1024, 32], P(('dp', 'fsdp')), may hold values from -0.09375 to 0.09375
- expert_gate: bfloat16 [32, 1024, 512], P('dp', 'fsdp'), may hold values from -0.1875 to 0.1875
- expert_up: bfloat16 [32, 1024, 512], P('dp', 'fsdp'), may hold values from -0.1875 to 0.1875
- expert_down: bfloat16 [32, 512, 1024], P('dp', 'fsdp'), may hold values from -6 to 6
Outputs:
- layer_output: bfloat16 [8192, 1024], P(('dp', 'fsdp'))
- loss: float32 [], replicated
- tokens_grad: float32 [8192, 1024], P(('dp', 'fsdp'))
- gain_attn_grad: float32 [1024], P(('dp', 'fsdp'))
- w_query_grad: float32 [1024, 1024], P(('dp', 'fsdp'))
- w_key_grad: float32 [1024, 512], P(('dp', 'fsdp'))
- w_value_grad: float32 [1024, 512], P(('dp', 'fsdp'))
- w_out_grad: float32 [1024, 1024], P(('dp', 'fsdp'))
- gain_ffn_grad: float32 [1024], P(('dp', 'fsdp'))
- w_router_grad: float32 [1024, 32], P(('dp', 'fsdp'))
- expert_gate_grad: float32 [32, 1024, 512], P('dp', 'fsdp')
- expert_up_grad: float32 [32, 1024, 512], P('dp', 'fsdp')
- expert_down_grad: float32 [32, 512, 1024], P('dp', 'fsdp')
Inputs may be any that keep to these rules, and one draw needn't show every extreme that they name: `lengths`: the last sequence is full. Among the 256 rows of one sequence no expert is named by more than 96 routes, a bound that some block reaches; a token's 8 experts differ.
All inputs are finite; a program needn't handle non-finite values.
Results may differ from a plain program's by a relative error of at most 0.015.
Values may be sent and summed in bfloat16 or wider, within the bound.
No kernel may reach another device: no remote copies, remote signals or barrier semaphores. Data moves between devices by JAX's collectives and lax.ppermute only.
A program may use at most 256 MiB of HBM per device.

v0:
```python
import jax
import jax.numpy as jnp
from jax import lax
from jax.sharding import PartitionSpec as P

HEADS = 16
KV_HEADS = 8
HEAD_DIM = 64
CAP = 96


epsilon = 1e-06
score_scale = 0.015625
residual_scale = 0.22
rotary_base = 10000.0
masked_score = -1e30
highest = lax.Precision.HIGHEST


def rotary_tables(seq_len, half_dim):
    positions = jnp.arange(seq_len, dtype=jnp.float32)
    frequency = rotary_base ** (-jnp.arange(half_dim, dtype=jnp.float32) / half_dim)
    angles = positions[:, None] * frequency[None, :]
    return (jnp.cos(angles)[:, None, :], jnp.sin(angles)[:, None, :])


def rotate(values, cos_part, sin_part):
    half_dim = values.shape[-1] // 2
    leading = values[..., :half_dim]
    trailing = values[..., half_dim:]
    return jnp.concatenate(
        [leading * cos_part - trailing * sin_part, trailing * cos_part + leading * sin_part],
        axis=-1,
    )


def unrotate(values, cos_part, sin_part):
    half_dim = values.shape[-1] // 2
    leading = values[..., :half_dim]
    trailing = values[..., half_dim:]
    return jnp.concatenate(
        [leading * cos_part + trailing * sin_part, trailing * cos_part - leading * sin_part],
        axis=-1,
    )


def route_slots(routes_in, experts):
    flat_routes = routes_in.reshape(-1)
    member = (flat_routes[:, None] == jnp.arange(experts, dtype=jnp.int32)[None, :]).astype(
        jnp.int32
    )
    earlier = jnp.cumsum(member, axis=0) - member
    return (flat_routes, jnp.sum(earlier * member, axis=1))


def norm_back(grad_rows, rows_in, inverse, gain_vec):
    scaled = grad_rows * gain_vec
    gain_grad = jnp.sum(grad_rows * rows_in * inverse, axis=0)
    cubed = inverse * inverse * inverse
    rows_grad = inverse * scaled - rows_in * cubed * jnp.mean(
        scaled * rows_in, axis=1, keepdims=True
    )
    return (rows_grad, gain_grad)


def on_device(
    tokens,
    teacher,
    lengths,
    routes,
    gain_attn,
    w_query,
    w_key,
    w_value,
    w_out,
    gain_ffn,
    w_router,
    expert_gate,
    expert_up,
    expert_down,
):
    seq_len, model_width = tokens.shape
    route_width = routes.shape[1]
    groups = lax.axis_size("dp")
    owned_count = expert_gate.shape[0]
    experts = owned_count * groups
    group_size = HEADS // KV_HEADS
    length_float = lengths.astype(jnp.float32)[0]
    gain_one, query_w, key_w, value_w, out_w, gain_two, router_w = (
        lax.all_gather(gain_attn, ("dp", "fsdp"), axis=0, tiled=True),
        lax.all_gather(w_query, ("dp", "fsdp"), axis=0, tiled=True),
        lax.all_gather(w_key, ("dp", "fsdp"), axis=0, tiled=True),
        lax.all_gather(w_value, ("dp", "fsdp"), axis=0, tiled=True),
        lax.all_gather(w_out, ("dp", "fsdp"), axis=0, tiled=True),
        lax.all_gather(gain_ffn, ("dp", "fsdp"), axis=0, tiled=True),
        lax.all_gather(w_router, ("dp", "fsdp"), axis=0, tiled=True),
    )
    gate_w, up_w, down_w = (
        lax.all_gather(expert_gate, "fsdp", axis=1, tiled=True),
        lax.all_gather(expert_up, "fsdp", axis=1, tiled=True),
        lax.all_gather(expert_down, "fsdp", axis=1, tiled=True),
    )
    tok_float = tokens.astype(jnp.float32)
    inv_one = lax.rsqrt(jnp.mean(tok_float * tok_float, axis=1, keepdims=True) + epsilon)
    gain_float = gain_one.astype(jnp.float32)
    normed = (tok_float * inv_one * gain_float).astype(jnp.bfloat16)
    cos_part, sin_part = rotary_tables(seq_len, HEAD_DIM // 2)
    query_f = jnp.dot(normed, query_w, preferred_element_type=jnp.float32).reshape(
        seq_len, HEADS, HEAD_DIM
    )
    key_f = jnp.dot(normed, key_w, preferred_element_type=jnp.float32).reshape(
        seq_len, KV_HEADS, HEAD_DIM
    )
    value_b = (
        jnp.dot(normed, value_w, preferred_element_type=jnp.float32)
        .astype(jnp.bfloat16)
        .reshape(seq_len, KV_HEADS, HEAD_DIM)
    )
    query_b = rotate(query_f, cos_part, sin_part).astype(jnp.bfloat16)
    key_b = rotate(key_f, cos_part, sin_part).astype(jnp.bfloat16)
    query_heads = query_b.reshape(seq_len, KV_HEADS, group_size, HEAD_DIM).transpose(1, 0, 2, 3)
    key_heads = key_b.transpose(1, 0, 2)
    value_heads = value_b.transpose(1, 0, 2)
    positions = jnp.arange(seq_len, dtype=jnp.int32)
    allowed = (positions[None, :] <= positions[:, None]) & (positions[None, :] < lengths[0])

    def head_forward(pieces):
        query_h, key_h, value_h = pieces
        raw_scores = jnp.einsum("qgd,sd->gqs", query_h, key_h, preferred_element_type=jnp.float32)
        scores = jnp.where(allowed, score_scale * raw_scores, masked_score)
        row_max = jnp.max(scores, axis=-1, keepdims=True)
        log_total = row_max + jnp.log(jnp.sum(jnp.exp(scores - row_max), axis=-1, keepdims=True))
        soft_weights = jnp.exp(scores - log_total).astype(jnp.bfloat16)
        mixed_h = jnp.einsum(
            "gqs,sd->qgd", soft_weights, value_h, preferred_element_type=jnp.float32
        )
        return (mixed_h.astype(jnp.bfloat16), log_total)

    def head_backward(pieces):
        query_h, key_h, value_h, log_total, mixed_grad_h = pieces
        raw_scores = jnp.einsum("qgd,sd->gqs", query_h, key_h, preferred_element_type=jnp.float32)
        scores = jnp.where(allowed, score_scale * raw_scores, masked_score)
        soft_float = jnp.exp(scores - log_total)
        soft_weights = soft_float.astype(jnp.bfloat16)
        soft_grad = jnp.einsum(
            "qgd,sd->gqs", mixed_grad_h, value_h, preferred_element_type=jnp.float32
        )
        value_grad_h = jnp.einsum(
            "gqs,qgd->sd", soft_weights, mixed_grad_h, preferred_element_type=jnp.float32
        )
        row_delta = jnp.sum(soft_float * soft_grad, axis=-1, keepdims=True)
        score_grad = (score_scale * (soft_float * (soft_grad - row_delta))).astype(jnp.bfloat16)
        query_grad_h = jnp.einsum(
            "gqs,sd->qgd", score_grad, key_h, preferred_element_type=jnp.float32
        )
        key_grad_h = jnp.einsum(
            "gqs,qgd->sd", score_grad, query_h, preferred_element_type=jnp.float32
        )
        return (query_grad_h, key_grad_h, value_grad_h)

    mixed_heads, log_totals = lax.map(head_forward, (query_heads, key_heads, value_heads))
    mixed_rows = mixed_heads.transpose(1, 0, 2, 3).reshape(seq_len, HEADS * HEAD_DIM)
    attended = jnp.dot(mixed_rows, out_w, preferred_element_type=jnp.float32)
    hidden = tok_float + residual_scale * attended
    inv_two = lax.rsqrt(jnp.mean(hidden * hidden, axis=1, keepdims=True) + epsilon)
    gain_second = gain_two.astype(jnp.float32)
    normed_ffn = hidden * inv_two * gain_second
    router_float = router_w.astype(jnp.float32)
    logits = jnp.dot(
        normed_ffn, router_float, precision=highest, preferred_element_type=jnp.float32
    )
    chosen = jnp.take_along_axis(logits, routes, axis=1)
    gate_weights = jax.nn.softmax(chosen, axis=-1)
    flat_routes, slot_index = route_slots(routes, experts)
    target = flat_routes * CAP + slot_index
    route_count = seq_len * route_width
    route_ids = jnp.arange(route_count, dtype=jnp.int32)
    source_token = (
        jnp.full((experts * CAP,), seq_len, jnp.int32).at[target].set(route_ids // route_width)
    )
    source_route = jnp.full((experts * CAP,), route_count, jnp.int32).at[target].set(route_ids)
    normed_pad = jnp.concatenate(
        [normed_ffn.astype(jnp.bfloat16), jnp.zeros((1, model_width), jnp.bfloat16)], axis=0
    )
    outgoing = normed_pad[source_token].reshape(groups, owned_count, CAP, model_width)
    arrived_in = lax.all_to_all(outgoing, "dp", split_axis=0, concat_axis=0, tiled=True)
    gate_in = jnp.einsum("glcd,ldf->glcf", arrived_in, gate_w, preferred_element_type=jnp.float32)
    up_in = jnp.einsum("glcd,ldf->glcf", arrived_in, up_w, preferred_element_type=jnp.float32)
    inner_act = (jax.nn.silu(gate_in) * up_in).astype(jnp.bfloat16)
    result = jnp.einsum(
        "glcf,lfd->glcd", inner_act, down_w, preferred_element_type=jnp.float32
    ).astype(jnp.bfloat16)
    returned = lax.all_to_all(result, "dp", split_axis=0, concat_axis=0, tiled=True).reshape(
        experts * CAP, model_width
    )
    picked = returned[target].astype(jnp.float32).reshape(seq_len, route_width, model_width)
    combined = jnp.sum(gate_weights[:, :, None] * picked, axis=1)
    output = hidden + residual_scale * combined
    valid_rows = (positions < lengths[0]).astype(jnp.float32)[:, None]
    deviation = (output - teacher.astype(jnp.float32)) * valid_rows
    part_loss = jnp.sum(deviation * deviation)
    loss_total, valid_total = lax.psum((part_loss, length_float), ("dp", "fsdp"))
    gain_one, query_w, key_w, value_w, out_w, gain_two, router_w = (
        lax.all_gather(gain_attn, ("dp", "fsdp"), axis=0, tiled=True),
        lax.all_gather(w_query, ("dp", "fsdp"), axis=0, tiled=True),
        lax.all_gather(w_key, ("dp", "fsdp"), axis=0, tiled=True),
        lax.all_gather(w_value, ("dp", "fsdp"), axis=0, tiled=True),
        lax.all_gather(w_out, ("dp", "fsdp"), axis=0, tiled=True),
        lax.all_gather(gain_ffn, ("dp", "fsdp"), axis=0, tiled=True),
        lax.all_gather(w_router, ("dp", "fsdp"), axis=0, tiled=True),
    )
    gate_w, up_w, down_w = (
        lax.all_gather(expert_gate, "fsdp", axis=1, tiled=True),
        lax.all_gather(expert_up, "fsdp", axis=1, tiled=True),
        lax.all_gather(expert_down, "fsdp", axis=1, tiled=True),
    )
    gain_float = gain_one.astype(jnp.float32)
    gain_second = gain_two.astype(jnp.float32)
    router_float = router_w.astype(jnp.float32)
    slot_total = seq_len * lax.axis_size("dp") * lax.axis_size("fsdp")
    out_grad = deviation * (slot_total / valid_total)
    comb_grad = residual_scale * out_grad
    gate_grad = jnp.sum(comb_grad[:, None, :] * picked, axis=2)
    slot_grad = (
        (gate_weights[:, :, None] * comb_grad[:, None, :])
        .astype(jnp.bfloat16)
        .reshape(route_count, model_width)
    )
    grad_pad = jnp.concatenate([slot_grad, jnp.zeros((1, model_width), jnp.bfloat16)], axis=0)
    grad_out = grad_pad[source_route].reshape(groups, owned_count, CAP, model_width)
    grad_in = lax.all_to_all(grad_out, "dp", split_axis=0, concat_axis=0, tiled=True)
    sigmoid_gate = jax.nn.sigmoid(gate_in)
    silu_gate = jax.nn.silu(gate_in)
    inner_act = (silu_gate * up_in).astype(jnp.bfloat16)
    down_grad = jnp.einsum("glcf,glcd->lfd", inner_act, grad_in, preferred_element_type=jnp.float32)
    inner_grad = jnp.einsum("glcd,lfd->glcf", grad_in, down_w, preferred_element_type=jnp.float32)
    gate_pre_grad = (
        inner_grad * up_in * sigmoid_gate * (1.0 + gate_in * (1.0 - sigmoid_gate))
    ).astype(jnp.bfloat16)
    up_pre_grad = (inner_grad * silu_gate).astype(jnp.bfloat16)
    gate_grad_w = jnp.einsum(
        "glcd,glcf->ldf", arrived_in, gate_pre_grad, preferred_element_type=jnp.float32
    )
    up_grad_w = jnp.einsum(
        "glcd,glcf->ldf", arrived_in, up_pre_grad, preferred_element_type=jnp.float32
    )
    arrived_grad = jnp.einsum(
        "glcf,ldf->glcd", gate_pre_grad, gate_w, preferred_element_type=jnp.float32
    )
    arrived_grad = (
        arrived_grad
        + jnp.einsum("glcf,ldf->glcd", up_pre_grad, up_w, preferred_element_type=jnp.float32)
    ).astype(jnp.bfloat16)
    back_grad = lax.all_to_all(arrived_grad, "dp", split_axis=0, concat_axis=0, tiled=True).reshape(
        experts * CAP, model_width
    )
    ffn_in_grad = jnp.sum(
        back_grad[target].astype(jnp.float32).reshape(seq_len, route_width, model_width), axis=1
    )
    chosen_grad = gate_weights * (
        gate_grad - jnp.sum(gate_weights * gate_grad, axis=1, keepdims=True)
    )
    expert_ids = jnp.arange(experts, dtype=jnp.int32)
    logit_grad = jnp.sum(
        (routes[:, :, None] == expert_ids[None, None, :]).astype(jnp.float32)
        * chosen_grad[:, :, None],
        axis=1,
    )
    router_grad = jnp.einsum(
        "td,te->de", normed_ffn, logit_grad, precision=highest, preferred_element_type=jnp.float32
    )
    ffn_in_grad = ffn_in_grad + jnp.einsum(
        "te,de->td", logit_grad, router_float, precision=highest, preferred_element_type=jnp.float32
    )
    hidden_part, gain_two_grad = norm_back(ffn_in_grad, hidden, inv_two, gain_second)
    hidden_grad = out_grad + hidden_part
    attended_grad = (residual_scale * hidden_grad).astype(jnp.bfloat16)
    out_grad_w = jnp.einsum(
        "tk,td->kd", mixed_rows, attended_grad, preferred_element_type=jnp.float32
    )
    mixed_grad = jnp.einsum(
        "td,kd->tk", attended_grad, out_w, preferred_element_type=jnp.float32
    ).astype(jnp.bfloat16)
    mixed_grad_heads = mixed_grad.reshape(seq_len, KV_HEADS, group_size, HEAD_DIM).transpose(
        1, 0, 2, 3
    )
    query_grad_all, key_grad_all, value_grad_all = lax.map(
        head_backward, (query_heads, key_heads, value_heads, log_totals, mixed_grad_heads)
    )
    query_grad = unrotate(
        query_grad_all.transpose(1, 0, 2, 3).reshape(seq_len, HEADS, HEAD_DIM), cos_part, sin_part
    )
    query_grad = query_grad.astype(jnp.bfloat16).reshape(seq_len, HEADS * HEAD_DIM)
    key_grad = (
        unrotate(key_grad_all.transpose(1, 0, 2), cos_part, sin_part)
        .astype(jnp.bfloat16)
        .reshape(seq_len, KV_HEADS * HEAD_DIM)
    )
    value_grad = (
        value_grad_all.transpose(1, 0, 2).reshape(seq_len, KV_HEADS * HEAD_DIM).astype(jnp.bfloat16)
    )
    query_grad_w = jnp.einsum("td,tk->dk", normed, query_grad, preferred_element_type=jnp.float32)
    key_grad_w = jnp.einsum("td,tk->dk", normed, key_grad, preferred_element_type=jnp.float32)
    value_grad_w = jnp.einsum("td,tk->dk", normed, value_grad, preferred_element_type=jnp.float32)
    normed_grad = jnp.einsum("tk,dk->td", query_grad, query_w, preferred_element_type=jnp.float32)
    normed_grad = normed_grad + jnp.einsum(
        "tk,dk->td", key_grad, key_w, preferred_element_type=jnp.float32
    )
    normed_grad = normed_grad + jnp.einsum(
        "tk,dk->td", value_grad, value_w, preferred_element_type=jnp.float32
    )
    token_part, gain_one_grad = norm_back(normed_grad, tok_float, inv_one, gain_float)
    token_grad = hidden_grad + token_part
    dense_grads = (
        lax.psum_scatter(gain_one_grad, ("dp", "fsdp"), scatter_dimension=0, tiled=True),
        lax.psum_scatter(query_grad_w, ("dp", "fsdp"), scatter_dimension=0, tiled=True),
        lax.psum_scatter(key_grad_w, ("dp", "fsdp"), scatter_dimension=0, tiled=True),
        lax.psum_scatter(value_grad_w, ("dp", "fsdp"), scatter_dimension=0, tiled=True),
        lax.psum_scatter(out_grad_w, ("dp", "fsdp"), scatter_dimension=0, tiled=True),
        lax.psum_scatter(gain_two_grad, ("dp", "fsdp"), scatter_dimension=0, tiled=True),
        lax.psum_scatter(router_grad, ("dp", "fsdp"), scatter_dimension=0, tiled=True),
    )
    expert_grads = (
        lax.psum_scatter(
            gate_grad_w.astype(jnp.bfloat16), "fsdp", scatter_dimension=1, tiled=True
        ).astype(jnp.float32),
        lax.psum_scatter(
            up_grad_w.astype(jnp.bfloat16), "fsdp", scatter_dimension=1, tiled=True
        ).astype(jnp.float32),
        lax.psum_scatter(
            down_grad.astype(jnp.bfloat16), "fsdp", scatter_dimension=1, tiled=True
        ).astype(jnp.float32),
    )
    loss_value = loss_total / (valid_total * model_width)
    return (
        output.astype(jnp.bfloat16),
        loss_value,
        token_grad,
        dense_grads[0],
        dense_grads[1],
        dense_grads[2],
        dense_grads[3],
        dense_grads[4],
        dense_grads[5],
        dense_grads[6],
        expert_grads[0],
        expert_grads[1],
        expert_grads[2],
    )


def solution(mesh):
    in_specs = (
        P(("dp", "fsdp"), None),
        P(("dp", "fsdp"), None),
        P(("dp", "fsdp")),
        P(("dp", "fsdp"), None),
        P(("dp", "fsdp")),
        P(("dp", "fsdp"), None),
        P(("dp", "fsdp"), None),
        P(("dp", "fsdp"), None),
        P(("dp", "fsdp"), None),
        P(("dp", "fsdp")),
        P(("dp", "fsdp"), None),
        P("dp", "fsdp", None),
        P("dp", "fsdp", None),
        P("dp", "fsdp", None),
    )
    out_specs = (
        P(("dp", "fsdp"), None),
        P(),
        P(("dp", "fsdp"), None),
        P(("dp", "fsdp")),
        P(("dp", "fsdp"), None),
        P(("dp", "fsdp"), None),
        P(("dp", "fsdp"), None),
        P(("dp", "fsdp"), None),
        P(("dp", "fsdp")),
        P(("dp", "fsdp"), None),
        P("dp", "fsdp", None),
        P("dp", "fsdp", None),
        P("dp", "fsdp", None),
    )
    return jax.shard_map(
        on_device, mesh=mesh, in_specs=in_specs, out_specs=out_specs, check_vma=False
    )
```

profile of v0, /device:TPU:0, one launch (start us, length us, event | category | flops | bytes accessed | tf_op | source)
XLA Modules:
  0.0 2116.9 jit_solution(6242141481519468158)
XLA Ops:
  15.4 41.9 %all-reduce.7 = (bf16[1024]{0:T(1024)(128)(2,1)S(1)}, bf16[1024]{0:T(1024)(128)(2,1)S(1)}) all-reduce(bf16[1024]{0:T(1024)(128)(2,1)S(1)} %dynamic-update-slice, bf16[1024]{0:T(1024)(128)(2,1)S(1)} %dynamic-update-slice.1), channel_id=1, replica_groups=mesh['dp'=4,'fsdp'=8] {'dp','fsdp'}, use_global_device_ids=true, to_apply=%add.2 | all-reduce | flops 2048 | bytes 8192
  80.2 43.3 %all-gather.10.cloned.1.call-done = bf16[1024,512]{1,0:T(8,128)(2,1)} async-done(((bf16[32,512]{1,0:T(8,128)(2,1)}), bf16[1024,512]{1,0:T(8,128)(2,1)}) %all-gather.10.cloned.1.call-update) | async-done | bytes 1048592 | tf_op jit(solution)/shard_map/all_gather | solution.py:92
  125.5 56.5 %all-gather.12.cloned.1.call-done = bf16[1024,1024]{1,0:T(8,128)(2,1)} async-done(((bf16[32,1024]{1,0:T(8,128)(2,1)}), bf16[1024,1024]{1,0:T(8,128)(2,1)}) %all-gather.12.cloned.1.call-update) | async-done | bytes 2097168 | tf_op jit(solution)/shard_map/all_gather | solution.py:91
  195.3 44.9 %all-gather.14.cloned.1.call-done = bf16[1024,1024]{1,0:T(8,128)(2,1)} async-done(((bf16[32,1024]{1,0:T(8,128)(2,1)}), bf16[1024,1024]{1,0:T(8,128)(2,1)}) %all-gather.14.cloned.1.call-update) | async-done | bytes 2097168 | tf_op jit(solution)/shard_map/all_gather | solution.py:94
  243.3 13.9 gather_fusion
  257.3 77.5 %all_to_all.20 = bf16[4,8,96,1024]{3,2,1,0:T(8,128)(2,1)} all-to-all(bf16[4,8,96,1024]{3,2,1,0:T(8,128)(2,1)} %bitcast.286), channel_id=1, replica_groups=mesh['dp'=4,'fsdp'=8] {'dp'}, dimensions={0} | all-to-all | bytes 12582912 | tf_op jit(solution)/shard_map/all_to_all | solution.py:186
  334.8 30.7 %all-gather.16.cloned.1.call-done = bf16[8,1024,512]{2,1,0:T(8,128)(2,1)} async-done(((bf16[8,128,512]{2,1,0:T(8,128)(2,1)}), bf16[8,1024,512]{2,1,0:T(8,128)(2,1)}) %all-gather.16.cloned.1.call-update) | async-done | bytes 8388624 | tf_op jit(solution)/shard_map/all_gather | solution.py:99
  365.5 11.3 fusion.70
  376.8 113.4 %all-gather.18.cloned.1.call-done = bf16[8,1024,512]{2,1,0:T(8,128)(2,1)} async-done(((bf16[8,128,512]{2,1,0:T(8,128)(2,1)}), bf16[8,1024,512]{2,1,0:T(8,128)(2,1)}) %all-gather.18.cloned.1.call-update) | async-done | bytes 8388624 | tf_op jit(solution)/shard_map/all_gather | solution.py:100
  490.2 14.1 fusion.82
  504.3 110.7 %all-gather.20.cloned.1.call-done = bf16[8,512,1024]{2,1,0:T(8,128)(2,1)} async-done(((bf16[8,64,1024]{2,1,0:T(8,128)(2,1)}), bf16[8,512,1024]{2,1,0:T(8,128)(2,1)}) %all-gather.20.cloned.1.call-update) | async-done | bytes 8388624 | tf_op jit(solution)/shard_map/all_gather | solution.py:101
  631.5 102.0 %psum.15 = f32[]{:T(128)} all-reduce(f32[]{:T(128)} %bitcast.29), channel_id=1, replica_groups=mesh['dp'=4,'fsdp'=8] {'dp','fsdp'}, use_global_device_ids=true, to_apply=%region_15.16 | all-reduce | flops 1 | bytes 8 | tf_op jit(solution)/shard_map/psum | solution.py:202
  742.6 68.0 %all_gather.46 = bf16[1024,32]{1,0:T(8,128)(2,1)S(1)} all-gather(bf16[32,32]{1,0:T(8,128)(2,1)S(1)} %copy-done.30), channel_id=1, replica_groups=mesh['dp'=4,'fsdp'=8] {'dp','fsdp'}, dimensions={0}, use_global_device_ids=true | all-gather | bytes 67584 | tf_op jit(solution)/shard_map/all_gather | solution.py:96
  812.1 16.8 gather_fusion.4
  829.4 14.6 gather_fusion.1
  853.9 18.6 gather_fusion.2
  872.6 77.6 %all_to_all.21 = bf16[4,8,96,1024]{3,2,1,0:T(8,128)(2,1)} all-to-all(bf16[4,8,96,1024]{3,2,1,0:T(8,128)(2,1)} %bitcast.287), channel_id=1, replica_groups=mesh['dp'=4,'fsdp'=8] {'dp'}, dimensions={0} | all-to-all | bytes 12582912 | tf_op jit(solution)/shard_map/all_to_all | solution.py:231
  959.9 15.6 fusion.80
  975.6 11.5 bitcast_convert_fusion.2
  987.4 11.5 bitcast_convert_fusion.1
  998.9 12.6 fusion.64
  1011.5 13.4 fusion.77
  1044.8 63.0 %all-to-all-done.3 = bf16[4,8,96,1024]{3,2,1,0:T(8,128)(2,1)} async-done(((bf16[4,8,96,1024]{3,2,1,0:T(8,128)(2,1)}), bf16[4,8,96,1024]{3,2,1,0:T(8,128)(2,1)}, u32[]{:S(2)}, u32[]{:S(2)}) %all-to-all-start.3) | async-done | bytes 6291488 | tf_op jit(solution)/shard_map/all_to_all | solution.py:254
  1107.8 14.9 gather_fusion.3
  1131.5 52.9 %while.29 = (s32[]{:T(128)}, f32[8,256,2,64]{1,3,2,0:T(8,128)}, f32[8,256,64]{1,2,0:T(8,128)}, bf16[8,256,64]{1,2,0:T(8,128)(2,1)S(1)}, bf16[8,256,64]{1,2,0:T(8...) while((s32[]{:T(128)}, f32[8,256,2,64]{1,3,2,0:T(8,128)}, ...), condition=%wide.region_24.25_spmd.clone, body=%wide.region_22.24_spmd.clone.sunk | while | flops 85853696 | bytes 6532465 | solution.py:287
  1202.9 39.7 %all-reduce.6 = (f32[]{:T(128)}, f32[1024]{0:T(1024)S(1)}, f32[1024]{0:T(1024)S(1)}) all-reduce(f32[]{:T(128)} %get-tuple-element.207, f32[1024]{0:T(1024)S(1)} %get-tuple-element.152, f32[1024]{0:T(1024)S(1)} %get-tuple-element.150), channel_id=1, replica_groups=mesh['dp'=4,'fsdp'=8] {'dp','fsdp'}, use_global_device_ids=true, to_apply=%region_14.15 | all-reduce | flops 2049 | bytes 16392 | tf_op jit(solution)/shard_map/psum | solution.py:202
  1257.8 147.2 %reduce-scatter.21.cloned.1.call-done = bf16[8,128,512]{2,1,0:T(8,128)(2,1)} async-done(((bf16[8,1024,512]{2,1,0:T(8,128)(2,1)}), bf16[8,128,512]{2,1,0:T(8,128)(2,1)}) %reduce-scatter.21.cloned.1.call-update) | async-done | bytes 1048592 | tf_op jit(solution)/shard_map/reduce_scatter | solution.py:327
  1407.9 134.9 %reduce-scatter.17.cloned.1.call-done = f32[32,32]{1,0:T(8,128)} async-done(((f32[1024,32]{1,0:T(8,128)}), f32[32,32]{1,0:T(8,128)}) %reduce-scatter.17.cloned.1.call-update) | async-done | bytes 4112 | tf_op jit(solution)/shard_map/reduce_scatter | solution.py:321
  1542.8 138.2 %reduce-scatter.11.cloned.1.call-done = f32[32,512]{1,0:T(8,128)} async-done(((f32[1024,512]{1,0:T(8,128)}), f32[32,512]{1,0:T(8,128)}) %reduce-scatter.11.cloned.1.call-update) | async-done | bytes 65552 | tf_op jit(solution)/shard_map/reduce_scatter | solution.py:317
  1681.0 138.8 %reduce-scatter.13.cloned.1.call-done = f32[32,512]{1,0:T(8,128)} async-done(((f32[1024,512]{1,0:T(8,128)}), f32[32,512]{1,0:T(8,128)}) %reduce-scatter.13.cloned.1.call-update) | async-done | bytes 65552 | tf_op jit(solution)/shard_map/reduce_scatter | solution.py:318
  1819.8 143.6 %reduce-scatter.9.cloned.1.call-done = f32[32,1024]{1,0:T(8,128)} async-done(((f32[1024,1024]{1,0:T(8,128)}), f32[32,1024]{1,0:T(8,128)}) %reduce-scatter.9.cloned.1.call-update) | async-done | bytes 131088 | tf_op jit(solution)/shard_map/reduce_scatter | solution.py:316
  1963.3 145.4 %reduce-scatter.15.cloned.1.call-done = f32[32,1024]{1,0:T(8,128)} async-done(((f32[1024,1024]{1,0:T(8,128)}), f32[32,1024]{1,0:T(8,128)}) %reduce-scatter.15.cloned.1.call-update) | async-done | bytes 131088 | tf_op jit(solution)/shard_map/reduce_scatter | solution.py:319
  (300 shorter events, 221.5 us)
Async XLA Ops:
  7.2 71.2 %copy-start = (bf16[256,1024]{1,0:T(8,128)(2,1)S(1)}, bf16[256,1024]{1,0:T(8,128)(2,1)}, u32[]{:S(2)}) copy-start(bf16[256,1024]{1,0:T(8,128)(2,1)} %param.18) | copy-start | bytes 1572868
  7.2 71.2 %all-gather.8.cloned.1.call-start = ((), (), s32[]{:S(2)}) async-start(), calls=%async_computation.12 | async-start | bytes 1081344 | tf_op jit(solution)/shard_map/all_gather | solution.py:93
  7.9 115.7 %all-gather.10.cloned.1.call-start = ((), (), s32[]{:S(2)}) async-start(), calls=%async_computation.13 | async-start | bytes 1081344 | tf_op jit(solution)/shard_map/all_gather | solution.py:92
  8.7 173.3 %all-gather.12.cloned.1.call-start = ((), (), s32[]{:S(2)}) async-start(), calls=%async_computation.14 | async-start | bytes 2162688 | tf_op jit(solution)/shard_map/all_gather | solution.py:91
  9.4 230.7 %all-gather.14.cloned.1.call-start = ((), (), s32[]{:S(2)}) async-start(), calls=%async_computation.15 | async-start | bytes 2162688 | tf_op jit(solution)/shard_map/all_gather | solution.py:94
  10.0 355.5 %all-gather.16.cloned.1.call-start = ((), (), s32[]{:S(2)}) async-start(), calls=%async_computation.16 | async-start | bytes 9437184 | tf_op jit(solution)/shard_map/all_gather | solution.py:99
  10.6 479.6 %all-gather.18.cloned.1.call-start = ((), (), s32[]{:S(2)}) async-start(), calls=%async_computation.17 | async-start | bytes 9437184 | tf_op jit(solution)/shard_map/all_gather | solution.py:100
  11.1 603.9 %all-gather.20.cloned.1.call-start = ((), (), s32[]{:S(2)}) async-start(), calls=%async_computation.18 | async-start | bytes 9437184 | tf_op jit(solution)/shard_map/all_gather | solution.py:101
  57.3 127.3 %copy-start.18 = (f32[1024]{0:T(1024)}, f32[1024]{0:T(1024)S(1)}, u32[]{:S(2)}) copy-start(f32[1024]{0:T(1024)S(1)} %convert_element_type.152) | copy-start | bytes 12292
  59.1 125.5 %copy-start.26 = (f32[256]{0:T(256)}, f32[256]{0:T(256)S(1)}, u32[]{:S(2)}) copy-start(f32[256]{0:T(256)S(1)} %get-tuple-element.213) | copy-start | bytes 3076
  59.3 125.3 %copy-start.11 = (f32[256,32]{0,1:T(8,128)}, f32[256,32]{0,1:T(8,128)S(1)}, u32[]{:S(2)}) copy-start(f32[256,32]{0,1:T(8,128)S(1)} %get-tuple-element.216) | copy-start | bytes 98308
  59.3 125.3 %copy-start.13 = (f32[256,32]{0,1:T(8,128)}, f32[256,32]{0,1:T(8,128)S(1)}, u32[]{:S(2)}) copy-start(f32[256,32]{0,1:T(8,128)S(1)} %get-tuple-element.217) | copy-start | bytes 98308
  60.0 750.6 %copy-start.20 = (f32[1024]{0:T(1024)}, f32[1024]{0:T(1024)S(1)}, u32[]{:S(2)}) copy-start(f32[1024]{0:T(1024)S(1)} %convert_element_type.155) | copy-start | bytes 12292
  195.3 62.0 %copy-start.15 = (bf16[8,256,2,64]{1,3,2,0:T(8,128)(2,1)}, bf16[8,256,2,64]{1,3,2,0:T(8,128)(2,1)S(1)}, u32[]{:S(2)}) copy-start(bf16[8,256,2,64]{1,3,2,0:T(8,128)(2,1)S(1)} %get-tuple-element.444) | copy-start | bytes 1572868
  195.3 62.0 %copy-start.17 = (bf16[8,256,64]{1,2,0:T(8,128)(2,1)}, bf16[8,256,64]{1,2,0:T(8,128)(2,1)S(1)}, u32[]{:S(2)}) copy-start(bf16[8,256,64]{1,2,0:T(8,128)(2,1)S(1)} %get-tuple-element.445) | copy-start | bytes 786436
  243.1 567.5 %copy-start.28 = (f32[256]{0:T(256)}, f32[256]{0:T(256)S(1)}, u32[]{:S(2)}) copy-start(f32[256]{0:T(256)S(1)} %get-tuple-element.215) | copy-start | bytes 3076
  626.1 107.4 %copy-start.16 = (s32[256,8]{0,1:T(8,128)S(1)}, s32[256,8]{0,1:T(8,128)}, u32[]{:S(2)}) copy-start(s32[256,8]{0,1:T(8,128)} %param.21) | copy-start | bytes 24580
  626.1 116.4 %copy-start.30 = (bf16[32,32]{1,0:T(8,128)(2,1)S(1)}, bf16[32,32]{1,0:T(8,128)(2,1)}, u32[]{:S(2)}) copy-start(bf16[32,32]{1,0:T(8,128)(2,1)} %param.28) | copy-start | bytes 6148
  626.1 203.2 %all-to-all-start.1 = ((bf16[4,8,96,1024]{3,2,1,0:T(8,128)(2,1)}), bf16[4,8,96,1024]{3,2,1,0:T(8,128)(2,1)}, u32[]{:S(2)}, u32[]{:S(2)}) async-start(bf16[4,8,96,1024]{3,2,1,0:T(8,128)(2,1)} %copy.163), calls=%async_computation.1 | async-start | bytes 12582912 | tf_op jit(solution)/shard_map/all_to_all | solution.py:193
  631.5 614.2 %reduce-scatter.23.cloned.1.call-start = ((), (), s32[]{:S(2)}) async-start(), calls=%async_computation.26 | async-start | bytes 9437184 | tf_op jit(solution)/shard_map/reduce_scatter | solution.py:330
  872.6 77.6 %copy-start.33 = (bf16[4,8,96,512]{3,2,0,1:T(8,128)(2,1)S(1)}, bf16[4,8,96,512]{3,2,0,1:T(8,128)(2,1)}, u32[]{:S(2)}) copy-start(bf16[4,8,96,512]{3,2,0,1:T(8,128)(2,1)} %get-tuple-element.220) | copy-start | bytes 9437188
  959.7 295.3 %reduce-scatter.19.cloned.1.call-start = ((), (), s32[]{:S(2)}) async-start(), calls=%async_computation.24 | async-start | bytes 9437184 | tf_op jit(solution)/shard_map/reduce_scatter | solution.py:324
  987.1 417.9 %reduce-scatter.21.cloned.1.call-start = ((), (), s32[]{:S(2)}) async-start(), calls=%async_computation.25 | async-start | bytes 9437184 | tf_op jit(solution)/shard_map/reduce_scatter | solution.py:327
  1031.6 76.1 %all-to-all-start.3 = ((bf16[4,8,96,1024]{3,2,1,0:T(8,128)(2,1)}), bf16[4,8,96,1024]{3,2,1,0:T(8,128)(2,1)}, u32[]{:S(2)}, u32[]{:S(2)}) async-start(bf16[4,8,96,1024]{3,2,1,0:T(8,128)(2,1)} %copy.166), calls=%async_computation.3 | async-start | bytes 12582912 | tf_op jit(solution)/shard_map/all_to_all | solution.py:254
  1037.1 505.7 %reduce-scatter.17.cloned.1.call-start = ((), (), s32[]{:S(2)}) async-start(), calls=%async_computation.23 | async-start | bytes 540672 | tf_op jit(solution)/shard_map/reduce_scatter | solution.py:321
  1044.8 636.2 %reduce-scatter.11.cloned.1.call-start = ((), (), s32[]{:S(2)}) async-start(), calls=%async_computation.20 | async-start | bytes 2162688 | tf_op jit(solution)/shard_map/reduce_scatter | solution.py:317
  1131.4 54.2 %copy-start.1 = (bf16[256,1024]{1,0:T(8,128)(2,1)S(1)}, bf16[256,1024]{1,0:T(8,128)(2,1)}, u32[]{:S(2)}) copy-start(bf16[256,1024]{1,0:T(8,128)(2,1)} %param.18) | copy-start | bytes 1572868
  1131.5 54.2 %copy-start.19 = (f32[1024]{0:T(1024)S(1)}, f32[1024]{0:T(1024)}, u32[]{:S(2)}) copy-start(f32[1024]{0:T(1024)} %copy-done.18) | copy-start | bytes 12292
  1131.5 54.2 %copy-start.27 = (f32[256]{0:T(256)S(1)}, f32[256]{0:T(256)}, u32[]{:S(2)}) copy-start(f32[256]{0:T(256)} %copy-done.26) | copy-start | bytes 3076
  1187.7 632.1 %reduce-scatter.13.cloned.1.call-start = ((), (), s32[]{:S(2)}) async-start(), calls=%async_computation.21 | async-start | bytes 2162688 | tf_op jit(solution)/shard_map/reduce_scatter | solution.py:318
  1189.8 773.6 %reduce-scatter.9.cloned.1.call-start = ((), (), s32[]{:S(2)}) async-start(), calls=%async_computation.19 | async-start | bytes 4325376 | tf_op jit(solution)/shard_map/reduce_scatter | solution.py:316
  1194.5 914.3 %reduce-scatter.15.cloned.1.call-start = ((), (), s32[]{:S(2)}) async-start(), calls=%async_computation.22 | async-start | bytes 4325376 | tf_op jit(solution)/shard_map/reduce_scatter | solution.py:319
  (19 other events, 402.0 us)
Sparse Core Ops, SparseCore 0:
  11.0 56.6 all-gather.7
  70.7 52.8 all-gather.9
  126.6 55.3 all-gather.11
  184.8 55.2 all-gather.13
  242.2 123.2 all-gather.15
  367.5 122.6 all-gather.17
  492.4 122.6 all-gather.19
  959.8 143.6 reduce-scatter.22
  1107.2 147.7 reduce-scatter.18
  1258.5 146.5 reduce-scatter.20
  1407.9 134.8 reduce-scatter.16
  1545.5 135.4 reduce-scatter.10
  1683.8 135.8 reduce-scatter.12
  1822.5 140.8 reduce-scatter.8
  1966.0 142.6 reduce-scatter.14
where the time goes:
time: 2130 us; the launch traced here: 2120 us
  waiting for transfers between devices  1320 us (62%)
  blocking collectives  407 us (19%)
  matrix products  186 us (9%)
  local copies, waits for them, and re-layouts  119 us (6%)
  other arithmetic  51.7 us (2%)
    reduce_scatter x1, waiting for transfers between devices, on_device(): lax.psum_scatter(up_grad_w.astype(jnp.bfloat16), 'fsdp', scatter_dimensio...  147 us
    reduce_scatter x1, waiting for transfers between devices, on_device(): lax.psum_scatter(out_grad_w, ('dp', 'fsdp'), scatter_dimension=0, tiled=T...  145 us
    reduce_scatter x1, waiting for transfers between devices, on_device(): lax.psum_scatter(query_grad_w, ('dp', 'fsdp'), scatter_dimension=0, tiled...  144 us
    psum x2, blocking collectives, on_device(): lax.psum((part_loss, length_float), ('dp', 'fsdp'))  142 us
    reduce_scatter x1, waiting for transfers between devices, on_device(): lax.psum_scatter(value_grad_w, ('dp', 'fsdp'), scatter_dimension=0, tiled...  139 us
    reduce_scatter x1, waiting for transfers between devices, on_device(): lax.psum_scatter(key_grad_w, ('dp', 'fsdp'), scatter_dimension=0, tiled=T...  138 us
    reduce_scatter x1, waiting for transfers between devices, on_device(): lax.psum_scatter(router_grad, ('dp', 'fsdp'), scatter_dimension=0, tiled=...  135 us
    all_gather x1, waiting for transfers between devices, on_device(): lax.all_gather(expert_up, 'fsdp', axis=1, tiled=True)  113 us
  transfers between devices with their start and end apart: 17, of which 14 were waited for; matrix products, arithmetic and copies ran while one was open for 14% of the time, Pallas kernels for 0%

commit v1 on v0

v1 whole, which is shorter than its diff:
```python
import functools

import jax
import jax.numpy as jnp
from jax import lax
from jax.experimental import pallas as pl
from jax.experimental.pallas import tpu as pltpu
from jax.sharding import PartitionSpec as P

HEADS = 16
KV_HEADS = 8
HEAD_DIM = 64
CAP = 96
HOPS = 4
CORES = 2

epsilon = 1e-06
score_scale = 0.015625
residual_scale = 0.22
rotary_base = 10000.0
masked_score = -1e30
highest = lax.Precision.HIGHEST
bf16 = jnp.bfloat16
f32 = jnp.float32


def dot(a, b):
    return lax.dot_general(a, b, (((1,), (0,)), ((), ())), preferred_element_type=f32)


def dot_nt(a, b):
    return lax.dot_general(a, b, (((1,), (1,)), ((), ())), preferred_element_type=f32)


def dot_tn(a, b):
    return lax.dot_general(a, b, (((0,), (0,)), ((), ())), preferred_element_type=f32)


def swap(values, axis, mask):
    return lax.ppermute(values, axis, [(i, i ^ mask) for i in range(lax.axis_size(axis))])


def vmem():
    return pl.BlockSpec(memory_space=pltpu.VMEM)


def smem():
    return pl.BlockSpec(memory_space=pltpu.SMEM)


def kernel_call(body, out_shape, operands, first_smem=False, scratch=()):
    specs = [vmem() for _ in operands]
    if first_smem:
        specs[0] = smem()
    return pl.pallas_call(
        body,
        out_shape=out_shape,
        in_specs=specs,
        out_specs=jax.tree.map(lambda _: vmem(), out_shape),
        scratch_shapes=scratch,
        compiler_params=pltpu.CompilerParams(vmem_limit_bytes=56 * 1024 * 1024),
    )(*operands)


def rotary_lanes(seq_len):
    half_dim = HEAD_DIM // 2
    positions = jnp.arange(seq_len, dtype=f32)
    frequency = rotary_base ** (-jnp.arange(half_dim, dtype=f32) / half_dim)
    angles = positions[:, None] * frequency[None, :]
    cos_part, sin_part = jnp.cos(angles), jnp.sin(angles)
    cos_lanes = jnp.concatenate([cos_part] * 4, axis=1)
    sin_lanes = jnp.concatenate([-sin_part, sin_part] * 2, axis=1)
    return cos_lanes, sin_lanes


def half_swap(values):
    lane = lax.broadcasted_iota(jnp.int32, values.shape, 1)
    ahead = pltpu.roll(values, 128 - HEAD_DIM // 2, 1)
    behind = pltpu.roll(values, HEAD_DIM // 2, 1)
    return jnp.where(lane % HEAD_DIM < HEAD_DIM // 2, ahead, behind)


def allowed_mask(seq_len, length):
    row = lax.broadcasted_iota(jnp.int32, (seq_len, seq_len), 0)
    col = lax.broadcasted_iota(jnp.int32, (seq_len, seq_len), 1)
    return (col <= row) & (col < length)


def soft_rows(query_h, key_h, allowed):
    scores = jnp.where(allowed, score_scale * dot_nt(query_h, key_h), masked_score)
    weights = jnp.exp(scores - jnp.max(scores, axis=-1, keepdims=True))
    return weights / jnp.sum(weights, axis=-1, keepdims=True)


def attention_forward(length_ref, qkv_ref, cos_ref, sin_ref, rot_ref, mixed_ref):
    seq_len = qkv_ref.shape[0]
    width = HEADS * HEAD_DIM
    kv_width = KV_HEADS * HEAD_DIM
    group = HEADS // KV_HEADS
    cos_lanes, sin_lanes = cos_ref[...], sin_ref[...]
    for lanes in range(0, width + kv_width, 128):
        part = qkv_ref[:, lanes : lanes + 128]
        rot_ref[:, lanes : lanes + 128] = (part * cos_lanes + half_swap(part) * sin_lanes).astype(
            bf16
        )
    rot_ref[:, width + kv_width :] = qkv_ref[:, width + kv_width :].astype(bf16)
    allowed = allowed_mask(seq_len, length_ref[0])
    for head in range(HEADS):
        at = head * HEAD_DIM
        key_at = width + (head // group) * HEAD_DIM
        value_at = key_at + kv_width
        soft = soft_rows(
            rot_ref[:, at : at + HEAD_DIM], rot_ref[:, key_at : key_at + HEAD_DIM], allowed
        )
        mixed_ref[:, at : at + HEAD_DIM] = dot(
            soft.astype(bf16), rot_ref[:, value_at : value_at + HEAD_DIM]
        ).astype(bf16)


def attention_backward(length_ref, rot_ref, grad_ref, cos_ref, sin_ref, out_ref, work_ref):
    seq_len = rot_ref.shape[0]
    width = HEADS * HEAD_DIM
    kv_width = KV_HEADS * HEAD_DIM
    group = HEADS // KV_HEADS
    allowed = allowed_mask(seq_len, length_ref[0])
    for kv_head in range(KV_HEADS):
        key_at = width + kv_head * HEAD_DIM
        value_at = key_at + kv_width
        key_h = rot_ref[:, key_at : key_at + HEAD_DIM]
        value_h = rot_ref[:, value_at : value_at + HEAD_DIM]
        key_grad = jnp.zeros((seq_len, HEAD_DIM), f32)
        value_grad = jnp.zeros((seq_len, HEAD_DIM), f32)
        for head in range(kv_head * group, kv_head * group + group):
            at = head * HEAD_DIM
            query_h = rot_ref[:, at : at + HEAD_DIM]
            grad_h = grad_ref[:, at : at + HEAD_DIM]
            soft = soft_rows(query_h, key_h, allowed)
            soft_grad = dot_nt(grad_h, value_h)
            value_grad = value_grad + dot_tn(soft.astype(bf16), grad_h)
            delta = jnp.sum(soft * soft_grad, axis=-1, keepdims=True)
            score_grad = (score_scale * (soft * (soft_grad - delta))).astype(bf16)
            work_ref[:, at : at + HEAD_DIM] = dot(score_grad, key_h)
            key_grad = key_grad + dot_tn(score_grad, query_h)
        work_ref[:, key_at : key_at + HEAD_DIM] = key_grad
        out_ref[:, value_at : value_at + HEAD_DIM] = value_grad.astype(bf16)
    cos_lanes, sin_lanes = cos_ref[...], sin_ref[...]
    for lanes in range(0, width + kv_width, 128):
        part = work_ref[:, lanes : lanes + 128]
        out_ref[:, lanes : lanes + 128] = (part * cos_lanes - half_swap(part) * sin_lanes).astype(
            bf16
        )


def slot_match(place_row, seq_len):
    slot = lax.broadcasted_iota(jnp.int32, (CAP, seq_len), 0)
    return slot == place_row.astype(jnp.int32)


def expert_forward(count, seq_len, *refs):
    place_ref, gates_ref, wide_ref, down_ref = refs[:4]
    token_refs = refs[4 : 4 + count]
    out_refs = refs[4 + count : 4 + 2 * count]
    picked_ref, = refs[4 + 2 * count :]
    held = wide_ref.shape[0]
    hidden_units = down_ref.shape[1]
    for e in range(held):
        gate_slots = []
        for s in range(count):
            match = slot_match(place_ref[s, e : e + 1, :], seq_len)
            gate_slots.append(
                jnp.sum(jnp.where(match, gates_ref[s, e : e + 1, :], 0.0), axis=1, keepdims=True)
            )
            picked_ref[s * CAP : s * CAP + CAP, :] = dot(
                match.astype(f32).astype(bf16), token_refs[s][:seq_len, :]
            ).astype(bf16)
        pre = dot(picked_ref[...], wide_ref[e])
        gate_pre, up_pre = pre[:, :hidden_units], pre[:, hidden_units:]
        inner = (gate_pre / (1.0 + jnp.exp(-gate_pre)) * up_pre).astype(bf16)
        scaled = (dot(inner, down_ref[e]) * jnp.concatenate(gate_slots, axis=0)).astype(bf16)
        for s in range(count):
            match = slot_match(place_ref[s, e : e + 1, :], seq_len).astype(f32).astype(bf16)
            part = dot_tn(match, scaled[s * CAP : s * CAP + CAP, :])
            if e == 0:
                part_prev = part
            else:
                part_prev = out_refs[s][...].astype(f32) + part
            out_refs[s][...] = part_prev.astype(bf16)


def expert_backward(count, seq_len, *refs):
    place_ref, gates_ref, wide_ref, down_ref = refs[:4]
    token_refs = refs[4 : 4 + count]
    grad_refs = refs[4 + count : 4 + 2 * count]
    out_refs = refs[4 + 2 * count : 4 + 3 * count]
    gate_grad_ref, picked_ref, wide_grad_ref, routed_ref, inner_ref = refs[4 + 3 * count : 9 + 3 * count]
    acc_ref, = refs[9 + 3 * count :]
    held = wide_ref.shape[0]
    hidden_units = down_ref.shape[1]
    for e in range(held):
        gate_slots = []
        for s in range(count):
            match = slot_match(place_ref[s, e : e + 1, :], seq_len)
            gate_slots.append(
                jnp.sum(jnp.where(match, gates_ref[s, e : e + 1, :], 0.0), axis=1, keepdims=True)
            )
            select = match.astype(f32).astype(bf16)
            at = s * CAP
            picked_ref[e, at : at + CAP, :] = dot(select, token_refs[s][:seq_len, :]).astype(bf16)
            routed_ref[e, at : at + CAP, :] = dot(select, grad_refs[s][:seq_len, :]).astype(bf16)
        gate_col = residual_scale * jnp.concatenate(gate_slots, axis=0)
        pre = dot(picked_ref[e], wide_ref[e])
        gate_pre, up_pre = pre[:, :hidden_units], pre[:, hidden_units:]
        sigmoid = 1.0 / (1.0 + jnp.exp(-gate_pre))
        silu = gate_pre * sigmoid
        inner = (silu * up_pre).astype(bf16)
        inner_ref[e] = inner
        back = dot_nt(routed_ref[e], down_ref[e])
        gate_grad = residual_scale * jnp.sum(inner.astype(f32) * back, axis=1, keepdims=True)
        inner_grad = gate_col * back
        wide_grad_ref[e, :, :hidden_units] = (
            inner_grad * up_pre * sigmoid * (1.0 + gate_pre * (1.0 - sigmoid))
        ).astype(bf16)
        wide_grad_ref[e, :, hidden_units:] = (inner_grad * silu).astype(bf16)
        routed_ref[e] = (routed_ref[e].astype(f32) * gate_col).astype(bf16)
        arrived = dot_nt(wide_grad_ref[e], wide_ref[e]).astype(bf16)
        for s in range(count):
            match = slot_match(place_ref[s, e : e + 1, :], seq_len)
            at = s * CAP
            gate_grad_ref[s, e : e + 1, :] = jnp.sum(
                jnp.where(match, gate_grad[at : at + CAP, :], 0.0), axis=0, keepdims=True
            )
            part = dot_tn(match.astype(f32).astype(bf16), arrived[at : at + CAP, :])
            if e == 0:
                acc_ref[s] = part
            elif e < held - 1:
                acc_ref[s] = acc_ref[s] + part
            if e == held - 1:
                out_refs[s][...] = (part if e == 0 else acc_ref[s] + part).astype(bf16)


def expert_weight_grads(groups, *refs):
    picked = refs[:groups]
    wide_grads = refs[groups : 2 * groups]
    routed = refs[2 * groups : 3 * groups]
    inner = refs[3 * groups : 4 * groups]
    wide_ref, down_ref = refs[4 * groups :]
    wide = dot_tn(picked[0][0], wide_grads[0][0])
    down = dot_tn(inner[0][0], routed[0][0])
    for k in range(1, groups):
        wide = wide + dot_tn(picked[k][0], wide_grads[k][0])
        down = down + dot_tn(inner[k][0], routed[k][0])
    wide_ref[0] = wide.astype(bf16)
    down_ref[0] = down.astype(bf16)


def norm_back(grad_rows, rows_in, inverse, gain_vec):
    scaled = grad_rows * gain_vec
    gain_grad = jnp.sum(grad_rows * rows_in * inverse, axis=0)
    cubed = inverse * inverse * inverse
    rows_grad = inverse * scaled - rows_in * cubed * jnp.mean(
        scaled * rows_in, axis=1, keepdims=True
    )
    return (rows_grad, gain_grad)


def in_order(own, others, place):
    blocks = [own, *others]
    bit = 1
    while bit < len(blocks):
        flip = (place & bit) != 0
        swapped = [jnp.where(flip, blocks[i ^ bit], blocks[i]) for i in range(len(blocks))]
        blocks = swapped
        bit *= 2
    return blocks


def on_device(
    tokens,
    teacher,
    lengths,
    routes,
    gain_attn,
    w_query,
    w_key,
    w_value,
    w_out,
    gain_ffn,
    w_router,
    expert_gate,
    expert_up,
    expert_down,
):
    seq_len, model_width = tokens.shape
    groups = lax.axis_size("dp")
    shards = lax.axis_size("fsdp")
    owned = expert_gate.shape[0]
    experts = owned * groups
    lows = shards // HOPS
    rows_y = groups // CORES
    held = owned // HOPS
    hidden_units = expert_gate.shape[2]
    row_block = w_query.shape[0]
    kv_width = KV_HEADS * HEAD_DIM
    dp_at = lax.axis_index("dp")
    fsdp_at = lax.axis_index("fsdp")
    hop_at, low_at = fsdp_at // lows, fsdp_at % lows
    y_at, core_at = dp_at // CORES, dp_at % CORES

    def gather_sets(values):
        per_hop = [values] + [swap(values, "fsdp", lows * k) for k in range(1, HOPS)]
        sets = []
        for mine in per_hop:
            columns = [mine] + [swap(mine, "dp", CORES * j) for j in range(1, rows_y)]
            for column in columns:
                sets.extend([column, swap(column, "dp", 1)])
        return sets

    def return_sets(parts):
        total = None
        for k in range(HOPS):
            columns = []
            for j in range(rows_y):
                at = (k * rows_y + j) * CORES
                got = swap(parts[at + 1], "dp", 1)
                columns.append(parts[at].astype(f32) + got.astype(f32))
            mine = columns[0]
            for j in range(1, rows_y):
                mine = mine + swap(columns[j].astype(bf16), "dp", CORES * j).astype(f32)
            if k:
                mine = swap(mine.astype(bf16), "fsdp", lows * k).astype(f32)
            total = mine if total is None else total + mine
        return total

    def gather_dense(block):
        wide = block.shape[1]
        full = block.reshape(1, 1, 1, 1, row_block, wide)
        full = jnp.concatenate(
            in_order(full, [swap(full, "fsdp", lows * k) for k in range(1, HOPS)], hop_at), axis=2
        )
        full = jnp.concatenate(
            in_order(full, [swap(full, "dp", CORES * j) for j in range(1, rows_y)], y_at), axis=0
        )
        full = jnp.concatenate(
            in_order(full, [swap(full, "fsdp", m) for m in range(1, lows)], low_at), axis=3
        )
        full = jnp.concatenate(in_order(full, [swap(full, "dp", 1)], core_at), axis=1)
        return full.reshape(groups * shards * row_block, wide)

    def scatter_dense(grads):
        wide = grads.shape[1]
        part = grads.reshape(rows_y, CORES, HOPS, lows, row_block, wide)

        def stage(part, axis, name, place, size, unit):
            mine = lax.dynamic_slice_in_dim(part, place, 1, axis)
            for m in range(1, size):
                give = lax.dynamic_slice_in_dim(part, place ^ m, 1, axis).astype(bf16)
                mine = mine + swap(give, name, unit * m).astype(f32)
            return mine

        part = stage(part, 1, "dp", core_at, CORES, 1)
        part = stage(part, 0, "dp", y_at, rows_y, CORES)
        part = stage(part, 3, "fsdp", low_at, lows, 1)
        part = stage(part, 2, "fsdp", hop_at, HOPS, lows)
        return part.reshape(row_block, wide)

    expert_ids = jnp.arange(experts, dtype=jnp.int32)
    member = jnp.any(routes[:, :, None] == expert_ids[None, None, :], axis=1)
    positions = jnp.arange(seq_len, dtype=jnp.int32)
    before = (positions[None, :] < positions[:, None]).astype(bf16)
    rank = dot(before, member.astype(bf16))
    place = jnp.where(member, rank, -1.0).T.astype(bf16)
    first_held = dp_at * owned + hop_at * held
    place_sets = jnp.stack(
        [lax.dynamic_slice_in_dim(p, first_held, held, 0) for p in gather_sets(place)]
    ).astype(f32)

    length_col = jnp.zeros((row_block, 1), bf16).at[0, 0].set(lengths[0].astype(bf16))
    pack = jnp.concatenate(
        [
            w_query,
            w_key,
            w_value,
            w_router,
            gain_attn[:, None],
            gain_ffn[:, None],
            length_col,
            jnp.zeros((row_block, 128 - experts - 3), bf16),
        ],
        axis=1,
    )
    packed = gather_dense(pack)
    qkv_width = model_width + 2 * kv_width
    qkv_w = packed[:, :qkv_width]
    router_float = packed[:, qkv_width : qkv_width + experts].astype(f32)
    gain_float = packed[:, qkv_width + experts].astype(f32)
    gain_second = packed[:, qkv_width + experts + 1].astype(f32)
    valid_total = jnp.sum(packed[:, qkv_width + experts + 2].astype(f32))
    out_w = gather_dense(w_out)

    def gather_expert(shard):
        def owned_by(k):
            return lax.dynamic_slice_in_dim(shard, (hop_at ^ k) * held, held, 0)

        per_hop = [owned_by(0)] + [swap(owned_by(k), "fsdp", lows * k) for k in range(1, HOPS)]
        rows = shard.shape[1]
        full = jnp.zeros((held, shards * rows, shard.shape[2]), bf16)
        for k in range(HOPS):
            for m in range(lows):
                block = per_hop[k] if m == 0 else swap(per_hop[k], "fsdp", m)
                at = ((hop_at ^ k) * lows + (low_at ^ m)) * rows
                full = lax.dynamic_update_slice(full, block, (0, at, 0))
        return full

    wide_w = gather_expert(jnp.concatenate([expert_gate, expert_up], axis=2))
    down_w = gather_expert(expert_down)

    tok_float = tokens.astype(f32)
    inv_one = lax.rsqrt(jnp.mean(tok_float * tok_float, axis=1, keepdims=True) + epsilon)
    normed = (tok_float * inv_one * gain_float).astype(bf16)
    cos_lanes, sin_lanes = rotary_lanes(seq_len)
    qkv = dot(normed, qkv_w)
    rotated, mixed_rows = kernel_call(
        attention_forward,
        (
            jax.ShapeDtypeStruct((seq_len, qkv_width), bf16),
            jax.ShapeDtypeStruct((seq_len, HEADS * HEAD_DIM), bf16),
        ),
        (lengths, qkv, cos_lanes, sin_lanes),
        first_smem=True,
    )
    hidden = tok_float + residual_scale * dot(mixed_rows, out_w)
    inv_two = lax.rsqrt(jnp.mean(hidden * hidden, axis=1, keepdims=True) + epsilon)
    normed_ffn = hidden * inv_two * gain_second
    logits = jnp.dot(normed_ffn, router_float, precision=highest, preferred_element_type=f32)
    masked = jnp.where(member, logits, -jnp.inf)
    powers = jnp.exp(masked - jnp.max(masked, axis=1, keepdims=True))
    gate_weights = powers / jnp.sum(powers, axis=1, keepdims=True)

    gate_rows = seq_len * experts // model_width
    gate_high = gate_weights.T.astype(bf16)
    outgoing = jnp.concatenate(
        [normed_ffn.astype(bf16), gate_high.reshape(gate_rows, model_width)], axis=0
    )
    token_sets = gather_sets(outgoing)
    count = rows_y * CORES
    gate_sets = [
        lax.dynamic_slice_in_dim(
            s[seq_len:].reshape(experts, seq_len), first_held, held, 0
        ).astype(f32)
        for s in token_sets
    ]
    set_shape = jax.ShapeDtypeStruct((seq_len, model_width), bf16)
    parts = []
    per_hop = []
    for k in range(HOPS):
        at = slice(k * count, k * count + count)
        common = (place_sets[at], jnp.stack(gate_sets[at]), wide_w, down_w, *token_sets[at])
        per_hop.append(common)
        parts.extend(
            kernel_call(
                functools.partial(expert_forward, count, seq_len),
                (set_shape,) * count,
                common,
                scratch=(pltpu.VMEM((count * CAP, model_width), bf16),),
            )
        )
    combined = return_sets(parts)
    output = hidden + residual_scale * combined
    valid_rows = (positions < lengths[0]).astype(f32)[:, None]
    deviation = (output - teacher.astype(f32)) * valid_rows
    slot_total = seq_len * groups * shards
    out_grad = deviation * (slot_total / valid_total)

    loss_total = jnp.full((8, 128), jnp.sum(deviation * deviation), f32)
    for name, size in (("dp", groups), ("fsdp", shards)):
        mask = 1
        while mask < size:
            loss_total = loss_total + swap(loss_total, name, mask)
            mask *= 2
    loss_value = loss_total[0, 0] / (valid_total * model_width)

    grad_sets = gather_sets(out_grad.astype(bf16))
    parts = []
    saved = []
    for k in range(HOPS):
        rows = count * CAP
        results = kernel_call(
            functools.partial(expert_backward, count, seq_len),
            (set_shape,) * count
            + (
                jax.ShapeDtypeStruct((count, held, seq_len), f32),
                jax.ShapeDtypeStruct((held, rows, model_width), bf16),
                jax.ShapeDtypeStruct((held, rows, 2 * hidden_units), bf16),
                jax.ShapeDtypeStruct((held, rows, model_width), bf16),
                jax.ShapeDtypeStruct((held, rows, hidden_units), bf16),
            ),
            (*per_hop[k], *grad_sets[k * count : k * count + count]),
            scratch=(pltpu.VMEM((count, seq_len, model_width), f32),),
        )
        gate_grads = results[count]
        saved.append(results[count + 1 :])
        for s in range(count):
            spread = lax.dynamic_update_slice(
                jnp.zeros((experts, seq_len), f32), gate_grads[s], (first_held, 0)
            )
            high = spread.astype(bf16)
            low = (spread - high.astype(f32)).astype(bf16)
            parts.append(
                jnp.concatenate(
                    [
                        results[s],
                        high.reshape(gate_rows, model_width),
                        low.reshape(gate_rows, model_width),
                    ],
                    axis=0,
                )
            )
    returned = return_sets(parts)
    rows = count * CAP
    wide_grad, down_grad = pl.pallas_call(
        functools.partial(expert_weight_grads, HOPS),
        grid=(held,),
        out_shape=(
            jax.ShapeDtypeStruct((held, model_width, 2 * hidden_units), bf16),
            jax.ShapeDtypeStruct((held, hidden_units, model_width), bf16),
        ),
        in_specs=[
            pl.BlockSpec((1, rows, width), lambda e: (e, 0, 0))
            for width in (model_width, 2 * hidden_units, model_width, hidden_units)
            for _ in range(HOPS)
        ],
        out_specs=(
            pl.BlockSpec((1, model_width, 2 * hidden_units), lambda e: (e, 0, 0)),
            pl.BlockSpec((1, hidden_units, model_width), lambda e: (e, 0, 0)),
        ),
        compiler_params=pltpu.CompilerParams(vmem_limit_bytes=60 * 1024 * 1024),
    )(*[saved[k][i] for i in range(4) for k in range(HOPS)])

    def scatter_expert(grads):
        rows = grads.shape[1] // shards
        width = grads.shape[2]
        part = grads.reshape(held, HOPS, lows, rows, width)
        mine = lax.dynamic_slice_in_dim(part, low_at, 1, 2).astype(f32)
        for m in range(1, lows):
            give = lax.dynamic_slice_in_dim(part, low_at ^ m, 1, 2)
            mine = mine + swap(give, "fsdp", m).astype(f32)
        mine = mine.reshape(held, HOPS, rows, width)
        out = jnp.zeros((owned, rows, width), f32)
        for k in range(HOPS):
            block = lax.dynamic_slice_in_dim(mine, hop_at ^ k, 1, 1).reshape(held, rows, width)
            if k:
                block = swap(block.astype(bf16), "fsdp", lows * k).astype(f32)
            out = lax.dynamic_update_slice(out, block, ((hop_at ^ k) * held, 0, 0))
        return out

    wide_out = scatter_expert(wide_grad)
    expert_grads = (
        wide_out[:, :, :hidden_units],
        wide_out[:, :, hidden_units:],
        scatter_expert(down_grad),
    )

    gate_grad = (
        (returned[seq_len : seq_len + gate_rows] + returned[seq_len + gate_rows :])
        .reshape(experts, seq_len)
        .T
    )
    logit_grad = gate_weights * (
        gate_grad - jnp.sum(gate_weights * gate_grad, axis=1, keepdims=True)
    )
    router_grad = jnp.einsum(
        "td,te->de", normed_ffn, logit_grad, precision=highest, preferred_element_type=f32
    )
    ffn_in_grad = returned[:seq_len] + jnp.einsum(
        "te,de->td", logit_grad, router_float, precision=highest, preferred_element_type=f32
    )
    hidden_part, gain_two_grad = norm_back(ffn_in_grad, hidden, inv_two, gain_second)
    hidden_grad = out_grad + hidden_part
    attended_grad = (residual_scale * hidden_grad).astype(bf16)
    out_grad_w = scatter_dense(dot_tn(mixed_rows, attended_grad))
    mixed_grad = dot_nt(attended_grad, out_w).astype(bf16)
    qkv_grad = kernel_call(
        attention_backward,
        jax.ShapeDtypeStruct((seq_len, qkv_width), bf16),
        (lengths, rotated, mixed_grad, cos_lanes, sin_lanes),
        first_smem=True,
        scratch=(pltpu.VMEM((seq_len, model_width + kv_width), f32),),
    )
    normed_grad = dot_nt(qkv_grad, qkv_w)
    token_part, gain_one_grad = norm_back(normed_grad, tok_float, inv_one, gain_float)
    token_grad = hidden_grad + token_part
    small = scatter_dense(
        jnp.concatenate(
            [
                dot_tn(normed, qkv_grad),
                router_grad,
                gain_one_grad[:, None],
                gain_two_grad[:, None],
                jnp.zeros((model_width, 128 - experts - 2), f32),
            ],
            axis=1,
        )
    )
    return (
        output.astype(bf16),
        loss_value,
        token_grad,
        small[:, qkv_width + experts],
        small[:, :model_width],
        small[:, model_width : model_width + kv_width],
        small[:, model_width + kv_width : qkv_width],
        out_grad_w,
        small[:, qkv_width + experts + 1],
        small[:, qkv_width : qkv_width + experts],
        *expert_grads,
    )


def solution(mesh):
    both = ("dp", "fsdp")
    rows = P(both, None)
    expert = P("dp", "fsdp", None)
    in_specs = (rows, rows, P(both), rows, P(both), rows, rows, rows, rows, P(both), rows)
    in_specs = in_specs + (expert, expert, expert)
    out_specs = (rows, P(), rows, P(both), rows, rows, rows, rows, P(both), rows)
    out_specs = out_specs + (expert, expert, expert)
    return jax.shard_map(
        on_device, mesh=mesh, in_specs=in_specs, out_specs=out_specs, check_vma=False
    )
```

time: 2130 us -> 834 us (0.39)
  waiting for transfers between devices: 1320 us -> 355 us
  blocking collectives: 407 us -> 0 us
  matrix products: 186 us -> 25 us
  starting transfers between devices: 12.4 us -> 154 us
  Pallas kernels: 0 us -> 129 us
  local copies, waits for them, and re-layouts: 119 us -> 89.2 us
    reduce_scatter x8 -> x0, waiting for transfers between devices: 855 us -> none  [the longest x1 147 us: on_device(): lax.psum_scatter(up_grad_w.astype(jnp.bfloat16), 'fsdp', scatter_dimensio...]
    all_gather x7 -> x0, waiting for transfers between devices: 400 us -> none  [the longest x1 113 us: on_device(): lax.all_gather(expert_up, 'fsdp', axis=1, tiled=True)]
    ppermute x0 -> x126, waiting for transfers between devices: none -> 355 us  [swap(): lax.ppermute(values, axis, [(i, i ^ mask) for i in range(lax.axis_size(ax...]
    dot_general x78 -> x7, matrix products: 184 us -> 19.4 us  [the longest x3 7.58 us: dot(): lax.dot_general(a, b, (((1,), (0,)), ((), ())), preferred_element_type=f32)]
    all_to_all x2 -> x0, blocking collectives: 155 us -> none  [the longest x1 77.6 us: on_device(): lax.all_to_all(grad_out, 'dp', split_axis=0, concat_axis=0, tiled=True)]
    ppermute x0 -> x126, starting transfers between devices: none -> 154 us  [swap(): lax.ppermute(values, axis, [(i, i ^ mask) for i in range(lax.axis_size(ax...]
    psum x2 -> x0, blocking collectives: 142 us -> none  [on_device(): lax.psum((part_loss, length_float), ('dp', 'fsdp'))]
    pallas_call x0 -> x11, Pallas kernels: none -> 129 us  [the longest x10 109 us: kernel_call(): pl.pallas_call(body, out_shape=out_shape, in_specs=specs, out_specs=jax.t...]
  transfers between devices with their start and end apart: 17 -> 126, of which waited for: 14 -> 42; matrix products, arithmetic and copies ran while one was open for 14% -> 19% of each run, Pallas kernels for 0% -> 15%
where the time goes in v1:
time: 834 us; the launch traced here: 823 us
  waiting for transfers between devices  355 us (43%)
  starting transfers between devices  154 us (18%)
  Pallas kernels  129 us (15%)
  local copies, waits for them, and re-layouts  89.2 us (11%)
  other arithmetic  63.9 us (8%)
  matrix products  25 us (3%)
    ppermute x126, waiting for transfers between devices, swap(): lax.ppermute(values, axis, [(i, i ^ mask) for i in range(lax.axis_size(ax...  355 us
    ppermute x126, starting transfers between devices, swap(): lax.ppermute(values, axis, [(i, i ^ mask) for i in range(lax.axis_size(ax...  154 us
    pallas_call x10, Pallas kernels, kernel_call(): pl.pallas_call(body, out_shape=out_shape, in_specs=specs, out_specs=jax.t...  109 us
    pallas_call x1, Pallas kernels, on_device(): pl.pallas_call(functools.partial(expert_weight_grads, HOPS), grid=(held,)...  19.1 us
  transfers between devices with their start and end apart: 126, of which 42 were waited for; matrix products, arithmetic and copies ran while one was open for 19% of the time, Pallas kernels for 15%

profile of v1, /device:TPU:0, one launch (start us, length us, event | category | flops | bytes accessed | tf_op | source)
XLA Modules:
  0.0 822.9 jit_solution(7764232747113007891)
XLA Ops:
  35.7 10.1 %collective-permute-done.17 = bf16[32,256]{1,0:T(8,128)(2,1)S(1)} collective-permute-done((bf16[32,256]{1,0:T(8,128)(2,1)S(1)}, bf16[32,256]{1,0:T(8,128)(2,1)S(1)}, u32[]{:S(2)}, u32[]{:S(2)}) %collective-permute-start.17) | collective-permute-done | bytes 16416 | tf_op jit(solution)/shard_map/ppermute | solution.py:40
  65.6 11.0 %collective-permute-done.4 = bf16[2,1,4,1,32,2176]{5,4,3,2,1,0:T(8,128)(2,1)S(1)} collective-permute-done((bf16[2,1,4,1,32,2176]{5,4,3,2,1,0:T(8,128)(2,1)S(1)}, bf16[2,1,4,1,32,2176]{5,4,3,2,1,0:T(8,128)(2,1)S(1)}, u32[]{:S(2)}, u32[]{:S(2)}) %collective-permute-start.4) | collective-permute-done | bytes 1114144 | tf_op jit(solution)/shard_map/ppermute | solution.py:40
  79.4 13.4 %collective-permute-done.10 = bf16[2,1,4,1,32,1024]{5,4,3,2,1,0:T(8,128)(2,1)S(1)} collective-permute-done((bf16[2,1,4,1,32,1024]{5,4,3,2,1,0:T(8,128)(2,1)S(1)}, bf16[2,1,4,1,32,1024]{5,4,3,2,1,0:T(8,128)(2,1)S(1)}, u32[]{:S(2)}, u32[]{:S(2)}) %collective-permute-start.10) | collective-permute-done | bytes 524320 | tf_op jit(solution)/shard_map/ppermute | solution.py:40
  98.2 10.7 %collective-permute-done.40 = bf16[2,64,1024]{2,1,0:T(8,128)(2,1)S(1)} collective-permute-done((bf16[2,64,1024]{2,1,0:T(8,128)(2,1)S(1)}, bf16[2,64,1024]{2,1,0:T(8,128)(2,1)S(1)}, u32[]{:S(2)}, u32[]{:S(2)}) %collective-permute-start.40) | collective-permute-done | bytes 262176 | tf_op jit(solution)/shard_map/ppermute | solution.py:40
  121.9 22.2 %collective-permute-done.42 = bf16[2,64,1024]{2,1,0:T(8,128)(2,1)} collective-permute-done((bf16[2,64,1024]{2,1,0:T(8,128)(2,1)S(1)}, bf16[2,64,1024]{2,1,0:T(8,128)(2,1)}, u32[]{:S(2)}, u32[]{:S(2)}) %collective-permute-start.42) | collective-permute-done | bytes 262176 | tf_op jit(solution)/shard_map/ppermute | solution.py:40
  146.2 8.2 %collective-permute-done.33 = bf16[2,128,1024]{2,1,0:T(8,128)(2,1)} collective-permute-done((bf16[2,128,1024]{2,1,0:T(8,128)(2,1)S(1)}, bf16[2,128,1024]{2,1,0:T(8,128)(2,1)}, u32[]{:S(2)}, u32[]{:S(2)}) %collective-permute-start.33) | collective-permute-done | bytes 524320 | tf_op jit(solution)/shard_map/ppermute | solution.py:40
  166.1 10.2 %shard_map.237 = (bf16[256,2048]{1,0:T(8,128)(2,1)}, bf16[256,1024]{1,0:T(8,128)(2,1)}) custom-call(s32[1]{0:T(128)} %copy.125.length_ref, f32[256,2048]{1,0:T(8,128)} %fusion.2.qkv_ref, f32[256,128]{1,0:T(8,128)} %get-tuple-element.253.cos_ref, f32[256,128]{1,0:T(8,128)} %get-tuple-element.254.sin_ref), custom_call_target="tpu_custom_call" | custom-call | tf_op jit(solution)/shard_map/pallas_call | solution.py:55
  188.1 17.6 %collective-permute-start.55 = (bf16[264,1024]{1,0:T(8,128)(2,1)}, bf16[264,1024]{1,0:T(8,128)(2,1)S(1)}, u32[]{:S(2)}, u32[]{:S(2)}) collective-permute-start(bf16[264,1024]{1,0:T(8,128)(2,1)} %pad_maximum_fusion.14.refs_4_), channel_id=1, source_target_pairs={{0,4},{1,5},{2,6},{3,7},{4,0},{5,1},{6,2},{7,3},{8,12},{9,13},{10,... | collective-permute-start | bytes 1622024 | tf_op jit(solution)/shard_map/ppermute | solution.py:40
  215.9 21.9 %collective-permute-done.55.refs_4_ = bf16[264,1024]{1,0:T(8,128)(2,1)S(1)} collective-permute-done((bf16[264,1024]{1,0:T(8,128)(2,1)}, bf16[264,1024]{1,0:T(8,128)(2,1)S(1)}, u32[]{:S(2)}, u32[]{:S(2)}) %collective-permute-start.55) | collective-permute-done | bytes 540704 | tf_op jit(solution)/shard_map/ppermute | solution.py:40
  251.8 10.7 %collective-permute-done.57.refs_6_ = bf16[264,1024]{1,0:T(8,128)(2,1)S(1)} collective-permute-done((bf16[264,1024]{1,0:T(8,128)(2,1)S(1)}, bf16[264,1024]{1,0:T(8,128)(2,1)S(1)}, u32[]{:S(2)}, u32[]{:S(2)}) %collective-permute-start.57) | collective-permute-done | bytes 540704 | tf_op jit(solution)/shard_map/ppermute | solution.py:40
  263.4 10.3 %collective-permute-done.49.refs_6_ = bf16[264,1024]{1,0:T(8,128)(2,1)S(1)} collective-permute-done((bf16[264,1024]{1,0:T(8,128)(2,1)}, bf16[264,1024]{1,0:T(8,128)(2,1)S(1)}, u32[]{:S(2)}, u32[]{:S(2)}) %collective-permute-start.49) | collective-permute-done | bytes 540704 | tf_op jit(solution)/shard_map/ppermute | solution.py:40
  275.2 8.8 %shard_map.238 = (bf16[256,1024]{1,0:T(8,128)(2,1)}, bf16[256,1024]{1,0:T(8,128)(2,1)}, bf16[256,1024]{1,0:T(8,128)(2,1)}, bf16[256,1024]{1,0:T(8,128)(2,1)}) custom-call(f32[4,2,256]{2,1,0:T(2,128)} %get-tuple-element.236.refs_0_, f32[4,2,256]{2,1,0:T(2,128)} %maximum_convert_fusion.refs_1_, ...), custom_call_target="tpu_custom_call" | custom-call | tf_op jit(solution)/shard_map/pallas_call | solution.py:55
  289.1 9.0 %shard_map.241 = (bf16[256,1024]{1,0:T(8,128)(2,1)}, bf16[256,1024]{1,0:T(8,128)(2,1)}, bf16[256,1024]{1,0:T(8,128)(2,1)}, bf16[256,1024]{1,0:T(8,128)(2,1)}) custom-call(f32[4,2,256]{2,1,0:T(2,128)} %get-tuple-element.239.refs_0_, f32[4,2,256]{2,1,0:T(2,128)} %maximum_convert_fusion.3.refs_1_, ...), custom_call_target="tpu_custom_call" | custom-call | tf_op jit(solution)/shard_map/pallas_call | solution.py:55
  299.1 8.9 %shard_map.240 = (bf16[256,1024]{1,0:T(8,128)(2,1)}, bf16[256,1024]{1,0:T(8,128)(2,1)}, bf16[256,1024]{1,0:T(8,128)(2,1)}, bf16[256,1024]{1,0:T(8,128)(2,1)}) custom-call(f32[4,2,256]{2,1,0:T(2,128)} %get-tuple-element.238.refs_0_, f32[4,2,256]{2,1,0:T(2,128)} %maximum_convert_fusion.2.refs_1_, ...), custom_call_target="tpu_custom_call" | custom-call | tf_op jit(solution)/shard_map/pallas_call | solution.py:55
  310.9 9.1 %shard_map.239 = (bf16[256,1024]{1,0:T(8,128)(2,1)}, bf16[256,1024]{1,0:T(8,128)(2,1)}, bf16[256,1024]{1,0:T(8,128)(2,1)}, bf16[256,1024]{1,0:T(8,128)(2,1)}) custom-call(f32[4,2,256]{2,1,0:T(2,128)} %get-tuple-element.237.refs_0_, f32[4,2,256]{2,1,0:T(2,128)} %maximum_convert_fusion.1.refs_1_, ...), custom_call_target="tpu_custom_call" | custom-call | tf_op jit(solution)/shard_map/pallas_call | solution.py:55
  324.3 12.2 %collective-permute-done.69 = bf16[256,1024]{1,0:T(8,128)(2,1)S(1)} collective-permute-done((bf16[256,1024]{1,0:T(8,128)(2,1)S(1)}, bf16[256,1024]{1,0:T(8,128)(2,1)S(1)}, u32[]{:S(2)}, u32[]{:S(2)}) %collective-permute-start.69) | collective-permute-done | bytes 524320 | tf_op jit(solution)/shard_map/ppermute | solution.py:40
  369.7 24.2 %collective-permute-done.62 = bf16[256,1024]{1,0:T(8,128)(2,1)} collective-permute-done((bf16[256,1024]{1,0:T(8,128)(2,1)S(1)}, bf16[256,1024]{1,0:T(8,128)(2,1)}, u32[]{:S(2)}, u32[]{:S(2)}) %collective-permute-start.62) | collective-permute-done | bytes 524320 | tf_op jit(solution)/shard_map/ppermute | solution.py:40
  414.8 26.3 %collective-permute-done.90.refs_8_ = bf16[256,1024]{1,0:T(8,128)(2,1)S(1)} collective-permute-done((bf16[256,1024]{1,0:T(8,128)(2,1)S(1)}, bf16[256,1024]{1,0:T(8,128)(2,1)S(1)}, u32[]{:S(2)}, u32[]{:S(2)}) %collective-permute-start.90) | collective-permute-done | bytes 524320 | tf_op jit(solution)/shard_map/ppermute | solution.py:40
  444.8 12.6 %shard_map.242 = (bf16[256,1024]{1,0:T(8,128)(2,1)}, bf16[256,1024]{1,0:T(8,128)(2,1)}, bf16[256,1024]{1,0:T(8,128)(2,1)}, bf16[256,1024]{1,0:T(8,128)(2,1)}, f3...) custom-call(f32[4,2,256]{2,1,0:T(2,128)} %get-tuple-element.236.refs, ...), custom_call_target="tpu_custom_call" | custom-call | tf_op jit(solution)/shard_map/pallas_call | solution.py:55
  475.5 12.6 %shard_map.245 = (bf16[256,1024]{1,0:T(8,128)(2,1)}, bf16[256,1024]{1,0:T(8,128)(2,1)}, bf16[256,1024]{1,0:T(8,128)(2,1)}, bf16[256,1024]{1,0:T(8,128)(2,1)}, f3...) custom-call(f32[4,2,256]{2,1,0:T(2,128)} %get-tuple-element.239.refs, ...), custom_call_target="tpu_custom_call" | custom-call | tf_op jit(solution)/shard_map/pallas_call | solution.py:55
  495.5 13.0 %shard_map.244 = (bf16[256,1024]{1,0:T(8,128)(2,1)}, bf16[256,1024]{1,0:T(8,128)(2,1)}, bf16[256,1024]{1,0:T(8,128)(2,1)}, bf16[256,1024]{1,0:T(8,128)(2,1)}, f3...) custom-call(f32[4,2,256]{2,1,0:T(2,128)} %get-tuple-element.238.refs, ...), custom_call_target="tpu_custom_call" | custom-call | tf_op jit(solution)/shard_map/pallas_call | solution.py:55
  514.1 12.6 %shard_map.243 = (bf16[256,1024]{1,0:T(8,128)(2,1)}, bf16[256,1024]{1,0:T(8,128)(2,1)}, bf16[256,1024]{1,0:T(8,128)(2,1)}, bf16[256,1024]{1,0:T(8,128)(2,1)}, f3...) custom-call(f32[4,2,256]{2,1,0:T(2,128)} %get-tuple-element.237.refs, ...), custom_call_target="tpu_custom_call" | custom-call | tf_op jit(solution)/shard_map/pallas_call | solution.py:55
  530.3 19.1 %shard_map.247 = (bf16[2,1024,1024]{2,1,0:T(8,128)(2,1)}, bf16[2,512,1024]{2,1,0:T(8,128)(2,1)}) custom-call(bf16[2,384,1024]{2,1,0:T(8,128)(2,1)} %get-tuple-element.119.refs_0_, bf16[2,384,1024]{2,1,0:T(8,128)(2,1)} %get-tuple-element.120.refs_1_, bf16[2,384,1024]{2,1,0:T(8,128)(2,1)} %get-tuple-element.121.refs_2_, ...), custom_call_target="tpu_custom_call" | custom-call | tf_op jit(solution)/shard_map/pallas_call | solution.py:520
  569.4 9.4 %collective-permute-done.122 = bf16[2,4,1,64,1024]{4,3,0,2,1:T(8,128)(2,1)} collective-permute-done((bf16[2,4,1,64,1024]{4,3,0,2,1:T(8,128)(2,1)}, bf16[2,4,1,64,1024]{4,3,0,2,1:T(8,128)(2,1)}, u32[]{:S(2)}, u32[]{:S(2)}) %collective-permute-start.122) | collective-permute-done | bytes 1048608 | tf_op jit(solution)/shard_map/ppermute | solution.py:40
  586.2 8.8 %collective-permute-done.96 = bf16[272,1024]{1,0:T(8,128)(2,1)S(1)} collective-permute-done((bf16[272,1024]{1,0:T(8,128)(2,1)S(1)}, bf16[272,1024]{1,0:T(8,128)(2,1)S(1)}, u32[]{:S(2)}, u32[]{:S(2)}) %collective-permute-start.96) | collective-permute-done | bytes 557088 | tf_op jit(solution)/shard_map/ppermute | solution.py:40
  598.8 8.1 collective-permute-done.88
  618.0 28.2 %collective-permute-start.89 = (bf16[272,1024]{1,0:T(8,128)(2,1)S(1)}, bf16[272,1024]{1,0:T(8,128)(2,1)S(1)}, u32[]{:S(2)}, u32[]{:S(2)}) collective-permute-start(bf16[272,1024]{1,0:T(8,128)(2,1)S(1)} %add_convert_fusion.4), channel_id=1, source_target_pairs={{0,2},{1,3},{2,0},{3,1},{4,6},{5,7},{6,4},{7,5},{8,10},{9,11},{10,... | collective-permute-start | bytes 1671176 | tf_op jit(solution)/shard_map/ppermute | solution.py:40
  646.5 22.2 %collective-permute-done.97 = bf16[272,1024]{1,0:T(8,128)(2,1)S(1)} collective-permute-done((bf16[272,1024]{1,0:T(8,128)(2,1)S(1)}, bf16[272,1024]{1,0:T(8,128)(2,1)S(1)}, u32[]{:S(2)}, u32[]{:S(2)}) %collective-permute-start.97) | collective-permute-done | bytes 557088 | tf_op jit(solution)/shard_map/ppermute | solution.py:40
  676.0 12.6 %shard_map.246 = bf16[256,2048]{1,0:T(8,128)(2,1)} custom-call(s32[1]{0:T(128)} %copy.125.length_ref, bf16[256,2048]{1,0:T(8,128)(2,1)} %get-tuple-element.118.rot_ref, bf16[256,1024]{1,0:T(8,128)(2,1)} %convolution_convert_fusion.grad_ref, f32[256,128]{1,0:T(8,128)} %get-tuple-element.253.cos_ref, f32[256,128]{1,0:T(8,128)} %get-tuple-element.254.sin_ref), custom_call_target="tpu_custom_call" | custom-call | tf_op jit(solution)/shard_map/pallas_call | solution.py:55
  703.1 10.4 %concatenate.134 = f32[2,2,4,2,32,2176]{5,4,3,2,1,0:T(8,128)} concatenate(f32[2,2,4,2,32,2048]{5,4,3,2,1,0:T(8,128)} %bitcast.205, f32[2,2,4,2,32,32]{5,4,3,2,1,0:T(8,128)S(1)} %bitcast.217, f32[2,2,4,2,32,1]{5,4,3,2,1,0:T(8,128)S(1)} %copy-done.24, f32[2,2,4,2,32,1]{5,4,3,2,1,0:T(8,128)S(1)} %copy-done.25, f32[2,2,4,2,32,94]{5,4,3,2,1,0:T(8,128)} %broadcast_in_dim.66), dimensions={5} | concatenate | bytes 17825792 | tf_op jit(solution)/shard_map/concatenate | solution.py:593
  759.2 20.2 %collective-permute-done.120 = bf16[2,128,1024]{2,1,0:T(8,128)(2,1)S(1)} collective-permute-done((bf16[2,128,1024]{2,1,0:T(8,128)(2,1)}, bf16[2,128,1024]{2,1,0:T(8,128)(2,1)S(1)}, u32[]{:S(2)}, u32[]{:S(2)}) %collective-permute-start.120) | collective-permute-done | bytes 524320 | tf_op jit(solution)/shard_map/ppermute | solution.py:40
  779.7 9.1 %collective-permute-done.113 = bf16[1,1,4,2,32,1024]{5,4,3,2,1,0:T(8,128)(2,1)S(1)} collective-permute-done((bf16[1,1,4,2,32,1024]{5,4,3,2,1,0:T(8,128)(2,1)S(1)}, bf16[1,1,4,2,32,1024]{5,4,3,2,1,0:T(8,128)(2,1)S(1)}, u32[]{:S(2)}, u32[]{:S(2)}) %collective-permute-start.113) | collective-permute-done | bytes 524320 | tf_op jit(solution)/shard_map/ppermute | solution.py:40
  (704 shorter events, 372.0 us)
Async XLA Ops:
  54.2 42.6 %collective-permute-start.37 = (bf16[2,64,1024]{2,1,0:T(8,128)(2,1)S(1)}, bf16[2,64,1024]{2,1,0:T(8,128)(2,1)S(1)}, u32[]{:S(2)}, u32[]{:S(2)}) collective-permute-start(bf16[2,64,1024]{2,1,0:T(8,128)(2,1)S(1)} %copy-done.67), channel_id=1, source_target_pairs={{0,1},{1,0},{2,3},{3,2},{4,5},{5,4},{6,7},{7,6},{8,9},{9,8},{10,11... | collective-permute-start | bytes 786440 | tf_op jit(solution)/shard_map/ppermute | solution.py:40
  58.0 36.7 %collective-permute-start.38 = (bf16[2,64,1024]{2,1,0:T(8,128)(2,1)S(1)}, bf16[2,64,1024]{2,1,0:T(8,128)(2,1)S(1)}, u32[]{:S(2)}, u32[]{:S(2)}) collective-permute-start(bf16[2,64,1024]{2,1,0:T(8,128)(2,1)S(1)} %copy-done.68), channel_id=1, source_target_pairs={{0,2},{1,3},{2,0},{3,1},{4,6},{5,7},{6,4},{7,5},{8,10},{9,11},{10,... | collective-permute-start | bytes 786440 | tf_op jit(solution)/shard_map/ppermute | solution.py:40
  78.6 77.8 %collective-permute-start.5 = (bf16[2,1,4,2,32,2176]{5,4,3,2,1,0:T(8,128)(2,1)S(1)}, bf16[2,1,4,2,32,2176]{5,4,3,2,1,0:T(8,128)(2,1)S(1)}, u32[]{:S(2)}, u32[]{:S(2)}) collective-permute-start(bf16[2,1,4,2,32,2176]{5,4,3,2,1,0:T(8,128)(2,1)S(1)} %pad_maximum_fusion.1), channel_id=1, source_target_pairs={{0,8},{8,0},{16,24},{24,16},{1,9},{9,1},{17,25},{25,17},{2,10},{10... | collective-permute-start | bytes 6684680 | tf_op jit(solution)/shard_map/ppermute | solution.py:40
  96.8 48.8 %collective-permute-start.31 = (bf16[2,128,1024]{2,1,0:T(8,128)(2,1)S(1)}, bf16[2,128,1024]{2,1,0:T(8,128)(2,1)}, u32[]{:S(2)}, u32[]{:S(2)}) collective-permute-start(bf16[2,128,1024]{2,1,0:T(8,128)(2,1)S(1)} %copy-done.40), channel_id=1, source_target_pairs={{0,2},{1,3},{2,0},{3,1},{4,6},{5,7},{6,4},{7,5},{8,10},{9,11},{10,... | collective-permute-start | bytes 1572872 | tf_op jit(solution)/shard_map/ppermute | solution.py:40
  110.5 44.0 %collective-permute-start.33 = (bf16[2,128,1024]{2,1,0:T(8,128)(2,1)S(1)}, bf16[2,128,1024]{2,1,0:T(8,128)(2,1)}, u32[]{:S(2)}, u32[]{:S(2)}) collective-permute-start(bf16[2,128,1024]{2,1,0:T(8,128)(2,1)S(1)} %copy-done.39), channel_id=1, source_target_pairs={{0,4},{1,5},{2,6},{3,7},{4,0},{5,1},{6,2},{7,3},{8,12},{9,13},{10,... | collective-permute-start | bytes 1572872 | tf_op jit(solution)/shard_map/ppermute | solution.py:40
  116.4 38.6 %collective-permute-start.35 = (bf16[2,128,1024]{2,1,0:T(8,128)(2,1)S(1)}, bf16[2,128,1024]{2,1,0:T(8,128)(2,1)}, u32[]{:S(2)}, u32[]{:S(2)}) collective-permute-start(bf16[2,128,1024]{2,1,0:T(8,128)(2,1)S(1)} %copy-done.38), channel_id=1, source_target_pairs={{0,6},{1,7},{2,4},{3,5},{4,2},{5,3},{6,0},{7,1},{8,14},{9,15},{10,... | collective-permute-start | bytes 1572872 | tf_op jit(solution)/shard_map/ppermute | solution.py:40
  144.2 41.6 %collective-permute-start.30 = (bf16[2,128,1024]{2,1,0:T(8,128)(2,1)}, bf16[2,128,1024]{2,1,0:T(8,128)(2,1)}, u32[]{:S(2)}, u32[]{:S(2)}) collective-permute-start(bf16[2,128,1024]{2,1,0:T(8,128)(2,1)} %get-tuple-element.203), channel_id=1, source_target_pairs={{0,1},{1,0},{2,3},{3,2},{4,5},{5,4},{6,7},{7,6},{8,9},{9,8},{10,11... | collective-permute-start | bytes 1572872 | tf_op jit(solution)/shard_map/ppermute | solution.py:40
  145.6 42.5 %collective-permute-start.43 = (bf16[2,64,1024]{2,1,0:T(8,128)(2,1)}, bf16[2,64,1024]{2,1,0:T(8,128)(2,1)S(1)}, u32[]{:S(2)}, u32[]{:S(2)}) collective-permute-start(bf16[2,64,1024]{2,1,0:T(8,128)(2,1)} %collective-permute-done.42), channel_id=1, source_target_pairs={{0,1},{1,0},{2,3},{3,2},{4,5},{5,4},{6,7},{7,6},{8,9},{9,8},{10,11... | collective-permute-start | bytes 786440 | tf_op jit(solution)/shard_map/ppermute | solution.py:40
  154.4 55.5 %collective-permute-start.32 = (bf16[2,128,1024]{2,1,0:T(8,128)(2,1)}, bf16[2,128,1024]{2,1,0:T(8,128)(2,1)}, u32[]{:S(2)}, u32[]{:S(2)}) collective-permute-start(bf16[2,128,1024]{2,1,0:T(8,128)(2,1)} %collective-permute-done.31), channel_id=1, source_target_pairs={{0,1},{1,0},{2,3},{3,2},{4,5},{5,4},{6,7},{7,6},{8,9},{9,8},{10,11... | collective-permute-start | bytes 1572872 | tf_op jit(solution)/shard_map/ppermute | solution.py:40
  155.0 56.8 %collective-permute-start.34 = (bf16[2,128,1024]{2,1,0:T(8,128)(2,1)}, bf16[2,128,1024]{2,1,0:T(8,128)(2,1)}, u32[]{:S(2)}, u32[]{:S(2)}) collective-permute-start(bf16[2,128,1024]{2,1,0:T(8,128)(2,1)} %collective-permute-done.33), channel_id=1, source_target_pairs={{0,1},{1,0},{2,3},{3,2},{4,5},{5,4},{6,7},{7,6},{8,9},{9,8},{10,11... | collective-permute-start | bytes 1572872 | tf_op jit(solution)/shard_map/ppermute | solution.py:40
  156.5 55.9 %collective-permute-start.36 = (bf16[2,128,1024]{2,1,0:T(8,128)(2,1)}, bf16[2,128,1024]{2,1,0:T(8,128)(2,1)}, u32[]{:S(2)}, u32[]{:S(2)}) collective-permute-start(bf16[2,128,1024]{2,1,0:T(8,128)(2,1)} %collective-permute-done.35), channel_id=1, source_target_pairs={{0,1},{1,0},{2,3},{3,2},{4,5},{5,4},{6,7},{7,6},{8,9},{9,8},{10,11... | collective-permute-start | bytes 1572872 | tf_op jit(solution)/shard_map/ppermute | solution.py:40
  188.1 49.6 %collective-permute-start.55 = (bf16[264,1024]{1,0:T(8,128)(2,1)}, bf16[264,1024]{1,0:T(8,128)(2,1)S(1)}, u32[]{:S(2)}, u32[]{:S(2)}) collective-permute-start(bf16[264,1024]{1,0:T(8,128)(2,1)} %pad_maximum_fusion.14.refs_4_), channel_id=1, source_target_pairs={{0,4},{1,5},{2,6},{3,7},{4,0},{5,1},{6,2},{7,3},{8,12},{9,13},{10,... | collective-permute-start | bytes 1622024 | tf_op jit(solution)/shard_map/ppermute | solution.py:40
  212.3 37.3 %collective-permute-start.65 = (bf16[264,1024]{1,0:T(8,128)(2,1)}, bf16[264,1024]{1,0:T(8,128)(2,1)}, u32[]{:S(2)}, u32[]{:S(2)}) collective-permute-start(bf16[264,1024]{1,0:T(8,128)(2,1)} %collective-permute-done.63.refs_4_), channel_id=1, source_target_pairs={{0,16},{8,24},{16,0},{24,8},{1,17},{9,25},{17,1},{25,9},{2,18},{10... | collective-permute-start | bytes 1622024 | tf_op jit(solution)/shard_map/ppermute | solution.py:40
  284.0 77.7 %collective-permute-start.44 = (bf16[256,1024]{1,0:T(8,128)(2,1)}, bf16[256,1024]{1,0:T(8,128)(2,1)}, u32[]{:S(2)}, u32[]{:S(2)}) collective-permute-start(bf16[256,1024]{1,0:T(8,128)(2,1)} %get-tuple-element.83), channel_id=1, source_target_pairs={{0,8},{8,0},{16,24},{24,16},{1,9},{9,1},{17,25},{25,17},{2,10},{10... | collective-permute-start | bytes 1572872 | tf_op jit(solution)/shard_map/ppermute | solution.py:40
  351.8 42.1 %collective-permute-start.62 = (bf16[256,1024]{1,0:T(8,128)(2,1)S(1)}, bf16[256,1024]{1,0:T(8,128)(2,1)}, u32[]{:S(2)}, u32[]{:S(2)}) collective-permute-start(bf16[256,1024]{1,0:T(8,128)(2,1)S(1)} %add_convert_fusion.9), channel_id=1, source_target_pairs={{0,4},{1,5},{2,6},{3,7},{4,0},{5,1},{6,2},{7,3},{8,12},{9,13},{10,... | collective-permute-start | bytes 1572872 | tf_op jit(solution)/shard_map/ppermute | solution.py:40
  399.2 41.9 %collective-permute-start.90 = (bf16[256,1024]{1,0:T(8,128)(2,1)S(1)}, bf16[256,1024]{1,0:T(8,128)(2,1)S(1)}, u32[]{:S(2)}, u32[]{:S(2)}) collective-permute-start(bf16[256,1024]{1,0:T(8,128)(2,1)S(1)} %get-tuple-element.175.refs_8_), channel_id=1, source_target_pairs={{0,4},{1,5},{2,6},{3,7},{4,0},{5,1},{6,2},{7,3},{8,12},{9,13},{10,... | collective-permute-start | bytes 1572872 | tf_op jit(solution)/shard_map/ppermute | solution.py:40
  399.2 43.5 %collective-permute-start.82 = (bf16[256,1024]{1,0:T(8,128)(2,1)S(1)}, bf16[256,1024]{1,0:T(8,128)(2,1)S(1)}, u32[]{:S(2)}, u32[]{:S(2)}) collective-permute-start(bf16[256,1024]{1,0:T(8,128)(2,1)S(1)} %get-tuple-element.175.refs_8_), channel_id=1, source_target_pairs={{0,2},{1,3},{2,0},{3,1},{4,6},{5,7},{6,4},{7,5},{8,10},{9,11},{10,... | collective-permute-start | bytes 1572872 | tf_op jit(solution)/shard_map/ppermute | solution.py:40
  402.4 40.3 %collective-permute-start.76 = (bf16[256,1024]{1,0:T(8,128)(2,1)S(1)}, bf16[256,1024]{1,0:T(8,128)(2,1)}, u32[]{:S(2)}, u32[]{:S(2)}) collective-permute-start(bf16[256,1024]{1,0:T(8,128)(2,1)S(1)} %get-tuple-element.175.refs_8_), channel_id=1, source_target_pairs={{0,8},{8,0},{16,24},{24,16},{1,9},{9,1},{17,25},{25,17},{2,10},{10... | collective-permute-start | bytes 1572872 | tf_op jit(solution)/shard_map/ppermute | solution.py:40
  414.8 48.5 %collective-permute-start.99 = (bf16[256,1024]{1,0:T(8,128)(2,1)}, bf16[256,1024]{1,0:T(8,128)(2,1)}, u32[]{:S(2)}, u32[]{:S(2)}) collective-permute-start(bf16[256,1024]{1,0:T(8,128)(2,1)} %collective-permute-done.98.refs_8_), channel_id=1, source_target_pairs={{0,8},{8,0},{16,24},{24,16},{1,9},{9,1},{17,25},{25,17},{2,10},{10... | collective-permute-start | bytes 1572872 | tf_op jit(solution)/shard_map/ppermute | solution.py:40
  442.7 52.2 %collective-permute-start.91 = (bf16[256,1024]{1,0:T(8,128)(2,1)S(1)}, bf16[256,1024]{1,0:T(8,128)(2,1)}, u32[]{:S(2)}, u32[]{:S(2)}) collective-permute-start(bf16[256,1024]{1,0:T(8,128)(2,1)S(1)} %collective-permute-done.90.refs_8_), channel_id=1, source_target_pairs={{0,8},{8,0},{16,24},{24,16},{1,9},{9,1},{17,25},{25,17},{2,10},{10... | collective-permute-start | bytes 1572872 | tf_op jit(solution)/shard_map/ppermute | solution.py:40
  463.3 50.0 %collective-permute-start.83 = (bf16[256,1024]{1,0:T(8,128)(2,1)S(1)}, bf16[256,1024]{1,0:T(8,128)(2,1)S(1)}, u32[]{:S(2)}, u32[]{:S(2)}) collective-permute-start(bf16[256,1024]{1,0:T(8,128)(2,1)S(1)} %collective-permute-done.82.refs_8_), channel_id=1, source_target_pairs={{0,8},{8,0},{16,24},{24,16},{1,9},{9,1},{17,25},{25,17},{2,10},{10... | collective-permute-start | bytes 1572872 | tf_op jit(solution)/shard_map/ppermute | solution.py:40
  467.4 95.3 %collective-permute-start.80 = (bf16[272,1024]{1,0:T(8,128)(2,1)}, bf16[272,1024]{1,0:T(8,128)(2,1)}, u32[]{:S(2)}, u32[]{:S(2)}) collective-permute-start(bf16[272,1024]{1,0:T(8,128)(2,1)} %pad_maximum_fusion.7), channel_id=1, source_target_pairs={{0,8},{8,0},{16,24},{24,16},{1,9},{9,1},{17,25},{25,17},{2,10},{10... | collective-permute-start | bytes 1671176 | tf_op jit(solution)/shard_map/ppermute | solution.py:40
  474.6 38.9 %collective-permute-start.85 = (bf16[256,1024]{1,0:T(8,128)(2,1)S(1)}, bf16[256,1024]{1,0:T(8,128)(2,1)}, u32[]{:S(2)}, u32[]{:S(2)}) collective-permute-start(bf16[256,1024]{1,0:T(8,128)(2,1)S(1)} %collective-permute-done.84.refs_10_), channel_id=1, source_target_pairs={{0,8},{8,0},{16,24},{24,16},{1,9},{9,1},{17,25},{25,17},{2,10},{10... | collective-permute-start | bytes 1572872 | tf_op jit(solution)/shard_map/ppermute | solution.py:40
  494.9 69.3 %collective-permute-start.103 = (bf16[272,1024]{1,0:T(8,128)(2,1)}, bf16[272,1024]{1,0:T(8,128)(2,1)}, u32[]{:S(2)}, u32[]{:S(2)}) collective-permute-start(bf16[272,1024]{1,0:T(8,128)(2,1)} %pad_maximum_fusion.13), channel_id=1, source_target_pairs={{0,8},{8,0},{16,24},{24,16},{1,9},{9,1},{17,25},{25,17},{2,10},{10... | collective-permute-start | bytes 1671176 | tf_op jit(solution)/shard_map/ppermute | solution.py:40
  495.0 87.1 %collective-permute-start.102 = (bf16[272,1024]{1,0:T(8,128)(2,1)}, bf16[272,1024]{1,0:T(8,128)(2,1)}, u32[]{:S(2)}, u32[]{:S(2)}) collective-permute-start(bf16[272,1024]{1,0:T(8,128)(2,1)} %pad_maximum_fusion.12), channel_id=1, source_target_pairs={{0,8},{8,0},{16,24},{24,16},{1,9},{9,1},{17,25},{25,17},{2,10},{10... | collective-permute-start | bytes 1671176 | tf_op jit(solution)/shard_map/ppermute | solution.py:40
  513.3 52.7 %collective-permute-start.95 = (bf16[272,1024]{1,0:T(8,128)(2,1)}, bf16[272,1024]{1,0:T(8,128)(2,1)}, u32[]{:S(2)}, u32[]{:S(2)}) collective-permute-start(bf16[272,1024]{1,0:T(8,128)(2,1)} %pad_maximum_fusion.11), channel_id=1, source_target_pairs={{0,8},{8,0},{16,24},{24,16},{1,9},{9,1},{17,25},{25,17},{2,10},{10... | collective-permute-start | bytes 1671176 | tf_op jit(solution)/shard_map/ppermute | solution.py:40
  583.1 63.3 %collective-permute-start.79 = (bf16[272,1024]{1,0:T(8,128)(2,1)S(1)}, bf16[272,1024]{1,0:T(8,128)(2,1)S(1)}, u32[]{:S(2)}, u32[]{:S(2)}) collective-permute-start(bf16[272,1024]{1,0:T(8,128)(2,1)S(1)} %copy-done.33), channel_id=1, source_target_pairs={{0,8},{8,0},{16,24},{24,16},{1,9},{9,1},{17,25},{25,17},{2,10},{10... | collective-permute-start | bytes 1671176 | tf_op jit(solution)/shard_map/ppermute | solution.py:40
  584.6 61.9 %collective-permute-start.81 = (bf16[272,1024]{1,0:T(8,128)(2,1)S(1)}, bf16[272,1024]{1,0:T(8,128)(2,1)S(1)}, u32[]{:S(2)}, u32[]{:S(2)}) collective-permute-start(bf16[272,1024]{1,0:T(8,128)(2,1)S(1)} %add_convert_fusion.6), channel_id=1, source_target_pairs={{0,16},{8,24},{16,0},{24,8},{1,17},{9,25},{17,1},{25,9},{2,18},{10... | collective-permute-start | bytes 1671176 | tf_op jit(solution)/shard_map/ppermute | solution.py:40
  611.1 57.6 %collective-permute-start.97 = (bf16[272,1024]{1,0:T(8,128)(2,1)S(1)}, bf16[272,1024]{1,0:T(8,128)(2,1)S(1)}, u32[]{:S(2)}, u32[]{:S(2)}) collective-permute-start(bf16[272,1024]{1,0:T(8,128)(2,1)S(1)} %add_convert_fusion.2), channel_id=1, source_target_pairs={{0,4},{1,5},{2,6},{3,7},{4,0},{5,1},{6,2},{7,3},{8,12},{9,13},{10,... | collective-permute-start | bytes 1671176 | tf_op jit(solution)/shard_map/ppermute | solution.py:40
  618.0 50.8 %collective-permute-start.89 = (bf16[272,1024]{1,0:T(8,128)(2,1)S(1)}, bf16[272,1024]{1,0:T(8,128)(2,1)S(1)}, u32[]{:S(2)}, u32[]{:S(2)}) collective-permute-start(bf16[272,1024]{1,0:T(8,128)(2,1)S(1)} %add_convert_fusion.4), channel_id=1, source_target_pairs={{0,2},{1,3},{2,0},{3,1},{4,6},{5,7},{6,4},{7,5},{8,10},{9,11},{10,... | collective-permute-start | bytes 1671176 | tf_op jit(solution)/shard_map/ppermute | solution.py:40
  646.4 80.4 %collective-permute-start.118 = (bf16[2,4,1,128,1024]{4,3,0,2,1:T(8,128)(2,1)}, bf16[2,4,1,128,1024]{4,3,0,2,1:T(8,128)(2,1)}, u32[]{:S(2)}, u32[]{:S(2)}) collective-permute-start(bf16[2,4,1,128,1024]{4,3,0,2,1:T(8,128)(2,1)} %copy.62), channel_id=1, source_target_pairs={{0,1},{1,0},{2,3},{3,2},{4,5},{5,4},{6,7},{7,6},{8,9},{9,8},{10,11... | collective-permute-start | bytes 6291464 | tf_op jit(solution)/shard_map/ppermute | solution.py:40
  674.3 43.7 %collective-permute-start.71 = (f32[8,128]{1,0:T(8,128)S(1)}, f32[8,128]{1,0:T(8,128)S(1)}, u32[]{:S(2)}, u32[]{:S(2)}) collective-permute-start(f32[8,128]{1,0:T(8,128)S(1)} %broadcast_in_dim.65), channel_id=1, source_target_pairs={{0,8},{8,0},{16,24},{24,16},{1,9},{9,1},{17,25},{25,17},{2,10},{10... | collective-permute-start | bytes 12296 | tf_op jit(solution)/shard_map/ppermute | solution.py:40
  (183 other events, 2549.9 us)

commit v2 on v1

--- a/solution.py
+++ b/solution.py
@@ -38,6 +38,10 @@
 
 def swap(values, axis, mask):
     return lax.ppermute(values, axis, [(i, i ^ mask) for i in range(lax.axis_size(axis))])
+
+
+def after(values, *earlier):
+    return lax.optimization_barrier((values, earlier))[0]
 
 
 def vmem():
@@ -156,65 +160,105 @@
     return slot == place_row.astype(jnp.int32)
 
 
-def expert_forward(count, seq_len, *refs):
-    place_ref, gates_ref, wide_ref, down_ref = refs[:4]
-    token_refs = refs[4 : 4 + count]
-    out_refs = refs[4 + count : 4 + 2 * count]
-    picked_ref, = refs[4 + 2 * count :]
-    held = wide_ref.shape[0]
-    hidden_units = down_ref.shape[1]
+def expert_row(block, expert, seq_len):
+    per_row = block.shape[1] // seq_len
+    row = lax.broadcasted_iota(jnp.int32, block.shape, 0)
+    line = jnp.sum(jnp.where(row == expert // per_row, block, 0.0), axis=0, keepdims=True)
+    found = line[:, :seq_len]
+    for part in range(1, per_row):
+        found = jnp.where(
+            expert % per_row == part, line[:, part * seq_len : part * seq_len + seq_len], found
+        )
+    return found
+
+
+def place_row_at(block, values, expert):
+    seq_len = values.shape[1]
+    per_row = block.shape[1] // seq_len
+    row = lax.broadcasted_iota(jnp.int32, block.shape, 0)
+    lane = lax.broadcasted_iota(jnp.int32, block.shape, 1)
+    spread = jnp.concatenate([values] * per_row, axis=1)
+    here = (row == expert // per_row) & (lane // seq_len == expert % per_row)
+    return jnp.where(here, spread, block)
+
+
+def set_rows(ref, expert, seq_len, rows):
+    block = ref[seq_len:, :].astype(f32)
+    gate = expert_row(block[:rows], expert, seq_len)
+    match = slot_match(expert_row(block[rows:], expert, seq_len), seq_len)
+    gate_slots = jnp.sum(jnp.where(match, gate, 0.0), axis=1, keepdims=True)
+    return match, gate_slots
+
+
+def expert_weights(weights_ref, e, split):
+    blocks = weights_ref.shape[1]
+    width = weights_ref.shape[3]
+    wide = weights_ref[e, :, :split, :].reshape(blocks * split, width)
+    down = weights_ref[e, :, split:, :].reshape(-1, width)
+    return wide, down
+
+
+def expert_forward(count, seq_len, first_ref, weights_ref, *refs):
+    token_refs = refs[:count]
+    out_refs = refs[count : 2 * count]
+    picked_ref, acc_ref, match_ref = refs[2 * count :]
+    held = weights_ref.shape[0]
+    hidden_units = weights_ref.shape[3] // 2
+    split = token_refs[0].shape[1] // weights_ref.shape[1]
+    rows = (token_refs[0].shape[0] - seq_len) // 2
     for e in range(held):
         gate_slots = []
         for s in range(count):
-            match = slot_match(place_ref[s, e : e + 1, :], seq_len)
-            gate_slots.append(
-                jnp.sum(jnp.where(match, gates_ref[s, e : e + 1, :], 0.0), axis=1, keepdims=True)
-            )
+            match, gate = set_rows(token_refs[s], first_ref[0] + e, seq_len, rows)
+            gate_slots.append(gate)
+            match_ref[s] = match.astype(f32).astype(bf16)
             picked_ref[s * CAP : s * CAP + CAP, :] = dot(
-                match.astype(f32).astype(bf16), token_refs[s][:seq_len, :]
+                match_ref[s], token_refs[s][:seq_len, :]
             ).astype(bf16)
-        pre = dot(picked_ref[...], wide_ref[e])
+        wide_e, down_e = expert_weights(weights_ref, e, split)
+        pre = dot(picked_ref[...], wide_e)
         gate_pre, up_pre = pre[:, :hidden_units], pre[:, hidden_units:]
         inner = (gate_pre / (1.0 + jnp.exp(-gate_pre)) * up_pre).astype(bf16)
-        scaled = (dot(inner, down_ref[e]) * jnp.concatenate(gate_slots, axis=0)).astype(bf16)
+        scaled = (dot(inner, down_e) * jnp.concatenate(gate_slots, axis=0)).astype(bf16)
         for s in range(count):
-            match = slot_match(place_ref[s, e : e + 1, :], seq_len).astype(f32).astype(bf16)
-            part = dot_tn(match, scaled[s * CAP : s * CAP + CAP, :])
-            if e == 0:
-                part_prev = part
+            part = dot_tn(match_ref[s], scaled[s * CAP : s * CAP + CAP, :])
+            if e:
+                part = acc_ref[s] + part
+            if e < held - 1:
+                acc_ref[s] = part
             else:
-                part_prev = out_refs[s][...].astype(f32) + part
-            out_refs[s][...] = part_prev.astype(bf16)
-
-
-def expert_backward(count, seq_len, *refs):
-    place_ref, gates_ref, wide_ref, down_ref = refs[:4]
-    token_refs = refs[4 : 4 + count]
-    grad_refs = refs[4 + count : 4 + 2 * count]
-    out_refs = refs[4 + 2 * count : 4 + 3 * count]
-    gate_grad_ref, picked_ref, wide_grad_ref, routed_ref, inner_ref = refs[4 + 3 * count : 9 + 3 * count]
-    acc_ref, = refs[9 + 3 * count :]
-    held = wide_ref.shape[0]
-    hidden_units = down_ref.shape[1]
+                out_refs[s][...] = part.astype(bf16)
+
+
+def expert_backward(count, seq_len, first_ref, weights_ref, *refs):
+    token_refs = refs[:count]
+    grad_refs = refs[count : 2 * count]
+    out_refs = refs[2 * count : 3 * count]
+    picked_ref, wide_grad_ref, routed_ref, inner_ref = refs[3 * count : 3 * count + 4]
+    acc_ref, match_ref, gate_acc_ref = refs[3 * count + 4 :]
+    held = weights_ref.shape[0]
+    hidden_units = weights_ref.shape[3] // 2
+    split = token_refs[0].shape[1] // weights_ref.shape[1]
+    rows = (token_refs[0].shape[0] - seq_len) // 2
     for e in range(held):
         gate_slots = []
         for s in range(count):
-            match = slot_match(place_ref[s, e : e + 1, :], seq_len)
-            gate_slots.append(
-                jnp.sum(jnp.where(match, gates_ref[s, e : e + 1, :], 0.0), axis=1, keepdims=True)
-            )
+            match, gate = set_rows(token_refs[s], first_ref[0] + e, seq_len, rows)
+            gate_slots.append(gate)
             select = match.astype(f32).astype(bf16)
+            match_ref[s] = select
             at = s * CAP
             picked_ref[e, at : at + CAP, :] = dot(select, token_refs[s][:seq_len, :]).astype(bf16)
-            routed_ref[e, at : at + CAP, :] = dot(select, grad_refs[s][:seq_len, :]).astype(bf16)
+            routed_ref[e, at : at + CAP, :] = dot(select, grad_refs[s][...]).astype(bf16)
         gate_col = residual_scale * jnp.concatenate(gate_slots, axis=0)
-        pre = dot(picked_ref[e], wide_ref[e])
+        wide_e, down_e = expert_weights(weights_ref, e, split)
+        pre = dot(picked_ref[e], wide_e)
         gate_pre, up_pre = pre[:, :hidden_units], pre[:, hidden_units:]
         sigmoid = 1.0 / (1.0 + jnp.exp(-gate_pre))
         silu = gate_pre * sigmoid
         inner = (silu * up_pre).astype(bf16)
         inner_ref[e] = inner
-        back = dot_nt(routed_ref[e], down_ref[e])
+        back = dot_nt(routed_ref[e], down_e)
         gate_grad = residual_scale * jnp.sum(inner.astype(f32) * back, axis=1, keepdims=True)
         inner_grad = gate_col * back
         wide_grad_ref[e, :, :hidden_units] = (
@@ -222,20 +266,31 @@
         ).astype(bf16)
         wide_grad_ref[e, :, hidden_units:] = (inner_grad * silu).astype(bf16)
         routed_ref[e] = (routed_ref[e].astype(f32) * gate_col).astype(bf16)
-        arrived = dot_nt(wide_grad_ref[e], wide_ref[e]).astype(bf16)
+        arrived = dot_nt(wide_grad_ref[e], wide_e).astype(bf16)
         for s in range(count):
-            match = slot_match(place_ref[s, e : e + 1, :], seq_len)
             at = s * CAP
-            gate_grad_ref[s, e : e + 1, :] = jnp.sum(
-                jnp.where(match, gate_grad[at : at + CAP, :], 0.0), axis=0, keepdims=True
+            match = match_ref[s]
+            gate_row = jnp.sum(
+                jnp.where(match.astype(f32) > 0.5, gate_grad[at : at + CAP, :], 0.0),
+                axis=0,
+                keepdims=True,
             )
-            part = dot_tn(match.astype(f32).astype(bf16), arrived[at : at + CAP, :])
-            if e == 0:
+            spread = place_row_at(
+                jnp.zeros((rows, acc_ref.shape[2]), f32) if e == 0 else gate_acc_ref[s],
+                gate_row,
+                first_ref[0] + e,
+            )
+            part = dot_tn(match, arrived[at : at + CAP, :])
+            if e:
+                part = acc_ref[s] + part
+            if e < held - 1:
                 acc_ref[s] = part
-            elif e < held - 1:
-                acc_ref[s] = acc_ref[s] + part
-            if e == held - 1:
-                out_refs[s][...] = (part if e == 0 else acc_ref[s] + part).astype(bf16)
+                gate_acc_ref[s] = spread
+            else:
+                out_refs[s][:seq_len, :] = part.astype(bf16)
+                high = spread.astype(bf16)
+                low = (spread - high.astype(f32)).astype(bf16)
+                out_refs[s][seq_len:, :] = jnp.concatenate([high, low], axis=0)
 
 
 def expert_weight_grads(groups, *refs):
@@ -243,14 +298,17 @@
     wide_grads = refs[groups : 2 * groups]
     routed = refs[2 * groups : 3 * groups]
     inner = refs[3 * groups : 4 * groups]
-    wide_ref, down_ref = refs[4 * groups :]
+    out_ref, = refs[4 * groups :]
+    blocks, width = out_ref.shape[1], out_ref.shape[3]
+    split = picked[0].shape[2] // blocks
     wide = dot_tn(picked[0][0], wide_grads[0][0])
+    for k in range(1, groups):
+        wide = wide + dot_tn(picked[k][0], wide_grads[k][0])
+    out_ref[0, :, :split, :] = wide.astype(bf16).reshape(blocks, split, width)
     down = dot_tn(inner[0][0], routed[0][0])
     for k in range(1, groups):
-        wide = wide + dot_tn(picked[k][0], wide_grads[k][0])
         down = down + dot_tn(inner[k][0], routed[k][0])
-    wide_ref[0] = wide.astype(bf16)
-    down_ref[0] = down.astype(bf16)
+    out_ref[0, :, split:, :] = down.astype(bf16).reshape(blocks, -1, width)
 
 
 def norm_back(grad_rows, rows_in, inverse, gain_vec):
@@ -306,17 +364,21 @@
     hop_at, low_at = fsdp_at // lows, fsdp_at % lows
     y_at, core_at = dp_at // CORES, dp_at % CORES
 
-    def gather_sets(values):
+    def exchange(values, lag, compute):
         per_hop = [values] + [swap(values, "fsdp", lows * k) for k in range(1, HOPS)]
-        sets = []
-        for mine in per_hop:
-            columns = [mine] + [swap(mine, "dp", CORES * j) for j in range(1, rows_y)]
-            for column in columns:
+        results = []
+        for k in range(HOPS):
+            mine = per_hop[k]
+            if k >= lag:
+                mine = after(mine, results[k - lag][0])
+            sets = []
+            for column in [mine] + [swap(mine, "dp", CORES * j) for j in range(1, rows_y)]:
                 sets.extend([column, swap(column, "dp", 1)])
-        return sets
-
-    def return_sets(parts):
-        total = None
+            results.append(compute(k, sets))
+        return results
+
+    def return_sets(parts, hold=None):
+        hops = []
         for k in range(HOPS):
             columns = []
             for j in range(rows_y):
@@ -326,32 +388,35 @@
             mine = columns[0]
             for j in range(1, rows_y):
                 mine = mine + swap(columns[j].astype(bf16), "dp", CORES * j).astype(f32)
-            if k:
-                mine = swap(mine.astype(bf16), "fsdp", lows * k).astype(f32)
-            total = mine if total is None else total + mine
+            hops.append(swap(mine.astype(bf16), "fsdp", lows * k) if k else mine)
+        if hold is not None:
+            hops = after(hops, hold)
+        total = hops[0]
+        for k in range(1, HOPS):
+            total = total + hops[k].astype(f32)
         return total
 
-    def gather_dense(block):
-        wide = block.shape[1]
-        full = block.reshape(1, 1, 1, 1, row_block, wide)
-        full = jnp.concatenate(
-            in_order(full, [swap(full, "fsdp", lows * k) for k in range(1, HOPS)], hop_at), axis=2
-        )
-        full = jnp.concatenate(
-            in_order(full, [swap(full, "dp", CORES * j) for j in range(1, rows_y)], y_at), axis=0
-        )
-        full = jnp.concatenate(
-            in_order(full, [swap(full, "fsdp", m) for m in range(1, lows)], low_at), axis=3
-        )
-        full = jnp.concatenate(in_order(full, [swap(full, "dp", 1)], core_at), axis=1)
-        return full.reshape(groups * shards * row_block, wide)
+    steps = (
+        (2, "fsdp", lows, HOPS, hop_at),
+        (0, "dp", CORES, rows_y, y_at),
+        (3, "fsdp", 1, lows, low_at),
+        (1, "dp", 1, CORES, core_at),
+    )
+
+    def send(full, step):
+        _, name, unit, size, _ = steps[step]
+        return [swap(full, name, unit * m) for m in range(1, size)]
+
+    def merge(full, others, step):
+        axis, _, _, _, at = steps[step]
+        return jnp.concatenate(in_order(full, others, at), axis=axis)
 
     def scatter_dense(grads):
         wide = grads.shape[1]
         part = grads.reshape(rows_y, CORES, HOPS, lows, row_block, wide)
 
         def stage(part, axis, name, place, size, unit):
-            mine = lax.dynamic_slice_in_dim(part, place, 1, axis)
+            mine = lax.dynamic_slice_in_dim(part, place, 1, axis).astype(f32)
             for m in range(1, size):
                 give = lax.dynamic_slice_in_dim(part, place ^ m, 1, axis).astype(bf16)
                 mine = mine + swap(give, name, unit * m).astype(f32)
@@ -369,10 +434,7 @@
     before = (positions[None, :] < positions[:, None]).astype(bf16)
     rank = dot(before, member.astype(bf16))
     place = jnp.where(member, rank, -1.0).T.astype(bf16)
-    first_held = dp_at * owned + hop_at * held
-    place_sets = jnp.stack(
-        [lax.dynamic_slice_in_dim(p, first_held, held, 0) for p in gather_sets(place)]
-    ).astype(f32)
+    first_held = (dp_at * owned + hop_at * held).astype(jnp.int32)[None]
 
     length_col = jnp.zeros((row_block, 1), bf16).at[0, 0].set(lengths[0].astype(bf16))
     pack = jnp.concatenate(
@@ -388,37 +450,57 @@
         ],
         axis=1,
     )
-    packed = gather_dense(pack)
+
+    split = expert_gate.shape[1]
+    shard = jnp.concatenate(
+        [jnp.concatenate([expert_gate, expert_up], axis=2), expert_down], axis=1
+    )
+
+    def owned_by(k):
+        return lax.dynamic_slice_in_dim(shard, (hop_at ^ k) * held, held, 0)
+
+    def low_swaps(block):
+        return [swap(block, "fsdp", m) for m in range(1, lows)]
+
+    join = lax.optimization_barrier
+    blocks = {0: owned_by(0)}
+    lows_of = {}
+    pack = pack.reshape(1, 1, 1, 1, row_block, -1)
+    lows_of[0] = low_swaps(blocks[0])
+    pack = merge(pack, send(pack, 0), 0)
+    others = send(pack, 1)
+    blocks[1] = swap(after(owned_by(1), pack), "fsdp", lows)
+    pack, others, blocks[1], lows_of[0] = join((pack, others, blocks[1], lows_of[0]))
+    pack = merge(pack, others, 1)
+    others = send(pack, 2)
+    blocks[3] = swap(after(owned_by(3), pack), "fsdp", lows * 3)
+    pack, others, blocks[3] = join((pack, others, blocks[3]))
+    pack = merge(pack, others, 2)
+    others = send(pack, 3)
+    out_w = after(w_out, pack).reshape(1, 1, 1, 1, row_block, -1)
+    lows_of[1] = low_swaps(after(blocks[1], pack))
+    out_others = send(out_w, 0)
+    pack, others, out_w, out_others = join((pack, others, out_w, out_others))
+    blocks[2] = swap(after(owned_by(2), others), "fsdp", lows * 2)
+    packed = merge(pack, others, 3).reshape(model_width, -1)
+    out_w = merge(out_w, out_others, 0)
+    out_others = send(out_w, 1)
     qkv_width = model_width + 2 * kv_width
     qkv_w = packed[:, :qkv_width]
     router_float = packed[:, qkv_width : qkv_width + experts].astype(f32)
     gain_float = packed[:, qkv_width + experts].astype(f32)
     gain_second = packed[:, qkv_width + experts + 1].astype(f32)
     valid_total = jnp.sum(packed[:, qkv_width + experts + 2].astype(f32))
-    out_w = gather_dense(w_out)
-
-    def gather_expert(shard):
-        def owned_by(k):
-            return lax.dynamic_slice_in_dim(shard, (hop_at ^ k) * held, held, 0)
-
-        per_hop = [owned_by(0)] + [swap(owned_by(k), "fsdp", lows * k) for k in range(1, HOPS)]
-        rows = shard.shape[1]
-        full = jnp.zeros((held, shards * rows, shard.shape[2]), bf16)
-        for k in range(HOPS):
-            for m in range(lows):
-                block = per_hop[k] if m == 0 else swap(per_hop[k], "fsdp", m)
-                at = ((hop_at ^ k) * lows + (low_at ^ m)) * rows
-                full = lax.dynamic_update_slice(full, block, (0, at, 0))
-        return full
-
-    wide_w = gather_expert(jnp.concatenate([expert_gate, expert_up], axis=2))
-    down_w = gather_expert(expert_down)
 
     tok_float = tokens.astype(f32)
     inv_one = lax.rsqrt(jnp.mean(tok_float * tok_float, axis=1, keepdims=True) + epsilon)
     normed = (tok_float * inv_one * gain_float).astype(bf16)
     cos_lanes, sin_lanes = rotary_lanes(seq_len)
     qkv = dot(normed, qkv_w)
+    qkv, out_w, out_others = join((qkv, out_w, out_others))
+    out_w = merge(out_w, out_others, 1)
+    out_others = send(out_w, 2)
+    lows_of[3] = low_swaps(after(blocks[3], qkv))
     rotated, mixed_rows = kernel_call(
         attention_forward,
         (
@@ -428,6 +510,15 @@
         (lengths, qkv, cos_lanes, sin_lanes),
         first_smem=True,
     )
+    mixed_rows, out_w, out_others = join((mixed_rows, out_w, out_others))
+    out_w = merge(out_w, out_others, 2)
+    out_w = merge(out_w, send(out_w, 3), 3).reshape(model_width, -1)
+    lows_of[2] = low_swaps(after(blocks[2], mixed_rows))
+    expert_w = jnp.zeros((held, shards, shard.shape[1], model_width), bf16)
+    for k in (0, 1, 3, 2):
+        for m, part in enumerate([blocks[k], *lows_of[k]]):
+            at = (hop_at ^ k) * lows + (low_at ^ m)
+            expert_w = lax.dynamic_update_slice(expert_w, part[:, None], (0, at, 0, 0))
     hidden = tok_float + residual_scale * dot(mixed_rows, out_w)
     inv_two = lax.rsqrt(jnp.mean(hidden * hidden, axis=1, keepdims=True) + epsilon)
     normed_ffn = hidden * inv_two * gain_second
@@ -437,34 +528,39 @@
     gate_weights = powers / jnp.sum(powers, axis=1, keepdims=True)
 
     gate_rows = seq_len * experts // model_width
-    gate_high = gate_weights.T.astype(bf16)
     outgoing = jnp.concatenate(
-        [normed_ffn.astype(bf16), gate_high.reshape(gate_rows, model_width)], axis=0
-    )
-    token_sets = gather_sets(outgoing)
+        [
+            normed_ffn.astype(bf16),
+            gate_weights.T.astype(bf16).reshape(gate_rows, model_width),
+            place.reshape(gate_rows, model_width),
+        ],
+        axis=0,
+    )
     count = rows_y * CORES
-    gate_sets = [
-        lax.dynamic_slice_in_dim(
-            s[seq_len:].reshape(experts, seq_len), first_held, held, 0
-        ).astype(f32)
-        for s in token_sets
-    ]
+    rows = count * CAP
     set_shape = jax.ShapeDtypeStruct((seq_len, model_width), bf16)
-    parts = []
-    per_hop = []
-    for k in range(HOPS):
-        at = slice(k * count, k * count + count)
-        common = (place_sets[at], jnp.stack(gate_sets[at]), wide_w, down_w, *token_sets[at])
-        per_hop.append(common)
-        parts.extend(
-            kernel_call(
-                functools.partial(expert_forward, count, seq_len),
-                (set_shape,) * count,
-                common,
-                scratch=(pltpu.VMEM((count * CAP, model_width), bf16),),
-            )
+    token_sets = []
+
+    def forward(k, sets):
+        first_now = after(first_held, forward_parts[-1]) if k else first_held
+        token_sets.append(sets)
+        results = kernel_call(
+            functools.partial(expert_forward, count, seq_len),
+            (set_shape,) * count,
+            (first_now, expert_w, *sets),
+            first_smem=True,
+            scratch=(
+                pltpu.VMEM((rows, model_width), bf16),
+                pltpu.VMEM((count, seq_len, model_width), f32),
+                pltpu.VMEM((count, CAP, seq_len), bf16),
+            ),
         )
-    combined = return_sets(parts)
+        forward_parts.extend(results)
+        return results
+
+    forward_parts = []
+    exchange(outgoing, 3, forward)
+    combined = return_sets(forward_parts)
     output = hidden + residual_scale * combined
     valid_rows = (positions < lengths[0]).astype(f32)[:, None]
     deviation = (output - teacher.astype(f32)) * valid_rows
@@ -479,85 +575,64 @@
             mask *= 2
     loss_value = loss_total[0, 0] / (valid_total * model_width)
 
-    grad_sets = gather_sets(out_grad.astype(bf16))
-    parts = []
+    back_shape = jax.ShapeDtypeStruct((seq_len + 2 * gate_rows, model_width), bf16)
+    back_parts = []
     saved = []
-    for k in range(HOPS):
-        rows = count * CAP
+
+    def backward(k, sets):
+        first_now = after(first_held, back_parts[-1]) if k else first_held
         results = kernel_call(
             functools.partial(expert_backward, count, seq_len),
-            (set_shape,) * count
+            (back_shape,) * count
             + (
-                jax.ShapeDtypeStruct((count, held, seq_len), f32),
                 jax.ShapeDtypeStruct((held, rows, model_width), bf16),
                 jax.ShapeDtypeStruct((held, rows, 2 * hidden_units), bf16),
                 jax.ShapeDtypeStruct((held, rows, model_width), bf16),
                 jax.ShapeDtypeStruct((held, rows, hidden_units), bf16),
             ),
-            (*per_hop[k], *grad_sets[k * count : k * count + count]),
-            scratch=(pltpu.VMEM((count, seq_len, model_width), f32),),
+            (first_now, expert_w, *token_sets[k], *sets),
+            first_smem=True,
+            scratch=(
+                pltpu.VMEM((count, seq_len, model_width), f32),
+                pltpu.VMEM((count, CAP, seq_len), bf16),
+                pltpu.VMEM((count, gate_rows, model_width), f32),
+            ),
         )
-        gate_grads = results[count]
-        saved.append(results[count + 1 :])
-        for s in range(count):
-            spread = lax.dynamic_update_slice(
-                jnp.zeros((experts, seq_len), f32), gate_grads[s], (first_held, 0)
-            )
-            high = spread.astype(bf16)
-            low = (spread - high.astype(f32)).astype(bf16)
-            parts.append(
-                jnp.concatenate(
-                    [
-                        results[s],
-                        high.reshape(gate_rows, model_width),
-                        low.reshape(gate_rows, model_width),
-                    ],
-                    axis=0,
-                )
-            )
-    returned = return_sets(parts)
-    rows = count * CAP
-    wide_grad, down_grad = pl.pallas_call(
+        saved.append(results[count:])
+        back_parts.extend(results[:count])
+        return results
+
+    exchange(out_grad.astype(bf16), 2, backward)
+    expert_grad = pl.pallas_call(
         functools.partial(expert_weight_grads, HOPS),
         grid=(held,),
-        out_shape=(
-            jax.ShapeDtypeStruct((held, model_width, 2 * hidden_units), bf16),
-            jax.ShapeDtypeStruct((held, hidden_units, model_width), bf16),
-        ),
+        out_shape=jax.ShapeDtypeStruct((held, shards, shard.shape[1], model_width), bf16),
         in_specs=[
             pl.BlockSpec((1, rows, width), lambda e: (e, 0, 0))
             for width in (model_width, 2 * hidden_units, model_width, hidden_units)
             for _ in range(HOPS)
         ],
-        out_specs=(
-            pl.BlockSpec((1, model_width, 2 * hidden_units), lambda e: (e, 0, 0)),
-            pl.BlockSpec((1, hidden_units, model_width), lambda e: (e, 0, 0)),
-        ),
+        out_specs=pl.BlockSpec((1, shards, shard.shape[1], model_width), lambda e: (e, 0, 0, 0)),
         compiler_params=pltpu.CompilerParams(vmem_limit_bytes=60 * 1024 * 1024),
     )(*[saved[k][i] for i in range(4) for k in range(HOPS)])
-
-    def scatter_expert(grads):
-        rows = grads.shape[1] // shards
-        width = grads.shape[2]
-        part = grads.reshape(held, HOPS, lows, rows, width)
-        mine = lax.dynamic_slice_in_dim(part, low_at, 1, 2).astype(f32)
+    returned = return_sets(back_parts, expert_grad)
+    part = expert_grad.reshape(held, HOPS, lows, shard.shape[1], model_width)
+    expert_out = jnp.zeros((owned, shard.shape[1], model_width), f32)
+    for k in (*range(HOPS - 1, 0, -1), 0):
+        at = hop_at ^ k
+        both_lows = lax.dynamic_slice_in_dim(part, at, 1, 1)
+        block = lax.dynamic_slice_in_dim(both_lows, low_at, 1, 2).astype(f32)
         for m in range(1, lows):
-            give = lax.dynamic_slice_in_dim(part, low_at ^ m, 1, 2)
-            mine = mine + swap(give, "fsdp", m).astype(f32)
-        mine = mine.reshape(held, HOPS, rows, width)
-        out = jnp.zeros((owned, rows, width), f32)
-        for k in range(HOPS):
-            block = lax.dynamic_slice_in_dim(mine, hop_at ^ k, 1, 1).reshape(held, rows, width)
-            if k:
-                block = swap(block.astype(bf16), "fsdp", lows * k).astype(f32)
-            out = lax.dynamic_update_slice(out, block, ((hop_at ^ k) * held, 0, 0))
-        return out
-
-    wide_out = scatter_expert(wide_grad)
+            give = lax.dynamic_slice_in_dim(both_lows, low_at ^ m, 1, 2)
+            block = block + swap(give, "fsdp", m).astype(f32)
+        block = block.reshape(held, shard.shape[1], model_width)
+        if k:
+            block = swap(after(block.astype(bf16), returned), "fsdp", lows * k).astype(f32)
+        expert_out = lax.dynamic_update_slice(expert_out, block, (at * held, 0, 0))
     expert_grads = (
-        wide_out[:, :, :hidden_units],
-        wide_out[:, :, hidden_units:],
-        scatter_expert(down_grad),
+        expert_out[:, :split, :hidden_units],
+        expert_out[:, :split, hidden_units:],
+        expert_out[:, split:, :],
     )
 
     gate_grad = (
@@ -577,7 +652,7 @@
     hidden_part, gain_two_grad = norm_back(ffn_in_grad, hidden, inv_two, gain_second)
     hidden_grad = out_grad + hidden_part
     attended_grad = (residual_scale * hidden_grad).astype(bf16)
-    out_grad_w = scatter_dense(dot_tn(mixed_rows, attended_grad))
+    out_grad_w = scatter_dense(dot_tn(mixed_rows, attended_grad).astype(bf16))
     mixed_grad = dot_nt(attended_grad, out_w).astype(bf16)
     qkv_grad = kernel_call(
         attention_backward,
@@ -589,18 +664,16 @@
     normed_grad = dot_nt(qkv_grad, qkv_w)
     token_part, gain_one_grad = norm_back(normed_grad, tok_float, inv_one, gain_float)
     token_grad = hidden_grad + token_part
-    small = scatter_dense(
-        jnp.concatenate(
-            [
-                dot_tn(normed, qkv_grad),
-                router_grad,
-                gain_one_grad[:, None],
-                gain_two_grad[:, None],
-                jnp.zeros((model_width, 128 - experts - 2), f32),
-            ],
-            axis=1,
-        )
-    )
+    small = jnp.concatenate(
+        [
+            router_grad,
+            gain_one_grad[:, None],
+            gain_two_grad[:, None],
+            jnp.zeros((model_width, 128 - experts - 2), f32),
+        ],
+        axis=1,
+    ).astype(bf16)
+    small = scatter_dense(jnp.concatenate([dot_tn(normed, qkv_grad).astype(bf16), small], axis=1))
     return (
         output.astype(bf16),
         loss_value,

time: 834 us -> 748 us (0.90)
  starting transfers between devices: 154 us -> 114 us
  local copies, waits for them, and re-layouts: 89.2 us -> 62 us
  other arithmetic: 63.9 us -> 53 us
    ppermute x126 -> x103, starting transfers between devices: 154 us -> 114 us  [swap(): lax.ppermute(values, axis, [(i, i ^ mask) for i in range(lax.axis_size(ax...]
    dynamic_update_slice x32 -> x8, local copies, waits for them, and re-layouts: 27.1 us -> 15.1 us  [on_device(): expert_w = lax.dynamic_update_slice(expert_w, part[:, None], (0, at, 0, 0))]
    concatenate x17 -> x10, other arithmetic: 15.4 us -> 4.29 us  [the longest x8 2.21 us: merge(): return jnp.concatenate(in_order(full, others, at), axis=axis)]
    unnamed x196 -> x155, local copies, waits for them, and re-layouts: 14.1 us -> 18.5 us
    ppermute x126 -> x103, waiting for transfers between devices: 355 us -> 351 us  [swap(): lax.ppermute(values, axis, [(i, i ^ mask) for i in range(lax.axis_size(ax...]
  transfers between devices with their start and end apart: 126 -> 103, of which waited for: 42 -> 36; matrix products, arithmetic and copies ran while one was open for 19% -> 15% of each run, Pallas kernels for 15% -> 17%
where the time goes in v2:
time: 748 us; the launch traced here: 738 us
  waiting for transfers between devices  351 us (47%)
  Pallas kernels  129 us (17%)
  starting transfers between devices  114 us (15%)
  local copies, waits for them, and re-layouts  62 us (8%)
  other arithmetic  53 us (7%)
  matrix products  22.8 us (3%)
    ppermute x103, waiting for transfers between devices, swap(): lax.ppermute(values, axis, [(i, i ^ mask) for i in range(lax.axis_size(ax...  351 us
    ppermute x103, starting transfers between devices, swap(): lax.ppermute(values, axis, [(i, i ^ mask) for i in range(lax.axis_size(ax...  114 us
    pallas_call x10, Pallas kernels, kernel_call(): pl.pallas_call(body, out_shape=out_shape, in_specs=specs, out_specs=jax.t...  110 us
    pallas_call x1, Pallas kernels, on_device(): pl.pallas_call(functools.partial(expert_weight_grads, HOPS), grid=(held,)...  19.5 us
    unnamed x155, local copies, waits for them, and re-layouts  18.5 us
    dynamic_update_slice x8, local copies, waits for them, and re-layouts, on_device(): expert_w = lax.dynamic_update_slice(expert_w, part[:, None], (0, at, 0, 0))  15.1 us
  transfers between devices with their start and end apart: 103, of which 36 were waited for; matrix products, arithmetic and copies ran while one was open for 15% of the time, Pallas kernels for 17%

profile of v2, /device:TPU:0, one launch (start us, length us, event | category | flops | bytes accessed | tf_op | source)
XLA Modules:
  0.0 738.1 jit_solution(3576896318729244216)
XLA Ops:
  23.6 12.2 %collective-permute-done.3 = bf16[1,1,4,1,32,2176]{5,4,3,2,1,0:T(8,128)(2,1)S(1)} collective-permute-done((bf16[1,1,4,1,32,2176]{5,4,3,2,1,0:T(8,128)(2,1)S(1)}, bf16[1,1,4,1,32,2176]{5,4,3,2,1,0:T(8,128)(2,1)S(1)}, u32[]{:S(2)}, u32[]{:S(2)}) %collective-permute-start.3) | collective-permute-done | bytes 557088 | tf_op jit(solution)/shard_map/ppermute | solution.py:40
  44.9 17.4 %collective-permute-done.7 = bf16[2,192,1024]{2,1,0:T(8,128)(2,1)} collective-permute-done((bf16[2,192,1024]{2,1,0:T(8,128)(2,1)}, bf16[2,192,1024]{2,1,0:T(8,128)(2,1)}, u32[]{:S(2)}, u32[]{:S(2)}) %collective-permute-start.7) | collective-permute-done | bytes 786464 | tf_op jit(solution)/shard_map/ppermute | solution.py:40
  67.3 12.0 %collective-permute-start.9 = (bf16[1,1,1,1,32,1024]{5,4,3,2,1,0:T(8,128)(2,1)}, bf16[1,1,1,1,32,1024]{5,4,3,2,1,0:T(8,128)(2,1)}, u32[]{:S(2)}, u32[]{:S(2)}) collective-permute-start(bf16[1,1,1,1,32,1024]{5,4,3,2,1,0:T(8,128)(2,1)} %bitcast.5), channel_id=1, source_target_pairs={{0,2},{1,3},{2,0},{3,1},{4,6},{5,7},{6,4},{7,5},{8,10},{9,11},{10,... | collective-permute-start | bytes 196616 | tf_op jit(solution)/shard_map/ppermute | solution.py:40
  102.2 9.6 %shard_map.237 = (bf16[256,2048]{1,0:T(8,128)(2,1)}, bf16[256,1024]{1,0:T(8,128)(2,1)}) custom-call(s32[1]{0:T(128)} %copy.133.length_ref, f32[256,2048]{1,0:T(8,128)} %fusion.2.qkv_ref, f32[256,128]{1,0:T(8,128)} %get-tuple-element.277.cos_ref, f32[256,128]{1,0:T(8,128)} %get-tuple-element.278.sin_ref), custom_call_target="tpu_custom_call" | custom-call | tf_op jit(solution)/shard_map/pallas_call | solution.py:59
  120.9 30.4 %collective-permute-done.17 = bf16[2,192,1024]{2,1,0:T(8,128)(2,1)} collective-permute-done((bf16[2,192,1024]{2,1,0:T(8,128)(2,1)}, bf16[2,192,1024]{2,1,0:T(8,128)(2,1)}, u32[]{:S(2)}, u32[]{:S(2)}) %collective-permute-start.17) | collective-permute-done | bytes 786464 | tf_op jit(solution)/shard_map/ppermute | solution.py:40
  174.2 10.8 %collective-permute-done.25.refs_0_ = bf16[272,1024]{1,0:T(8,128)(2,1)S(1)} collective-permute-done((bf16[272,1024]{1,0:T(8,128)(2,1)S(1)}, bf16[272,1024]{1,0:T(8,128)(2,1)S(1)}, u32[]{:S(2)}, u32[]{:S(2)}) %collective-permute-start.25) | collective-permute-done | bytes 557088 | tf_op jit(solution)/shard_map/ppermute | solution.py:40
  187.5 14.8 %collective-permute-done.33.refs_0_ = bf16[272,1024]{1,0:T(8,128)(2,1)S(1)} collective-permute-done((bf16[272,1024]{1,0:T(8,128)(2,1)S(1)}, bf16[272,1024]{1,0:T(8,128)(2,1)S(1)}, u32[]{:S(2)}, u32[]{:S(2)}) %collective-permute-start.33) | collective-permute-done | bytes 557088 | tf_op jit(solution)/shard_map/ppermute | solution.py:40
  208.6 8.8 %shard_map.238 = (bf16[256,1024]{1,0:T(8,128)(2,1)}, bf16[256,1024]{1,0:T(8,128)(2,1)}, bf16[256,1024]{1,0:T(8,128)(2,1)}, bf16[256,1024]{1,0:T(8,128)(2,1)}) custom-call(s32[1]{0:T(128)} %bitcast.9.first_ref, bf16[2,8,192,1024]{3,2,1,0:T(8,128)(2,1)} %bitcast_dynamic-update-slice_fusion.7.weights_ref, bf16[272,1024]{1,0:T(8,128)(2,1)} %copy-done.6, ...), custom_call_target="tpu_custom_call" | custom-call | tf_op jit(solution)/shard_map/pallas_call | solution.py:59
  220.1 12.2 %collective-permute-done.43.refs_2_ = bf16[272,1024]{1,0:T(8,128)(2,1)S(1)} collective-permute-done((bf16[272,1024]{1,0:T(8,128)(2,1)S(1)}, bf16[272,1024]{1,0:T(8,128)(2,1)S(1)}, u32[]{:S(2)}, u32[]{:S(2)}) %collective-permute-start.43) | collective-permute-done | bytes 557088 | tf_op jit(solution)/shard_map/ppermute | solution.py:40
  232.3 9.1 %shard_map.239 = (bf16[256,1024]{1,0:T(8,128)(2,1)}, bf16[256,1024]{1,0:T(8,128)(2,1)}, bf16[256,1024]{1,0:T(8,128)(2,1)}, bf16[256,1024]{1,0:T(8,128)(2,1)}) custom-call(s32[1]{0:T(128)} %bitcast.9.first_ref, bf16[2,8,192,1024]{3,2,1,0:T(8,128)(2,1)} %bitcast_dynamic-update-slice_fusion.7.weights_ref, bf16[272,1024]{1,0:T(8,128)(2,1)} %copy-done.11, ...), custom_call_target="tpu_custom_call" | custom-call | tf_op jit(solution)/shard_map/pallas_call | solution.py:59
  243.0 8.9 %shard_map.240 = (bf16[256,1024]{1,0:T(8,128)(2,1)}, bf16[256,1024]{1,0:T(8,128)(2,1)}, bf16[256,1024]{1,0:T(8,128)(2,1)}, bf16[256,1024]{1,0:T(8,128)(2,1)}) custom-call(s32[1]{0:T(128)} %bitcast.9.first_ref, bf16[2,8,192,1024]{3,2,1,0:T(8,128)(2,1)} %bitcast_dynamic-update-slice_fusion.7.weights_ref, bf16[272,1024]{1,0:T(8,128)(2,1)} %copy-done.9, ...), custom_call_target="tpu_custom_call" | custom-call | tf_op jit(solution)/shard_map/pallas_call | solution.py:59
  255.8 8.8 %shard_map.241 = (bf16[256,1024]{1,0:T(8,128)(2,1)}, bf16[256,1024]{1,0:T(8,128)(2,1)}, bf16[256,1024]{1,0:T(8,128)(2,1)}, bf16[256,1024]{1,0:T(8,128)(2,1)}) custom-call(s32[1]{0:T(128)} %bitcast.9.first_ref, bf16[2,8,192,1024]{3,2,1,0:T(8,128)(2,1)} %bitcast_dynamic-update-slice_fusion.7.weights_ref, bf16[272,1024]{1,0:T(8,128)(2,1)} %copy-done.8, ...), custom_call_target="tpu_custom_call" | custom-call | tf_op jit(solution)/shard_map/pallas_call | solution.py:59
  268.6 11.4 %collective-permute-done.39 = bf16[256,1024]{1,0:T(8,128)(2,1)S(1)} collective-permute-done((bf16[256,1024]{1,0:T(8,128)(2,1)S(1)}, bf16[256,1024]{1,0:T(8,128)(2,1)S(1)}, u32[]{:S(2)}, u32[]{:S(2)}) %collective-permute-start.39) | collective-permute-done | bytes 524320 | tf_op jit(solution)/shard_map/ppermute | solution.py:40
  317.6 10.5 %collective-permute-done.32 = bf16[256,1024]{1,0:T(8,128)(2,1)} collective-permute-done((bf16[256,1024]{1,0:T(8,128)(2,1)S(1)}, bf16[256,1024]{1,0:T(8,128)(2,1)}, u32[]{:S(2)}, u32[]{:S(2)}) %collective-permute-start.32) | collective-permute-done | bytes 524320 | tf_op jit(solution)/shard_map/ppermute | solution.py:40
  332.1 10.4 %collective-permute-start.60 = (bf16[256,1024]{1,0:T(8,128)(2,1)S(1)}, bf16[256,1024]{1,0:T(8,128)(2,1)S(1)}, u32[]{:S(2)}, u32[]{:S(2)}) collective-permute-start(bf16[256,1024]{1,0:T(8,128)(2,1)S(1)} %get-tuple-element.215.refs_4_), channel_id=1, source_target_pairs={{0,2},{1,3},{2,0},{3,1},{4,6},{5,7},{6,4},{7,5},{8,10},{9,11},{10,... | collective-permute-start | bytes 1572872 | tf_op jit(solution)/shard_map/ppermute | solution.py:40
  344.0 10.6 %collective-permute-done.60.refs_4_ = bf16[256,1024]{1,0:T(8,128)(2,1)S(1)} collective-permute-done((bf16[256,1024]{1,0:T(8,128)(2,1)S(1)}, bf16[256,1024]{1,0:T(8,128)(2,1)S(1)}, u32[]{:S(2)}, u32[]{:S(2)}) %collective-permute-start.60) | collective-permute-done | bytes 524320 | tf_op jit(solution)/shard_map/ppermute | solution.py:40
  358.8 9.0 %collective-permute-done.62.refs_6_ = bf16[256,1024]{1,0:T(8,128)(2,1)S(1)} collective-permute-done((bf16[256,1024]{1,0:T(8,128)(2,1)S(1)}, bf16[256,1024]{1,0:T(8,128)(2,1)S(1)}, u32[]{:S(2)}, u32[]{:S(2)}) %collective-permute-start.62) | collective-permute-done | bytes 524320 | tf_op jit(solution)/shard_map/ppermute | solution.py:40
  370.7 12.9 %shard_map.242 = (bf16[272,1024]{1,0:T(8,128)(2,1)}, bf16[272,1024]{1,0:T(8,128)(2,1)}, bf16[272,1024]{1,0:T(8,128)(2,1)}, bf16[272,1024]{1,0:T(8,128)(2,1)}, bf...) custom-call(s32[1]{0:T(128)} %bitcast.9.first_ref, ...), custom_call_target="tpu_custom_call" | custom-call | tf_op jit(solution)/shard_map/pallas_call | solution.py:59
  383.6 11.2 %collective-permute-done.68.refs_4_ = bf16[256,1024]{1,0:T(8,128)(2,1)S(1)} collective-permute-done((bf16[256,1024]{1,0:T(8,128)(2,1)S(1)}, bf16[256,1024]{1,0:T(8,128)(2,1)S(1)}, u32[]{:S(2)}, u32[]{:S(2)}) %collective-permute-start.68) | collective-permute-done | bytes 524320 | tf_op jit(solution)/shard_map/ppermute | solution.py:40
  397.2 13.3 %shard_map.243 = (bf16[272,1024]{1,0:T(8,128)(2,1)}, bf16[272,1024]{1,0:T(8,128)(2,1)}, bf16[272,1024]{1,0:T(8,128)(2,1)}, bf16[272,1024]{1,0:T(8,128)(2,1)}, bf...) custom-call(s32[1]{0:T(128)} %bitcast.9.first_ref, ...), custom_call_target="tpu_custom_call" | custom-call | tf_op jit(solution)/shard_map/pallas_call | solution.py:59
  412.8 10.7 %collective-permute-done.78.refs_6_ = bf16[256,1024]{1,0:T(8,128)(2,1)S(1)} collective-permute-done((bf16[256,1024]{1,0:T(8,128)(2,1)S(1)}, bf16[256,1024]{1,0:T(8,128)(2,1)S(1)}, u32[]{:S(2)}, u32[]{:S(2)}) %collective-permute-start.78) | collective-permute-done | bytes 524320 | tf_op jit(solution)/shard_map/ppermute | solution.py:40
  425.1 12.9 %shard_map.244 = (bf16[272,1024]{1,0:T(8,128)(2,1)}, bf16[272,1024]{1,0:T(8,128)(2,1)}, bf16[272,1024]{1,0:T(8,128)(2,1)}, bf16[272,1024]{1,0:T(8,128)(2,1)}, bf...) custom-call(s32[1]{0:T(128)} %bitcast.9.first_ref, ...), custom_call_target="tpu_custom_call" | custom-call | tf_op jit(solution)/shard_map/pallas_call | solution.py:59
  440.1 13.1 %shard_map.245 = (bf16[272,1024]{1,0:T(8,128)(2,1)}, bf16[272,1024]{1,0:T(8,128)(2,1)}, bf16[272,1024]{1,0:T(8,128)(2,1)}, bf16[272,1024]{1,0:T(8,128)(2,1)}, bf...) custom-call(s32[1]{0:T(128)} %bitcast.9.first_ref, ...), custom_call_target="tpu_custom_call" | custom-call | tf_op jit(solution)/shard_map/pallas_call | solution.py:59
  458.0 11.4 %collective-permute-done.66 = bf16[272,1024]{1,0:T(8,128)(2,1)S(1)} collective-permute-done((bf16[272,1024]{1,0:T(8,128)(2,1)S(1)}, bf16[272,1024]{1,0:T(8,128)(2,1)S(1)}, u32[]{:S(2)}, u32[]{:S(2)}) %collective-permute-start.66) | collective-permute-done | bytes 557088 | tf_op jit(solution)/shard_map/ppermute | solution.py:40
  472.5 8.8 %collective-permute-done.74 = bf16[272,1024]{1,0:T(8,128)(2,1)S(1)} collective-permute-done((bf16[272,1024]{1,0:T(8,128)(2,1)S(1)}, bf16[272,1024]{1,0:T(8,128)(2,1)S(1)}, u32[]{:S(2)}, u32[]{:S(2)}) %collective-permute-start.74) | collective-permute-done | bytes 557088 | tf_op jit(solution)/shard_map/ppermute | solution.py:40
  485.0 8.3 %collective-permute-done.82 = bf16[272,1024]{1,0:T(8,128)(2,1)S(1)} collective-permute-done((bf16[272,1024]{1,0:T(8,128)(2,1)S(1)}, bf16[272,1024]{1,0:T(8,128)(2,1)S(1)}, u32[]{:S(2)}, u32[]{:S(2)}) %collective-permute-start.82) | collective-permute-done | bytes 557088 | tf_op jit(solution)/shard_map/ppermute | solution.py:40
  506.2 19.5 %shard_map.246 = bf16[2,8,192,1024]{3,2,1,0:T(8,128)(2,1)} custom-call(bf16[2,384,1024]{2,1,0:T(8,128)(2,1)} %get-tuple-element.185.refs_0_, bf16[2,384,1024]{2,1,0:T(8,128)(2,1)} %get-tuple-element.186.refs_1_, bf16[2,384,1024]{2,1,0:T(8,128)(2,1)} %get-tuple-element.187.refs_2_, bf16[2,384,1024]{2,1,0:T(8,128)(2,1)} %get-tuple-element.188.refs_3_, ...), custom_call_target="tpu_custom_call" | custom-call | tf_op jit(solution)/shard_map/pallas_call | solution.py:606
  544.7 12.1 %shard_map.247 = bf16[256,2048]{1,0:T(8,128)(2,1)} custom-call(s32[1]{0:T(128)} %copy.133.length_ref, bf16[256,2048]{1,0:T(8,128)(2,1)} %get-tuple-element.205.rot_ref, bf16[256,1024]{1,0:T(8,128)(2,1)} %convolution_convert_fusion.2.grad_ref, f32[256,128]{1,0:T(8,128)} %get-tuple-element.277.cos_ref, f32[256,128]{1,0:T(8,128)} %get-tuple-element.278.sin_ref), custom_call_target="tpu_custom_call" | custom-call | tf_op jit(solution)/shard_map/pallas_call | solution.py:59
  600.1 22.5 %collective-permute-done.52 = f32[8,128]{1,0:T(8,128)S(1)} collective-permute-done((f32[8,128]{1,0:T(8,128)S(1)}, f32[8,128]{1,0:T(8,128)S(1)}, u32[]{:S(2)}, u32[]{:S(2)}) %collective-permute-start.52) | collective-permute-done | bytes 4128 | tf_op jit(solution)/shard_map/ppermute | solution.py:40
  625.5 29.8 %collective-permute-done.53 = f32[8,128]{1,0:T(8,128)S(1)} collective-permute-done((f32[8,128]{1,0:T(8,128)S(1)}, f32[8,128]{1,0:T(8,128)S(1)}, u32[]{:S(2)}, u32[]{:S(2)}) %collective-permute-start.53) | collective-permute-done | bytes 4128 | tf_op jit(solution)/shard_map/ppermute | solution.py:40
  665.3 11.5 %collective-permute-done.101 = bf16[2,192,1024]{2,1,0:T(8,128)(2,1)S(1)} collective-permute-done((bf16[2,192,1024]{2,1,0:T(8,128)(2,1)}, bf16[2,192,1024]{2,1,0:T(8,128)(2,1)S(1)}, u32[]{:S(2)}, u32[]{:S(2)}) %collective-permute-start.101) | collective-permute-done | bytes 786464 | tf_op jit(solution)/shard_map/ppermute | solution.py:40
  680.2 19.7 %collective-permute-done.91 = bf16[1,1,4,2,32,1024]{5,4,3,2,1,0:T(8,128)(2,1)S(1)} collective-permute-done((bf16[1,1,4,2,32,1024]{5,4,3,2,1,0:T(8,128)(2,1)S(1)}, bf16[1,1,4,2,32,1024]{5,4,3,2,1,0:T(8,128)(2,1)S(1)}, u32[]{:S(2)}, u32[]{:S(2)}) %collective-permute-start.91) | collective-permute-done | bytes 524320 | tf_op jit(solution)/shard_map/ppermute | solution.py:40
  (463 shorter events, 307.3 us)
Async XLA Ops:
  113.0 39.5 %collective-permute-start.14 = (bf16[2,1,4,2,32,1024]{5,4,3,2,1,0:T(8,128)(2,1)}, bf16[2,1,4,2,32,1024]{5,4,3,2,1,0:T(8,128)(2,1)}, u32[]{:S(2)}, u32[]{:S(2)}) collective-permute-start(bf16[2,1,4,2,32,1024]{5,4,3,2,1,0:T(8,128)(2,1)} %pad_maximum_fusion.5), channel_id=1, source_target_pairs={{0,8},{8,0},{16,24},{24,16},{1,9},{9,1},{17,25},{25,17},{2,10},{10... | collective-permute-start | bytes 3145736 | tf_op jit(solution)/shard_map/ppermute | solution.py:40
  113.0 38.3 %collective-permute-start.17 = (bf16[2,192,1024]{2,1,0:T(8,128)(2,1)}, bf16[2,192,1024]{2,1,0:T(8,128)(2,1)}, u32[]{:S(2)}, u32[]{:S(2)}) collective-permute-start(bf16[2,192,1024]{2,1,0:T(8,128)(2,1)} %get-tuple-element.142), channel_id=1, source_target_pairs={{0,4},{1,5},{2,6},{3,7},{4,0},{5,1},{6,2},{7,3},{8,12},{9,13},{10,... | collective-permute-start | bytes 2359304 | tf_op jit(solution)/shard_map/ppermute | solution.py:40
  118.6 43.5 %collective-permute-start.15 = (bf16[2,192,1024]{2,1,0:T(8,128)(2,1)S(1)}, bf16[2,192,1024]{2,1,0:T(8,128)(2,1)}, u32[]{:S(2)}, u32[]{:S(2)}) collective-permute-start(bf16[2,192,1024]{2,1,0:T(8,128)(2,1)S(1)} %collective-permute-done.4), channel_id=1, source_target_pairs={{0,1},{1,0},{2,3},{3,2},{4,5},{5,4},{6,7},{7,6},{8,9},{9,8},{10,11... | collective-permute-start | bytes 2359304 | tf_op jit(solution)/shard_map/ppermute | solution.py:40
  120.0 46.6 %collective-permute-start.16 = (bf16[2,192,1024]{2,1,0:T(8,128)(2,1)}, bf16[2,192,1024]{2,1,0:T(8,128)(2,1)}, u32[]{:S(2)}, u32[]{:S(2)}) collective-permute-start(bf16[2,192,1024]{2,1,0:T(8,128)(2,1)} %collective-permute-done.7), channel_id=1, source_target_pairs={{0,1},{1,0},{2,3},{3,2},{4,5},{5,4},{6,7},{7,6},{8,9},{9,8},{10,11... | collective-permute-start | bytes 2359304 | tf_op jit(solution)/shard_map/ppermute | solution.py:40
  162.1 40.3 %collective-permute-start.33 = (bf16[272,1024]{1,0:T(8,128)(2,1)S(1)}, bf16[272,1024]{1,0:T(8,128)(2,1)S(1)}, u32[]{:S(2)}, u32[]{:S(2)}) collective-permute-start(bf16[272,1024]{1,0:T(8,128)(2,1)S(1)} %pad_maximum_fusion.7.refs_0_), channel_id=1, source_target_pairs={{0,4},{1,5},{2,6},{3,7},{4,0},{5,1},{6,2},{7,3},{8,12},{9,13},{10,... | collective-permute-start | bytes 1671176 | tf_op jit(solution)/shard_map/ppermute | solution.py:40
  166.6 38.3 %collective-permute-start.19 = (bf16[272,1024]{1,0:T(8,128)(2,1)S(1)}, bf16[272,1024]{1,0:T(8,128)(2,1)S(1)}, u32[]{:S(2)}, u32[]{:S(2)}) collective-permute-start(bf16[272,1024]{1,0:T(8,128)(2,1)S(1)} %pad_maximum_fusion.7.refs_0_), channel_id=1, source_target_pairs={{0,8},{8,0},{16,24},{24,16},{1,9},{9,1},{17,25},{25,17},{2,10},{10... | collective-permute-start | bytes 1671176 | tf_op jit(solution)/shard_map/ppermute | solution.py:40
  172.1 45.3 %collective-permute-start.41 = (bf16[272,1024]{1,0:T(8,128)(2,1)S(1)}, bf16[272,1024]{1,0:T(8,128)(2,1)S(1)}, u32[]{:S(2)}, u32[]{:S(2)}) collective-permute-start(bf16[272,1024]{1,0:T(8,128)(2,1)S(1)} %pad_maximum_fusion.7.refs_0_), channel_id=1, source_target_pairs={{0,6},{1,7},{2,4},{3,5},{4,2},{5,3},{6,0},{7,1},{8,14},{9,15},{10,... | collective-permute-start | bytes 1671176 | tf_op jit(solution)/shard_map/ppermute | solution.py:40
  174.2 33.5 %collective-permute-start.21 = (bf16[272,1024]{1,0:T(8,128)(2,1)S(1)}, bf16[272,1024]{1,0:T(8,128)(2,1)S(1)}, u32[]{:S(2)}, u32[]{:S(2)}) collective-permute-start(bf16[272,1024]{1,0:T(8,128)(2,1)S(1)} %collective-permute-done.20.refs_2_), channel_id=1, source_target_pairs={{0,8},{8,0},{16,24},{24,16},{1,9},{9,1},{17,25},{25,17},{2,10},{10... | collective-permute-start | bytes 1671176 | tf_op jit(solution)/shard_map/ppermute | solution.py:40
  219.5 32.9 %collective-permute-start.23 = (bf16[256,1024]{1,0:T(8,128)(2,1)}, bf16[256,1024]{1,0:T(8,128)(2,1)}, u32[]{:S(2)}, u32[]{:S(2)}) collective-permute-start(bf16[256,1024]{1,0:T(8,128)(2,1)} %get-tuple-element.147), channel_id=1, source_target_pairs={{0,8},{8,0},{16,24},{24,16},{1,9},{9,1},{17,25},{25,17},{2,10},{10... | collective-permute-start | bytes 1572872 | tf_op jit(solution)/shard_map/ppermute | solution.py:40
  219.6 35.1 %collective-permute-start.42 = (bf16[272,1024]{1,0:T(8,128)(2,1)S(1)}, bf16[272,1024]{1,0:T(8,128)(2,1)S(1)}, u32[]{:S(2)}, u32[]{:S(2)}) collective-permute-start(bf16[272,1024]{1,0:T(8,128)(2,1)S(1)} %collective-permute-done.41.refs_0_), channel_id=1, source_target_pairs={{0,8},{8,0},{16,24},{24,16},{1,9},{9,1},{17,25},{25,17},{2,10},{10... | collective-permute-start | bytes 1671176 | tf_op jit(solution)/shard_map/ppermute | solution.py:40
  252.2 55.0 %collective-permute-start.22 = (bf16[256,1024]{1,0:T(8,128)(2,1)}, bf16[256,1024]{1,0:T(8,128)(2,1)}, u32[]{:S(2)}, u32[]{:S(2)}) collective-permute-start(bf16[256,1024]{1,0:T(8,128)(2,1)} %get-tuple-element.145), channel_id=1, source_target_pairs={{0,8},{8,0},{16,24},{24,16},{1,9},{9,1},{17,25},{25,17},{2,10},{10... | collective-permute-start | bytes 1572872 | tf_op jit(solution)/shard_map/ppermute | solution.py:40
  292.7 35.4 %collective-permute-start.32 = (bf16[256,1024]{1,0:T(8,128)(2,1)S(1)}, bf16[256,1024]{1,0:T(8,128)(2,1)}, u32[]{:S(2)}, u32[]{:S(2)}) collective-permute-start(bf16[256,1024]{1,0:T(8,128)(2,1)S(1)} %add_convert_fusion.14), channel_id=1, source_target_pairs={{0,2},{1,3},{2,0},{3,1},{4,6},{5,7},{6,4},{7,5},{8,10},{9,11},{10,... | collective-permute-start | bytes 1572872 | tf_op jit(solution)/shard_map/ppermute | solution.py:40
  356.6 38.2 %collective-permute-start.68 = (bf16[256,1024]{1,0:T(8,128)(2,1)S(1)}, bf16[256,1024]{1,0:T(8,128)(2,1)S(1)}, u32[]{:S(2)}, u32[]{:S(2)}) collective-permute-start(bf16[256,1024]{1,0:T(8,128)(2,1)S(1)} %get-tuple-element.215.refs_4_), channel_id=1, source_target_pairs={{0,4},{1,5},{2,6},{3,7},{4,0},{5,1},{6,2},{7,3},{8,12},{9,13},{10,... | collective-permute-start | bytes 1572872 | tf_op jit(solution)/shard_map/ppermute | solution.py:40
  358.8 36.8 %collective-permute-start.61 = (bf16[256,1024]{1,0:T(8,128)(2,1)S(1)}, bf16[256,1024]{1,0:T(8,128)(2,1)S(1)}, u32[]{:S(2)}, u32[]{:S(2)}) collective-permute-start(bf16[256,1024]{1,0:T(8,128)(2,1)S(1)} %collective-permute-done.60.refs_4_), channel_id=1, source_target_pairs={{0,8},{8,0},{16,24},{24,16},{1,9},{9,1},{17,25},{25,17},{2,10},{10... | collective-permute-start | bytes 1572872 | tf_op jit(solution)/shard_map/ppermute | solution.py:40
  367.8 42.7 %collective-permute-start.76 = (bf16[256,1024]{1,0:T(8,128)(2,1)S(1)}, bf16[256,1024]{1,0:T(8,128)(2,1)S(1)}, u32[]{:S(2)}, u32[]{:S(2)}) collective-permute-start(bf16[256,1024]{1,0:T(8,128)(2,1)S(1)} %get-tuple-element.215.refs_4_), channel_id=1, source_target_pairs={{0,6},{1,7},{2,4},{3,5},{4,2},{5,3},{6,0},{7,1},{8,14},{9,15},{10,... | collective-permute-start | bytes 1572872 | tf_op jit(solution)/shard_map/ppermute | solution.py:40
  412.2 41.0 %collective-permute-start.65 = (bf16[272,1024]{1,0:T(8,128)(2,1)}, bf16[272,1024]{1,0:T(8,128)(2,1)S(1)}, u32[]{:S(2)}, u32[]{:S(2)}) collective-permute-start(bf16[272,1024]{1,0:T(8,128)(2,1)} %get-tuple-element.172), channel_id=1, source_target_pairs={{0,8},{8,0},{16,24},{24,16},{1,9},{9,1},{17,25},{25,17},{2,10},{10... | collective-permute-start | bytes 1671176 | tf_op jit(solution)/shard_map/ppermute | solution.py:40
  457.2 39.8 %collective-permute-start.57 = (bf16[272,1024]{1,0:T(8,128)(2,1)}, bf16[272,1024]{1,0:T(8,128)(2,1)S(1)}, u32[]{:S(2)}, u32[]{:S(2)}) collective-permute-start(bf16[272,1024]{1,0:T(8,128)(2,1)} %get-tuple-element.165), channel_id=1, source_target_pairs={{0,8},{8,0},{16,24},{24,16},{1,9},{9,1},{17,25},{25,17},{2,10},{10... | collective-permute-start | bytes 1671176 | tf_op jit(solution)/shard_map/ppermute | solution.py:40
  470.8 33.8 %collective-permute-start.59 = (bf16[272,1024]{1,0:T(8,128)(2,1)}, bf16[272,1024]{1,0:T(8,128)(2,1)}, u32[]{:S(2)}, u32[]{:S(2)}) collective-permute-start(bf16[272,1024]{1,0:T(8,128)(2,1)} %add_convert_fusion.9), channel_id=1, source_target_pairs={{0,16},{8,24},{16,0},{24,8},{1,17},{9,25},{17,1},{25,9},{2,18},{10... | collective-permute-start | bytes 1671176 | tf_op jit(solution)/shard_map/ppermute | solution.py:40
  481.3 50.3 %collective-permute-start.67 = (bf16[272,1024]{1,0:T(8,128)(2,1)}, bf16[272,1024]{1,0:T(8,128)(2,1)}, u32[]{:S(2)}, u32[]{:S(2)}) collective-permute-start(bf16[272,1024]{1,0:T(8,128)(2,1)} %add_convert_fusion.7), channel_id=1, source_target_pairs={{0,2},{1,3},{2,0},{3,1},{4,6},{5,7},{6,4},{7,5},{8,10},{9,11},{10,... | collective-permute-start | bytes 1671176 | tf_op jit(solution)/shard_map/ppermute | solution.py:40
  482.4 50.0 %collective-permute-start.75 = (bf16[272,1024]{1,0:T(8,128)(2,1)}, bf16[272,1024]{1,0:T(8,128)(2,1)}, u32[]{:S(2)}, u32[]{:S(2)}) collective-permute-start(bf16[272,1024]{1,0:T(8,128)(2,1)} %add_convert_fusion.5), channel_id=1, source_target_pairs={{0,4},{1,5},{2,6},{3,7},{4,0},{5,1},{6,2},{7,3},{8,12},{9,13},{10,... | collective-permute-start | bytes 1671176 | tf_op jit(solution)/shard_map/ppermute | solution.py:40
  494.3 39.3 %collective-permute-start.83 = (bf16[272,1024]{1,0:T(8,128)(2,1)}, bf16[272,1024]{1,0:T(8,128)(2,1)}, u32[]{:S(2)}, u32[]{:S(2)}) collective-permute-start(bf16[272,1024]{1,0:T(8,128)(2,1)} %add_convert_fusion.3), channel_id=1, source_target_pairs={{0,6},{1,7},{2,4},{3,5},{4,2},{5,3},{6,0},{7,1},{8,14},{9,15},{10,... | collective-permute-start | bytes 1671176 | tf_op jit(solution)/shard_map/ppermute | solution.py:40
  529.5 49.6 %collective-permute-start.100 = (bf16[2,1,1,192,1024]{4,3,0,2,1:T(8,128)(2,1)}, bf16[2,1,1,192,1024]{4,3,0,2,1:T(8,128)(2,1)}, u32[]{:S(2)}, u32[]{:S(2)}) collective-permute-start(bf16[2,1,1,192,1024]{4,3,0,2,1:T(8,128)(2,1)} %get-tuple-element.222), channel_id=1, source_target_pairs={{0,1},{1,0},{2,3},{3,2},{4,5},{5,4},{6,7},{7,6},{8,9},{9,8},{10,11... | collective-permute-start | bytes 2359304 | tf_op jit(solution)/shard_map/ppermute | solution.py:40
  530.4 49.2 %collective-permute-start.98 = (bf16[2,1,1,192,1024]{4,3,0,2,1:T(8,128)(2,1)}, bf16[2,1,1,192,1024]{4,3,0,2,1:T(8,128)(2,1)}, u32[]{:S(2)}, u32[]{:S(2)}) collective-permute-start(bf16[2,1,1,192,1024]{4,3,0,2,1:T(8,128)(2,1)} %get-tuple-element.223), channel_id=1, source_target_pairs={{0,1},{1,0},{2,3},{3,2},{4,5},{5,4},{6,7},{7,6},{8,9},{9,8},{10,11... | collective-permute-start | bytes 2359304 | tf_op jit(solution)/shard_map/ppermute | solution.py:40
  531.6 52.4 %collective-permute-start.96 = (bf16[2,1,1,192,1024]{4,3,0,2,1:T(8,128)(2,1)}, bf16[2,1,1,192,1024]{4,3,0,2,1:T(8,128)(2,1)}, u32[]{:S(2)}, u32[]{:S(2)}) collective-permute-start(bf16[2,1,1,192,1024]{4,3,0,2,1:T(8,128)(2,1)} %get-tuple-element.224), channel_id=1, source_target_pairs={{0,1},{1,0},{2,3},{3,2},{4,5},{5,4},{6,7},{7,6},{8,9},{9,8},{10,11... | collective-permute-start | bytes 2359304 | tf_op jit(solution)/shard_map/ppermute | solution.py:40
  532.5 144.5 %collective-permute-start.102 = (bf16[2,1,1,192,1024]{4,3,0,2,1:T(8,128)(2,1)}, bf16[2,1,1,192,1024]{4,3,0,2,1:T(8,128)(2,1)}, u32[]{:S(2)}, u32[]{:S(2)}) collective-permute-start(bf16[2,1,1,192,1024]{4,3,0,2,1:T(8,128)(2,1)} %get-tuple-element.221), channel_id=1, source_target_pairs={{0,1},{1,0},{2,3},{3,2},{4,5},{5,4},{6,7},{7,6},{8,9},{9,8},{10,11... | collective-permute-start | bytes 2359304 | tf_op jit(solution)/shard_map/ppermute | solution.py:40
  543.1 45.4 %collective-permute-start.49 = (f32[8,128]{1,0:T(8,128)S(1)}, f32[8,128]{1,0:T(8,128)S(1)}, u32[]{:S(2)}, u32[]{:S(2)}) collective-permute-start(f32[8,128]{1,0:T(8,128)S(1)} %broadcast_in_dim.100), channel_id=1, source_target_pairs={{0,8},{8,0},{16,24},{24,16},{1,9},{9,1},{17,25},{25,17},{2,10},{10... | collective-permute-start | bytes 12296 | tf_op jit(solution)/shard_map/ppermute | solution.py:40
  579.1 80.2 %collective-permute-start.84 = (bf16[2,1,4,2,32,2176]{5,4,3,2,1,0:T(8,128)(2,1)}, bf16[2,1,4,2,32,2176]{5,4,3,2,1,0:T(8,128)(2,1)}, u32[]{:S(2)}, u32[]{:S(2)}) collective-permute-start(bf16[2,1,4,2,32,2176]{5,4,3,2,1,0:T(8,128)(2,1)} %constant_dynamic-slice_fusion.1), channel_id=1, source_target_pairs={{0,8},{8,0},{16,24},{24,16},{1,9},{9,1},{17,25},{25,17},{2,10},{10... | collective-permute-start | bytes 6684680 | tf_op jit(solution)/shard_map/ppermute | solution.py:40
  589.6 66.9 %collective-permute-start.97 = (bf16[2,192,1024]{2,1,0:T(8,128)(2,1)}, bf16[2,192,1024]{2,1,0:T(8,128)(2,1)}, u32[]{:S(2)}, u32[]{:S(2)}) collective-permute-start(bf16[2,192,1024]{2,1,0:T(8,128)(2,1)} %get-tuple-element.206), channel_id=1, source_target_pairs={{0,6},{1,7},{2,4},{3,5},{4,2},{5,3},{6,0},{7,1},{8,14},{9,15},{10,... | collective-permute-start | bytes 2359304 | tf_op jit(solution)/shard_map/ppermute | solution.py:40
  591.6 67.5 %collective-permute-start.99 = (bf16[2,192,1024]{2,1,0:T(8,128)(2,1)}, bf16[2,192,1024]{2,1,0:T(8,128)(2,1)S(1)}, u32[]{:S(2)}, u32[]{:S(2)}) collective-permute-start(bf16[2,192,1024]{2,1,0:T(8,128)(2,1)} %get-tuple-element.207), channel_id=1, source_target_pairs={{0,4},{1,5},{2,6},{3,7},{4,0},{5,1},{6,2},{7,3},{8,12},{9,13},{10,... | collective-permute-start | bytes 2359304 | tf_op jit(solution)/shard_map/ppermute | solution.py:40
  622.6 32.8 %collective-permute-start.53 = (f32[8,128]{1,0:T(8,128)S(1)}, f32[8,128]{1,0:T(8,128)S(1)}, u32[]{:S(2)}, u32[]{:S(2)}) collective-permute-start(f32[8,128]{1,0:T(8,128)S(1)} %add.410), channel_id=1, source_target_pairs={{0,4},{1,5},{2,6},{3,7},{4,0},{5,1},{6,2},{7,3},{8,12},{9,13},{10,... | collective-permute-start | bytes 12296 | tf_op jit(solution)/shard_map/ppermute | solution.py:40
  661.6 39.3 %collective-permute-start.85 = (bf16[1,1,4,2,32,2176]{5,4,3,2,1,0:T(8,128)(2,1)S(1)}, bf16[1,1,4,2,32,2176]{5,4,3,2,1,0:T(8,128)(2,1)S(1)}, u32[]{:S(2)}, u32[]{:S(2)}) collective-permute-start(bf16[1,1,4,2,32,2176]{5,4,3,2,1,0:T(8,128)(2,1)S(1)} %dynamic-slice_convert_fusion), channel_id=1, source_target_pairs={{0,16},{8,24},{16,0},{24,8},{1,17},{9,25},{17,1},{25,9},{2,18},{10... | collective-permute-start | bytes 3342344 | tf_op jit(solution)/shard_map/ppermute | solution.py:40
  663.9 36.1 %collective-permute-start.91 = (bf16[1,1,4,2,32,1024]{5,4,3,2,1,0:T(8,128)(2,1)S(1)}, bf16[1,1,4,2,32,1024]{5,4,3,2,1,0:T(8,128)(2,1)S(1)}, u32[]{:S(2)}, u32[]{:S(2)}) collective-permute-start(bf16[1,1,4,2,32,1024]{5,4,3,2,1,0:T(8,128)(2,1)S(1)} %dynamic-slice_convert_fusion.2), channel_id=1, source_target_pairs={{0,16},{8,24},{16,0},{24,8},{1,17},{9,25},{17,1},{25,9},{2,18},{10... | collective-permute-start | bytes 1572872 | tf_op jit(solution)/shard_map/ppermute | solution.py:40
  (147 other events, 1995.9 us)

commit v3 on v2

--- a/solution.py
+++ b/solution.py
@@ -200,8 +200,8 @@
 
 def expert_forward(count, seq_len, first_ref, weights_ref, *refs):
     token_refs = refs[:count]
-    out_refs = refs[count : 2 * count]
-    picked_ref, acc_ref, match_ref = refs[2 * count :]
+    out_refs = refs[count : count + CORES]
+    picked_ref, acc_ref, match_ref = refs[count + CORES :]
     held = weights_ref.shape[0]
     hidden_units = weights_ref.shape[3] // 2
     split = token_refs[0].shape[1] // weights_ref.shape[1]
@@ -227,15 +227,15 @@
             if e < held - 1:
                 acc_ref[s] = part
             else:
-                out_refs[s][...] = part.astype(bf16)
+                out_refs[s % CORES][s // CORES] = part.astype(bf16)
 
 
 def expert_backward(count, seq_len, first_ref, weights_ref, *refs):
     token_refs = refs[:count]
     grad_refs = refs[count : 2 * count]
-    out_refs = refs[2 * count : 3 * count]
-    picked_ref, wide_grad_ref, routed_ref, inner_ref = refs[3 * count : 3 * count + 4]
-    acc_ref, match_ref, gate_acc_ref = refs[3 * count + 4 :]
+    out_refs = refs[2 * count : 2 * count + CORES]
+    picked_ref, wide_grad_ref, routed_ref, inner_ref = refs[2 * count + CORES :][:4]
+    acc_ref, match_ref, gate_acc_ref = refs[2 * count + CORES + 4 :]
     held = weights_ref.shape[0]
     hidden_units = weights_ref.shape[3] // 2
     split = token_refs[0].shape[1] // weights_ref.shape[1]
@@ -287,10 +287,10 @@
                 acc_ref[s] = part
                 gate_acc_ref[s] = spread
             else:
-                out_refs[s][:seq_len, :] = part.astype(bf16)
+                out_refs[s % CORES][s // CORES, :seq_len, :] = part.astype(bf16)
                 high = spread.astype(bf16)
                 low = (spread - high.astype(f32)).astype(bf16)
-                out_refs[s][seq_len:, :] = jnp.concatenate([high, low], axis=0)
+                out_refs[s % CORES][s // CORES, seq_len:, :] = jnp.concatenate([high, low], axis=0)
 
 
 def expert_weight_grads(groups, *refs):
@@ -309,6 +309,45 @@
     for k in range(1, groups):
         down = down + dot_tn(inner[k][0], routed[k][0])
     out_ref[0, :, split:, :] = down.astype(bf16).reshape(blocks, -1, width)
+
+
+def dense_backward(
+    experts,
+    qkv_grad_ref,
+    normed_ref,
+    weights_ref,
+    tok_ref,
+    inverse_ref,
+    gain_ref,
+    hidden_grad_ref,
+    small_ref,
+    grads_ref,
+    token_grad_ref,
+):
+    seq_len, width = qkv_grad_ref.shape
+    normed = normed_ref[...]
+    for lanes in range(0, width, 512):
+        grads_ref[:, lanes : lanes + 512] = dot_tn(
+            normed, qkv_grad_ref[:, lanes : lanes + 512]
+        ).astype(bf16)
+    normed_grad = dot_nt(qkv_grad_ref[...], weights_ref[:, :width])
+    rows_in, inverse = tok_ref[...], inverse_ref[...]
+    scaled = normed_grad * gain_ref[...]
+    cubed = inverse * inverse * inverse
+    token_grad_ref[...] = (
+        hidden_grad_ref[...]
+        + inverse * scaled
+        - rows_in * cubed * jnp.mean(scaled * rows_in, axis=1, keepdims=True)
+    )
+    lane = lax.broadcasted_iota(jnp.int32, (seq_len, 128), 1)
+    gain_grad = lax.dot_general(
+        normed_grad * rows_in * inverse,
+        jnp.where(lane == experts, 1.0, 0.0),
+        (((0,), (0,)), ((), ())),
+        precision=highest,
+        preferred_element_type=f32,
+    )
+    grads_ref[:, width:] = (small_ref[...] + gain_grad).astype(bf16)
 
 
 def norm_back(grad_rows, rows_in, inverse, gain_vec):
@@ -366,7 +405,7 @@
 
     def exchange(values, lag, compute):
         per_hop = [values] + [swap(values, "fsdp", lows * k) for k in range(1, HOPS)]
-        results = []
+        results, sums, ready = [], [], []
         for k in range(HOPS):
             mine = per_hop[k]
             if k >= lag:
@@ -374,27 +413,29 @@
             sets = []
             for column in [mine] + [swap(mine, "dp", CORES * j) for j in range(1, rows_y)]:
                 sets.extend([column, swap(column, "dp", 1)])
-            results.append(compute(k, sets))
-        return results
-
-    def return_sets(parts, hold=None):
-        hops = []
-        for k in range(HOPS):
-            columns = []
-            for j in range(rows_y):
-                at = (k * rows_y + j) * CORES
-                got = swap(parts[at + 1], "dp", 1)
-                columns.append(parts[at].astype(f32) + got.astype(f32))
-            mine = columns[0]
-            for j in range(1, rows_y):
-                mine = mine + swap(columns[j].astype(bf16), "dp", CORES * j).astype(f32)
-            hops.append(swap(mine.astype(bf16), "fsdp", lows * k) if k else mine)
-        if hold is not None:
-            hops = after(hops, hold)
-        total = hops[0]
-        for k in range(1, HOPS):
-            total = total + hops[k].astype(f32)
-        return total
+            if k >= 2:
+                ready.append(sums[k - 2][1])
+            results.append(compute(k, sets, [r[0] for r in results[-1:]] + ready[-1:]))
+            own, given = results[k][:CORES]
+            got = swap(given, "dp", 1)
+            both = [own[j].astype(f32) + got[j].astype(f32) for j in range(rows_y)]
+            sums.append([both[0], *[c.astype(bf16) for c in both[1:]]])
+
+        def finish(hold=None):
+            hops = []
+            for k in range(HOPS):
+                mine = sums[k][0]
+                for j in range(1, rows_y):
+                    mine = mine + swap(sums[k][j], "dp", CORES * j).astype(f32)
+                hops.append(swap(mine.astype(bf16), "fsdp", lows * k) if k else mine)
+            if hold is not None:
+                hops = after(hops, hold)
+            total = hops[0]
+            for k in range(1, HOPS):
+                total = total + hops[k].astype(f32)
+            return total
+
+        return finish
 
     steps = (
         (2, "fsdp", lows, HOPS, hop_at),
@@ -410,23 +451,6 @@
     def merge(full, others, step):
         axis, _, _, _, at = steps[step]
         return jnp.concatenate(in_order(full, others, at), axis=axis)
-
-    def scatter_dense(grads):
-        wide = grads.shape[1]
-        part = grads.reshape(rows_y, CORES, HOPS, lows, row_block, wide)
-
-        def stage(part, axis, name, place, size, unit):
-            mine = lax.dynamic_slice_in_dim(part, place, 1, axis).astype(f32)
-            for m in range(1, size):
-                give = lax.dynamic_slice_in_dim(part, place ^ m, 1, axis).astype(bf16)
-                mine = mine + swap(give, name, unit * m).astype(f32)
-            return mine
-
-        part = stage(part, 1, "dp", core_at, CORES, 1)
-        part = stage(part, 0, "dp", y_at, rows_y, CORES)
-        part = stage(part, 3, "fsdp", low_at, lows, 1)
-        part = stage(part, 2, "fsdp", hop_at, HOPS, lows)
-        return part.reshape(row_block, wide)
 
     expert_ids = jnp.arange(experts, dtype=jnp.int32)
     member = jnp.any(routes[:, :, None] == expert_ids[None, None, :], axis=1)
@@ -481,7 +505,7 @@
     lows_of[1] = low_swaps(after(blocks[1], pack))
     out_others = send(out_w, 0)
     pack, others, out_w, out_others = join((pack, others, out_w, out_others))
-    blocks[2] = swap(after(owned_by(2), others), "fsdp", lows * 2)
+    far_first = swap(after(owned_by(2)[:, : shard.shape[1] // 2], others), "fsdp", lows * 2)
     packed = merge(pack, others, 3).reshape(model_width, -1)
     out_w = merge(out_w, out_others, 0)
     out_others = send(out_w, 1)
@@ -497,7 +521,8 @@
     normed = (tok_float * inv_one * gain_float).astype(bf16)
     cos_lanes, sin_lanes = rotary_lanes(seq_len)
     qkv = dot(normed, qkv_w)
-    qkv, out_w, out_others = join((qkv, out_w, out_others))
+    qkv, out_w, out_others, far_first = join((qkv, out_w, out_others, far_first))
+    far_second = swap(after(owned_by(2)[:, shard.shape[1] // 2 :], qkv), "fsdp", lows * 2)
     out_w = merge(out_w, out_others, 1)
     out_others = send(out_w, 2)
     lows_of[3] = low_swaps(after(blocks[3], qkv))
@@ -513,12 +538,18 @@
     mixed_rows, out_w, out_others = join((mixed_rows, out_w, out_others))
     out_w = merge(out_w, out_others, 2)
     out_w = merge(out_w, send(out_w, 3), 3).reshape(model_width, -1)
-    lows_of[2] = low_swaps(after(blocks[2], mixed_rows))
+    low_first = low_swaps(after(far_first, mixed_rows))
+    blocks[2] = (far_first, far_second)
+    lows_of[2] = list(zip(low_first, low_swaps(far_second), strict=True))
     expert_w = jnp.zeros((held, shards, shard.shape[1], model_width), bf16)
     for k in (0, 1, 3, 2):
         for m, part in enumerate([blocks[k], *lows_of[k]]):
             at = (hop_at ^ k) * lows + (low_at ^ m)
-            expert_w = lax.dynamic_update_slice(expert_w, part[:, None], (0, at, 0, 0))
+            pieces = part if k == 2 else (part,)
+            for i, piece in enumerate(pieces):
+                expert_w = lax.dynamic_update_slice(
+                    expert_w, piece[:, None], (0, at, i * (shard.shape[1] // 2), 0)
+                )
     hidden = tok_float + residual_scale * dot(mixed_rows, out_w)
     inv_two = lax.rsqrt(jnp.mean(hidden * hidden, axis=1, keepdims=True) + epsilon)
     normed_ffn = hidden * inv_two * gain_second
@@ -538,16 +569,15 @@
     )
     count = rows_y * CORES
     rows = count * CAP
-    set_shape = jax.ShapeDtypeStruct((seq_len, model_width), bf16)
+    set_shape = jax.ShapeDtypeStruct((rows_y, seq_len, model_width), bf16)
     token_sets = []
 
-    def forward(k, sets):
-        first_now = after(first_held, forward_parts[-1]) if k else first_held
+    def forward(k, sets, ready):
         token_sets.append(sets)
-        results = kernel_call(
+        return kernel_call(
             functools.partial(expert_forward, count, seq_len),
-            (set_shape,) * count,
-            (first_now, expert_w, *sets),
+            (set_shape,) * CORES,
+            (after(first_held, *ready), expert_w, *sets),
             first_smem=True,
             scratch=(
                 pltpu.VMEM((rows, model_width), bf16),
@@ -555,12 +585,8 @@
                 pltpu.VMEM((count, CAP, seq_len), bf16),
             ),
         )
-        forward_parts.extend(results)
-        return results
-
-    forward_parts = []
-    exchange(outgoing, 3, forward)
-    combined = return_sets(forward_parts)
+
+    combined = exchange(outgoing, 3, forward)()
     output = hidden + residual_scale * combined
     valid_rows = (positions < lengths[0]).astype(f32)[:, None]
     deviation = (output - teacher.astype(f32)) * valid_rows
@@ -575,22 +601,22 @@
             mask *= 2
     loss_value = loss_total[0, 0] / (valid_total * model_width)
 
-    back_shape = jax.ShapeDtypeStruct((seq_len + 2 * gate_rows, model_width), bf16)
-    back_parts = []
+    back_shape = jax.ShapeDtypeStruct((rows_y, seq_len + 2 * gate_rows, model_width), bf16)
     saved = []
 
-    def backward(k, sets):
-        first_now = after(first_held, back_parts[-1]) if k else first_held
+    def backward(k, sets, ready):
+        if k == 2:
+            ready = [*ready, loss_total]
         results = kernel_call(
             functools.partial(expert_backward, count, seq_len),
-            (back_shape,) * count
+            (back_shape,) * CORES
             + (
                 jax.ShapeDtypeStruct((held, rows, model_width), bf16),
                 jax.ShapeDtypeStruct((held, rows, 2 * hidden_units), bf16),
                 jax.ShapeDtypeStruct((held, rows, model_width), bf16),
                 jax.ShapeDtypeStruct((held, rows, hidden_units), bf16),
             ),
-            (first_now, expert_w, *token_sets[k], *sets),
+            (after(first_held, *ready), expert_w, *token_sets[k], *sets),
             first_smem=True,
             scratch=(
                 pltpu.VMEM((count, seq_len, model_width), f32),
@@ -598,11 +624,10 @@
                 pltpu.VMEM((count, gate_rows, model_width), f32),
             ),
         )
-        saved.append(results[count:])
-        back_parts.extend(results[:count])
+        saved.append(results[CORES:])
         return results
 
-    exchange(out_grad.astype(bf16), 2, backward)
+    finish = exchange(out_grad.astype(bf16), 2, backward)
     expert_grad = pl.pallas_call(
         functools.partial(expert_weight_grads, HOPS),
         grid=(held,),
@@ -615,25 +640,26 @@
         out_specs=pl.BlockSpec((1, shards, shard.shape[1], model_width), lambda e: (e, 0, 0, 0)),
         compiler_params=pltpu.CompilerParams(vmem_limit_bytes=60 * 1024 * 1024),
     )(*[saved[k][i] for i in range(4) for k in range(HOPS)])
-    returned = return_sets(back_parts, expert_grad)
     part = expert_grad.reshape(held, HOPS, lows, shard.shape[1], model_width)
-    expert_out = jnp.zeros((owned, shard.shape[1], model_width), f32)
+    low_parts = {}
     for k in (*range(HOPS - 1, 0, -1), 0):
-        at = hop_at ^ k
-        both_lows = lax.dynamic_slice_in_dim(part, at, 1, 1)
-        block = lax.dynamic_slice_in_dim(both_lows, low_at, 1, 2).astype(f32)
-        for m in range(1, lows):
-            give = lax.dynamic_slice_in_dim(both_lows, low_at ^ m, 1, 2)
-            block = block + swap(give, "fsdp", m).astype(f32)
-        block = block.reshape(held, shard.shape[1], model_width)
-        if k:
-            block = swap(after(block.astype(bf16), returned), "fsdp", lows * k).astype(f32)
-        expert_out = lax.dynamic_update_slice(expert_out, block, (at * held, 0, 0))
-    expert_grads = (
-        expert_out[:, :split, :hidden_units],
-        expert_out[:, :split, hidden_units:],
-        expert_out[:, split:, :],
-    )
+        both_lows = lax.dynamic_slice_in_dim(part, hop_at ^ k, 1, 1)
+        low_parts[k] = [lax.dynamic_slice_in_dim(both_lows, low_at, 1, 2)] + [
+            swap(lax.dynamic_slice_in_dim(both_lows, low_at ^ m, 1, 2), "fsdp", m)
+            for m in range(1, lows)
+        ]
+
+    returned, low_parts[3] = join((finish(expert_grad), low_parts[3]))
+
+    def low_sum(k):
+        pieces = low_parts[k]
+        total = pieces[0].astype(f32)
+        for piece in pieces[1:]:
+            total = total + piece.astype(f32)
+        return total.reshape(held, shard.shape[1], model_width)
+
+    def hop_send(k):
+        return swap(low_sum(k).astype(bf16), "fsdp", lows * k)
 
     gate_grad = (
         (returned[seq_len : seq_len + gate_rows] + returned[seq_len + gate_rows :])
@@ -643,17 +669,45 @@
     logit_grad = gate_weights * (
         gate_grad - jnp.sum(gate_weights * gate_grad, axis=1, keepdims=True)
     )
-    router_grad = jnp.einsum(
-        "td,te->de", normed_ffn, logit_grad, precision=highest, preferred_element_type=f32
-    )
     ffn_in_grad = returned[:seq_len] + jnp.einsum(
         "te,de->td", logit_grad, router_float, precision=highest, preferred_element_type=f32
     )
-    hidden_part, gain_two_grad = norm_back(ffn_in_grad, hidden, inv_two, gain_second)
+    hidden_part, _ = norm_back(ffn_in_grad, hidden, inv_two, gain_second)
     hidden_grad = out_grad + hidden_part
     attended_grad = (residual_scale * hidden_grad).astype(bf16)
-    out_grad_w = scatter_dense(dot_tn(mixed_rows, attended_grad).astype(bf16))
+
+    def halve(part, step):
+        axis, name, unit, size, at = steps[step]
+        mine = lax.dynamic_slice_in_dim(part, at, 1, axis).astype(f32)
+        return mine, [
+            swap(lax.dynamic_slice_in_dim(part, at ^ m, 1, axis).astype(bf16), name, unit * m)
+            for m in range(1, size)
+        ]
+
+    def total(mine, others):
+        for other in others:
+            mine = mine + other.astype(f32)
+        return mine
+
+    order = (rows_y, CORES, HOPS, lows, row_block, -1)
     mixed_grad = dot_nt(attended_grad, out_w).astype(bf16)
+    hop_got = {3: hop_send(3)}
+    out_sum = halve(dot_tn(mixed_rows, attended_grad).astype(bf16).reshape(order), 3)
+    lane = jnp.arange(128, dtype=jnp.int32)[None, :]
+    ones = jnp.ones((seq_len, 1), f32)
+    small = jnp.einsum(
+        "td,te->de",
+        jnp.concatenate([normed_ffn, ffn_in_grad * hidden * inv_two], axis=0),
+        jnp.concatenate(
+            [
+                jnp.pad(logit_grad, ((0, 0), (0, 128 - experts))),
+                jnp.where(lane == experts + 1, ones, 0.0),
+            ],
+            axis=0,
+        ),
+        precision=highest,
+        preferred_element_type=f32,
+    )
     qkv_grad = kernel_call(
         attention_backward,
         jax.ShapeDtypeStruct((seq_len, qkv_width), bf16),
@@ -661,19 +715,41 @@
         first_smem=True,
         scratch=(pltpu.VMEM((seq_len, model_width + kv_width), f32),),
     )
-    normed_grad = dot_nt(qkv_grad, qkv_w)
-    token_part, gain_one_grad = norm_back(normed_grad, tok_float, inv_one, gain_float)
-    token_grad = hidden_grad + token_part
-    small = jnp.concatenate(
-        [
-            router_grad,
-            gain_one_grad[:, None],
-            gain_two_grad[:, None],
-            jnp.zeros((model_width, 128 - experts - 2), f32),
-        ],
-        axis=1,
-    ).astype(bf16)
-    small = scatter_dense(jnp.concatenate([dot_tn(normed, qkv_grad).astype(bf16), small], axis=1))
+    qkv_grad, out_sum, low_parts[2] = join((qkv_grad, out_sum, low_parts[2]))
+    out_sum = halve(total(*out_sum), 1)
+    hop_got[2] = hop_send(2)
+    grads, token_grad = kernel_call(
+        functools.partial(dense_backward, experts),
+        (
+            jax.ShapeDtypeStruct((model_width, qkv_width + 128), bf16),
+            jax.ShapeDtypeStruct((seq_len, model_width), f32),
+        ),
+        (qkv_grad, normed, packed, tok_float, inv_one, gain_float[None, :], hidden_grad, small),
+    )
+    grads, out_sum, low_parts[1], hop_got[3] = join((grads, out_sum, low_parts[1], hop_got[3]))
+    part_sum = halve(grads.reshape(order), 3)
+    out_sum = halve(total(*out_sum), 2)
+    part_sum, out_sum = join((part_sum, out_sum))
+    part_sum = halve(total(*part_sum), 1)
+    hop_got[1] = hop_send(1)
+    out_sum = halve(total(*out_sum), 0)
+    part_sum, out_sum, low_parts[0], hop_got[2] = join(
+        (part_sum, out_sum, low_parts[0], hop_got[2])
+    )
+    out_grad_w = total(*out_sum).reshape(row_block, -1)
+    part_sum, hop_got[1] = join((halve(total(*part_sum), 2), hop_got[1]))
+    part_sum = halve(total(*part_sum), 0)
+    small = total(*part_sum).reshape(row_block, -1)
+
+    expert_out = jnp.zeros((owned, shard.shape[1], model_width), f32)
+    for k in range(HOPS):
+        block = hop_got[k].astype(f32) if k else low_sum(0)
+        expert_out = lax.dynamic_update_slice(expert_out, block, ((hop_at ^ k) * held, 0, 0))
+    expert_grads = (
+        expert_out[:, :split, :hidden_units],
+        expert_out[:, :split, hidden_units:],
+        expert_out[:, split:, :],
+    )
     return (
         output.astype(bf16),
         loss_value,

time: 748 us -> 726 us (0.971)
  waiting for transfers between devices: 351 us -> 310 us
  other arithmetic: 53 us -> 77.8 us
  local copies, waits for them, and re-layouts: 62 us -> 45.3 us
  Pallas kernels: 129 us -> 141 us
  matrix products: 22.8 us -> 14.9 us
    ppermute x103 -> x97, waiting for transfers between devices: 351 us -> 310 us  [swap(): lax.ppermute(values, axis, [(i, i ^ mask) for i in range(lax.axis_size(ax...]
    convert_element_type x17 -> x20, other arithmetic: 20 us -> 32.9 us  [the longest x8 11.9 us: exchange(): sums.append([both[0], *[c.astype(bf16) for c in both[1:]]])]
    pallas_call x10 -> x11, Pallas kernels: 110 us -> 122 us  [kernel_call(): pl.pallas_call(body, out_shape=out_shape, in_specs=specs, out_specs=jax.t...]
    unnamed x155 -> x115, local copies, waits for them, and re-layouts: 18.5 us -> 10.3 us
    concatenate x1 -> x0, local copies, waits for them, and re-layouts: 7.85 us -> none  [on_device(): jnp.concatenate([dot_tn(normed, qkv_grad).astype(bf16), small], axis=1)]
    dynamic_slice x0 -> x2, other arithmetic: none -> 7.8 us  [halve(): lax.dynamic_slice_in_dim(part, at ^ m, 1, axis).astype(bf16)]
    ppermute x103 -> x97, starting transfers between devices: 114 us -> 121 us  [swap(): lax.ppermute(values, axis, [(i, i ^ mask) for i in range(lax.axis_size(ax...]
    dynamic_update_slice x8 -> x10, local copies, waits for them, and re-layouts: 15.1 us -> 15.8 us  [on_device(): lax.dynamic_update_slice(expert_w, piece[:, None], (0, at, i * (shard.sha...]
  transfers between devices with their start and end apart: 103 -> 97, of which waited for: 36 -> 42; matrix products, arithmetic and copies ran while one was open for 15% -> 13% of each run, Pallas kernels for 17% -> 20%
where the time goes in v3:
time: 726 us; the launch traced here: 715 us
  waiting for transfers between devices  310 us (43%)
  Pallas kernels  141 us (19%)
  starting transfers between devices  121 us (17%)
  other arithmetic  77.8 us (11%)
  local copies, waits for them, and re-layouts  45.3 us (6%)
  matrix products  14.9 us (2%)
    ppermute x97, waiting for transfers between devices, swap(): lax.ppermute(values, axis, [(i, i ^ mask) for i in range(lax.axis_size(ax...  310 us
    pallas_call x11, Pallas kernels, kernel_call(): pl.pallas_call(body, out_shape=out_shape, in_specs=specs, out_specs=jax.t...  122 us
    ppermute x97, starting transfers between devices, swap(): lax.ppermute(values, axis, [(i, i ^ mask) for i in range(lax.axis_size(ax...  121 us
    pallas_call x1, Pallas kernels, on_device(): pl.pallas_call(functools.partial(expert_weight_grads, HOPS), grid=(held,)...  19.5 us
    dynamic_update_slice x10, local copies, waits for them, and re-layouts, on_device(): lax.dynamic_update_slice(expert_w, piece[:, None], (0, at, i * (shard.sha...  15.8 us
  transfers between devices with their start and end apart: 97, of which 42 were waited for; matrix products, arithmetic and copies ran while one was open for 13% of the time, Pallas kernels for 20%

profile of v3, /device:TPU:0, one launch (start us, length us, event | category | flops | bytes accessed | tf_op | source)
XLA Modules:
  0.0 715.4 jit_solution(3105161351216535076)
XLA Ops:
  24.3 12.5 %collective-permute-done.3 = bf16[1,1,4,1,32,2176]{5,4,3,2,1,0:T(8,128)(2,1)} collective-permute-done((bf16[1,1,4,1,32,2176]{5,4,3,2,1,0:T(8,128)(2,1)}, bf16[1,1,4,1,32,2176]{5,4,3,2,1,0:T(8,128)(2,1)}, u32[]{:S(2)}, u32[]{:S(2)}) %collective-permute-start.3) | collective-permute-done | bytes 557088 | tf_op jit(solution)/shard_map/ppermute | solution.py:40
  47.9 17.4 %collective-permute-done.7 = bf16[2,192,1024]{2,1,0:T(8,128)(2,1)} collective-permute-done((bf16[2,192,1024]{2,1,0:T(8,128)(2,1)}, bf16[2,192,1024]{2,1,0:T(8,128)(2,1)}, u32[]{:S(2)}, u32[]{:S(2)}) %collective-permute-start.7) | collective-permute-done | bytes 786464 | tf_op jit(solution)/shard_map/ppermute | solution.py:40
  73.9 11.7 %collective-permute-start.9 = (bf16[1,1,1,1,32,1024]{5,4,3,2,1,0:T(8,128)(2,1)}, bf16[1,1,1,1,32,1024]{5,4,3,2,1,0:T(8,128)(2,1)}, u32[]{:S(2)}, u32[]{:S(2)}) collective-permute-start(bf16[1,1,1,1,32,1024]{5,4,3,2,1,0:T(8,128)(2,1)} %bitcast.5), channel_id=1, source_target_pairs={{0,2},{1,3},{2,0},{3,1},{4,6},{5,7},{6,4},{7,5},{8,10},{9,11},{10,... | collective-permute-start | bytes 196616 | tf_op jit(solution)/shard_map/ppermute | solution.py:40
  106.8 13.9 %collective-permute-done.13 = bf16[2,96,1024]{2,1,0:T(8,128)(2,1)S(1)} collective-permute-done((bf16[2,96,1024]{2,1,0:T(8,128)(2,1)S(1)}, bf16[2,96,1024]{2,1,0:T(8,128)(2,1)S(1)}, u32[]{:S(2)}, u32[]{:S(2)}) %collective-permute-start.13) | collective-permute-done | bytes 393248 | tf_op jit(solution)/shard_map/ppermute | solution.py:40
  122.9 9.6 %shard_map.237 = (bf16[256,2048]{1,0:T(8,128)(2,1)}, bf16[256,1024]{1,0:T(8,128)(2,1)}) custom-call(s32[1]{0:T(128)} %copy.107.length_ref, f32[256,2048]{1,0:T(8,128)} %fusion.qkv_ref, f32[256,128]{1,0:T(8,128)} %get-tuple-element.310.cos_ref, f32[256,128]{1,0:T(8,128)} %get-tuple-element.311.sin_ref), custom_call_target="tpu_custom_call" | custom-call | tf_op jit(solution)/shard_map/pallas_call | solution.py:59
  148.4 9.8 %collective-permute-done.16 = bf16[2,192,1024]{2,1,0:T(8,128)(2,1)} collective-permute-done((bf16[2,192,1024]{2,1,0:T(8,128)(2,1)}, bf16[2,192,1024]{2,1,0:T(8,128)(2,1)}, u32[]{:S(2)}, u32[]{:S(2)}) %collective-permute-start.16) | collective-permute-done | bytes 786464 | tf_op jit(solution)/shard_map/ppermute | solution.py:40
  195.6 9.1 %shard_map.238 = (bf16[2,256,1024]{2,1,0:T(8,128)(2,1)}, bf16[2,256,1024]{2,1,0:T(8,128)(2,1)}) custom-call(s32[1]{0:T(128)} %bitcast.8.first_ref, bf16[2,8,192,1024]{3,2,1,0:T(8,128)(2,1)} %bitcast_dynamic-update-slice_fusion.10.weights_ref, bf16[272,1024]{1,0:T(8,128)(2,1)} %copy-done.8, bf16[272,1024]{1,0:T(8,128)(2,1)} %copy-done.28, ...), custom_call_target="tpu_custom_call" | custom-call | tf_op jit(solution)/shard_map/pallas_call | solution.py:59
  204.6 16.7 %collective-permute-done.33.refs_0_ = bf16[272,1024]{1,0:T(8,128)(2,1)S(1)} collective-permute-done((bf16[272,1024]{1,0:T(8,128)(2,1)S(1)}, bf16[272,1024]{1,0:T(8,128)(2,1)S(1)}, u32[]{:S(2)}, u32[]{:S(2)}) %collective-permute-start.33) | collective-permute-done | bytes 557088 | tf_op jit(solution)/shard_map/ppermute | solution.py:40
  223.5 9.1 %shard_map.239 = (bf16[2,256,1024]{2,1,0:T(8,128)(2,1)}, bf16[2,256,1024]{2,1,0:T(8,128)(2,1)}) custom-call(s32[1]{0:T(128)} %bitcast.8.first_ref, bf16[2,8,192,1024]{3,2,1,0:T(8,128)(2,1)} %bitcast_dynamic-update-slice_fusion.10.weights_ref, bf16[272,1024]{1,0:T(8,128)(2,1)} %copy-done.19, bf16[272,1024]{1,0:T(8,128)(2,1)} %copy-done.27, ...), custom_call_target="tpu_custom_call" | custom-call | tf_op jit(solution)/shard_map/pallas_call | solution.py:59
  236.1 11.6 %collective-permute-done.42.refs_2_ = bf16[272,1024]{1,0:T(8,128)(2,1)S(1)} collective-permute-done((bf16[272,1024]{1,0:T(8,128)(2,1)S(1)}, bf16[272,1024]{1,0:T(8,128)(2,1)S(1)}, u32[]{:S(2)}, u32[]{:S(2)}) %collective-permute-start.42) | collective-permute-done | bytes 557088 | tf_op jit(solution)/shard_map/ppermute | solution.py:40
  252.1 9.1 %shard_map.240 = (bf16[2,256,1024]{2,1,0:T(8,128)(2,1)}, bf16[2,256,1024]{2,1,0:T(8,128)(2,1)}) custom-call(s32[1]{0:T(128)} %bitcast.8.first_ref, bf16[2,8,192,1024]{3,2,1,0:T(8,128)(2,1)} %bitcast_dynamic-update-slice_fusion.10.weights_ref, bf16[272,1024]{1,0:T(8,128)(2,1)} %copy-done.17, bf16[272,1024]{1,0:T(8,128)(2,1)} %copy-done.23, ...), custom_call_target="tpu_custom_call" | custom-call | tf_op jit(solution)/shard_map/pallas_call | solution.py:59
  264.3 9.1 %shard_map.241 = (bf16[2,256,1024]{2,1,0:T(8,128)(2,1)}, bf16[2,256,1024]{2,1,0:T(8,128)(2,1)}) custom-call(s32[1]{0:T(128)} %bitcast.8.first_ref, bf16[2,8,192,1024]{3,2,1,0:T(8,128)(2,1)} %bitcast_dynamic-update-slice_fusion.10.weights_ref, bf16[272,1024]{1,0:T(8,128)(2,1)} %copy-done.16, bf16[272,1024]{1,0:T(8,128)(2,1)} %copy-done.21, ...), custom_call_target="tpu_custom_call" | custom-call | tf_op jit(solution)/shard_map/pallas_call | solution.py:59
  280.5 19.6 %collective-permute-done.31 = bf16[256,1024]{1,0:T(8,128)(2,1)S(1)} collective-permute-done((bf16[256,1024]{1,0:T(8,128)(2,1)S(1)}, bf16[256,1024]{1,0:T(8,128)(2,1)S(1)}, u32[]{:S(2)}, u32[]{:S(2)}) %collective-permute-start.31) | collective-permute-done | bytes 524320 | tf_op jit(solution)/shard_map/ppermute | solution.py:40
  302.8 8.6 %collective-permute-done.38 = bf16[256,1024]{1,0:T(8,128)(2,1)S(1)} collective-permute-done((bf16[256,1024]{1,0:T(8,128)(2,1)S(1)}, bf16[256,1024]{1,0:T(8,128)(2,1)S(1)}, u32[]{:S(2)}, u32[]{:S(2)}) %collective-permute-start.38) | collective-permute-done | bytes 524320 | tf_op jit(solution)/shard_map/ppermute | solution.py:40
  324.5 24.9 %collective-permute-done.39 = bf16[256,1024]{1,0:T(8,128)(2,1)} collective-permute-done((bf16[256,1024]{1,0:T(8,128)(2,1)}, bf16[256,1024]{1,0:T(8,128)(2,1)}, u32[]{:S(2)}, u32[]{:S(2)}) %collective-permute-start.39) | collective-permute-done | bytes 524320 | tf_op jit(solution)/shard_map/ppermute | solution.py:40
  352.2 11.8 %collective-permute-start.57 = (bf16[256,1024]{1,0:T(8,128)(2,1)S(1)}, bf16[256,1024]{1,0:T(8,128)(2,1)S(1)}, u32[]{:S(2)}, u32[]{:S(2)}) collective-permute-start(bf16[256,1024]{1,0:T(8,128)(2,1)S(1)} %get-tuple-element.244.refs_4_), channel_id=1, source_target_pairs={{0,2},{1,3},{2,0},{3,1},{4,6},{5,7},{6,4},{7,5},{8,10},{9,11},{10,... | collective-permute-start | bytes 1572872 | tf_op jit(solution)/shard_map/ppermute | solution.py:40
  364.6 11.5 %collective-permute-done.57.refs_4_ = bf16[256,1024]{1,0:T(8,128)(2,1)S(1)} collective-permute-done((bf16[256,1024]{1,0:T(8,128)(2,1)S(1)}, bf16[256,1024]{1,0:T(8,128)(2,1)S(1)}, u32[]{:S(2)}, u32[]{:S(2)}) %collective-permute-start.57) | collective-permute-done | bytes 524320 | tf_op jit(solution)/shard_map/ppermute | solution.py:40
  379.7 9.9 %collective-permute-done.59.refs_6_ = bf16[256,1024]{1,0:T(8,128)(2,1)} collective-permute-done((bf16[256,1024]{1,0:T(8,128)(2,1)S(1)}, bf16[256,1024]{1,0:T(8,128)(2,1)}, u32[]{:S(2)}, u32[]{:S(2)}) %collective-permute-start.59) | collective-permute-done | bytes 524320 | tf_op jit(solution)/shard_map/ppermute | solution.py:40
  392.4 13.4 %shard_map.242 = (bf16[2,272,1024]{2,1,0:T(8,128)(2,1)}, bf16[2,272,1024]{2,1,0:T(8,128)(2,1)}, bf16[2,384,1024]{2,1,0:T(8,128)(2,1)}, bf16[2,384,1024]{2,1,0:T(...) custom-call(s32[1]{0:T(128)} %bitcast.8.first_ref, ...), custom_call_target="tpu_custom_call" | custom-call | tf_op jit(solution)/shard_map/pallas_call | solution.py:59
  405.9 9.8 %collective-permute-done.64.refs_4_ = bf16[256,1024]{1,0:T(8,128)(2,1)} collective-permute-done((bf16[256,1024]{1,0:T(8,128)(2,1)S(1)}, bf16[256,1024]{1,0:T(8,128)(2,1)}, u32[]{:S(2)}, u32[]{:S(2)}) %collective-permute-start.64) | collective-permute-done | bytes 524320 | tf_op jit(solution)/shard_map/ppermute | solution.py:40
  417.1 13.9 %shard_map.243 = (bf16[2,272,1024]{2,1,0:T(8,128)(2,1)}, bf16[2,272,1024]{2,1,0:T(8,128)(2,1)}, bf16[2,384,1024]{2,1,0:T(8,128)(2,1)}, bf16[2,384,1024]{2,1,0:T(...) custom-call(s32[1]{0:T(128)} %bitcast.8.first_ref, ...), custom_call_target="tpu_custom_call" | custom-call | tf_op jit(solution)/shard_map/pallas_call | solution.py:59
  436.0 11.3 %collective-permute-done.48 = f32[8,128]{1,0:T(8,128)S(1)} collective-permute-done((f32[8,128]{1,0:T(8,128)S(1)}, f32[8,128]{1,0:T(8,128)S(1)}, u32[]{:S(2)}, u32[]{:S(2)}) %collective-permute-start.48) | collective-permute-done | bytes 4128 | tf_op jit(solution)/shard_map/ppermute | solution.py:40
  463.5 13.4 %shard_map.244 = (bf16[2,272,1024]{2,1,0:T(8,128)(2,1)}, bf16[2,272,1024]{2,1,0:T(8,128)(2,1)}, bf16[2,384,1024]{2,1,0:T(8,128)(2,1)}, bf16[2,384,1024]{2,1,0:T(...) custom-call(s32[1]{0:T(128)} %bitcast.8.first_ref, ...), custom_call_target="tpu_custom_call" | custom-call | tf_op jit(solution)/shard_map/pallas_call | solution.py:59
  479.2 13.6 %shard_map.245 = (bf16[2,272,1024]{2,1,0:T(8,128)(2,1)}, bf16[2,272,1024]{2,1,0:T(8,128)(2,1)}, bf16[2,384,1024]{2,1,0:T(8,128)(2,1)}, bf16[2,384,1024]{2,1,0:T(...) custom-call(s32[1]{0:T(128)} %bitcast.8.first_ref, ...), custom_call_target="tpu_custom_call" | custom-call | tf_op jit(solution)/shard_map/pallas_call | solution.py:59
  497.2 19.5 %shard_map.246 = bf16[2,8,192,1024]{3,2,1,0:T(8,128)(2,1)} custom-call(bf16[2,384,1024]{2,1,0:T(8,128)(2,1)} %get-tuple-element.187.refs_0_, bf16[2,384,1024]{2,1,0:T(8,128)(2,1)} %get-tuple-element.188.refs_1_, bf16[2,384,1024]{2,1,0:T(8,128)(2,1)} %get-tuple-element.189.refs_2_, bf16[2,384,1024]{2,1,0:T(8,128)(2,1)} %get-tuple-element.190.refs_3_, ...), custom_call_target="tpu_custom_call" | custom-call | tf_op jit(solution)/shard_map/pallas_call | solution.py:631
  526.9 17.0 %collective-permute-done.76 = bf16[272,1024]{1,0:T(8,128)(2,1)S(1)} collective-permute-done((bf16[272,1024]{1,0:T(8,128)(2,1)S(1)}, bf16[272,1024]{1,0:T(8,128)(2,1)S(1)}, u32[]{:S(2)}, u32[]{:S(2)}) %collective-permute-start.76) | collective-permute-done | bytes 557088 | tf_op jit(solution)/shard_map/ppermute | solution.py:40
  552.8 12.2 %collective-permute-done.70 = bf16[272,1024]{1,0:T(8,128)(2,1)} collective-permute-done((bf16[272,1024]{1,0:T(8,128)(2,1)}, bf16[272,1024]{1,0:T(8,128)(2,1)}, u32[]{:S(2)}, u32[]{:S(2)}) %collective-permute-start.70) | collective-permute-done | bytes 557088 | tf_op jit(solution)/shard_map/ppermute | solution.py:40
  585.6 12.7 %shard_map.247.qkv_grad_ref = bf16[256,2048]{1,0:T(8,128)(2,1)} custom-call(s32[1]{0:T(128)} %copy.107.length_ref, bf16[256,2048]{1,0:T(8,128)(2,1)} %get-tuple-element.173.rot_ref, bf16[256,1024]{1,0:T(8,128)(2,1)} %convolution_convert_fusion.1.grad_ref, f32[256,128]{1,0:T(8,128)} %get-tuple-element.310.cos_ref, f32[256,128]{1,0:T(8,128)} %get-tuple-element.311.sin_ref), custom_call_target="tpu_custom_call" | custom-call | tf_op jit(solution)/shard_map/pallas_call | solution.py:59
  609.1 9.0 %shard_map.248 = (bf16[1024,2176]{1,0:T(8,128)(2,1)}, f32[256,1024]{1,0:T(8,128)}) custom-call(bf16[256,2048]{1,0:T(8,128)(2,1)} %shard_map.247.qkv_grad_ref, bf16[256,1024]{1,0:T(8,128)(2,1)} %copy-done.30, bf16[1024,2176]{1,0:T(8,128)(2,1)} %bitcast.173, f32[256,1024]{1,0:T(8,128)} %convert_element_type.440.tok_ref, f32[256,1]{1,0:T(8,128)} %copy.80.inverse_ref, ...), custom_call_target="tpu_custom_call" | custom-call | tf_op jit(solution)/shard_map/pallas_call | solution.py:59
  639.2 12.3 %collective-permute-done.85 = bf16[1,1,4,1,32,1024]{5,4,3,2,1,0:T(8,128)(2,1)S(1)} collective-permute-done((bf16[1,1,4,1,32,1024]{5,4,3,2,1,0:T(8,128)(2,1)S(1)}, bf16[1,1,4,1,32,1024]{5,4,3,2,1,0:T(8,128)(2,1)S(1)}, u32[]{:S(2)}, u32[]{:S(2)}) %collective-permute-start.85) | collective-permute-done | bytes 262176 | tf_op jit(solution)/shard_map/ppermute | solution.py:40
  667.3 10.0 %collective-permute-done.91 = bf16[2,192,1024]{2,1,0:T(8,128)(2,1)S(1)} collective-permute-done((bf16[2,192,1024]{2,1,0:T(8,128)(2,1)S(1)}, bf16[2,192,1024]{2,1,0:T(8,128)(2,1)S(1)}, u32[]{:S(2)}, u32[]{:S(2)}) %collective-permute-start.91) | collective-permute-done | bytes 786464 | tf_op jit(solution)/shard_map/ppermute | solution.py:40
  682.9 12.5 %collective-permute-done.93 = bf16[2,192,1024]{2,1,0:T(8,128)(2,1)S(1)} collective-permute-done((bf16[2,192,1024]{2,1,0:T(8,128)(2,1)S(1)}, bf16[2,192,1024]{2,1,0:T(8,128)(2,1)S(1)}, u32[]{:S(2)}, u32[]{:S(2)}) %collective-permute-start.93) | collective-permute-done | bytes 786464 | tf_op jit(solution)/shard_map/ppermute | solution.py:40
  (418 shorter events, 303.2 us)
Async XLA Ops:
  138.0 37.1 %collective-permute-start.17 = (bf16[2,192,1024]{2,1,0:T(8,128)(2,1)}, bf16[2,192,1024]{2,1,0:T(8,128)(2,1)}, u32[]{:S(2)}, u32[]{:S(2)}) collective-permute-start(bf16[2,192,1024]{2,1,0:T(8,128)(2,1)} %collective-permute-done.7), channel_id=1, source_target_pairs={{0,1},{1,0},{2,3},{3,2},{4,5},{5,4},{6,7},{7,6},{8,9},{9,8},{10,11... | collective-permute-start | bytes 2359304 | tf_op jit(solution)/shard_map/ppermute | solution.py:40
  164.9 26.4 %collective-permute-start.19 = (bf16[2,96,1024]{2,1,0:T(8,128)(2,1)S(1)}, bf16[2,96,1024]{2,1,0:T(8,128)(2,1)S(1)}, u32[]{:S(2)}, u32[]{:S(2)}) collective-permute-start(bf16[2,96,1024]{2,1,0:T(8,128)(2,1)S(1)} %copy-done.54), channel_id=1, source_target_pairs={{0,1},{1,0},{2,3},{3,2},{4,5},{5,4},{6,7},{7,6},{8,9},{9,8},{10,11... | collective-permute-start | bytes 1179656 | tf_op jit(solution)/shard_map/ppermute | solution.py:40
  183.4 38.0 %collective-permute-start.33 = (bf16[272,1024]{1,0:T(8,128)(2,1)S(1)}, bf16[272,1024]{1,0:T(8,128)(2,1)S(1)}, u32[]{:S(2)}, u32[]{:S(2)}) collective-permute-start(bf16[272,1024]{1,0:T(8,128)(2,1)S(1)} %pad_maximum_fusion.7.refs_0_), channel_id=1, source_target_pairs={{0,4},{1,5},{2,6},{3,7},{4,0},{5,1},{6,2},{7,3},{8,12},{9,13},{10,... | collective-permute-start | bytes 1671176 | tf_op jit(solution)/shard_map/ppermute | solution.py:40
  191.4 30.5 %collective-permute-start.27 = (bf16[272,1024]{1,0:T(8,128)(2,1)S(1)}, bf16[272,1024]{1,0:T(8,128)(2,1)S(1)}, u32[]{:S(2)}, u32[]{:S(2)}) collective-permute-start(bf16[272,1024]{1,0:T(8,128)(2,1)S(1)} %collective-permute-done.26.refs_0_), channel_id=1, source_target_pairs={{0,8},{8,0},{16,24},{24,16},{1,9},{9,1},{17,25},{25,17},{2,10},{10... | collective-permute-start | bytes 1671176 | tf_op jit(solution)/shard_map/ppermute | solution.py:40
  191.4 30.5 %collective-permute-start.29 = (bf16[272,1024]{1,0:T(8,128)(2,1)S(1)}, bf16[272,1024]{1,0:T(8,128)(2,1)S(1)}, u32[]{:S(2)}, u32[]{:S(2)}) collective-permute-start(bf16[272,1024]{1,0:T(8,128)(2,1)S(1)} %collective-permute-done.28.refs_2_), channel_id=1, source_target_pairs={{0,8},{8,0},{16,24},{24,16},{1,9},{9,1},{17,25},{25,17},{2,10},{10... | collective-permute-start | bytes 1671176 | tf_op jit(solution)/shard_map/ppermute | solution.py:40
  192.7 40.0 %collective-permute-start.40 = (bf16[272,1024]{1,0:T(8,128)(2,1)S(1)}, bf16[272,1024]{1,0:T(8,128)(2,1)S(1)}, u32[]{:S(2)}, u32[]{:S(2)}) collective-permute-start(bf16[272,1024]{1,0:T(8,128)(2,1)S(1)} %pad_maximum_fusion.7.refs_0_), channel_id=1, source_target_pairs={{0,6},{1,7},{2,4},{3,5},{4,2},{5,3},{6,0},{7,1},{8,14},{9,15},{10,... | collective-permute-start | bytes 1671176 | tf_op jit(solution)/shard_map/ppermute | solution.py:40
  204.6 43.1 %collective-permute-start.24 = (bf16[2,256,1024]{2,1,0:T(8,128)(2,1)}, bf16[2,256,1024]{2,1,0:T(8,128)(2,1)}, u32[]{:S(2)}, u32[]{:S(2)}) collective-permute-start(bf16[2,256,1024]{2,1,0:T(8,128)(2,1)} %get-tuple-element.162), channel_id=1, source_target_pairs={{0,8},{8,0},{16,24},{24,16},{1,9},{9,1},{17,25},{25,17},{2,10},{10... | collective-permute-start | bytes 3145736 | tf_op jit(solution)/shard_map/ppermute | solution.py:40
  232.6 28.6 %collective-permute-start.30 = (bf16[2,256,1024]{2,1,0:T(8,128)(2,1)}, bf16[2,256,1024]{2,1,0:T(8,128)(2,1)}, u32[]{:S(2)}, u32[]{:S(2)}) collective-permute-start(bf16[2,256,1024]{2,1,0:T(8,128)(2,1)} %get-tuple-element.165), channel_id=1, source_target_pairs={{0,8},{8,0},{16,24},{24,16},{1,9},{9,1},{17,25},{25,17},{2,10},{10... | collective-permute-start | bytes 3145736 | tf_op jit(solution)/shard_map/ppermute | solution.py:40
  273.9 50.7 %collective-permute-start.25 = (bf16[256,1024]{1,0:T(8,128)(2,1)}, bf16[256,1024]{1,0:T(8,128)(2,1)}, u32[]{:S(2)}, u32[]{:S(2)}) collective-permute-start(bf16[256,1024]{1,0:T(8,128)(2,1)} %fusion.26), channel_id=1, source_target_pairs={{0,16},{8,24},{16,0},{24,8},{1,17},{9,25},{17,1},{25,9},{2,18},{10... | collective-permute-start | bytes 1572872 | tf_op jit(solution)/shard_map/ppermute | solution.py:40
  277.1 34.2 %collective-permute-start.38 = (bf16[256,1024]{1,0:T(8,128)(2,1)S(1)}, bf16[256,1024]{1,0:T(8,128)(2,1)S(1)}, u32[]{:S(2)}, u32[]{:S(2)}) collective-permute-start(bf16[256,1024]{1,0:T(8,128)(2,1)S(1)} %fusion.28), channel_id=1, source_target_pairs={{0,16},{8,24},{16,0},{24,8},{1,17},{9,25},{17,1},{25,9},{2,18},{10... | collective-permute-start | bytes 1572872 | tf_op jit(solution)/shard_map/ppermute | solution.py:40
  279.9 41.8 %collective-permute-start.45 = (bf16[256,1024]{1,0:T(8,128)(2,1)S(1)}, bf16[256,1024]{1,0:T(8,128)(2,1)S(1)}, u32[]{:S(2)}, u32[]{:S(2)}) collective-permute-start(bf16[256,1024]{1,0:T(8,128)(2,1)S(1)} %fusion.29), channel_id=1, source_target_pairs={{0,16},{8,24},{16,0},{24,8},{1,17},{9,25},{17,1},{25,9},{2,18},{10... | collective-permute-start | bytes 1572872 | tf_op jit(solution)/shard_map/ppermute | solution.py:40
  313.4 36.0 %collective-permute-start.39 = (bf16[256,1024]{1,0:T(8,128)(2,1)}, bf16[256,1024]{1,0:T(8,128)(2,1)}, u32[]{:S(2)}, u32[]{:S(2)}) collective-permute-start(bf16[256,1024]{1,0:T(8,128)(2,1)} %fusion.12), channel_id=1, source_target_pairs={{0,4},{1,5},{2,6},{3,7},{4,0},{5,1},{6,2},{7,3},{8,12},{9,13},{10,... | collective-permute-start | bytes 1572872 | tf_op jit(solution)/shard_map/ppermute | solution.py:40
  321.9 27.5 %collective-permute-start.46 = (bf16[256,1024]{1,0:T(8,128)(2,1)S(1)}, bf16[256,1024]{1,0:T(8,128)(2,1)}, u32[]{:S(2)}, u32[]{:S(2)}) collective-permute-start(bf16[256,1024]{1,0:T(8,128)(2,1)S(1)} %fusion.11), channel_id=1, source_target_pairs={{0,6},{1,7},{2,4},{3,5},{4,2},{5,3},{6,0},{7,1},{8,14},{9,15},{10,... | collective-permute-start | bytes 1572872 | tf_op jit(solution)/shard_map/ppermute | solution.py:40
  377.5 38.3 %collective-permute-start.64 = (bf16[256,1024]{1,0:T(8,128)(2,1)S(1)}, bf16[256,1024]{1,0:T(8,128)(2,1)}, u32[]{:S(2)}, u32[]{:S(2)}) collective-permute-start(bf16[256,1024]{1,0:T(8,128)(2,1)S(1)} %get-tuple-element.244.refs_4_), channel_id=1, source_target_pairs={{0,4},{1,5},{2,6},{3,7},{4,0},{5,1},{6,2},{7,3},{8,12},{9,13},{10,... | collective-permute-start | bytes 1572872 | tf_op jit(solution)/shard_map/ppermute | solution.py:40
  379.7 37.4 %collective-permute-start.58 = (bf16[256,1024]{1,0:T(8,128)(2,1)S(1)}, bf16[256,1024]{1,0:T(8,128)(2,1)}, u32[]{:S(2)}, u32[]{:S(2)}) collective-permute-start(bf16[256,1024]{1,0:T(8,128)(2,1)S(1)} %collective-permute-done.57.refs_4_), channel_id=1, source_target_pairs={{0,8},{8,0},{16,24},{24,16},{1,9},{9,1},{17,25},{25,17},{2,10},{10... | collective-permute-start | bytes 1572872 | tf_op jit(solution)/shard_map/ppermute | solution.py:40
  389.6 27.5 %collective-permute-start.60 = (bf16[256,1024]{1,0:T(8,128)(2,1)}, bf16[256,1024]{1,0:T(8,128)(2,1)}, u32[]{:S(2)}, u32[]{:S(2)}) collective-permute-start(bf16[256,1024]{1,0:T(8,128)(2,1)} %collective-permute-done.59.refs_6_), channel_id=1, source_target_pairs={{0,8},{8,0},{16,24},{24,16},{1,9},{9,1},{17,25},{25,17},{2,10},{10... | collective-permute-start | bytes 1572872 | tf_op jit(solution)/shard_map/ppermute | solution.py:40
  389.6 43.6 %collective-permute-start.71 = (bf16[256,1024]{1,0:T(8,128)(2,1)S(1)}, bf16[256,1024]{1,0:T(8,128)(2,1)S(1)}, u32[]{:S(2)}, u32[]{:S(2)}) collective-permute-start(bf16[256,1024]{1,0:T(8,128)(2,1)S(1)} %get-tuple-element.244.refs_4_), channel_id=1, source_target_pairs={{0,6},{1,7},{2,4},{3,5},{4,2},{5,3},{6,0},{7,1},{8,14},{9,15},{10,... | collective-permute-start | bytes 1572872 | tf_op jit(solution)/shard_map/ppermute | solution.py:40
  405.7 54.6 %collective-permute-start.55 = (bf16[2,272,1024]{2,1,0:T(8,128)(2,1)}, bf16[2,272,1024]{2,1,0:T(8,128)(2,1)S(1)}, u32[]{:S(2)}, u32[]{:S(2)}) collective-permute-start(bf16[2,272,1024]{2,1,0:T(8,128)(2,1)} %get-tuple-element.175), channel_id=1, source_target_pairs={{0,8},{8,0},{16,24},{24,16},{1,9},{9,1},{17,25},{25,17},{2,10},{10... | collective-permute-start | bytes 3342344 | tf_op jit(solution)/shard_map/ppermute | solution.py:40
  415.8 44.0 %collective-permute-start.66 = (bf16[256,1024]{1,0:T(8,128)(2,1)}, bf16[256,1024]{1,0:T(8,128)(2,1)}, u32[]{:S(2)}, u32[]{:S(2)}) collective-permute-start(bf16[256,1024]{1,0:T(8,128)(2,1)} %collective-permute-done.64.refs_4_), channel_id=1, source_target_pairs={{0,16},{8,24},{16,0},{24,8},{1,17},{9,25},{17,1},{25,9},{2,18},{10... | collective-permute-start | bytes 1572872 | tf_op jit(solution)/shard_map/ppermute | solution.py:40
  430.9 46.2 %collective-permute-start.61 = (bf16[2,272,1024]{2,1,0:T(8,128)(2,1)}, bf16[2,272,1024]{2,1,0:T(8,128)(2,1)}, u32[]{:S(2)}, u32[]{:S(2)}) collective-permute-start(bf16[2,272,1024]{2,1,0:T(8,128)(2,1)} %get-tuple-element.178), channel_id=1, source_target_pairs={{0,8},{8,0},{16,24},{24,16},{1,9},{9,1},{17,25},{25,17},{2,10},{10... | collective-permute-start | bytes 3342344 | tf_op jit(solution)/shard_map/ppermute | solution.py:40
  433.2 27.0 %collective-permute-start.73 = (bf16[256,1024]{1,0:T(8,128)(2,1)S(1)}, bf16[256,1024]{1,0:T(8,128)(2,1)}, u32[]{:S(2)}, u32[]{:S(2)}) collective-permute-start(bf16[256,1024]{1,0:T(8,128)(2,1)S(1)} %collective-permute-done.71.refs_4_), channel_id=1, source_target_pairs={{0,16},{8,24},{16,0},{24,8},{1,17},{9,25},{17,1},{25,9},{2,18},{10... | collective-permute-start | bytes 1572872 | tf_op jit(solution)/shard_map/ppermute | solution.py:40
  493.2 26.4 %collective-permute-start.62 = (bf16[272,1024]{1,0:T(8,128)(2,1)}, bf16[272,1024]{1,0:T(8,128)(2,1)}, u32[]{:S(2)}, u32[]{:S(2)}) collective-permute-start(bf16[272,1024]{1,0:T(8,128)(2,1)} %fusion.23), channel_id=1, source_target_pairs={{0,16},{8,24},{16,0},{24,8},{1,17},{9,25},{17,1},{25,9},{2,18},{10... | collective-permute-start | bytes 1671176 | tf_op jit(solution)/shard_map/ppermute | solution.py:40
  495.2 26.9 %collective-permute-start.69 = (bf16[272,1024]{1,0:T(8,128)(2,1)}, bf16[272,1024]{1,0:T(8,128)(2,1)}, u32[]{:S(2)}, u32[]{:S(2)}) collective-permute-start(bf16[272,1024]{1,0:T(8,128)(2,1)} %fusion.24), channel_id=1, source_target_pairs={{0,16},{8,24},{16,0},{24,8},{1,17},{9,25},{17,1},{25,9},{2,18},{10... | collective-permute-start | bytes 1671176 | tf_op jit(solution)/shard_map/ppermute | solution.py:40
  496.5 54.9 %collective-permute-start.56 = (bf16[272,1024]{1,0:T(8,128)(2,1)}, bf16[272,1024]{1,0:T(8,128)(2,1)}, u32[]{:S(2)}, u32[]{:S(2)}) collective-permute-start(bf16[272,1024]{1,0:T(8,128)(2,1)} %fusion.22), channel_id=1, source_target_pairs={{0,16},{8,24},{16,0},{24,8},{1,17},{9,25},{17,1},{25,9},{2,18},{10... | collective-permute-start | bytes 1671176 | tf_op jit(solution)/shard_map/ppermute | solution.py:40
  522.1 30.7 %collective-permute-start.63 = (bf16[272,1024]{1,0:T(8,128)(2,1)}, bf16[272,1024]{1,0:T(8,128)(2,1)}, u32[]{:S(2)}, u32[]{:S(2)}) collective-permute-start(bf16[272,1024]{1,0:T(8,128)(2,1)} %fusion.9), channel_id=1, source_target_pairs={{0,2},{1,3},{2,0},{3,1},{4,6},{5,7},{6,4},{7,5},{8,10},{9,11},{10,... | collective-permute-start | bytes 1671176 | tf_op jit(solution)/shard_map/ppermute | solution.py:40
  524.5 40.6 %collective-permute-start.70 = (bf16[272,1024]{1,0:T(8,128)(2,1)}, bf16[272,1024]{1,0:T(8,128)(2,1)}, u32[]{:S(2)}, u32[]{:S(2)}) collective-permute-start(bf16[272,1024]{1,0:T(8,128)(2,1)} %fusion.8), channel_id=1, source_target_pairs={{0,4},{1,5},{2,6},{3,7},{4,0},{5,1},{6,2},{7,3},{8,12},{9,13},{10,... | collective-permute-start | bytes 1671176 | tf_op jit(solution)/shard_map/ppermute | solution.py:40
  578.2 40.0 %collective-permute-start.82 = (bf16[2,1,1,192,1024]{4,3,0,2,1:T(8,128)(2,1)}, bf16[2,1,1,192,1024]{4,3,0,2,1:T(8,128)(2,1)}, u32[]{:S(2)}, u32[]{:S(2)}) collective-permute-start(bf16[2,1,1,192,1024]{4,3,0,2,1:T(8,128)(2,1)} %get-tuple-element.254), channel_id=1, source_target_pairs={{0,1},{1,0},{2,3},{3,2},{4,5},{5,4},{6,7},{7,6},{8,9},{9,8},{10,11... | collective-permute-start | bytes 2359304 | tf_op jit(solution)/shard_map/ppermute | solution.py:40
  582.0 36.1 %collective-permute-start.83 = (bf16[2,192,1024]{2,1,0:T(8,128)(2,1)}, bf16[2,192,1024]{2,1,0:T(8,128)(2,1)}, u32[]{:S(2)}, u32[]{:S(2)}) collective-permute-start(bf16[2,192,1024]{2,1,0:T(8,128)(2,1)} %fusion.19), channel_id=1, source_target_pairs={{0,6},{1,7},{2,4},{3,5},{4,2},{5,3},{6,0},{7,1},{8,14},{9,15},{10,... | collective-permute-start | bytes 2359304 | tf_op jit(solution)/shard_map/ppermute | solution.py:40
  624.0 27.5 %collective-permute-start.84 = (bf16[2,1,4,2,32,2176]{5,4,3,2,1,0:T(8,128)(2,1)}, bf16[2,1,4,2,32,2176]{5,4,3,2,1,0:T(8,128)(2,1)}, u32[]{:S(2)}, u32[]{:S(2)}) collective-permute-start(bf16[2,1,4,2,32,2176]{5,4,3,2,1,0:T(8,128)(2,1)} %get-tuple-element.260), channel_id=1, source_target_pairs={{0,8},{8,0},{16,24},{24,16},{1,9},{9,1},{17,25},{25,17},{2,10},{10... | collective-permute-start | bytes 6684680 | tf_op jit(solution)/shard_map/ppermute | solution.py:40
  625.9 39.3 %collective-permute-start.90 = (bf16[2,1,1,192,1024]{4,3,0,2,1:T(8,128)(2,1)S(1)}, bf16[2,1,1,192,1024]{4,3,0,2,1:T(8,128)(2,1)S(1)}, u32[]{:S(2)}, u32[]{:S(2)}) collective-permute-start(bf16[2,1,1,192,1024]{4,3,0,2,1:T(8,128)(2,1)S(1)} %copy-done.42), channel_id=1, source_target_pairs={{0,1},{1,0},{2,3},{3,2},{4,5},{5,4},{6,7},{7,6},{8,9},{9,8},{10,11... | collective-permute-start | bytes 2359304 | tf_op jit(solution)/shard_map/ppermute | solution.py:40
  630.9 46.3 %collective-permute-start.91 = (bf16[2,192,1024]{2,1,0:T(8,128)(2,1)S(1)}, bf16[2,192,1024]{2,1,0:T(8,128)(2,1)S(1)}, u32[]{:S(2)}, u32[]{:S(2)}) collective-permute-start(bf16[2,192,1024]{2,1,0:T(8,128)(2,1)S(1)} %fusion.20), channel_id=1, source_target_pairs={{0,4},{1,5},{2,6},{3,7},{4,0},{5,1},{6,2},{7,3},{8,12},{9,13},{10,... | collective-permute-start | bytes 2359304 | tf_op jit(solution)/shard_map/ppermute | solution.py:40
  653.8 26.1 %collective-permute-start.86 = (bf16[1,1,4,2,32,2176]{5,4,3,2,1,0:T(8,128)(2,1)S(1)}, bf16[1,1,4,2,32,2176]{5,4,3,2,1,0:T(8,128)(2,1)S(1)}, u32[]{:S(2)}, u32[]{:S(2)}) collective-permute-start(bf16[1,1,4,2,32,2176]{5,4,3,2,1,0:T(8,128)(2,1)S(1)} %dynamic-slice_convert_fusion), channel_id=1, source_target_pairs={{0,16},{8,24},{16,0},{24,8},{1,17},{9,25},{17,1},{25,9},{2,18},{10... | collective-permute-start | bytes 3342344 | tf_op jit(solution)/shard_map/ppermute | solution.py:40
  (122 other events, 1798.4 us)

commit v4 on v3

--- a/solution.py
+++ b/solution.py
@@ -403,30 +403,39 @@
     hop_at, low_at = fsdp_at // lows, fsdp_at % lows
     y_at, core_at = dp_at // CORES, dp_at % CORES
 
-    def exchange(values, lag, compute):
+    def exchange(values, compute):
         per_hop = [values] + [swap(values, "fsdp", lows * k) for k in range(1, HOPS)]
-        results, sums, ready = [], [], []
+        columns = [
+            [mine, *[swap(mine, "dp", CORES * j) for j in range(1, rows_y)]] for mine in per_hop
+        ]
+        results, sums = [], []
         for k in range(HOPS):
-            mine = per_hop[k]
-            if k >= lag:
-                mine = after(mine, results[k - lag][0])
             sets = []
-            for column in [mine] + [swap(mine, "dp", CORES * j) for j in range(1, rows_y)]:
+            for column in columns[k]:
                 sets.extend([column, swap(column, "dp", 1)])
-            if k >= 2:
-                ready.append(sums[k - 2][1])
-            results.append(compute(k, sets, [r[0] for r in results[-1:]] + ready[-1:]))
+            ready = [r[0] for r in results[-1:]]
+            if k == 0:
+                ready.append(per_hop[2])
+            elif k == 1:
+                ready.extend([columns[2][1:], per_hop[3]])
+            elif k == 2:
+                ready.extend([columns[3][1:], sums[0][0]])
+            else:
+                ready.extend([sums[0][1:], sums[1][1:]])
+            results.append(compute(k, sets, ready))
             own, given = results[k][:CORES]
             got = swap(given, "dp", 1)
             both = [own[j].astype(f32) + got[j].astype(f32) for j in range(rows_y)]
-            sums.append([both[0], *[c.astype(bf16) for c in both[1:]]])
+            sums.append(
+                [both[0], *[swap(both[j].astype(bf16), "dp", CORES * j) for j in range(1, rows_y)]]
+            )
 
         def finish(hold=None):
             hops = []
             for k in range(HOPS):
                 mine = sums[k][0]
-                for j in range(1, rows_y):
-                    mine = mine + swap(sums[k][j], "dp", CORES * j).astype(f32)
+                for got in sums[k][1:]:
+                    mine = mine + got.astype(f32)
                 hops.append(swap(mine.astype(bf16), "fsdp", lows * k) if k else mine)
             if hold is not None:
                 hops = after(hops, hold)
@@ -449,8 +458,11 @@
         return [swap(full, name, unit * m) for m in range(1, size)]
 
     def merge(full, others, step):
-        axis, _, _, _, at = steps[step]
-        return jnp.concatenate(in_order(full, others, at), axis=axis)
+        axis, _, _, size, at = steps[step]
+        if size > 2:
+            return jnp.concatenate(in_order(full, others, at), axis=axis)
+        first = jnp.concatenate([full, *others], axis=axis)
+        return jnp.where(at == 0, first, jnp.concatenate([*others, full], axis=axis))
 
     expert_ids = jnp.arange(experts, dtype=jnp.int32)
     member = jnp.any(routes[:, :, None] == expert_ids[None, None, :], axis=1)
@@ -586,7 +598,7 @@
             ),
         )
 
-    combined = exchange(outgoing, 3, forward)()
+    combined = exchange(outgoing, forward)()
     output = hidden + residual_scale * combined
     valid_rows = (positions < lengths[0]).astype(f32)[:, None]
     deviation = (output - teacher.astype(f32)) * valid_rows
@@ -594,10 +606,12 @@
     out_grad = deviation * (slot_total / valid_total)
 
     loss_total = jnp.full((8, 128), jnp.sum(deviation * deviation), f32)
+    loss_steps = []
     for name, size in (("dp", groups), ("fsdp", shards)):
         mask = 1
         while mask < size:
             loss_total = loss_total + swap(loss_total, name, mask)
+            loss_steps.append(loss_total)
             mask *= 2
     loss_value = loss_total[0, 0] / (valid_total * model_width)
 
@@ -605,8 +619,8 @@
     saved = []
 
     def backward(k, sets, ready):
-        if k == 2:
-            ready = [*ready, loss_total]
+        if k:
+            ready = [*ready, loss_steps[k - 1]]
         results = kernel_call(
             functools.partial(expert_backward, count, seq_len),
             (back_shape,) * CORES
@@ -627,7 +641,7 @@
         saved.append(results[CORES:])
         return results
 
-    finish = exchange(out_grad.astype(bf16), 2, backward)
+    finish = exchange(out_grad.astype(bf16), backward)
     expert_grad = pl.pallas_call(
         functools.partial(expert_weight_grads, HOPS),
         grid=(held,),
@@ -649,7 +663,7 @@
             for m in range(1, lows)
         ]
 
-    returned, low_parts[3] = join((finish(expert_grad), low_parts[3]))
+    returned, low_parts[3] = join((finish((expert_grad, loss_steps[3])), low_parts[3]))
 
     def low_sum(k):
         pieces = low_parts[k]

time: 726 us -> 686 us (0.945)
  waiting for transfers between devices: 310 us -> 282 us
  starting transfers between devices: 121 us -> 111 us
    ppermute x97, waiting for transfers between devices: 310 us -> 282 us  [swap(): lax.ppermute(values, axis, [(i, i ^ mask) for i in range(lax.axis_size(ax...]
    select_n x0 -> x6, other arithmetic: none -> 12.2 us  [merge(): jnp.where(at == 0, first, jnp.concatenate([*others, full], axis=axis))]
    ppermute x97, starting transfers between devices: 121 us -> 111 us  [swap(): lax.ppermute(values, axis, [(i, i ^ mask) for i in range(lax.axis_size(ax...]
  transfers between devices with their start and end apart: 97 -> 97, of which waited for: 42 -> 42; matrix products, arithmetic and copies ran while one was open for 13% -> 14% of each run, Pallas kernels for 20% -> 21%
where the time goes in v4:
time: 686 us; the launch traced here: 681 us
  waiting for transfers between devices  282 us (41%)
  Pallas kernels  142 us (21%)
  starting transfers between devices  111 us (16%)
  other arithmetic  77.4 us (11%)
  local copies, waits for them, and re-layouts  48 us (7%)
  matrix products  14.8 us (2%)
    ppermute x97, waiting for transfers between devices, swap(): lax.ppermute(values, axis, [(i, i ^ mask) for i in range(lax.axis_size(ax...  282 us
    pallas_call x11, Pallas kernels, kernel_call(): pl.pallas_call(body, out_shape=out_shape, in_specs=specs, out_specs=jax.t...  122 us
    ppermute x97, starting transfers between devices, swap(): lax.ppermute(values, axis, [(i, i ^ mask) for i in range(lax.axis_size(ax...  111 us
    pallas_call x1, Pallas kernels, on_device(): pl.pallas_call(functools.partial(expert_weight_grads, HOPS), grid=(held,)...  19.5 us
    dynamic_update_slice x10, local copies, waits for them, and re-layouts, on_device(): lax.dynamic_update_slice(expert_w, piece[:, None], (0, at, i * (shard.sha...  16.3 us
  transfers between devices with their start and end apart: 97, of which 42 were waited for; matrix products, arithmetic and copies ran while one was open for 14% of the time, Pallas kernels for 21%

profile of v4, /device:TPU:0, one launch (start us, length us, event | category | flops | bytes accessed | tf_op | source)
XLA Modules:
  0.0 681.2 jit_solution(4568428700183661916)
XLA Ops:
  24.3 12.5 %collective-permute-done.3 = bf16[1,1,4,1,32,2176]{5,4,3,2,1,0:T(8,128)(2,1)} collective-permute-done((bf16[1,1,4,1,32,2176]{5,4,3,2,1,0:T(8,128)(2,1)}, bf16[1,1,4,1,32,2176]{5,4,3,2,1,0:T(8,128)(2,1)}, u32[]{:S(2)}, u32[]{:S(2)}) %collective-permute-start.3) | collective-permute-done | bytes 557088 | tf_op jit(solution)/shard_map/ppermute | solution.py:40
  48.3 17.4 %collective-permute-done.7 = bf16[2,192,1024]{2,1,0:T(8,128)(2,1)} collective-permute-done((bf16[2,192,1024]{2,1,0:T(8,128)(2,1)}, bf16[2,192,1024]{2,1,0:T(8,128)(2,1)}, u32[]{:S(2)}, u32[]{:S(2)}) %collective-permute-start.7) | collective-permute-done | bytes 786464 | tf_op jit(solution)/shard_map/ppermute | solution.py:40
  75.0 11.7 %collective-permute-start.9 = (bf16[1,1,1,1,32,1024]{5,4,3,2,1,0:T(8,128)(2,1)}, bf16[1,1,1,1,32,1024]{5,4,3,2,1,0:T(8,128)(2,1)}, u32[]{:S(2)}, u32[]{:S(2)}) collective-permute-start(bf16[1,1,1,1,32,1024]{5,4,3,2,1,0:T(8,128)(2,1)} %bitcast.5), channel_id=1, source_target_pairs={{0,2},{1,3},{2,0},{3,1},{4,6},{5,7},{6,4},{7,5},{8,10},{9,11},{10,... | collective-permute-start | bytes 196616 | tf_op jit(solution)/shard_map/ppermute | solution.py:40
  109.4 13.9 %collective-permute-done.13 = bf16[2,96,1024]{2,1,0:T(8,128)(2,1)S(1)} collective-permute-done((bf16[2,96,1024]{2,1,0:T(8,128)(2,1)S(1)}, bf16[2,96,1024]{2,1,0:T(8,128)(2,1)S(1)}, u32[]{:S(2)}, u32[]{:S(2)}) %collective-permute-start.13) | collective-permute-done | bytes 393248 | tf_op jit(solution)/shard_map/ppermute | solution.py:40
  126.3 9.6 %shard_map.237 = (bf16[256,2048]{1,0:T(8,128)(2,1)}, bf16[256,1024]{1,0:T(8,128)(2,1)}) custom-call(s32[1]{0:T(128)} %copy.107.length_ref, f32[256,2048]{1,0:T(8,128)} %fusion.qkv_ref, f32[256,128]{1,0:T(8,128)} %get-tuple-element.296.cos_ref, f32[256,128]{1,0:T(8,128)} %get-tuple-element.297.sin_ref), custom_call_target="tpu_custom_call" | custom-call | tf_op jit(solution)/shard_map/pallas_call | solution.py:59
  149.8 10.4 %collective-permute-done.17 = bf16[2,192,1024]{2,1,0:T(8,128)(2,1)} collective-permute-done((bf16[2,192,1024]{2,1,0:T(8,128)(2,1)}, bf16[2,192,1024]{2,1,0:T(8,128)(2,1)}, u32[]{:S(2)}, u32[]{:S(2)}) %collective-permute-start.17) | collective-permute-done | bytes 786464 | tf_op jit(solution)/shard_map/ppermute | solution.py:40
  165.5 11.6 %collective-permute-done.18 = bf16[2,192,1024]{2,1,0:T(8,128)(2,1)} collective-permute-done((bf16[2,192,1024]{2,1,0:T(8,128)(2,1)}, bf16[2,192,1024]{2,1,0:T(8,128)(2,1)}, u32[]{:S(2)}, u32[]{:S(2)}) %collective-permute-start.18) | collective-permute-done | bytes 786464 | tf_op jit(solution)/shard_map/ppermute | solution.py:40
  199.8 9.5 %shard_map.238 = (bf16[2,256,1024]{2,1,0:T(8,128)(2,1)}, bf16[2,256,1024]{2,1,0:T(8,128)(2,1)}) custom-call(s32[1]{0:T(128)} %bitcast.8.first_ref, bf16[2,8,192,1024]{3,2,1,0:T(8,128)(2,1)} %bitcast_dynamic-update-slice_fusion.10.weights_ref, bf16[272,1024]{1,0:T(8,128)(2,1)} %copy-done.7, bf16[272,1024]{1,0:T(8,128)(2,1)} %copy-done.26, ...), custom_call_target="tpu_custom_call" | custom-call | tf_op jit(solution)/shard_map/pallas_call | solution.py:59
  213.4 9.1 %shard_map.239 = (bf16[2,256,1024]{2,1,0:T(8,128)(2,1)}, bf16[2,256,1024]{2,1,0:T(8,128)(2,1)}) custom-call(s32[1]{0:T(128)} %bitcast.8.first_ref, bf16[2,8,192,1024]{3,2,1,0:T(8,128)(2,1)} %bitcast_dynamic-update-slice_fusion.10.weights_ref, bf16[272,1024]{1,0:T(8,128)(2,1)} %copy-done.17, bf16[272,1024]{1,0:T(8,128)(2,1)} %copy-done.27, ...), custom_call_target="tpu_custom_call" | custom-call | tf_op jit(solution)/shard_map/pallas_call | solution.py:59
  223.5 14.0 %collective-permute-done.36.refs_2_ = bf16[272,1024]{1,0:T(8,128)(2,1)S(1)} collective-permute-done((bf16[272,1024]{1,0:T(8,128)(2,1)S(1)}, bf16[272,1024]{1,0:T(8,128)(2,1)S(1)}, u32[]{:S(2)}, u32[]{:S(2)}) %collective-permute-start.36) | collective-permute-done | bytes 557088 | tf_op jit(solution)/shard_map/ppermute | solution.py:40
  244.4 9.3 %shard_map.240 = (bf16[2,256,1024]{2,1,0:T(8,128)(2,1)}, bf16[2,256,1024]{2,1,0:T(8,128)(2,1)}) custom-call(s32[1]{0:T(128)} %bitcast.8.first_ref, bf16[2,8,192,1024]{3,2,1,0:T(8,128)(2,1)} %bitcast_dynamic-update-slice_fusion.10.weights_ref, bf16[272,1024]{1,0:T(8,128)(2,1)} %copy-done.15, bf16[272,1024]{1,0:T(8,128)(2,1)} %copy-done.24, ...), custom_call_target="tpu_custom_call" | custom-call | tf_op jit(solution)/shard_map/pallas_call | solution.py:59
  254.4 10.3 %collective-permute-done.34 = bf16[256,1024]{1,0:T(8,128)(2,1)} collective-permute-done((bf16[256,1024]{1,0:T(8,128)(2,1)}, bf16[256,1024]{1,0:T(8,128)(2,1)}, u32[]{:S(2)}, u32[]{:S(2)}) %collective-permute-start.34) | collective-permute-done | bytes 524320 | tf_op jit(solution)/shard_map/ppermute | solution.py:40
  266.4 9.1 %shard_map.241 = (bf16[2,256,1024]{2,1,0:T(8,128)(2,1)}, bf16[2,256,1024]{2,1,0:T(8,128)(2,1)}) custom-call(s32[1]{0:T(128)} %bitcast.8.first_ref, bf16[2,8,192,1024]{3,2,1,0:T(8,128)(2,1)} %bitcast_dynamic-update-slice_fusion.10.weights_ref, bf16[272,1024]{1,0:T(8,128)(2,1)} %copy-done.16, bf16[272,1024]{1,0:T(8,128)(2,1)} %copy-done.20, ...), custom_call_target="tpu_custom_call" | custom-call | tf_op jit(solution)/shard_map/pallas_call | solution.py:59
  280.2 10.4 %collective-permute-done.40 = bf16[256,1024]{1,0:T(8,128)(2,1)S(1)} collective-permute-done((bf16[256,1024]{1,0:T(8,128)(2,1)S(1)}, bf16[256,1024]{1,0:T(8,128)(2,1)S(1)}, u32[]{:S(2)}, u32[]{:S(2)}) %collective-permute-start.40) | collective-permute-done | bytes 524320 | tf_op jit(solution)/shard_map/ppermute | solution.py:40
  291.7 7.7 %collective-permute-start.41 = (bf16[256,1024]{1,0:T(8,128)(2,1)}, bf16[256,1024]{1,0:T(8,128)(2,1)}, u32[]{:S(2)}, u32[]{:S(2)}) collective-permute-start(bf16[256,1024]{1,0:T(8,128)(2,1)} %fusion.12), channel_id=1, source_target_pairs={{0,4},{1,5},{2,6},{3,7},{4,0},{5,1},{6,2},{7,3},{8,12},{9,13},{10,... | collective-permute-start | bytes 1572872 | tf_op jit(solution)/shard_map/ppermute | solution.py:40
  305.0 20.3 %collective-permute-done.41 = bf16[256,1024]{1,0:T(8,128)(2,1)} collective-permute-done((bf16[256,1024]{1,0:T(8,128)(2,1)}, bf16[256,1024]{1,0:T(8,128)(2,1)}, u32[]{:S(2)}, u32[]{:S(2)}) %collective-permute-start.41) | collective-permute-done | bytes 524320 | tf_op jit(solution)/shard_map/ppermute | solution.py:40
  325.3 10.0 %collective-permute-done.46 = bf16[256,1024]{1,0:T(8,128)(2,1)} collective-permute-done((bf16[256,1024]{1,0:T(8,128)(2,1)}, bf16[256,1024]{1,0:T(8,128)(2,1)}, u32[]{:S(2)}, u32[]{:S(2)}) %collective-permute-start.46) | collective-permute-done | bytes 524320 | tf_op jit(solution)/shard_map/ppermute | solution.py:40
  338.0 10.0 %collective-permute-start.60 = (bf16[256,1024]{1,0:T(8,128)(2,1)S(1)}, bf16[256,1024]{1,0:T(8,128)(2,1)S(1)}, u32[]{:S(2)}, u32[]{:S(2)}) collective-permute-start(bf16[256,1024]{1,0:T(8,128)(2,1)S(1)} %get-tuple-element.242.refs_4_), channel_id=1, source_target_pairs={{0,2},{1,3},{2,0},{3,1},{4,6},{5,7},{6,4},{7,5},{8,10},{9,11},{10,... | collective-permute-start | bytes 1572872 | tf_op jit(solution)/shard_map/ppermute | solution.py:40
  349.2 20.0 %collective-permute-done.60.refs_4_ = bf16[256,1024]{1,0:T(8,128)(2,1)S(1)} collective-permute-done((bf16[256,1024]{1,0:T(8,128)(2,1)S(1)}, bf16[256,1024]{1,0:T(8,128)(2,1)S(1)}, u32[]{:S(2)}, u32[]{:S(2)}) %collective-permute-start.60) | collective-permute-done | bytes 524320 | tf_op jit(solution)/shard_map/ppermute | solution.py:40
  375.1 8.9 %collective-permute-done.62.refs_6_ = bf16[256,1024]{1,0:T(8,128)(2,1)S(1)} collective-permute-done((bf16[256,1024]{1,0:T(8,128)(2,1)S(1)}, bf16[256,1024]{1,0:T(8,128)(2,1)S(1)}, u32[]{:S(2)}, u32[]{:S(2)}) %collective-permute-start.62) | collective-permute-done | bytes 524320 | tf_op jit(solution)/shard_map/ppermute | solution.py:40
  386.3 13.6 %shard_map.242 = (bf16[2,272,1024]{2,1,0:T(8,128)(2,1)}, bf16[2,272,1024]{2,1,0:T(8,128)(2,1)}, bf16[2,384,1024]{2,1,0:T(8,128)(2,1)}, bf16[2,384,1024]{2,1,0:T(...) custom-call(s32[1]{0:T(128)} %bitcast.8.first_ref, ...), custom_call_target="tpu_custom_call" | custom-call | tf_op jit(solution)/shard_map/pallas_call | solution.py:59
  402.3 13.4 %shard_map.243 = (bf16[2,272,1024]{2,1,0:T(8,128)(2,1)}, bf16[2,272,1024]{2,1,0:T(8,128)(2,1)}, bf16[2,384,1024]{2,1,0:T(8,128)(2,1)}, bf16[2,384,1024]{2,1,0:T(...) custom-call(s32[1]{0:T(128)} %bitcast.8.first_ref, ...), custom_call_target="tpu_custom_call" | custom-call | tf_op jit(solution)/shard_map/pallas_call | solution.py:59
  423.1 8.2 %collective-permute-done.67.refs_6_ = bf16[256,1024]{1,0:T(8,128)(2,1)} collective-permute-done((bf16[256,1024]{1,0:T(8,128)(2,1)}, bf16[256,1024]{1,0:T(8,128)(2,1)}, u32[]{:S(2)}, u32[]{:S(2)}) %collective-permute-start.67) | collective-permute-done | bytes 524320 | tf_op jit(solution)/shard_map/ppermute | solution.py:40
  433.2 13.7 %shard_map.244 = (bf16[2,272,1024]{2,1,0:T(8,128)(2,1)}, bf16[2,272,1024]{2,1,0:T(8,128)(2,1)}, bf16[2,384,1024]{2,1,0:T(8,128)(2,1)}, bf16[2,384,1024]{2,1,0:T(...) custom-call(s32[1]{0:T(128)} %bitcast.8.first_ref, ...), custom_call_target="tpu_custom_call" | custom-call | tf_op jit(solution)/shard_map/pallas_call | solution.py:59
  454.3 13.7 %shard_map.245 = (bf16[2,272,1024]{2,1,0:T(8,128)(2,1)}, bf16[2,272,1024]{2,1,0:T(8,128)(2,1)}, bf16[2,384,1024]{2,1,0:T(8,128)(2,1)}, bf16[2,384,1024]{2,1,0:T(...) custom-call(s32[1]{0:T(128)} %bitcast.8.first_ref, ...), custom_call_target="tpu_custom_call" | custom-call | tf_op jit(solution)/shard_map/pallas_call | solution.py:59
  477.5 7.6 %collective-permute-done.71 = bf16[272,1024]{1,0:T(8,128)(2,1)} collective-permute-done((bf16[272,1024]{1,0:T(8,128)(2,1)}, bf16[272,1024]{1,0:T(8,128)(2,1)}, u32[]{:S(2)}, u32[]{:S(2)}) %collective-permute-start.71) | collective-permute-done | bytes 557088 | tf_op jit(solution)/shard_map/ppermute | solution.py:40
  487.3 19.5 %shard_map.246 = bf16[2,8,192,1024]{3,2,1,0:T(8,128)(2,1)} custom-call(bf16[2,384,1024]{2,1,0:T(8,128)(2,1)} %get-tuple-element.185.refs_0_, bf16[2,384,1024]{2,1,0:T(8,128)(2,1)} %get-tuple-element.186.refs_1_, bf16[2,384,1024]{2,1,0:T(8,128)(2,1)} %get-tuple-element.187.refs_2_, bf16[2,384,1024]{2,1,0:T(8,128)(2,1)} %get-tuple-element.188.refs_3_, ...), custom_call_target="tpu_custom_call" | custom-call | tf_op jit(solution)/shard_map/pallas_call | solution.py:645
  551.1 12.5 %shard_map.247.qkv_grad_ref = bf16[256,2048]{1,0:T(8,128)(2,1)} custom-call(s32[1]{0:T(128)} %copy.107.length_ref, bf16[256,2048]{1,0:T(8,128)(2,1)} %get-tuple-element.172.rot_ref, bf16[256,1024]{1,0:T(8,128)(2,1)} %convolution_convert_fusion.1.grad_ref, f32[256,128]{1,0:T(8,128)} %get-tuple-element.296.cos_ref, f32[256,128]{1,0:T(8,128)} %get-tuple-element.297.sin_ref), custom_call_target="tpu_custom_call" | custom-call | tf_op jit(solution)/shard_map/pallas_call | solution.py:59
  575.4 8.9 %shard_map.248 = (bf16[1024,2176]{1,0:T(8,128)(2,1)}, f32[256,1024]{1,0:T(8,128)}) custom-call(bf16[256,2048]{1,0:T(8,128)(2,1)} %shard_map.247.qkv_grad_ref, bf16[256,1024]{1,0:T(8,128)(2,1)} %copy-done.28, bf16[1024,2176]{1,0:T(8,128)(2,1)} %bitcast.167, f32[256,1024]{1,0:T(8,128)} %convert_element_type.440.tok_ref, f32[256,1]{1,0:T(8,128)} %copy.80.inverse_ref, ...), custom_call_target="tpu_custom_call" | custom-call | tf_op jit(solution)/shard_map/pallas_call | solution.py:59
  606.7 16.7 %collective-permute-done.85 = bf16[1,1,4,1,32,1024]{5,4,3,2,1,0:T(8,128)(2,1)S(1)} collective-permute-done((bf16[1,1,4,1,32,1024]{5,4,3,2,1,0:T(8,128)(2,1)S(1)}, bf16[1,1,4,1,32,1024]{5,4,3,2,1,0:T(8,128)(2,1)S(1)}, u32[]{:S(2)}, u32[]{:S(2)}) %collective-permute-start.85) | collective-permute-done | bytes 262176 | tf_op jit(solution)/shard_map/ppermute | solution.py:40
  633.2 11.1 %collective-permute-done.91 = bf16[2,192,1024]{2,1,0:T(8,128)(2,1)S(1)} collective-permute-done((bf16[2,192,1024]{2,1,0:T(8,128)(2,1)S(1)}, bf16[2,192,1024]{2,1,0:T(8,128)(2,1)S(1)}, u32[]{:S(2)}, u32[]{:S(2)}) %collective-permute-start.91) | collective-permute-done | bytes 786464 | tf_op jit(solution)/shard_map/ppermute | solution.py:40
  654.1 7.7 %collective-permute-done.93 = bf16[2,192,1024]{2,1,0:T(8,128)(2,1)S(1)} collective-permute-done((bf16[2,192,1024]{2,1,0:T(8,128)(2,1)S(1)}, bf16[2,192,1024]{2,1,0:T(8,128)(2,1)S(1)}, u32[]{:S(2)}, u32[]{:S(2)}) %collective-permute-start.93) | collective-permute-done | bytes 786464 | tf_op jit(solution)/shard_map/ppermute | solution.py:40
  (416 shorter events, 292.6 us)
Async XLA Ops:
  44.5 25.1 %collective-permute-start.6 = (bf16[2,1,4,1,32,2176]{5,4,3,2,1,0:T(8,128)(2,1)}, bf16[2,1,4,1,32,2176]{5,4,3,2,1,0:T(8,128)(2,1)}, u32[]{:S(2)}, u32[]{:S(2)}) collective-permute-start(bf16[2,1,4,1,32,2176]{5,4,3,2,1,0:T(8,128)(2,1)} %maximum_select_fusion.3), channel_id=1, source_target_pairs={{0,1},{1,0},{2,3},{3,2},{4,5},{5,4},{6,7},{7,6},{8,9},{9,8},{10,11... | collective-permute-start | bytes 3342344 | tf_op jit(solution)/shard_map/ppermute | solution.py:40
  140.1 37.0 %collective-permute-start.18 = (bf16[2,192,1024]{2,1,0:T(8,128)(2,1)}, bf16[2,192,1024]{2,1,0:T(8,128)(2,1)}, u32[]{:S(2)}, u32[]{:S(2)}) collective-permute-start(bf16[2,192,1024]{2,1,0:T(8,128)(2,1)} %collective-permute-done.7), channel_id=1, source_target_pairs={{0,1},{1,0},{2,3},{3,2},{4,5},{5,4},{6,7},{7,6},{8,9},{9,8},{10,11... | collective-permute-start | bytes 2359304 | tf_op jit(solution)/shard_map/ppermute | solution.py:40
  145.4 31.7 %collective-permute-start.29 = (bf16[272,1024]{1,0:T(8,128)(2,1)S(1)}, bf16[272,1024]{1,0:T(8,128)(2,1)S(1)}, u32[]{:S(2)}, u32[]{:S(2)}) collective-permute-start(bf16[272,1024]{1,0:T(8,128)(2,1)S(1)} %pad_maximum_fusion.2.refs_0_), channel_id=1, source_target_pairs={{0,2},{1,3},{2,0},{3,1},{4,6},{5,7},{6,4},{7,5},{8,10},{9,11},{10,... | collective-permute-start | bytes 1671176 | tf_op jit(solution)/shard_map/ppermute | solution.py:40
  162.9 23.4 %collective-permute-start.23 = (bf16[272,1024]{1,0:T(8,128)(2,1)S(1)}, bf16[272,1024]{1,0:T(8,128)(2,1)S(1)}, u32[]{:S(2)}, u32[]{:S(2)}) collective-permute-start(bf16[272,1024]{1,0:T(8,128)(2,1)S(1)} %pad_maximum_fusion.2.refs_0_), channel_id=1, source_target_pairs={{0,16},{8,24},{16,0},{24,8},{1,17},{9,25},{17,1},{25,9},{2,18},{10... | collective-permute-start | bytes 1671176 | tf_op jit(solution)/shard_map/ppermute | solution.py:40
  165.5 32.0 %collective-permute-start.16 = (bf16[272,1024]{1,0:T(8,128)(2,1)S(1)}, bf16[272,1024]{1,0:T(8,128)(2,1)S(1)}, u32[]{:S(2)}, u32[]{:S(2)}) collective-permute-start(bf16[272,1024]{1,0:T(8,128)(2,1)S(1)} %pad_maximum_fusion.2.refs_0_), channel_id=1, source_target_pairs={{0,4},{1,5},{2,6},{3,7},{4,0},{5,1},{6,2},{7,3},{8,12},{9,13},{10,... | collective-permute-start | bytes 1671176 | tf_op jit(solution)/shard_map/ppermute | solution.py:40
  209.3 28.2 %collective-permute-start.25 = (bf16[2,256,1024]{2,1,0:T(8,128)(2,1)}, bf16[2,256,1024]{2,1,0:T(8,128)(2,1)}, u32[]{:S(2)}, u32[]{:S(2)}) collective-permute-start(bf16[2,256,1024]{2,1,0:T(8,128)(2,1)} %get-tuple-element.162), channel_id=1, source_target_pairs={{0,8},{8,0},{16,24},{24,16},{1,9},{9,1},{17,25},{25,17},{2,10},{10... | collective-permute-start | bytes 3145736 | tf_op jit(solution)/shard_map/ppermute | solution.py:40
  237.5 27.2 %collective-permute-start.42 = (bf16[272,1024]{1,0:T(8,128)(2,1)S(1)}, bf16[272,1024]{1,0:T(8,128)(2,1)S(1)}, u32[]{:S(2)}, u32[]{:S(2)}) collective-permute-start(bf16[272,1024]{1,0:T(8,128)(2,1)S(1)} %collective-permute-done.28.refs_0_), channel_id=1, source_target_pairs={{0,8},{8,0},{16,24},{24,16},{1,9},{9,1},{17,25},{25,17},{2,10},{10... | collective-permute-start | bytes 1671176 | tf_op jit(solution)/shard_map/ppermute | solution.py:40
  237.5 27.2 %collective-permute-start.43 = (bf16[272,1024]{1,0:T(8,128)(2,1)S(1)}, bf16[272,1024]{1,0:T(8,128)(2,1)S(1)}, u32[]{:S(2)}, u32[]{:S(2)}) collective-permute-start(bf16[272,1024]{1,0:T(8,128)(2,1)S(1)} %collective-permute-done.36.refs_2_), channel_id=1, source_target_pairs={{0,8},{8,0},{16,24},{24,16},{1,9},{9,1},{17,25},{25,17},{2,10},{10... | collective-permute-start | bytes 1671176 | tf_op jit(solution)/shard_map/ppermute | solution.py:40
  242.0 22.7 %collective-permute-start.34 = (bf16[256,1024]{1,0:T(8,128)(2,1)}, bf16[256,1024]{1,0:T(8,128)(2,1)}, u32[]{:S(2)}, u32[]{:S(2)}) collective-permute-start(bf16[256,1024]{1,0:T(8,128)(2,1)} %fusion.22), channel_id=1, source_target_pairs={{0,16},{8,24},{16,0},{24,8},{1,17},{9,25},{17,1},{25,9},{2,18},{10... | collective-permute-start | bytes 1572872 | tf_op jit(solution)/shard_map/ppermute | solution.py:40
  291.7 33.6 %collective-permute-start.41 = (bf16[256,1024]{1,0:T(8,128)(2,1)}, bf16[256,1024]{1,0:T(8,128)(2,1)}, u32[]{:S(2)}, u32[]{:S(2)}) collective-permute-start(bf16[256,1024]{1,0:T(8,128)(2,1)} %fusion.12), channel_id=1, source_target_pairs={{0,4},{1,5},{2,6},{3,7},{4,0},{5,1},{6,2},{7,3},{8,12},{9,13},{10,... | collective-permute-start | bytes 1572872 | tf_op jit(solution)/shard_map/ppermute | solution.py:40
  300.7 24.6 %collective-permute-start.35 = (bf16[256,1024]{1,0:T(8,128)(2,1)S(1)}, bf16[256,1024]{1,0:T(8,128)(2,1)}, u32[]{:S(2)}, u32[]{:S(2)}) collective-permute-start(bf16[256,1024]{1,0:T(8,128)(2,1)S(1)} %fusion.13), channel_id=1, source_target_pairs={{0,2},{1,3},{2,0},{3,1},{4,6},{5,7},{6,4},{7,5},{8,10},{9,11},{10,... | collective-permute-start | bytes 1572872 | tf_op jit(solution)/shard_map/ppermute | solution.py:40
  302.4 32.8 %collective-permute-start.46 = (bf16[256,1024]{1,0:T(8,128)(2,1)}, bf16[256,1024]{1,0:T(8,128)(2,1)}, u32[]{:S(2)}, u32[]{:S(2)}) collective-permute-start(bf16[256,1024]{1,0:T(8,128)(2,1)} %fusion.11), channel_id=1, source_target_pairs={{0,6},{1,7},{2,4},{3,5},{4,2},{5,3},{6,0},{7,1},{8,14},{9,15},{10,... | collective-permute-start | bytes 1572872 | tf_op jit(solution)/shard_map/ppermute | solution.py:40
  338.0 31.1 %collective-permute-start.60 = (bf16[256,1024]{1,0:T(8,128)(2,1)S(1)}, bf16[256,1024]{1,0:T(8,128)(2,1)S(1)}, u32[]{:S(2)}, u32[]{:S(2)}) collective-permute-start(bf16[256,1024]{1,0:T(8,128)(2,1)S(1)} %get-tuple-element.242.refs_4_), channel_id=1, source_target_pairs={{0,2},{1,3},{2,0},{3,1},{4,6},{5,7},{6,4},{7,5},{8,10},{9,11},{10,... | collective-permute-start | bytes 1572872 | tf_op jit(solution)/shard_map/ppermute | solution.py:40
  348.5 25.0 %collective-permute-start.52 = (bf16[256,1024]{1,0:T(8,128)(2,1)S(1)}, bf16[256,1024]{1,0:T(8,128)(2,1)}, u32[]{:S(2)}, u32[]{:S(2)}) collective-permute-start(bf16[256,1024]{1,0:T(8,128)(2,1)S(1)} %get-tuple-element.242.refs_4_), channel_id=1, source_target_pairs={{0,4},{1,5},{2,6},{3,7},{4,0},{5,1},{6,2},{7,3},{8,12},{9,13},{10,... | collective-permute-start | bytes 1572872 | tf_op jit(solution)/shard_map/ppermute | solution.py:40
  349.2 25.9 %collective-permute-start.53 = (bf16[256,1024]{1,0:T(8,128)(2,1)S(1)}, bf16[256,1024]{1,0:T(8,128)(2,1)S(1)}, u32[]{:S(2)}, u32[]{:S(2)}) collective-permute-start(bf16[256,1024]{1,0:T(8,128)(2,1)S(1)} %get-tuple-element.242.refs_4_), channel_id=1, source_target_pairs={{0,8},{8,0},{16,24},{24,16},{1,9},{9,1},{17,25},{25,17},{2,10},{10... | collective-permute-start | bytes 1572872 | tf_op jit(solution)/shard_map/ppermute | solution.py:40
  369.2 31.4 %collective-permute-start.59 = (bf16[256,1024]{1,0:T(8,128)(2,1)S(1)}, bf16[256,1024]{1,0:T(8,128)(2,1)}, u32[]{:S(2)}, u32[]{:S(2)}) collective-permute-start(bf16[256,1024]{1,0:T(8,128)(2,1)S(1)} %get-tuple-element.242.refs_4_), channel_id=1, source_target_pairs={{0,6},{1,7},{2,4},{3,5},{4,2},{5,3},{6,0},{7,1},{8,14},{9,15},{10,... | collective-permute-start | bytes 1572872 | tf_op jit(solution)/shard_map/ppermute | solution.py:40
  373.5 27.2 %collective-permute-start.58 = (bf16[256,1024]{1,0:T(8,128)(2,1)}, bf16[256,1024]{1,0:T(8,128)(2,1)}, u32[]{:S(2)}, u32[]{:S(2)}) collective-permute-start(bf16[256,1024]{1,0:T(8,128)(2,1)} %collective-permute-done.52.refs_4_), channel_id=1, source_target_pairs={{0,16},{8,24},{16,0},{24,8},{1,17},{9,25},{17,1},{25,9},{2,18},{10... | collective-permute-start | bytes 1572872 | tf_op jit(solution)/shard_map/ppermute | solution.py:40
  375.1 25.6 %collective-permute-start.61 = (bf16[256,1024]{1,0:T(8,128)(2,1)S(1)}, bf16[256,1024]{1,0:T(8,128)(2,1)S(1)}, u32[]{:S(2)}, u32[]{:S(2)}) collective-permute-start(bf16[256,1024]{1,0:T(8,128)(2,1)S(1)} %collective-permute-done.60.refs_4_), channel_id=1, source_target_pairs={{0,8},{8,0},{16,24},{24,16},{1,9},{9,1},{17,25},{25,17},{2,10},{10... | collective-permute-start | bytes 1572872 | tf_op jit(solution)/shard_map/ppermute | solution.py:40
  418.9 28.2 %collective-permute-start.57 = (bf16[272,1024]{1,0:T(8,128)(2,1)S(1)}, bf16[272,1024]{1,0:T(8,128)(2,1)S(1)}, u32[]{:S(2)}, u32[]{:S(2)}) collective-permute-start(bf16[272,1024]{1,0:T(8,128)(2,1)S(1)} %fusion.17), channel_id=1, source_target_pairs={{0,16},{8,24},{16,0},{24,8},{1,17},{9,25},{17,1},{25,9},{2,18},{10... | collective-permute-start | bytes 1671176 | tf_op jit(solution)/shard_map/ppermute | solution.py:40
  421.4 32.9 %collective-permute-start.65 = (bf16[272,1024]{1,0:T(8,128)(2,1)}, bf16[272,1024]{1,0:T(8,128)(2,1)S(1)}, u32[]{:S(2)}, u32[]{:S(2)}) collective-permute-start(bf16[272,1024]{1,0:T(8,128)(2,1)} %fusion.18), channel_id=1, source_target_pairs={{0,16},{8,24},{16,0},{24,8},{1,17},{9,25},{17,1},{25,9},{2,18},{10... | collective-permute-start | bytes 1671176 | tf_op jit(solution)/shard_map/ppermute | solution.py:40
  431.3 23.0 %collective-permute-start.73 = (bf16[256,1024]{1,0:T(8,128)(2,1)}, bf16[256,1024]{1,0:T(8,128)(2,1)}, u32[]{:S(2)}, u32[]{:S(2)}) collective-permute-start(bf16[256,1024]{1,0:T(8,128)(2,1)} %collective-permute-done.59.refs_4_), channel_id=1, source_target_pairs={{0,8},{8,0},{16,24},{24,16},{1,9},{9,1},{17,25},{25,17},{2,10},{10... | collective-permute-start | bytes 1572872 | tf_op jit(solution)/shard_map/ppermute | solution.py:40
  431.3 23.0 %collective-permute-start.74 = (bf16[256,1024]{1,0:T(8,128)(2,1)}, bf16[256,1024]{1,0:T(8,128)(2,1)}, u32[]{:S(2)}, u32[]{:S(2)}) collective-permute-start(bf16[256,1024]{1,0:T(8,128)(2,1)} %collective-permute-done.67.refs_6_), channel_id=1, source_target_pairs={{0,8},{8,0},{16,24},{24,16},{1,9},{9,1},{17,25},{25,17},{2,10},{10... | collective-permute-start | bytes 1572872 | tf_op jit(solution)/shard_map/ppermute | solution.py:40
  473.6 33.3 %collective-permute-start.76 = (bf16[272,1024]{1,0:T(8,128)(2,1)}, bf16[272,1024]{1,0:T(8,128)(2,1)S(1)}, u32[]{:S(2)}, u32[]{:S(2)}) collective-permute-start(bf16[272,1024]{1,0:T(8,128)(2,1)} %fusion.20), channel_id=1, source_target_pairs={{0,16},{8,24},{16,0},{24,8},{1,17},{9,25},{17,1},{25,9},{2,18},{10... | collective-permute-start | bytes 1671176 | tf_op jit(solution)/shard_map/ppermute | solution.py:40
  477.5 46.5 %collective-permute-start.66 = (bf16[272,1024]{1,0:T(8,128)(2,1)}, bf16[272,1024]{1,0:T(8,128)(2,1)}, u32[]{:S(2)}, u32[]{:S(2)}) collective-permute-start(bf16[272,1024]{1,0:T(8,128)(2,1)} %fusion.9), channel_id=1, source_target_pairs={{0,2},{1,3},{2,0},{3,1},{4,6},{5,7},{6,4},{7,5},{8,10},{9,11},{10,... | collective-permute-start | bytes 1671176 | tf_op jit(solution)/shard_map/ppermute | solution.py:40
  487.3 40.3 %collective-permute-start.72 = (bf16[272,1024]{1,0:T(8,128)(2,1)}, bf16[272,1024]{1,0:T(8,128)(2,1)}, u32[]{:S(2)}, u32[]{:S(2)}) collective-permute-start(bf16[272,1024]{1,0:T(8,128)(2,1)} %fusion.8), channel_id=1, source_target_pairs={{0,4},{1,5},{2,6},{3,7},{4,0},{5,1},{6,2},{7,3},{8,12},{9,13},{10,... | collective-permute-start | bytes 1671176 | tf_op jit(solution)/shard_map/ppermute | solution.py:40
  543.6 40.8 %collective-permute-start.82 = (bf16[2,1,1,192,1024]{4,3,0,2,1:T(8,128)(2,1)}, bf16[2,1,1,192,1024]{4,3,0,2,1:T(8,128)(2,1)}, u32[]{:S(2)}, u32[]{:S(2)}) collective-permute-start(bf16[2,1,1,192,1024]{4,3,0,2,1:T(8,128)(2,1)} %get-tuple-element.252), channel_id=1, source_target_pairs={{0,1},{1,0},{2,3},{3,2},{4,5},{5,4},{6,7},{7,6},{8,9},{9,8},{10,11... | collective-permute-start | bytes 2359304 | tf_op jit(solution)/shard_map/ppermute | solution.py:40
  547.5 36.9 %collective-permute-start.83 = (bf16[2,192,1024]{2,1,0:T(8,128)(2,1)}, bf16[2,192,1024]{2,1,0:T(8,128)(2,1)}, u32[]{:S(2)}, u32[]{:S(2)}) collective-permute-start(bf16[2,192,1024]{2,1,0:T(8,128)(2,1)} %fusion.14), channel_id=1, source_target_pairs={{0,6},{1,7},{2,4},{3,5},{4,2},{5,3},{6,0},{7,1},{8,14},{9,15},{10,... | collective-permute-start | bytes 2359304 | tf_op jit(solution)/shard_map/ppermute | solution.py:40
  590.3 33.1 %collective-permute-start.84 = (bf16[2,1,4,2,32,2176]{5,4,3,2,1,0:T(8,128)(2,1)}, bf16[2,1,4,2,32,2176]{5,4,3,2,1,0:T(8,128)(2,1)}, u32[]{:S(2)}, u32[]{:S(2)}) collective-permute-start(bf16[2,1,4,2,32,2176]{5,4,3,2,1,0:T(8,128)(2,1)} %get-tuple-element.258), channel_id=1, source_target_pairs={{0,8},{8,0},{16,24},{24,16},{1,9},{9,1},{17,25},{25,17},{2,10},{10... | collective-permute-start | bytes 6684680 | tf_op jit(solution)/shard_map/ppermute | solution.py:40
  598.6 32.5 %collective-permute-start.90 = (bf16[2,1,1,192,1024]{4,3,0,2,1:T(8,128)(2,1)S(1)}, bf16[2,1,1,192,1024]{4,3,0,2,1:T(8,128)(2,1)S(1)}, u32[]{:S(2)}, u32[]{:S(2)}) collective-permute-start(bf16[2,1,1,192,1024]{4,3,0,2,1:T(8,128)(2,1)S(1)} %copy-done.42), channel_id=1, source_target_pairs={{0,1},{1,0},{2,3},{3,2},{4,5},{5,4},{6,7},{7,6},{8,9},{9,8},{10,11... | collective-permute-start | bytes 2359304 | tf_op jit(solution)/shard_map/ppermute | solution.py:40
  600.6 22.8 %collective-permute-start.85 = (bf16[1,1,4,1,32,1024]{5,4,3,2,1,0:T(8,128)(2,1)S(1)}, bf16[1,1,4,1,32,1024]{5,4,3,2,1,0:T(8,128)(2,1)S(1)}, u32[]{:S(2)}, u32[]{:S(2)}) collective-permute-start(bf16[1,1,4,1,32,1024]{5,4,3,2,1,0:T(8,128)(2,1)S(1)} %dynamic-slice_convert_fusion.5), channel_id=1, source_target_pairs={{0,1},{1,0},{2,3},{3,2},{4,5},{5,4},{6,7},{7,6},{8,9},{9,8},{10,11... | collective-permute-start | bytes 786440 | tf_op jit(solution)/shard_map/ppermute | solution.py:40
  603.6 40.7 %collective-permute-start.91 = (bf16[2,192,1024]{2,1,0:T(8,128)(2,1)S(1)}, bf16[2,192,1024]{2,1,0:T(8,128)(2,1)S(1)}, u32[]{:S(2)}, u32[]{:S(2)}) collective-permute-start(bf16[2,192,1024]{2,1,0:T(8,128)(2,1)S(1)} %fusion.15), channel_id=1, source_target_pairs={{0,4},{1,5},{2,6},{3,7},{4,0},{5,1},{6,2},{7,3},{8,12},{9,13},{10,... | collective-permute-start | bytes 2359304 | tf_op jit(solution)/shard_map/ppermute | solution.py:40
  625.7 25.3 %collective-permute-start.86 = (bf16[1,1,4,2,32,2176]{5,4,3,2,1,0:T(8,128)(2,1)S(1)}, bf16[1,1,4,2,32,2176]{5,4,3,2,1,0:T(8,128)(2,1)S(1)}, u32[]{:S(2)}, u32[]{:S(2)}) collective-permute-start(bf16[1,1,4,2,32,2176]{5,4,3,2,1,0:T(8,128)(2,1)S(1)} %dynamic-slice_convert_fusion), channel_id=1, source_target_pairs={{0,16},{8,24},{16,0},{24,8},{1,17},{9,25},{17,1},{25,9},{2,18},{10... | collective-permute-start | bytes 3342344 | tf_op jit(solution)/shard_map/ppermute | solution.py:40
  (124 other events, 1769.8 us)

commit v5 on v4

--- a/solution.py
+++ b/solution.py
@@ -293,26 +293,33 @@
                 out_refs[s % CORES][s // CORES, seq_len:, :] = jnp.concatenate([high, low], axis=0)
 
 
-def expert_weight_grads(groups, *refs):
+def expert_weight_grads(groups, hops, at_ref, *refs):
     picked = refs[:groups]
     wide_grads = refs[groups : 2 * groups]
     routed = refs[2 * groups : 3 * groups]
     inner = refs[3 * groups : 4 * groups]
-    out_ref, = refs[4 * groups :]
-    blocks, width = out_ref.shape[1], out_ref.shape[3]
+    out_refs = refs[4 * groups : -1]
+    work_ref = refs[-1]
+    blocks, _, width = work_ref.shape
+    lows = blocks // hops
     split = picked[0].shape[2] // blocks
     wide = dot_tn(picked[0][0], wide_grads[0][0])
     for k in range(1, groups):
         wide = wide + dot_tn(picked[k][0], wide_grads[k][0])
-    out_ref[0, :, :split, :] = wide.astype(bf16).reshape(blocks, split, width)
+    work_ref[:, :split, :] = wide.astype(bf16).reshape(blocks, split, width)
     down = dot_tn(inner[0][0], routed[0][0])
     for k in range(1, groups):
         down = down + dot_tn(inner[k][0], routed[k][0])
-    out_ref[0, :, split:, :] = down.astype(bf16).reshape(blocks, -1, width)
+    work_ref[:, split:, :] = down.astype(bf16).reshape(blocks, -1, width)
+    for k in range(hops):
+        for m in range(lows):
+            block = (at_ref[0] ^ k) * lows + (at_ref[1] ^ m)
+            out_refs[k * lows + m][0] = work_ref[block]
 
 
 def dense_backward(
     experts,
+    core_ref,
     qkv_grad_ref,
     normed_ref,
     weights_ref,
@@ -321,9 +328,9 @@
     gain_ref,
     hidden_grad_ref,
     small_ref,
-    grads_ref,
-    token_grad_ref,
+    *refs,
 ):
+    *share_refs, token_grad_ref, grads_ref = refs
     seq_len, width = qkv_grad_ref.shape
     normed = normed_ref[...]
     for lanes in range(0, width, 512):
@@ -344,10 +351,14 @@
         normed_grad * rows_in * inverse,
         jnp.where(lane == experts, 1.0, 0.0),
         (((0,), (0,)), ((), ())),
-        precision=highest,
         preferred_element_type=f32,
     )
     grads_ref[:, width:] = (small_ref[...] + gain_grad).astype(bf16)
+    rows = share_refs[0].shape[1]
+    for j in range(share_refs[0].shape[0]):
+        for c, share_ref in enumerate(share_refs):
+            at = pl.multiple_of((j * len(share_refs) + (core_ref[0] ^ c)) * rows, rows)
+            share_ref[j] = grads_ref[pl.ds(at, rows), :]
 
 
 def norm_back(grad_rows, rows_in, inverse, gain_vec):
@@ -421,7 +432,7 @@
             elif k == 2:
                 ready.extend([columns[3][1:], sums[0][0]])
             else:
-                ready.extend([sums[0][1:], sums[1][1:]])
+                ready.extend([sums[0][1:], sums[1][1:], sums[2][0]])
             results.append(compute(k, sets, ready))
             own, given = results[k][:CORES]
             got = swap(given, "dp", 1)
@@ -433,8 +444,10 @@
         def finish(hold=None):
             hops = []
             for k in range(HOPS):
-                mine = sums[k][0]
-                for got in sums[k][1:]:
+                mine, others = sums[k][0], sums[k][1:]
+                if k == HOPS - 1:
+                    others = after(others, hops[1])
+                for got in others:
                     mine = mine + got.astype(f32)
                 hops.append(swap(mine.astype(bf16), "fsdp", lows * k) if k else mine)
             if hold is not None:
@@ -509,15 +522,17 @@
     pack, others, blocks[1], lows_of[0] = join((pack, others, blocks[1], lows_of[0]))
     pack = merge(pack, others, 1)
     others = send(pack, 2)
-    blocks[3] = swap(after(owned_by(3), pack), "fsdp", lows * 3)
-    pack, others, blocks[3] = join((pack, others, blocks[3]))
+    third = shard.shape[1] // 3
+    far3 = [swap(after(owned_by(3)[:, third:], pack), "fsdp", lows * 3)]
+    pack, others, far3 = join((pack, others, far3))
     pack = merge(pack, others, 2)
     others = send(pack, 3)
     out_w = after(w_out, pack).reshape(1, 1, 1, 1, row_block, -1)
     lows_of[1] = low_swaps(after(blocks[1], pack))
+    far3.insert(0, swap(after(owned_by(3)[:, :third], pack), "fsdp", lows * 3))
     out_others = send(out_w, 0)
-    pack, others, out_w, out_others = join((pack, others, out_w, out_others))
-    far_first = swap(after(owned_by(2)[:, : shard.shape[1] // 2], others), "fsdp", lows * 2)
+    pack, others, out_w, out_others, far3 = join((pack, others, out_w, out_others, far3))
+    far2 = [swap(after(owned_by(2)[:, :third], others), "fsdp", lows * 2)]
     packed = merge(pack, others, 3).reshape(model_width, -1)
     out_w = merge(out_w, out_others, 0)
     out_others = send(out_w, 1)
@@ -533,11 +548,11 @@
     normed = (tok_float * inv_one * gain_float).astype(bf16)
     cos_lanes, sin_lanes = rotary_lanes(seq_len)
     qkv = dot(normed, qkv_w)
-    qkv, out_w, out_others, far_first = join((qkv, out_w, out_others, far_first))
-    far_second = swap(after(owned_by(2)[:, shard.shape[1] // 2 :], qkv), "fsdp", lows * 2)
+    qkv, out_w, out_others, far2, lows_of[1] = join((qkv, out_w, out_others, far2, lows_of[1]))
+    far2.append(swap(after(owned_by(2)[:, third:], qkv), "fsdp", lows * 2))
     out_w = merge(out_w, out_others, 1)
     out_others = send(out_w, 2)
-    lows_of[3] = low_swaps(after(blocks[3], qkv))
+    low3 = [low_swaps(after(piece, qkv)) for piece in far3]
     rotated, mixed_rows = kernel_call(
         attention_forward,
         (
@@ -547,21 +562,19 @@
         (lengths, qkv, cos_lanes, sin_lanes),
         first_smem=True,
     )
-    mixed_rows, out_w, out_others = join((mixed_rows, out_w, out_others))
+    mixed_rows, out_w, out_others, far2, low3 = join((mixed_rows, out_w, out_others, far2, low3))
     out_w = merge(out_w, out_others, 2)
     out_w = merge(out_w, send(out_w, 3), 3).reshape(model_width, -1)
-    low_first = low_swaps(after(far_first, mixed_rows))
-    blocks[2] = (far_first, far_second)
-    lows_of[2] = list(zip(low_first, low_swaps(far_second), strict=True))
+    low2 = [low_swaps(piece) for piece in far2]
+    parts_of = {k: [([blocks[k], *lows_of[k]], 0)] for k in (0, 1)}
+    for k, far, low in ((3, far3, low3), (2, far2, low2)):
+        parts_of[k] = [([far[i], *low[i]], i * third) for i in range(2)]
     expert_w = jnp.zeros((held, shards, shard.shape[1], model_width), bf16)
     for k in (0, 1, 3, 2):
-        for m, part in enumerate([blocks[k], *lows_of[k]]):
-            at = (hop_at ^ k) * lows + (low_at ^ m)
-            pieces = part if k == 2 else (part,)
-            for i, piece in enumerate(pieces):
-                expert_w = lax.dynamic_update_slice(
-                    expert_w, piece[:, None], (0, at, i * (shard.shape[1] // 2), 0)
-                )
+        for pieces, row in parts_of[k]:
+            for m, piece in enumerate(pieces):
+                at = (hop_at ^ k) * lows + (low_at ^ m)
+                expert_w = lax.dynamic_update_slice(expert_w, piece[:, None], (0, at, row, 0))
     hidden = tok_float + residual_scale * dot(mixed_rows, out_w)
     inv_two = lax.rsqrt(jnp.mean(hidden * hidden, axis=1, keepdims=True) + epsilon)
     normed_ffn = hidden * inv_two * gain_second
@@ -642,35 +655,37 @@
         return results
 
     finish = exchange(out_grad.astype(bf16), backward)
+    block_shape = (1, shard.shape[1], model_width)
     expert_grad = pl.pallas_call(
-        functools.partial(expert_weight_grads, HOPS),
+        functools.partial(expert_weight_grads, HOPS, HOPS),
         grid=(held,),
-        out_shape=jax.ShapeDtypeStruct((held, shards, shard.shape[1], model_width), bf16),
-        in_specs=[
+        out_shape=(jax.ShapeDtypeStruct((held, *block_shape[1:]), bf16),) * shards,
+        in_specs=[smem()]
+        + [
             pl.BlockSpec((1, rows, width), lambda e: (e, 0, 0))
             for width in (model_width, 2 * hidden_units, model_width, hidden_units)
             for _ in range(HOPS)
         ],
-        out_specs=pl.BlockSpec((1, shards, shard.shape[1], model_width), lambda e: (e, 0, 0, 0)),
+        out_specs=(pl.BlockSpec(block_shape, lambda e: (e, 0, 0)),) * shards,
+        scratch_shapes=(pltpu.VMEM((shards, shard.shape[1], model_width), bf16),),
         compiler_params=pltpu.CompilerParams(vmem_limit_bytes=60 * 1024 * 1024),
-    )(*[saved[k][i] for i in range(4) for k in range(HOPS)])
-    part = expert_grad.reshape(held, HOPS, lows, shard.shape[1], model_width)
-    low_parts = {}
-    for k in (*range(HOPS - 1, 0, -1), 0):
-        both_lows = lax.dynamic_slice_in_dim(part, hop_at ^ k, 1, 1)
-        low_parts[k] = [lax.dynamic_slice_in_dim(both_lows, low_at, 1, 2)] + [
-            swap(lax.dynamic_slice_in_dim(both_lows, low_at ^ m, 1, 2), "fsdp", m)
-            for m in range(1, lows)
-        ]
-
-    returned, low_parts[3] = join((finish((expert_grad, loss_steps[3])), low_parts[3]))
+    )(
+        jnp.stack([hop_at, low_at]).astype(jnp.int32),
+        *[saved[k][i] for i in range(4) for k in range(HOPS)],
+    )
+    low_parts = {
+        k: [expert_grad[k * lows]]
+        + [swap(expert_grad[k * lows + m], "fsdp", m) for m in range(1, lows)]
+        for k in range(HOPS - 1, -1, -1)
+    }
+    returned, low_parts[3] = join((finish((expert_grad[0], loss_steps[3])), low_parts[3]))
 
     def low_sum(k):
         pieces = low_parts[k]
         total = pieces[0].astype(f32)
         for piece in pieces[1:]:
             total = total + piece.astype(f32)
-        return total.reshape(held, shard.shape[1], model_width)
+        return total
 
     def hop_send(k):
         return swap(low_sum(k).astype(bf16), "fsdp", lows * k)
@@ -719,7 +734,6 @@
             ],
             axis=0,
         ),
-        precision=highest,
         preferred_element_type=f32,
     )
     qkv_grad = kernel_call(
@@ -732,16 +746,27 @@
     qkv_grad, out_sum, low_parts[2] = join((qkv_grad, out_sum, low_parts[2]))
     out_sum = halve(total(*out_sum), 1)
     hop_got[2] = hop_send(2)
-    grads, token_grad = kernel_call(
+    share = jax.ShapeDtypeStruct((rows_y, HOPS * lows * row_block, qkv_width + 128), bf16)
+    *grads, token_grad = kernel_call(
         functools.partial(dense_backward, experts),
+        (share,) * CORES + (jax.ShapeDtypeStruct((seq_len, model_width), f32),),
         (
-            jax.ShapeDtypeStruct((model_width, qkv_width + 128), bf16),
-            jax.ShapeDtypeStruct((seq_len, model_width), f32),
+            core_at.astype(jnp.int32)[None],
+            qkv_grad,
+            normed,
+            packed,
+            tok_float,
+            inv_one,
+            gain_float[None, :],
+            hidden_grad,
+            small,
         ),
-        (qkv_grad, normed, packed, tok_float, inv_one, gain_float[None, :], hidden_grad, small),
+        first_smem=True,
+        scratch=(pltpu.VMEM((model_width, qkv_width + 128), bf16),),
     )
     grads, out_sum, low_parts[1], hop_got[3] = join((grads, out_sum, low_parts[1], hop_got[3]))
-    part_sum = halve(grads.reshape(order), 3)
+    grads = [g.reshape(rows_y, 1, HOPS, lows, row_block, -1) for g in grads]
+    part_sum = (grads[0].astype(f32), [swap(g, "dp", m + 1) for m, g in enumerate(grads[1:])])
     out_sum = halve(total(*out_sum), 2)
     part_sum, out_sum = join((part_sum, out_sum))
     part_sum = halve(total(*part_sum), 1)

time: 686 us -> 689 us (level)
  waiting for transfers between devices: 282 us -> 317 us
  other arithmetic: 77.4 us -> 57.6 us
  starting transfers between devices: 111 us -> 101 us
    ppermute x97 -> x99, waiting for transfers between devices: 282 us -> 317 us  [swap(): lax.ppermute(values, axis, [(i, i ^ mask) for i in range(lax.axis_size(ax...]
    ppermute x97 -> x99, starting transfers between devices: 111 us -> 101 us  [swap(): lax.ppermute(values, axis, [(i, i ^ mask) for i in range(lax.axis_size(ax...]
    unnamed x119 -> x152, local copies, waits for them, and re-layouts: 12.5 us -> 15.1 us
    dynamic_update_slice x10 -> x12, local copies, waits for them, and re-layouts: 16.3 us -> 16.1 us  [on_device(): lax.dynamic_update_slice(expert_w, piece[:, None], (0, at, row, 0))]
  transfers between devices with their start and end apart: 97 -> 99, of which waited for: 42 -> 40; matrix products, arithmetic and copies ran while one was open for 14% -> 11% of each run, Pallas kernels for 21% -> 21%
where the time goes in v5:
time: 689 us; the launch traced here: 685 us
  waiting for transfers between devices  317 us (46%)
  Pallas kernels  142 us (21%)
  starting transfers between devices  101 us (15%)
  other arithmetic  57.6 us (8%)
  local copies, waits for them, and re-layouts  50.3 us (7%)
  matrix products  10.6 us (2%)
    ppermute x99, waiting for transfers between devices, swap(): lax.ppermute(values, axis, [(i, i ^ mask) for i in range(lax.axis_size(ax...  317 us
    pallas_call x11, Pallas kernels, kernel_call(): pl.pallas_call(body, out_shape=out_shape, in_specs=specs, out_specs=jax.t...  122 us
    ppermute x99, starting transfers between devices, swap(): lax.ppermute(values, axis, [(i, i ^ mask) for i in range(lax.axis_size(ax...  101 us
    pallas_call x1, Pallas kernels, on_device(): pl.pallas_call(functools.partial(expert_weight_grads, HOPS, HOPS), grid=(...  19.7 us
    dynamic_update_slice x12, local copies, waits for them, and re-layouts, on_device(): lax.dynamic_update_slice(expert_w, piece[:, None], (0, at, row, 0))  16.1 us
    unnamed x152, local copies, waits for them, and re-layouts  15.1 us
  transfers between devices with their start and end apart: 99, of which 40 were waited for; matrix products, arithmetic and copies ran while one was open for 11% of the time, Pallas kernels for 21%

profile of v5, /device:TPU:0, one launch (start us, length us, event | category | flops | bytes accessed | tf_op | source)
XLA Modules:
  0.0 684.5 jit_solution(6519254871381136315)
XLA Ops:
  24.3 12.5 %collective-permute-done.3 = bf16[1,1,4,1,32,2176]{5,4,3,2,1,0:T(8,128)(2,1)} collective-permute-done((bf16[1,1,4,1,32,2176]{5,4,3,2,1,0:T(8,128)(2,1)}, bf16[1,1,4,1,32,2176]{5,4,3,2,1,0:T(8,128)(2,1)}, u32[]{:S(2)}, u32[]{:S(2)}) %collective-permute-start.3) | collective-permute-done | bytes 557088 | tf_op jit(solution)/shard_map/ppermute | solution.py:40
  49.3 11.8 %collective-permute-done.7 = bf16[2,128,1024]{2,1,0:T(8,128)(2,1)} collective-permute-done((bf16[2,128,1024]{2,1,0:T(8,128)(2,1)}, bf16[2,128,1024]{2,1,0:T(8,128)(2,1)}, u32[]{:S(2)}, u32[]{:S(2)}) %collective-permute-start.7) | collective-permute-done | bytes 524320 | tf_op jit(solution)/shard_map/ppermute | solution.py:40
  114.7 9.6 %shard_map.237 = (bf16[256,2048]{1,0:T(8,128)(2,1)}, bf16[256,1024]{1,0:T(8,128)(2,1)}) custom-call(s32[1]{0:T(128)} %copy.89.length_ref, f32[256,2048]{1,0:T(8,128)} %fusion.qkv_ref, f32[256,128]{1,0:T(8,128)} %get-tuple-element.325.cos_ref, f32[256,128]{1,0:T(8,128)} %get-tuple-element.326.sin_ref), custom_call_target="tpu_custom_call" | custom-call | tf_op jit(solution)/shard_map/pallas_call | solution.py:59
  124.4 15.4 %collective-permute-done.18 = bf16[2,64,1024]{2,1,0:T(8,128)(2,1)S(1)} collective-permute-done((bf16[2,64,1024]{2,1,0:T(8,128)(2,1)S(1)}, bf16[2,64,1024]{2,1,0:T(8,128)(2,1)S(1)}, u32[]{:S(2)}, u32[]{:S(2)}) %collective-permute-start.18) | collective-permute-done | bytes 262176 | tf_op jit(solution)/shard_map/ppermute | solution.py:40
  162.0 10.6 %collective-permute-done.31.refs_0_ = bf16[272,1024]{1,0:T(8,128)(2,1)S(1)} collective-permute-done((bf16[272,1024]{1,0:T(8,128)(2,1)S(1)}, bf16[272,1024]{1,0:T(8,128)(2,1)S(1)}, u32[]{:S(2)}, u32[]{:S(2)}) %collective-permute-start.31) | collective-permute-done | bytes 557088 | tf_op jit(solution)/shard_map/ppermute | solution.py:40
  178.9 19.2 %collective-permute-done.21.refs_0_ = bf16[272,1024]{1,0:T(8,128)(2,1)S(1)} collective-permute-done((bf16[272,1024]{1,0:T(8,128)(2,1)S(1)}, bf16[272,1024]{1,0:T(8,128)(2,1)S(1)}, u32[]{:S(2)}, u32[]{:S(2)}) %collective-permute-start.21) | collective-permute-done | bytes 557088 | tf_op jit(solution)/shard_map/ppermute | solution.py:40
  202.3 9.3 %shard_map.238 = (bf16[2,256,1024]{2,1,0:T(8,128)(2,1)}, bf16[2,256,1024]{2,1,0:T(8,128)(2,1)}) custom-call(s32[1]{0:T(128)} %bitcast.8.first_ref, bf16[2,8,192,1024]{3,2,1,0:T(8,128)(2,1)} %bitcast_dynamic-update-slice_fusion.7.weights_ref, bf16[272,1024]{1,0:T(8,128)(2,1)} %copy-done.6, bf16[272,1024]{1,0:T(8,128)(2,1)} %copy-done.25, ...), custom_call_target="tpu_custom_call" | custom-call | tf_op jit(solution)/shard_map/pallas_call | solution.py:59
  214.8 9.1 %shard_map.239 = (bf16[2,256,1024]{2,1,0:T(8,128)(2,1)}, bf16[2,256,1024]{2,1,0:T(8,128)(2,1)}) custom-call(s32[1]{0:T(128)} %bitcast.8.first_ref, bf16[2,8,192,1024]{3,2,1,0:T(8,128)(2,1)} %bitcast_dynamic-update-slice_fusion.7.weights_ref, bf16[272,1024]{1,0:T(8,128)(2,1)} %copy-done.16, bf16[272,1024]{1,0:T(8,128)(2,1)} %copy-done.26, ...), custom_call_target="tpu_custom_call" | custom-call | tf_op jit(solution)/shard_map/pallas_call | solution.py:59
  225.9 13.0 %collective-permute-done.38.refs_2_ = bf16[272,1024]{1,0:T(8,128)(2,1)S(1)} collective-permute-done((bf16[272,1024]{1,0:T(8,128)(2,1)S(1)}, bf16[272,1024]{1,0:T(8,128)(2,1)S(1)}, u32[]{:S(2)}, u32[]{:S(2)}) %collective-permute-start.38) | collective-permute-done | bytes 557088 | tf_op jit(solution)/shard_map/ppermute | solution.py:40
  240.6 9.5 %shard_map.240 = (bf16[2,256,1024]{2,1,0:T(8,128)(2,1)}, bf16[2,256,1024]{2,1,0:T(8,128)(2,1)}) custom-call(s32[1]{0:T(128)} %bitcast.8.first_ref, bf16[2,8,192,1024]{3,2,1,0:T(8,128)(2,1)} %bitcast_dynamic-update-slice_fusion.7.weights_ref, bf16[272,1024]{1,0:T(8,128)(2,1)} %copy-done.15, bf16[272,1024]{1,0:T(8,128)(2,1)} %copy-done.23, ...), custom_call_target="tpu_custom_call" | custom-call | tf_op jit(solution)/shard_map/pallas_call | solution.py:59
  254.3 12.5 %collective-permute-done.28 = bf16[256,1024]{1,0:T(8,128)(2,1)S(1)} collective-permute-done((bf16[256,1024]{1,0:T(8,128)(2,1)S(1)}, bf16[256,1024]{1,0:T(8,128)(2,1)S(1)}, u32[]{:S(2)}, u32[]{:S(2)}) %collective-permute-start.28) | collective-permute-done | bytes 524320 | tf_op jit(solution)/shard_map/ppermute | solution.py:40
  266.8 10.3 %collective-permute-done.36 = bf16[256,1024]{1,0:T(8,128)(2,1)S(1)} collective-permute-done((bf16[256,1024]{1,0:T(8,128)(2,1)S(1)}, bf16[256,1024]{1,0:T(8,128)(2,1)S(1)}, u32[]{:S(2)}, u32[]{:S(2)}) %collective-permute-start.36) | collective-permute-done | bytes 524320 | tf_op jit(solution)/shard_map/ppermute | solution.py:40
  279.6 9.1 %shard_map.241 = (bf16[2,256,1024]{2,1,0:T(8,128)(2,1)}, bf16[2,256,1024]{2,1,0:T(8,128)(2,1)}) custom-call(s32[1]{0:T(128)} %bitcast.8.first_ref, bf16[2,8,192,1024]{3,2,1,0:T(8,128)(2,1)} %bitcast_dynamic-update-slice_fusion.7.weights_ref, bf16[272,1024]{1,0:T(8,128)(2,1)} %copy-done.14, bf16[272,1024]{1,0:T(8,128)(2,1)} %copy-done.19, ...), custom_call_target="tpu_custom_call" | custom-call | tf_op jit(solution)/shard_map/pallas_call | solution.py:59
  293.3 11.5 %collective-permute-done.42 = bf16[256,1024]{1,0:T(8,128)(2,1)S(1)} collective-permute-done((bf16[256,1024]{1,0:T(8,128)(2,1)S(1)}, bf16[256,1024]{1,0:T(8,128)(2,1)S(1)}, u32[]{:S(2)}, u32[]{:S(2)}) %collective-permute-start.42) | collective-permute-done | bytes 524320 | tf_op jit(solution)/shard_map/ppermute | solution.py:40
  307.0 8.6 %collective-permute-done.47 = bf16[256,1024]{1,0:T(8,128)(2,1)S(1)} collective-permute-done((bf16[256,1024]{1,0:T(8,128)(2,1)S(1)}, bf16[256,1024]{1,0:T(8,128)(2,1)S(1)}, u32[]{:S(2)}, u32[]{:S(2)}) %collective-permute-start.47) | collective-permute-done | bytes 524320 | tf_op jit(solution)/shard_map/ppermute | solution.py:40
  318.6 24.3 %collective-permute-done.43 = bf16[256,1024]{1,0:T(8,128)(2,1)} collective-permute-done((bf16[256,1024]{1,0:T(8,128)(2,1)}, bf16[256,1024]{1,0:T(8,128)(2,1)}, u32[]{:S(2)}, u32[]{:S(2)}) %collective-permute-start.43) | collective-permute-done | bytes 524320 | tf_op jit(solution)/shard_map/ppermute | solution.py:40
  345.6 11.8 %collective-permute-start.62 = (bf16[256,1024]{1,0:T(8,128)(2,1)S(1)}, bf16[256,1024]{1,0:T(8,128)(2,1)S(1)}, u32[]{:S(2)}, u32[]{:S(2)}) collective-permute-start(bf16[256,1024]{1,0:T(8,128)(2,1)S(1)} %get-tuple-element.282.refs_4_), channel_id=1, source_target_pairs={{0,2},{1,3},{2,0},{3,1},{4,6},{5,7},{6,4},{7,5},{8,10},{9,11},{10,... | collective-permute-start | bytes 1572872 | tf_op jit(solution)/shard_map/ppermute | solution.py:40
  359.2 19.4 %collective-permute-done.62.refs_4_ = bf16[256,1024]{1,0:T(8,128)(2,1)S(1)} collective-permute-done((bf16[256,1024]{1,0:T(8,128)(2,1)S(1)}, bf16[256,1024]{1,0:T(8,128)(2,1)S(1)}, u32[]{:S(2)}, u32[]{:S(2)}) %collective-permute-start.62) | collective-permute-done | bytes 524320 | tf_op jit(solution)/shard_map/ppermute | solution.py:40
  396.1 13.5 %shard_map.242 = (bf16[2,272,1024]{2,1,0:T(8,128)(2,1)}, bf16[2,272,1024]{2,1,0:T(8,128)(2,1)}, bf16[2,384,1024]{2,1,0:T(8,128)(2,1)}, bf16[2,384,1024]{2,1,0:T(...) custom-call(s32[1]{0:T(128)} %bitcast.8.first_ref, ...), custom_call_target="tpu_custom_call" | custom-call | tf_op jit(solution)/shard_map/pallas_call | solution.py:59
  412.1 13.3 %shard_map.243 = (bf16[2,272,1024]{2,1,0:T(8,128)(2,1)}, bf16[2,272,1024]{2,1,0:T(8,128)(2,1)}, bf16[2,384,1024]{2,1,0:T(8,128)(2,1)}, bf16[2,384,1024]{2,1,0:T(...) custom-call(s32[1]{0:T(128)} %bitcast.8.first_ref, ...), custom_call_target="tpu_custom_call" | custom-call | tf_op jit(solution)/shard_map/pallas_call | solution.py:59
  432.7 10.0 %collective-permute-done.69.refs_6_ = bf16[256,1024]{1,0:T(8,128)(2,1)S(1)} collective-permute-done((bf16[256,1024]{1,0:T(8,128)(2,1)S(1)}, bf16[256,1024]{1,0:T(8,128)(2,1)S(1)}, u32[]{:S(2)}, u32[]{:S(2)}) %collective-permute-start.69) | collective-permute-done | bytes 524320 | tf_op jit(solution)/shard_map/ppermute | solution.py:40
  444.2 13.6 %shard_map.244 = (bf16[2,272,1024]{2,1,0:T(8,128)(2,1)}, bf16[2,272,1024]{2,1,0:T(8,128)(2,1)}, bf16[2,384,1024]{2,1,0:T(8,128)(2,1)}, bf16[2,384,1024]{2,1,0:T(...) custom-call(s32[1]{0:T(128)} %bitcast.8.first_ref, ...), custom_call_target="tpu_custom_call" | custom-call | tf_op jit(solution)/shard_map/pallas_call | solution.py:59
  466.3 13.9 %shard_map.245 = (bf16[2,272,1024]{2,1,0:T(8,128)(2,1)}, bf16[2,272,1024]{2,1,0:T(8,128)(2,1)}, bf16[2,384,1024]{2,1,0:T(8,128)(2,1)}, bf16[2,384,1024]{2,1,0:T(...) custom-call(s32[1]{0:T(128)} %bitcast.8.first_ref, ...), custom_call_target="tpu_custom_call" | custom-call | tf_op jit(solution)/shard_map/pallas_call | solution.py:59
  484.3 11.7 %collective-permute-done.73 = bf16[272,1024]{1,0:T(8,128)(2,1)S(1)} collective-permute-done((bf16[272,1024]{1,0:T(8,128)(2,1)S(1)}, bf16[272,1024]{1,0:T(8,128)(2,1)S(1)}, u32[]{:S(2)}, u32[]{:S(2)}) %collective-permute-start.73) | collective-permute-done | bytes 557088 | tf_op jit(solution)/shard_map/ppermute | solution.py:40
  497.3 10.2 %collective-permute-done.78 = bf16[272,1024]{1,0:T(8,128)(2,1)S(1)} collective-permute-done((bf16[272,1024]{1,0:T(8,128)(2,1)S(1)}, bf16[272,1024]{1,0:T(8,128)(2,1)S(1)}, u32[]{:S(2)}, u32[]{:S(2)}) %collective-permute-start.78) | collective-permute-done | bytes 557088 | tf_op jit(solution)/shard_map/ppermute | solution.py:40
  511.3 19.7 %shard_map.246 = (bf16[2,192,1024]{2,1,0:T(8,128)(2,1)}, bf16[2,192,1024]{2,1,0:T(8,128)(2,1)}, bf16[2,192,1024]{2,1,0:T(8,128)(2,1)}, bf16[2,192,1024]{2,1,0:T(...) custom-call(s32[2]{0:T(128)} %pad_add_fusion.at_ref, ...), custom_call_target="tpu_custom_call" | custom-call | tf_op jit(solution)/shard_map/pallas_call | solution.py:659
  538.2 11.9 %collective-permute-done.80 = bf16[2,192,1024]{2,1,0:T(8,128)(2,1)} collective-permute-done((bf16[2,192,1024]{2,1,0:T(8,128)(2,1)}, bf16[2,192,1024]{2,1,0:T(8,128)(2,1)}, u32[]{:S(2)}, u32[]{:S(2)}) %collective-permute-start.80) | collective-permute-done | bytes 786464 | tf_op jit(solution)/shard_map/ppermute | solution.py:40
  567.5 12.4 %shard_map.247.qkv_grad_ref = bf16[256,2048]{1,0:T(8,128)(2,1)} custom-call(s32[1]{0:T(128)} %copy.89.length_ref, bf16[256,2048]{1,0:T(8,128)(2,1)} %get-tuple-element.201.rot_ref, bf16[256,1024]{1,0:T(8,128)(2,1)} %convolution_convert_fusion.1.grad_ref, f32[256,128]{1,0:T(8,128)} %get-tuple-element.325.cos_ref, f32[256,128]{1,0:T(8,128)} %get-tuple-element.326.sin_ref), custom_call_target="tpu_custom_call" | custom-call | tf_op jit(solution)/shard_map/pallas_call | solution.py:59
  584.2 8.9 %shard_map.248 = (bf16[2,256,2176]{2,1,0:T(8,128)(2,1)}, bf16[2,256,2176]{2,1,0:T(8,128)(2,1)}, f32[256,1024]{1,0:T(8,128)}) custom-call(s32[1]{0:T(128)} %bitcast.42.core_ref, bf16[256,2048]{1,0:T(8,128)(2,1)} %shard_map.247.qkv_grad_ref, bf16[256,1024]{1,0:T(8,128)(2,1)} %copy-done.29, bf16[1024,2176]{1,0:T(8,128)(2,1)} %bitcast.158, ...), custom_call_target="tpu_custom_call" | custom-call | tf_op jit(solution)/shard_map/pallas_call | solution.py:59
  612.3 16.6 %collective-permute-done.87 = bf16[1,1,4,1,32,1024]{5,4,3,2,1,0:T(8,128)(2,1)S(1)} collective-permute-done((bf16[1,1,4,1,32,1024]{5,4,3,2,1,0:T(8,128)(2,1)S(1)}, bf16[1,1,4,1,32,1024]{5,4,3,2,1,0:T(8,128)(2,1)S(1)}, u32[]{:S(2)}, u32[]{:S(2)}) %collective-permute-start.87) | collective-permute-done | bytes 262176 | tf_op jit(solution)/shard_map/ppermute | solution.py:40
  637.2 12.4 %collective-permute-done.93 = bf16[2,192,1024]{2,1,0:T(8,128)(2,1)S(1)} collective-permute-done((bf16[2,192,1024]{2,1,0:T(8,128)(2,1)S(1)}, bf16[2,192,1024]{2,1,0:T(8,128)(2,1)S(1)}, u32[]{:S(2)}, u32[]{:S(2)}) %collective-permute-start.93) | collective-permute-done | bytes 786464 | tf_op jit(solution)/shard_map/ppermute | solution.py:40
  657.9 9.0 %collective-permute-done.95 = bf16[2,192,1024]{2,1,0:T(8,128)(2,1)S(1)} collective-permute-done((bf16[2,192,1024]{2,1,0:T(8,128)(2,1)S(1)}, bf16[2,192,1024]{2,1,0:T(8,128)(2,1)S(1)}, u32[]{:S(2)}, u32[]{:S(2)}) %collective-permute-start.95) | collective-permute-done | bytes 786464 | tf_op jit(solution)/shard_map/ppermute | solution.py:40
  (458 shorter events, 273.9 us)
Async XLA Ops:
  44.5 25.1 %collective-permute-start.6 = (bf16[2,1,4,1,32,2176]{5,4,3,2,1,0:T(8,128)(2,1)}, bf16[2,1,4,1,32,2176]{5,4,3,2,1,0:T(8,128)(2,1)}, u32[]{:S(2)}, u32[]{:S(2)}) collective-permute-start(bf16[2,1,4,1,32,2176]{5,4,3,2,1,0:T(8,128)(2,1)} %maximum_select_fusion.3), channel_id=1, source_target_pairs={{0,1},{1,0},{2,3},{3,2},{4,5},{5,4},{6,7},{7,6},{8,9},{9,8},{10,11... | collective-permute-start | bytes 3342344 | tf_op jit(solution)/shard_map/ppermute | solution.py:40
  110.4 29.4 %collective-permute-start.16 = (bf16[2,1,4,1,32,1024]{5,4,3,2,1,0:T(8,128)(2,1)S(1)}, bf16[2,1,4,1,32,1024]{5,4,3,2,1,0:T(8,128)(2,1)S(1)}, u32[]{:S(2)}, u32[]{:S(2)}) collective-permute-start(bf16[2,1,4,1,32,1024]{5,4,3,2,1,0:T(8,128)(2,1)S(1)} %maximum_select_fusion.5), channel_id=1, source_target_pairs={{0,1},{1,0},{2,3},{3,2},{4,5},{5,4},{6,7},{7,6},{8,9},{9,8},{10,11... | collective-permute-start | bytes 1572872 | tf_op jit(solution)/shard_map/ppermute | solution.py:40
  111.2 28.7 %collective-permute-start.17 = (bf16[2,128,1024]{2,1,0:T(8,128)(2,1)S(1)}, bf16[2,128,1024]{2,1,0:T(8,128)(2,1)S(1)}, u32[]{:S(2)}, u32[]{:S(2)}) collective-permute-start(bf16[2,128,1024]{2,1,0:T(8,128)(2,1)S(1)} %copy-done.53), channel_id=1, source_target_pairs={{0,4},{1,5},{2,6},{3,7},{4,0},{5,1},{6,2},{7,3},{8,12},{9,13},{10,... | collective-permute-start | bytes 1572872 | tf_op jit(solution)/shard_map/ppermute | solution.py:40
  111.2 28.7 %collective-permute-start.19 = (bf16[2,128,1024]{2,1,0:T(8,128)(2,1)}, bf16[2,128,1024]{2,1,0:T(8,128)(2,1)S(1)}, u32[]{:S(2)}, u32[]{:S(2)}) collective-permute-start(bf16[2,128,1024]{2,1,0:T(8,128)(2,1)} %collective-permute-done.7), channel_id=1, source_target_pairs={{0,1},{1,0},{2,3},{3,2},{4,5},{5,4},{6,7},{7,6},{8,9},{9,8},{10,11... | collective-permute-start | bytes 1572872 | tf_op jit(solution)/shard_map/ppermute | solution.py:40
  112.6 27.3 %collective-permute-start.18 = (bf16[2,64,1024]{2,1,0:T(8,128)(2,1)S(1)}, bf16[2,64,1024]{2,1,0:T(8,128)(2,1)S(1)}, u32[]{:S(2)}, u32[]{:S(2)}) collective-permute-start(bf16[2,64,1024]{2,1,0:T(8,128)(2,1)S(1)} %collective-permute-done.12), channel_id=1, source_target_pairs={{0,1},{1,0},{2,3},{3,2},{4,5},{5,4},{6,7},{7,6},{8,9},{9,8},{10,11... | collective-permute-start | bytes 786440 | tf_op jit(solution)/shard_map/ppermute | solution.py:40
  157.7 40.3 %collective-permute-start.21 = (bf16[272,1024]{1,0:T(8,128)(2,1)S(1)}, bf16[272,1024]{1,0:T(8,128)(2,1)S(1)}, u32[]{:S(2)}, u32[]{:S(2)}) collective-permute-start(bf16[272,1024]{1,0:T(8,128)(2,1)S(1)} %pad_maximum_fusion.2.refs_0_), channel_id=1, source_target_pairs={{0,4},{1,5},{2,6},{3,7},{4,0},{5,1},{6,2},{7,3},{8,12},{9,13},{10,... | collective-permute-start | bytes 1671176 | tf_op jit(solution)/shard_map/ppermute | solution.py:40
  162.0 36.1 %collective-permute-start.24 = (bf16[272,1024]{1,0:T(8,128)(2,1)S(1)}, bf16[272,1024]{1,0:T(8,128)(2,1)S(1)}, u32[]{:S(2)}, u32[]{:S(2)}) collective-permute-start(bf16[272,1024]{1,0:T(8,128)(2,1)S(1)} %pad_maximum_fusion.2.refs_0_), channel_id=1, source_target_pairs={{0,8},{8,0},{16,24},{24,16},{1,9},{9,1},{17,25},{25,17},{2,10},{10... | collective-permute-start | bytes 1671176 | tf_op jit(solution)/shard_map/ppermute | solution.py:40
  172.6 27.1 %collective-permute-start.33 = (bf16[272,1024]{1,0:T(8,128)(2,1)S(1)}, bf16[272,1024]{1,0:T(8,128)(2,1)S(1)}, u32[]{:S(2)}, u32[]{:S(2)}) collective-permute-start(bf16[272,1024]{1,0:T(8,128)(2,1)S(1)} %collective-permute-done.31.refs_0_), channel_id=1, source_target_pairs={{0,16},{8,24},{16,0},{24,8},{1,17},{9,25},{17,1},{25,9},{2,18},{10... | collective-permute-start | bytes 1671176 | tf_op jit(solution)/shard_map/ppermute | solution.py:40
  176.3 25.1 %collective-permute-start.26 = (bf16[272,1024]{1,0:T(8,128)(2,1)S(1)}, bf16[272,1024]{1,0:T(8,128)(2,1)S(1)}, u32[]{:S(2)}, u32[]{:S(2)}) collective-permute-start(bf16[272,1024]{1,0:T(8,128)(2,1)S(1)} %collective-permute-done.25.refs_2_), channel_id=1, source_target_pairs={{0,8},{8,0},{16,24},{24,16},{1,9},{9,1},{17,25},{25,17},{2,10},{10... | collective-permute-start | bytes 1671176 | tf_op jit(solution)/shard_map/ppermute | solution.py:40
  177.1 34.8 %collective-permute-start.30 = (bf16[272,1024]{1,0:T(8,128)(2,1)S(1)}, bf16[272,1024]{1,0:T(8,128)(2,1)S(1)}, u32[]{:S(2)}, u32[]{:S(2)}) collective-permute-start(bf16[272,1024]{1,0:T(8,128)(2,1)S(1)} %pad_maximum_fusion.2.refs_0_), channel_id=1, source_target_pairs={{0,6},{1,7},{2,4},{3,5},{4,2},{5,3},{6,0},{7,1},{8,14},{9,15},{10,... | collective-permute-start | bytes 1671176 | tf_op jit(solution)/shard_map/ppermute | solution.py:40
  211.6 38.9 %collective-permute-start.27 = (bf16[2,256,1024]{2,1,0:T(8,128)(2,1)}, bf16[2,256,1024]{2,1,0:T(8,128)(2,1)}, u32[]{:S(2)}, u32[]{:S(2)}) collective-permute-start(bf16[2,256,1024]{2,1,0:T(8,128)(2,1)} %get-tuple-element.190), channel_id=1, source_target_pairs={{0,8},{8,0},{16,24},{24,16},{1,9},{9,1},{17,25},{25,17},{2,10},{10... | collective-permute-start | bytes 3145736 | tf_op jit(solution)/shard_map/ppermute | solution.py:40
  223.9 29.7 %collective-permute-start.35 = (bf16[2,256,1024]{2,1,0:T(8,128)(2,1)}, bf16[2,256,1024]{2,1,0:T(8,128)(2,1)S(1)}, u32[]{:S(2)}, u32[]{:S(2)}) collective-permute-start(bf16[2,256,1024]{2,1,0:T(8,128)(2,1)} %get-tuple-element.193), channel_id=1, source_target_pairs={{0,8},{8,0},{16,24},{24,16},{1,9},{9,1},{17,25},{25,17},{2,10},{10... | collective-permute-start | bytes 3145736 | tf_op jit(solution)/shard_map/ppermute | solution.py:40
  238.9 39.0 %collective-permute-start.44 = (bf16[272,1024]{1,0:T(8,128)(2,1)S(1)}, bf16[272,1024]{1,0:T(8,128)(2,1)S(1)}, u32[]{:S(2)}, u32[]{:S(2)}) collective-permute-start(bf16[272,1024]{1,0:T(8,128)(2,1)S(1)} %collective-permute-done.30.refs_0_), channel_id=1, source_target_pairs={{0,8},{8,0},{16,24},{24,16},{1,9},{9,1},{17,25},{25,17},{2,10},{10... | collective-permute-start | bytes 1671176 | tf_op jit(solution)/shard_map/ppermute | solution.py:40
  239.0 39.0 %collective-permute-start.45 = (bf16[272,1024]{1,0:T(8,128)(2,1)S(1)}, bf16[272,1024]{1,0:T(8,128)(2,1)S(1)}, u32[]{:S(2)}, u32[]{:S(2)}) collective-permute-start(bf16[272,1024]{1,0:T(8,128)(2,1)S(1)} %collective-permute-done.38.refs_2_), channel_id=1, source_target_pairs={{0,8},{8,0},{16,24},{24,16},{1,9},{9,1},{17,25},{25,17},{2,10},{10... | collective-permute-start | bytes 1671176 | tf_op jit(solution)/shard_map/ppermute | solution.py:40
  250.1 38.6 %collective-permute-start.41 = (bf16[2,256,1024]{2,1,0:T(8,128)(2,1)}, bf16[2,256,1024]{2,1,0:T(8,128)(2,1)}, u32[]{:S(2)}, u32[]{:S(2)}) collective-permute-start(bf16[2,256,1024]{2,1,0:T(8,128)(2,1)} %get-tuple-element.196), channel_id=1, source_target_pairs={{0,8},{8,0},{16,24},{24,16},{1,9},{9,1},{17,25},{25,17},{2,10},{10... | collective-permute-start | bytes 3145736 | tf_op jit(solution)/shard_map/ppermute | solution.py:40
  307.0 36.0 %collective-permute-start.43 = (bf16[256,1024]{1,0:T(8,128)(2,1)}, bf16[256,1024]{1,0:T(8,128)(2,1)}, u32[]{:S(2)}, u32[]{:S(2)}) collective-permute-start(bf16[256,1024]{1,0:T(8,128)(2,1)} %add_convert_fusion.9), channel_id=1, source_target_pairs={{0,4},{1,5},{2,6},{3,7},{4,0},{5,1},{6,2},{7,3},{8,12},{9,13},{10,... | collective-permute-start | bytes 1572872 | tf_op jit(solution)/shard_map/ppermute | solution.py:40
  315.8 27.2 %collective-permute-start.48 = (bf16[256,1024]{1,0:T(8,128)(2,1)S(1)}, bf16[256,1024]{1,0:T(8,128)(2,1)}, u32[]{:S(2)}, u32[]{:S(2)}) collective-permute-start(bf16[256,1024]{1,0:T(8,128)(2,1)S(1)} %fusion.10), channel_id=1, source_target_pairs={{0,6},{1,7},{2,4},{3,5},{4,2},{5,3},{6,0},{7,1},{8,14},{9,15},{10,... | collective-permute-start | bytes 1572872 | tf_op jit(solution)/shard_map/ppermute | solution.py:40
  345.6 33.0 %collective-permute-start.62 = (bf16[256,1024]{1,0:T(8,128)(2,1)S(1)}, bf16[256,1024]{1,0:T(8,128)(2,1)S(1)}, u32[]{:S(2)}, u32[]{:S(2)}) collective-permute-start(bf16[256,1024]{1,0:T(8,128)(2,1)S(1)} %get-tuple-element.282.refs_4_), channel_id=1, source_target_pairs={{0,2},{1,3},{2,0},{3,1},{4,6},{5,7},{6,4},{7,5},{8,10},{9,11},{10,... | collective-permute-start | bytes 1572872 | tf_op jit(solution)/shard_map/ppermute | solution.py:40
  358.9 26.6 %collective-permute-start.54 = (bf16[256,1024]{1,0:T(8,128)(2,1)S(1)}, bf16[256,1024]{1,0:T(8,128)(2,1)S(1)}, u32[]{:S(2)}, u32[]{:S(2)}) collective-permute-start(bf16[256,1024]{1,0:T(8,128)(2,1)S(1)} %get-tuple-element.282.refs_4_), channel_id=1, source_target_pairs={{0,4},{1,5},{2,6},{3,7},{4,0},{5,1},{6,2},{7,3},{8,12},{9,13},{10,... | collective-permute-start | bytes 1572872 | tf_op jit(solution)/shard_map/ppermute | solution.py:40
  359.2 26.6 %collective-permute-start.55 = (bf16[256,1024]{1,0:T(8,128)(2,1)S(1)}, bf16[256,1024]{1,0:T(8,128)(2,1)S(1)}, u32[]{:S(2)}, u32[]{:S(2)}) collective-permute-start(bf16[256,1024]{1,0:T(8,128)(2,1)S(1)} %get-tuple-element.282.refs_4_), channel_id=1, source_target_pairs={{0,8},{8,0},{16,24},{24,16},{1,9},{9,1},{17,25},{25,17},{2,10},{10... | collective-permute-start | bytes 1572872 | tf_op jit(solution)/shard_map/ppermute | solution.py:40
  381.2 29.3 %collective-permute-start.61 = (bf16[256,1024]{1,0:T(8,128)(2,1)S(1)}, bf16[256,1024]{1,0:T(8,128)(2,1)S(1)}, u32[]{:S(2)}, u32[]{:S(2)}) collective-permute-start(bf16[256,1024]{1,0:T(8,128)(2,1)S(1)} %get-tuple-element.282.refs_4_), channel_id=1, source_target_pairs={{0,6},{1,7},{2,4},{3,5},{4,2},{5,3},{6,0},{7,1},{8,14},{9,15},{10,... | collective-permute-start | bytes 1572872 | tf_op jit(solution)/shard_map/ppermute | solution.py:40
  385.4 25.1 %collective-permute-start.60 = (bf16[256,1024]{1,0:T(8,128)(2,1)S(1)}, bf16[256,1024]{1,0:T(8,128)(2,1)}, u32[]{:S(2)}, u32[]{:S(2)}) collective-permute-start(bf16[256,1024]{1,0:T(8,128)(2,1)S(1)} %collective-permute-done.54.refs_4_), channel_id=1, source_target_pairs={{0,16},{8,24},{16,0},{24,8},{1,17},{9,25},{17,1},{25,9},{2,18},{10... | collective-permute-start | bytes 1572872 | tf_op jit(solution)/shard_map/ppermute | solution.py:40
  428.7 32.9 %collective-permute-start.59 = (bf16[272,1024]{1,0:T(8,128)(2,1)S(1)}, bf16[272,1024]{1,0:T(8,128)(2,1)S(1)}, u32[]{:S(2)}, u32[]{:S(2)}) collective-permute-start(bf16[272,1024]{1,0:T(8,128)(2,1)S(1)} %fusion.12), channel_id=1, source_target_pairs={{0,16},{8,24},{16,0},{24,8},{1,17},{9,25},{17,1},{25,9},{2,18},{10... | collective-permute-start | bytes 1671176 | tf_op jit(solution)/shard_map/ppermute | solution.py:40
  432.0 33.5 %collective-permute-start.67 = (bf16[272,1024]{1,0:T(8,128)(2,1)S(1)}, bf16[272,1024]{1,0:T(8,128)(2,1)S(1)}, u32[]{:S(2)}, u32[]{:S(2)}) collective-permute-start(bf16[272,1024]{1,0:T(8,128)(2,1)S(1)} %fusion.13), channel_id=1, source_target_pairs={{0,16},{8,24},{16,0},{24,8},{1,17},{9,25},{17,1},{25,9},{2,18},{10... | collective-permute-start | bytes 1671176 | tf_op jit(solution)/shard_map/ppermute | solution.py:40
  497.1 39.5 %collective-permute-start.74 = (bf16[272,1024]{1,0:T(8,128)(2,1)}, bf16[272,1024]{1,0:T(8,128)(2,1)}, u32[]{:S(2)}, u32[]{:S(2)}) collective-permute-start(bf16[272,1024]{1,0:T(8,128)(2,1)} %add_convert_fusion.4), channel_id=1, source_target_pairs={{0,4},{1,5},{2,6},{3,7},{4,0},{5,1},{6,2},{7,3},{8,12},{9,13},{10,... | collective-permute-start | bytes 1671176 | tf_op jit(solution)/shard_map/ppermute | solution.py:40
  508.6 28.0 %collective-permute-start.79 = (bf16[272,1024]{1,0:T(8,128)(2,1)}, bf16[272,1024]{1,0:T(8,128)(2,1)}, u32[]{:S(2)}, u32[]{:S(2)}) collective-permute-start(bf16[272,1024]{1,0:T(8,128)(2,1)} %fusion.7), channel_id=1, source_target_pairs={{0,6},{1,7},{2,4},{3,5},{4,2},{5,3},{6,0},{7,1},{8,14},{9,15},{10,... | collective-permute-start | bytes 1671176 | tf_op jit(solution)/shard_map/ppermute | solution.py:40
  560.3 34.6 %collective-permute-start.84 = (bf16[2,192,1024]{2,1,0:T(8,128)(2,1)}, bf16[2,192,1024]{2,1,0:T(8,128)(2,1)}, u32[]{:S(2)}, u32[]{:S(2)}) collective-permute-start(bf16[2,192,1024]{2,1,0:T(8,128)(2,1)} %get-tuple-element.248), channel_id=1, source_target_pairs={{0,1},{1,0},{2,3},{3,2},{4,5},{5,4},{6,7},{7,6},{8,9},{9,8},{10,11... | collective-permute-start | bytes 2359304 | tf_op jit(solution)/shard_map/ppermute | solution.py:40
  564.2 30.6 %collective-permute-start.85 = (bf16[2,192,1024]{2,1,0:T(8,128)(2,1)}, bf16[2,192,1024]{2,1,0:T(8,128)(2,1)}, u32[]{:S(2)}, u32[]{:S(2)}) collective-permute-start(bf16[2,192,1024]{2,1,0:T(8,128)(2,1)} %add_convert_fusion.2), channel_id=1, source_target_pairs={{0,6},{1,7},{2,4},{3,5},{4,2},{5,3},{6,0},{7,1},{8,14},{9,15},{10,... | collective-permute-start | bytes 2359304 | tf_op jit(solution)/shard_map/ppermute | solution.py:40
  596.1 32.8 %collective-permute-start.86 = (bf16[2,1,4,2,32,2176]{5,4,3,2,1,0:T(8,128)(2,1)}, bf16[2,1,4,2,32,2176]{5,4,3,2,1,0:T(8,128)(2,1)S(1)}, u32[]{:S(2)}, u32[]{:S(2)}) collective-permute-start(bf16[2,1,4,2,32,2176]{5,4,3,2,1,0:T(8,128)(2,1)} %bitcast.174), channel_id=1, source_target_pairs={{0,8},{8,0},{16,24},{24,16},{1,9},{9,1},{17,25},{25,17},{2,10},{10... | collective-permute-start | bytes 6684680 | tf_op jit(solution)/shard_map/ppermute | solution.py:40
  603.9 31.1 %collective-permute-start.92 = (bf16[2,192,1024]{2,1,0:T(8,128)(2,1)}, bf16[2,192,1024]{2,1,0:T(8,128)(2,1)S(1)}, u32[]{:S(2)}, u32[]{:S(2)}) collective-permute-start(bf16[2,192,1024]{2,1,0:T(8,128)(2,1)} %get-tuple-element.259), channel_id=1, source_target_pairs={{0,1},{1,0},{2,3},{3,2},{4,5},{5,4},{6,7},{7,6},{8,9},{9,8},{10,11... | collective-permute-start | bytes 2359304 | tf_op jit(solution)/shard_map/ppermute | solution.py:40
  608.8 40.7 %collective-permute-start.93 = (bf16[2,192,1024]{2,1,0:T(8,128)(2,1)S(1)}, bf16[2,192,1024]{2,1,0:T(8,128)(2,1)S(1)}, u32[]{:S(2)}, u32[]{:S(2)}) collective-permute-start(bf16[2,192,1024]{2,1,0:T(8,128)(2,1)S(1)} %add_convert_fusion.1), channel_id=1, source_target_pairs={{0,4},{1,5},{2,6},{3,7},{4,0},{5,1},{6,2},{7,3},{8,12},{9,13},{10,... | collective-permute-start | bytes 2359304 | tf_op jit(solution)/shard_map/ppermute | solution.py:40
  629.5 25.3 %collective-permute-start.88 = (bf16[1,1,4,2,32,2176]{5,4,3,2,1,0:T(8,128)(2,1)S(1)}, bf16[1,1,4,2,32,2176]{5,4,3,2,1,0:T(8,128)(2,1)S(1)}, u32[]{:S(2)}, u32[]{:S(2)}) collective-permute-start(bf16[1,1,4,2,32,2176]{5,4,3,2,1,0:T(8,128)(2,1)S(1)} %dynamic-slice_convert_fusion), channel_id=1, source_target_pairs={{0,16},{8,24},{16,0},{24,8},{1,17},{9,25},{17,1},{25,9},{2,18},{10... | collective-permute-start | bytes 3342344 | tf_op jit(solution)/shard_map/ppermute | solution.py:40
  (143 other events, 1896.2 us)

commit v6 on v5

--- a/solution.py
+++ b/solution.py
@@ -11,7 +11,8 @@
 KV_HEADS = 8
 HEAD_DIM = 64
 CAP = 96
-HOPS = 4
+HOPS = 2
+HOP_BIT = 2
 CORES = 2
 
 epsilon = 1e-06
@@ -63,6 +64,31 @@
         out_specs=jax.tree.map(lambda _: vmem(), out_shape),
         scratch_shapes=scratch,
         compiler_params=pltpu.CompilerParams(vmem_limit_bytes=56 * 1024 * 1024),
+    )(*operands)
+
+
+def expert_call(body, out_shape, operands, scratch):
+    held = operands[1].shape[0]
+
+    def spec(array):
+        if array.shape[0] != held or len(array.shape) < 3 or array.shape[1] % CAP:
+            return vmem()
+        rest = len(array.shape) - 1
+        return pl.BlockSpec((1, *array.shape[1:]), lambda e: (e,) + (0,) * rest)
+
+    weights = operands[1]
+    return pl.pallas_call(
+        body,
+        grid=(held,),
+        out_shape=out_shape,
+        in_specs=[
+            smem(),
+            pl.BlockSpec((1, *weights.shape[1:]), lambda e: (e, 0, 0, 0)),
+            *[vmem() for _ in operands[2:]],
+        ],
+        out_specs=tuple(spec(array) for array in out_shape),
+        scratch_shapes=scratch,
+        compiler_params=pltpu.CompilerParams(vmem_limit_bytes=58 * 1024 * 1024),
     )(*operands)
 
 
@@ -190,11 +216,11 @@
     return match, gate_slots
 
 
-def expert_weights(weights_ref, e, split):
+def expert_weights(weights_ref, split):
     blocks = weights_ref.shape[1]
     width = weights_ref.shape[3]
-    wide = weights_ref[e, :, :split, :].reshape(blocks * split, width)
-    down = weights_ref[e, :, split:, :].reshape(-1, width)
+    wide = weights_ref[0, :, :split, :].reshape(blocks * split, width)
+    down = weights_ref[0, :, split:, :].reshape(-1, width)
     return wide, down
 
 
@@ -202,32 +228,35 @@
     token_refs = refs[:count]
     out_refs = refs[count : count + CORES]
     picked_ref, acc_ref, match_ref = refs[count + CORES :]
-    held = weights_ref.shape[0]
+    e = pl.program_id(0)
     hidden_units = weights_ref.shape[3] // 2
     split = token_refs[0].shape[1] // weights_ref.shape[1]
     rows = (token_refs[0].shape[0] - seq_len) // 2
-    for e in range(held):
-        gate_slots = []
+
+    @pl.when(e == 0)
+    def _():
+        acc_ref[...] = jnp.zeros(acc_ref.shape, f32)
+
+    gate_slots = []
+    for s in range(count):
+        match, gate = set_rows(token_refs[s], first_ref[0] + e, seq_len, rows)
+        gate_slots.append(gate)
+        match_ref[s] = match.astype(f32).astype(bf16)
+        picked_ref[s * CAP : s * CAP + CAP, :] = dot(
+            match_ref[s], token_refs[s][:seq_len, :]
+        ).astype(bf16)
+    wide_e, down_e = expert_weights(weights_ref, split)
+    pre = dot(picked_ref[...], wide_e)
+    gate_pre, up_pre = pre[:, :hidden_units], pre[:, hidden_units:]
+    inner = (gate_pre / (1.0 + jnp.exp(-gate_pre)) * up_pre).astype(bf16)
+    scaled = (dot(inner, down_e) * jnp.concatenate(gate_slots, axis=0)).astype(bf16)
+    for s in range(count):
+        acc_ref[s] = acc_ref[s] + dot_tn(match_ref[s], scaled[s * CAP : s * CAP + CAP, :])
+
+    @pl.when(e == pl.num_programs(0) - 1)
+    def _():
         for s in range(count):
-            match, gate = set_rows(token_refs[s], first_ref[0] + e, seq_len, rows)
-            gate_slots.append(gate)
-            match_ref[s] = match.astype(f32).astype(bf16)
-            picked_ref[s * CAP : s * CAP + CAP, :] = dot(
-                match_ref[s], token_refs[s][:seq_len, :]
-            ).astype(bf16)
-        wide_e, down_e = expert_weights(weights_ref, e, split)
-        pre = dot(picked_ref[...], wide_e)
-        gate_pre, up_pre = pre[:, :hidden_units], pre[:, hidden_units:]
-        inner = (gate_pre / (1.0 + jnp.exp(-gate_pre)) * up_pre).astype(bf16)
-        scaled = (dot(inner, down_e) * jnp.concatenate(gate_slots, axis=0)).astype(bf16)
-        for s in range(count):
-            part = dot_tn(match_ref[s], scaled[s * CAP : s * CAP + CAP, :])
-            if e:
-                part = acc_ref[s] + part
-            if e < held - 1:
-                acc_ref[s] = part
-            else:
-                out_refs[s % CORES][s // CORES] = part.astype(bf16)
+            out_refs[s % CORES][s // CORES] = acc_ref[s].astype(bf16)
 
 
 def expert_backward(count, seq_len, first_ref, weights_ref, *refs):
@@ -236,64 +265,65 @@
     out_refs = refs[2 * count : 2 * count + CORES]
     picked_ref, wide_grad_ref, routed_ref, inner_ref = refs[2 * count + CORES :][:4]
     acc_ref, match_ref, gate_acc_ref = refs[2 * count + CORES + 4 :]
-    held = weights_ref.shape[0]
+    e = pl.program_id(0)
     hidden_units = weights_ref.shape[3] // 2
     split = token_refs[0].shape[1] // weights_ref.shape[1]
     rows = (token_refs[0].shape[0] - seq_len) // 2
-    for e in range(held):
-        gate_slots = []
+
+    @pl.when(e == 0)
+    def _():
+        acc_ref[...] = jnp.zeros(acc_ref.shape, f32)
+        gate_acc_ref[...] = jnp.zeros(gate_acc_ref.shape, f32)
+
+    gate_slots = []
+    for s in range(count):
+        match, gate = set_rows(token_refs[s], first_ref[0] + e, seq_len, rows)
+        gate_slots.append(gate)
+        select = match.astype(f32).astype(bf16)
+        match_ref[s] = select
+        at = s * CAP
+        picked_ref[0, at : at + CAP, :] = dot(select, token_refs[s][:seq_len, :]).astype(bf16)
+        routed_ref[0, at : at + CAP, :] = dot(select, grad_refs[s][...]).astype(bf16)
+    gate_col = residual_scale * jnp.concatenate(gate_slots, axis=0)
+    wide_e, down_e = expert_weights(weights_ref, split)
+    pre = dot(picked_ref[0], wide_e)
+    gate_pre, up_pre = pre[:, :hidden_units], pre[:, hidden_units:]
+    sigmoid = 1.0 / (1.0 + jnp.exp(-gate_pre))
+    silu = gate_pre * sigmoid
+    inner = (silu * up_pre).astype(bf16)
+    inner_ref[0] = inner
+    back = dot_nt(routed_ref[0], down_e)
+    gate_grad = residual_scale * jnp.sum(inner.astype(f32) * back, axis=1, keepdims=True)
+    inner_grad = gate_col * back
+    wide_grad_ref[0, :, :hidden_units] = (
+        inner_grad * up_pre * sigmoid * (1.0 + gate_pre * (1.0 - sigmoid))
+    ).astype(bf16)
+    wide_grad_ref[0, :, hidden_units:] = (inner_grad * silu).astype(bf16)
+    routed_ref[0] = (routed_ref[0].astype(f32) * gate_col).astype(bf16)
+    arrived = dot_nt(wide_grad_ref[0], wide_e).astype(bf16)
+    for s in range(count):
+        at = s * CAP
+        match = match_ref[s]
+        gate_row = jnp.sum(
+            jnp.where(match.astype(f32) > 0.5, gate_grad[at : at + CAP, :], 0.0),
+            axis=0,
+            keepdims=True,
+        )
+        gate_acc_ref[s] = place_row_at(gate_acc_ref[s], gate_row, first_ref[0] + e)
+        acc_ref[s] = acc_ref[s] + dot_tn(match, arrived[at : at + CAP, :])
+
+    @pl.when(e == pl.num_programs(0) - 1)
+    def _():
         for s in range(count):
-            match, gate = set_rows(token_refs[s], first_ref[0] + e, seq_len, rows)
-            gate_slots.append(gate)
-            select = match.astype(f32).astype(bf16)
-            match_ref[s] = select
-            at = s * CAP
-            picked_ref[e, at : at + CAP, :] = dot(select, token_refs[s][:seq_len, :]).astype(bf16)
-            routed_ref[e, at : at + CAP, :] = dot(select, grad_refs[s][...]).astype(bf16)
-        gate_col = residual_scale * jnp.concatenate(gate_slots, axis=0)
-        wide_e, down_e = expert_weights(weights_ref, e, split)
-        pre = dot(picked_ref[e], wide_e)
-        gate_pre, up_pre = pre[:, :hidden_units], pre[:, hidden_units:]
-        sigmoid = 1.0 / (1.0 + jnp.exp(-gate_pre))
-        silu = gate_pre * sigmoid
-        inner = (silu * up_pre).astype(bf16)
-        inner_ref[e] = inner
-        back = dot_nt(routed_ref[e], down_e)
-        gate_grad = residual_scale * jnp.sum(inner.astype(f32) * back, axis=1, keepdims=True)
-        inner_grad = gate_col * back
-        wide_grad_ref[e, :, :hidden_units] = (
-            inner_grad * up_pre * sigmoid * (1.0 + gate_pre * (1.0 - sigmoid))
-        ).astype(bf16)
-        wide_grad_ref[e, :, hidden_units:] = (inner_grad * silu).astype(bf16)
-        routed_ref[e] = (routed_ref[e].astype(f32) * gate_col).astype(bf16)
-        arrived = dot_nt(wide_grad_ref[e], wide_e).astype(bf16)
-        for s in range(count):
-            at = s * CAP
-            match = match_ref[s]
-            gate_row = jnp.sum(
-                jnp.where(match.astype(f32) > 0.5, gate_grad[at : at + CAP, :], 0.0),
-                axis=0,
-                keepdims=True,
-            )
-            spread = place_row_at(
-                jnp.zeros((rows, acc_ref.shape[2]), f32) if e == 0 else gate_acc_ref[s],
-                gate_row,
-                first_ref[0] + e,
-            )
-            part = dot_tn(match, arrived[at : at + CAP, :])
-            if e:
-                part = acc_ref[s] + part
-            if e < held - 1:
-                acc_ref[s] = part
-                gate_acc_ref[s] = spread
-            else:
-                out_refs[s % CORES][s // CORES, :seq_len, :] = part.astype(bf16)
-                high = spread.astype(bf16)
-                low = (spread - high.astype(f32)).astype(bf16)
-                out_refs[s % CORES][s // CORES, seq_len:, :] = jnp.concatenate([high, low], axis=0)
-
-
-def expert_weight_grads(groups, hops, at_ref, *refs):
+            out_ref, j = out_refs[s % CORES], s // CORES
+            out_ref[j, :seq_len, :] = acc_ref[s].astype(bf16)
+            spread = gate_acc_ref[s]
+            high = spread.astype(bf16)
+            low = (spread - high.astype(f32)).astype(bf16)
+            out_ref[j, seq_len:, :] = jnp.concatenate([high, low], axis=0)
+
+
+def expert_weight_grads(groups, at_ref, *refs):
     picked = refs[:groups]
     wide_grads = refs[groups : 2 * groups]
     routed = refs[2 * groups : 3 * groups]
@@ -301,7 +331,6 @@
     out_refs = refs[4 * groups : -1]
     work_ref = refs[-1]
     blocks, _, width = work_ref.shape
-    lows = blocks // hops
     split = picked[0].shape[2] // blocks
     wide = dot_tn(picked[0][0], wide_grads[0][0])
     for k in range(1, groups):
@@ -311,10 +340,8 @@
     for k in range(1, groups):
         down = down + dot_tn(inner[k][0], routed[k][0])
     work_ref[:, split:, :] = down.astype(bf16).reshape(blocks, -1, width)
-    for k in range(hops):
-        for m in range(lows):
-            block = (at_ref[0] ^ k) * lows + (at_ref[1] ^ m)
-            out_refs[k * lows + m][0] = work_ref[block]
+    for offset in range(blocks):
+        out_refs[offset][0] = work_ref[at_ref[0] ^ offset]
 
 
 def dense_backward(
@@ -403,7 +430,7 @@
     shards = lax.axis_size("fsdp")
     owned = expert_gate.shape[0]
     experts = owned * groups
-    lows = shards // HOPS
+    units = shards // 2
     rows_y = groups // CORES
     held = owned // HOPS
     hidden_units = expert_gate.shape[2]
@@ -411,11 +438,11 @@
     kv_width = KV_HEADS * HEAD_DIM
     dp_at = lax.axis_index("dp")
     fsdp_at = lax.axis_index("fsdp")
-    hop_at, low_at = fsdp_at // lows, fsdp_at % lows
+    hop_at = fsdp_at // HOP_BIT % HOPS
     y_at, core_at = dp_at // CORES, dp_at % CORES
 
     def exchange(values, compute):
-        per_hop = [values] + [swap(values, "fsdp", lows * k) for k in range(1, HOPS)]
+        per_hop = [values] + [swap(values, "fsdp", HOP_BIT * k) for k in range(1, HOPS)]
         columns = [
             [mine, *[swap(mine, "dp", CORES * j) for j in range(1, rows_y)]] for mine in per_hop
         ]
@@ -425,14 +452,10 @@
             for column in columns[k]:
                 sets.extend([column, swap(column, "dp", 1)])
             ready = [r[0] for r in results[-1:]]
-            if k == 0:
-                ready.append(per_hop[2])
-            elif k == 1:
-                ready.extend([columns[2][1:], per_hop[3]])
-            elif k == 2:
-                ready.extend([columns[3][1:], sums[0][0]])
-            else:
-                ready.extend([sums[0][1:], sums[1][1:], sums[2][0]])
+            if k + 1 < HOPS:
+                ready.append(per_hop[k + 1])
+            if k:
+                ready.append(sums[k - 1][0])
             results.append(compute(k, sets, ready))
             own, given = results[k][:CORES]
             got = swap(given, "dp", 1)
@@ -445,11 +468,9 @@
             hops = []
             for k in range(HOPS):
                 mine, others = sums[k][0], sums[k][1:]
-                if k == HOPS - 1:
-                    others = after(others, hops[1])
                 for got in others:
                     mine = mine + got.astype(f32)
-                hops.append(swap(mine.astype(bf16), "fsdp", lows * k) if k else mine)
+                hops.append(swap(mine.astype(bf16), "fsdp", HOP_BIT * k) if k else mine)
             if hold is not None:
                 hops = after(hops, hold)
             total = hops[0]
@@ -460,9 +481,9 @@
         return finish
 
     steps = (
-        (2, "fsdp", lows, HOPS, hop_at),
+        (2, "fsdp", 2, units, fsdp_at // 2),
         (0, "dp", CORES, rows_y, y_at),
-        (3, "fsdp", 1, lows, low_at),
+        (3, "fsdp", 1, 2, fsdp_at % 2),
         (1, "dp", 1, CORES, core_at),
     )
 
@@ -508,31 +529,35 @@
     def owned_by(k):
         return lax.dynamic_slice_in_dim(shard, (hop_at ^ k) * held, held, 0)
 
-    def low_swaps(block):
-        return [swap(block, "fsdp", m) for m in range(1, lows)]
-
     join = lax.optimization_barrier
-    blocks = {0: owned_by(0)}
-    lows_of = {}
+    half = shard.shape[1] // 2
+    far_bits = [HOP_BIT * 2**i for i in range(1, shards.bit_length()) if HOP_BIT * 2**i < shards]
+
+    def far_swaps(piece):
+        found = {0: piece}
+        for bit in far_bits:
+            found |= {bit ^ m: swap(p, "fsdp", bit) for m, p in found.items()}
+        return {m: p for m, p in found.items() if m}
+
+    arrived = {(0, 0): owned_by(0)}
     pack = pack.reshape(1, 1, 1, 1, row_block, -1)
-    lows_of[0] = low_swaps(blocks[0])
+    arrived[1, 0] = swap(arrived[0, 0], "fsdp", 1)
     pack = merge(pack, send(pack, 0), 0)
     others = send(pack, 1)
-    blocks[1] = swap(after(owned_by(1), pack), "fsdp", lows)
-    pack, others, blocks[1], lows_of[0] = join((pack, others, blocks[1], lows_of[0]))
+    near = [swap(after(owned_by(1), pack), "fsdp", HOP_BIT)]
+    far_own = far_swaps(after(arrived[0, 0], pack))
+    pack, others, arrived[1, 0] = join((pack, others, arrived[1, 0]))
     pack = merge(pack, others, 1)
     others = send(pack, 2)
-    third = shard.shape[1] // 3
-    far3 = [swap(after(owned_by(3)[:, third:], pack), "fsdp", lows * 3)]
-    pack, others, far3 = join((pack, others, far3))
+    pack, others, near = join((pack, others, near))
     pack = merge(pack, others, 2)
     others = send(pack, 3)
     out_w = after(w_out, pack).reshape(1, 1, 1, 1, row_block, -1)
-    lows_of[1] = low_swaps(after(blocks[1], pack))
-    far3.insert(0, swap(after(owned_by(3)[:, :third], pack), "fsdp", lows * 3))
+    arrived[HOP_BIT, 0] = near[0]
+    near_low = swap(after(near[0], pack), "fsdp", 1)
     out_others = send(out_w, 0)
-    pack, others, out_w, out_others, far3 = join((pack, others, out_w, out_others, far3))
-    far2 = [swap(after(owned_by(2)[:, :third], others), "fsdp", lows * 2)]
+    pack, others, out_w, out_others = join((pack, others, out_w, out_others))
+    far_near = [far_swaps(after(near[0][:, :half], others))]
     packed = merge(pack, others, 3).reshape(model_width, -1)
     out_w = merge(out_w, out_others, 0)
     out_others = send(out_w, 1)
@@ -548,11 +573,13 @@
     normed = (tok_float * inv_one * gain_float).astype(bf16)
     cos_lanes, sin_lanes = rotary_lanes(seq_len)
     qkv = dot(normed, qkv_w)
-    qkv, out_w, out_others, far2, lows_of[1] = join((qkv, out_w, out_others, far2, lows_of[1]))
-    far2.append(swap(after(owned_by(2)[:, third:], qkv), "fsdp", lows * 2))
+    qkv, out_w, out_others, far_own = join((qkv, out_w, out_others, far_own))
+    far_near.append(far_swaps(after(near[0][:, half:], qkv)))
     out_w = merge(out_w, out_others, 1)
     out_others = send(out_w, 2)
-    low3 = [low_swaps(after(piece, qkv)) for piece in far3]
+    for m, piece in far_own.items():
+        arrived[m, 0] = piece
+        arrived[m ^ 1, 0] = swap(piece, "fsdp", 1)
     rotated, mixed_rows = kernel_call(
         attention_forward,
         (
@@ -562,19 +589,19 @@
         (lengths, qkv, cos_lanes, sin_lanes),
         first_smem=True,
     )
-    mixed_rows, out_w, out_others, far2, low3 = join((mixed_rows, out_w, out_others, far2, low3))
+    mixed_rows, out_w, out_others, far_near[0], near_low = join(
+        (mixed_rows, out_w, out_others, far_near[0], near_low)
+    )
+    arrived[HOP_BIT ^ 1, 0] = near_low
     out_w = merge(out_w, out_others, 2)
     out_w = merge(out_w, send(out_w, 3), 3).reshape(model_width, -1)
-    low2 = [low_swaps(piece) for piece in far2]
-    parts_of = {k: [([blocks[k], *lows_of[k]], 0)] for k in (0, 1)}
-    for k, far, low in ((3, far3, low3), (2, far2, low2)):
-        parts_of[k] = [([far[i], *low[i]], i * third) for i in range(2)]
+    for i, pieces in enumerate(far_near):
+        for m, piece in pieces.items():
+            arrived[m ^ HOP_BIT, i * half] = piece
+            arrived[m ^ HOP_BIT ^ 1, i * half] = swap(piece, "fsdp", 1)
     expert_w = jnp.zeros((held, shards, shard.shape[1], model_width), bf16)
-    for k in (0, 1, 3, 2):
-        for pieces, row in parts_of[k]:
-            for m, piece in enumerate(pieces):
-                at = (hop_at ^ k) * lows + (low_at ^ m)
-                expert_w = lax.dynamic_update_slice(expert_w, piece[:, None], (0, at, row, 0))
+    for (m, row), piece in arrived.items():
+        expert_w = lax.dynamic_update_slice(expert_w, piece[:, None], (0, fsdp_at ^ m, row, 0))
     hidden = tok_float + residual_scale * dot(mixed_rows, out_w)
     inv_two = lax.rsqrt(jnp.mean(hidden * hidden, axis=1, keepdims=True) + epsilon)
     normed_ffn = hidden * inv_two * gain_second
@@ -599,12 +626,11 @@
 
     def forward(k, sets, ready):
         token_sets.append(sets)
-        return kernel_call(
+        return expert_call(
             functools.partial(expert_forward, count, seq_len),
             (set_shape,) * CORES,
             (after(first_held, *ready), expert_w, *sets),
-            first_smem=True,
-            scratch=(
+            (
                 pltpu.VMEM((rows, model_width), bf16),
                 pltpu.VMEM((count, seq_len, model_width), f32),
                 pltpu.VMEM((count, CAP, seq_len), bf16),
@@ -633,8 +659,8 @@
 
     def backward(k, sets, ready):
         if k:
-            ready = [*ready, loss_steps[k - 1]]
-        results = kernel_call(
+            ready = [*ready, loss_steps[1]]
+        results = expert_call(
             functools.partial(expert_backward, count, seq_len),
             (back_shape,) * CORES
             + (
@@ -644,8 +670,7 @@
                 jax.ShapeDtypeStruct((held, rows, hidden_units), bf16),
             ),
             (after(first_held, *ready), expert_w, *token_sets[k], *sets),
-            first_smem=True,
-            scratch=(
+            (
                 pltpu.VMEM((count, seq_len, model_width), f32),
                 pltpu.VMEM((count, CAP, seq_len), bf16),
                 pltpu.VMEM((count, gate_rows, model_width), f32),
@@ -657,7 +682,7 @@
     finish = exchange(out_grad.astype(bf16), backward)
     block_shape = (1, shard.shape[1], model_width)
     expert_grad = pl.pallas_call(
-        functools.partial(expert_weight_grads, HOPS, HOPS),
+        functools.partial(expert_weight_grads, HOPS),
         grid=(held,),
         out_shape=(jax.ShapeDtypeStruct((held, *block_shape[1:]), bf16),) * shards,
         in_specs=[smem()]
@@ -670,25 +695,20 @@
         scratch_shapes=(pltpu.VMEM((shards, shard.shape[1], model_width), bf16),),
         compiler_params=pltpu.CompilerParams(vmem_limit_bytes=60 * 1024 * 1024),
     )(
-        jnp.stack([hop_at, low_at]).astype(jnp.int32),
+        fsdp_at.astype(jnp.int32)[None],
         *[saved[k][i] for i in range(4) for k in range(HOPS)],
     )
-    low_parts = {
-        k: [expert_grad[k * lows]]
-        + [swap(expert_grad[k * lows + m], "fsdp", m) for m in range(1, lows)]
-        for k in range(HOPS - 1, -1, -1)
-    }
-    returned, low_parts[3] = join((finish((expert_grad[0], loss_steps[3])), low_parts[3]))
-
-    def low_sum(k):
-        pieces = low_parts[k]
-        total = pieces[0].astype(f32)
-        for piece in pieces[1:]:
-            total = total + piece.astype(f32)
-        return total
-
-    def hop_send(k):
-        return swap(low_sum(k).astype(bf16), "fsdp", lows * k)
+    order_of = sorted(range(0, shards, 2), key=lambda m: -m)
+    low_got = {m: swap(expert_grad[m ^ 1], "fsdp", 1) for m in order_of}
+    first_low = order_of[0]
+    returned, low_got[first_low] = join((finish((expert_grad[0], loss_steps[3])), low_got[first_low]))
+    sums_of = {}
+
+    def low_sum(m):
+        sums_of[m] = expert_grad[m].astype(f32) + low_got[m].astype(f32)
+
+    def far_send(bit, m):
+        return swap(sums_of[m].astype(bf16), "fsdp", bit)
 
     gate_grad = (
         (returned[seq_len : seq_len + gate_rows] + returned[seq_len + gate_rows :])
@@ -718,9 +738,16 @@
             mine = mine + other.astype(f32)
         return mine
 
-    order = (rows_y, CORES, HOPS, lows, row_block, -1)
+    order = (rows_y, CORES, units, 2, row_block, -1)
     mixed_grad = dot_nt(attended_grad, out_w).astype(bf16)
-    hop_got = {3: hop_send(3)}
+    low_sum(first_low)
+    far_got = {}
+    last_bit = far_bits[-1]
+
+    def start_far(m):
+        far_got[m ^ last_bit] = far_send(last_bit, m)
+
+    start_far(first_low)
     out_sum = halve(dot_tn(mixed_rows, attended_grad).astype(bf16).reshape(order), 3)
     lane = jnp.arange(128, dtype=jnp.int32)[None, :]
     ones = jnp.ones((seq_len, 1), f32)
@@ -743,10 +770,16 @@
         first_smem=True,
         scratch=(pltpu.VMEM((seq_len, model_width + kv_width), f32),),
     )
-    qkv_grad, out_sum, low_parts[2] = join((qkv_grad, out_sum, low_parts[2]))
+    steps_left = order_of[1:]
+    wait_for = steps_left[: len(steps_left) // 3]
+    qkv_grad, out_sum, got = join((qkv_grad, out_sum, [low_got[m] for m in wait_for]))
+    low_got |= dict(zip(wait_for, got, strict=True))
+    for m in wait_for:
+        low_sum(m)
+        if m & last_bit:
+            start_far(m)
     out_sum = halve(total(*out_sum), 1)
-    hop_got[2] = hop_send(2)
-    share = jax.ShapeDtypeStruct((rows_y, HOPS * lows * row_block, qkv_width + 128), bf16)
+    share = jax.ShapeDtypeStruct((rows_y, shards * row_block, qkv_width + 128), bf16)
     *grads, token_grad = kernel_call(
         functools.partial(dense_backward, experts),
         (share,) * CORES + (jax.ShapeDtypeStruct((seq_len, model_width), f32),),
@@ -764,25 +797,33 @@
         first_smem=True,
         scratch=(pltpu.VMEM((model_width, qkv_width + 128), bf16),),
     )
-    grads, out_sum, low_parts[1], hop_got[3] = join((grads, out_sum, low_parts[1], hop_got[3]))
-    grads = [g.reshape(rows_y, 1, HOPS, lows, row_block, -1) for g in grads]
+    grads, out_sum = join((grads, out_sum))
+    grads = [g.reshape(rows_y, 1, units, 2, row_block, -1) for g in grads]
     part_sum = (grads[0].astype(f32), [swap(g, "dp", m + 1) for m, g in enumerate(grads[1:])])
     out_sum = halve(total(*out_sum), 2)
     part_sum, out_sum = join((part_sum, out_sum))
     part_sum = halve(total(*part_sum), 1)
-    hop_got[1] = hop_send(1)
     out_sum = halve(total(*out_sum), 0)
-    part_sum, out_sum, low_parts[0], hop_got[2] = join(
-        (part_sum, out_sum, low_parts[0], hop_got[2])
-    )
+    part_sum, out_sum, low_got = join((part_sum, out_sum, low_got))
+    for m in order_of:
+        if m not in sums_of:
+            low_sum(m)
+            if m & last_bit:
+                start_far(m)
     out_grad_w = total(*out_sum).reshape(row_block, -1)
-    part_sum, hop_got[1] = join((halve(total(*part_sum), 2), hop_got[1]))
-    part_sum = halve(total(*part_sum), 0)
+    part_sum = halve(total(*part_sum), 2)
+    part_sum, far_got = join((part_sum, far_got))
+    for m, got in far_got.items():
+        sums_of[m] = sums_of[m] + got.astype(f32)
+    for bit in far_bits[-2::-1]:
+        far_got = {m ^ bit: far_send(bit, m) for m in sums_of if m & bit and m < 2 * bit}
+        for m, got in far_got.items():
+            sums_of[m] = sums_of[m] + got.astype(f32)
+    hop_got = far_send(HOP_BIT, HOP_BIT)
+    part_sum, hop_got = join((halve(total(*part_sum), 0), hop_got))
     small = total(*part_sum).reshape(row_block, -1)
-
     expert_out = jnp.zeros((owned, shard.shape[1], model_width), f32)
-    for k in range(HOPS):
-        block = hop_got[k].astype(f32) if k else low_sum(0)
+    for k, block in ((0, sums_of[0]), (1, hop_got.astype(f32))):
         expert_out = lax.dynamic_update_slice(expert_out, block, ((hop_at ^ k) * held, 0, 0))
     expert_grads = (
         expert_out[:, :split, :hidden_units],

time: 689 us -> 825 us (1.20)
  waiting for transfers between devices: 317 us -> 504 us
  starting transfers between devices: 101 us -> 70.1 us
  Pallas kernels: 142 us -> 121 us
    ppermute x99 -> x69, waiting for transfers between devices: 317 us -> 504 us  [swap(): lax.ppermute(values, axis, [(i, i ^ mask) for i in range(lax.axis_size(ax...]
    pallas_call x11 -> x3, Pallas kernels: 122 us -> 31 us  [kernel_call(): pl.pallas_call(body, out_shape=out_shape, in_specs=specs, out_specs=jax.t...]
    pallas_call x1 -> x5, Pallas kernels: 19.7 us -> 89.9 us  [the longest x4 70.7 us: expert_call(): pl.pallas_call(body, grid=(held,), out_shape=out_shape, in_specs=[smem(),...]
    ppermute x99 -> x69, starting transfers between devices: 101 us -> 70.1 us  [swap(): lax.ppermute(values, axis, [(i, i ^ mask) for i in range(lax.axis_size(ax...]
    dynamic_update_slice x12 -> x10, local copies, waits for them, and re-layouts: 16.1 us -> 17.9 us  [on_device(): lax.dynamic_update_slice(expert_w, piece[:, None], (0, fsdp_at ^ m, row, 0))]
  transfers between devices with their start and end apart: 99 -> 69, of which waited for: 40 -> 33; matrix products, arithmetic and copies ran while one was open for 11% -> 11% of each run, Pallas kernels for 21% -> 10%
where the time goes in v6:
time: 825 us; the launch traced here: 820 us
  waiting for transfers between devices  504 us (61%)
  Pallas kernels  121 us (15%)
  starting transfers between devices  70.1 us (8%)
  other arithmetic  55.7 us (7%)
  local copies, waits for them, and re-layouts  52.1 us (6%)
  matrix products  12.2 us (1%)
    ppermute x69, waiting for transfers between devices, swap(): lax.ppermute(values, axis, [(i, i ^ mask) for i in range(lax.axis_size(ax...  504 us
    pallas_call x4, Pallas kernels, expert_call(): pl.pallas_call(body, grid=(held,), out_shape=out_shape, in_specs=[smem(),...  70.7 us
    ppermute x69, starting transfers between devices, swap(): lax.ppermute(values, axis, [(i, i ^ mask) for i in range(lax.axis_size(ax...  70.1 us
    pallas_call x3, Pallas kernels, kernel_call(): pl.pallas_call(body, out_shape=out_shape, in_specs=specs, out_specs=jax.t...  31 us
    pallas_call x1, Pallas kernels, on_device(): pl.pallas_call(functools.partial(expert_weight_grads, HOPS), grid=(held,)...  19.1 us
    dynamic_update_slice x10, local copies, waits for them, and re-layouts, on_device(): lax.dynamic_update_slice(expert_w, piece[:, None], (0, fsdp_at ^ m, row, 0))  17.9 us
  transfers between devices with their start and end apart: 69, of which 33 were waited for; matrix products, arithmetic and copies ran while one was open for 11% of the time, Pallas kernels for 10%

profile of v6, /device:TPU:0, one launch (start us, length us, event | category | flops | bytes accessed | tf_op | source)
XLA Modules:
  0.0 820.5 jit_solution(13351347556243765666)
XLA Ops:
  3.8 5.1 collective-permute-start
  11.6 6.1 broadcast_in_dim.113
  27.4 9.8 %collective-permute-done.3 = bf16[1,1,4,1,32,2176]{5,4,3,2,1,0:T(8,128)(2,1)} collective-permute-done((bf16[1,1,4,1,32,2176]{5,4,3,2,1,0:T(8,128)(2,1)}, bf16[1,1,4,1,32,2176]{5,4,3,2,1,0:T(8,128)(2,1)}, u32[]{:S(2)}, u32[]{:S(2)}) %collective-permute-start.3) | collective-permute-done | bytes 557088 | tf_op jit(solution)/shard_map/ppermute | solution.py:41
  37.2 18.5 %collective-permute-done.4 = bf16[4,192,1024]{2,1,0:T(8,128)(2,1)} collective-permute-done((bf16[4,192,1024]{2,1,0:T(8,128)(2,1)}, bf16[4,192,1024]{2,1,0:T(8,128)(2,1)}, u32[]{:S(2)}, u32[]{:S(2)}) %collective-permute-start.4) | collective-permute-done | bytes 1572896 | tf_op jit(solution)/shard_map/ppermute | solution.py:41
  62.5 21.2 %collective-permute-done.5 = bf16[2,1,4,1,32,2176]{5,4,3,2,1,0:T(8,128)(2,1)} collective-permute-done((bf16[2,1,4,1,32,2176]{5,4,3,2,1,0:T(8,128)(2,1)}, bf16[2,1,4,1,32,2176]{5,4,3,2,1,0:T(8,128)(2,1)}, u32[]{:S(2)}, u32[]{:S(2)}) %collective-permute-start.5) | collective-permute-done | bytes 1114144 | tf_op jit(solution)/shard_map/ppermute | solution.py:41
  95.8 29.7 %collective-permute-done.8 = bf16[1,1,1,1,32,1024]{5,4,3,2,1,0:T(8,128)(2,1)S(1)} collective-permute-done((bf16[1,1,1,1,32,1024]{5,4,3,2,1,0:T(8,128)(2,1)}, bf16[1,1,1,1,32,1024]{5,4,3,2,1,0:T(8,128)(2,1)S(1)}, u32[]{:S(2)}, u32[]{:S(2)}) %collective-permute-start.8) | collective-permute-done | bytes 65568 | tf_op jit(solution)/shard_map/ppermute | solution.py:41
  127.0 36.0 %collective-permute-done.9 = bf16[1,1,1,1,32,1024]{5,4,3,2,1,0:T(8,128)(2,1)S(1)} collective-permute-done((bf16[1,1,1,1,32,1024]{5,4,3,2,1,0:T(8,128)(2,1)}, bf16[1,1,1,1,32,1024]{5,4,3,2,1,0:T(8,128)(2,1)S(1)}, u32[]{:S(2)}, u32[]{:S(2)}) %collective-permute-start.9) | collective-permute-done | bytes 65568 | tf_op jit(solution)/shard_map/ppermute | solution.py:41
  165.3 3.3 collective-permute-start.14
  179.0 9.6 %shard_map.237 = (bf16[256,2048]{1,0:T(8,128)(2,1)}, bf16[256,1024]{1,0:T(8,128)(2,1)}) custom-call(s32[1]{0:T(128)} %copy.79.length_ref, f32[256,2048]{1,0:T(8,128)} %fusion.qkv_ref, f32[256,128]{1,0:T(8,128)} %get-tuple-element.257.cos_ref, f32[256,128]{1,0:T(8,128)} %get-tuple-element.258.sin_ref), custom_call_target="tpu_custom_call" | custom-call | tf_op jit(solution)/shard_map/pallas_call | solution.py:60
  189.3 13.7 %collective-permute-done.14 = bf16[4,96,1024]{2,1,0:T(8,128)(2,1)S(1)} collective-permute-done((bf16[4,96,1024]{2,1,0:T(8,128)(2,1)S(1)}, bf16[4,96,1024]{2,1,0:T(8,128)(2,1)S(1)}, u32[]{:S(2)}, u32[]{:S(2)}) %collective-permute-start.14) | collective-permute-done | bytes 786464 | tf_op jit(solution)/shard_map/ppermute | solution.py:41
  223.1 24.2 %collective-permute-done.20 = bf16[4,96,1024]{2,1,0:T(8,128)(2,1)} collective-permute-done((bf16[4,96,1024]{2,1,0:T(8,128)(2,1)}, bf16[4,96,1024]{2,1,0:T(8,128)(2,1)}, u32[]{:S(2)}, u32[]{:S(2)}) %collective-permute-start.20) | collective-permute-done | bytes 786464 | tf_op jit(solution)/shard_map/ppermute | solution.py:41
  254.9 8.2 %collective-permute-done.19 = bf16[4,96,1024]{2,1,0:T(8,128)(2,1)S(1)} collective-permute-done((bf16[4,96,1024]{2,1,0:T(8,128)(2,1)S(1)}, bf16[4,96,1024]{2,1,0:T(8,128)(2,1)S(1)}, u32[]{:S(2)}, u32[]{:S(2)}) %collective-permute-start.19) | collective-permute-done | bytes 786464 | tf_op jit(solution)/shard_map/ppermute | solution.py:41
  263.6 11.3 %collective-permute-done.28.refs_2_ = bf16[272,1024]{1,0:T(8,128)(2,1)S(1)} collective-permute-done((bf16[272,1024]{1,0:T(8,128)(2,1)S(1)}, bf16[272,1024]{1,0:T(8,128)(2,1)S(1)}, u32[]{:S(2)}, u32[]{:S(2)}) %collective-permute-start.28) | collective-permute-done | bytes 557088 | tf_op jit(solution)/shard_map/ppermute | solution.py:41
  281.9 14.1 %shard_map.238 = (bf16[2,256,1024]{2,1,0:T(8,128)(2,1)}, bf16[2,256,1024]{2,1,0:T(8,128)(2,1)}) custom-call(s32[1]{0:T(128)} %bitcast.8.first_ref, bf16[4,8,192,1024]{3,2,1,0:T(8,128)(2,1)} %bitcast_dynamic-update-slice_fusion.9.weights_ref, bf16[272,1024]{1,0:T(8,128)(2,1)} %copy-done.8, bf16[272,1024]{1,0:T(8,128)(2,1)} %copy-done.16, ...), custom_call_target="tpu_custom_call" | custom-call | tf_op jit(solution)/shard_map/pallas_call | solution.py:80
  297.7 13.8 %shard_map.239 = (bf16[2,256,1024]{2,1,0:T(8,128)(2,1)}, bf16[2,256,1024]{2,1,0:T(8,128)(2,1)}) custom-call(s32[1]{0:T(128)} %bitcast.8.first_ref, bf16[4,8,192,1024]{3,2,1,0:T(8,128)(2,1)} %bitcast_dynamic-update-slice_fusion.9.weights_ref, bf16[272,1024]{1,0:T(8,128)(2,1)} %copy-done.14, bf16[272,1024]{1,0:T(8,128)(2,1)} %copy-done.18, ...), custom_call_target="tpu_custom_call" | custom-call | tf_op jit(solution)/shard_map/pallas_call | solution.py:80
  320.7 9.8 %collective-permute-done.31 = bf16[256,1024]{1,0:T(8,128)(2,1)S(1)} collective-permute-done((bf16[256,1024]{1,0:T(8,128)(2,1)S(1)}, bf16[256,1024]{1,0:T(8,128)(2,1)S(1)}, u32[]{:S(2)}, u32[]{:S(2)}) %collective-permute-start.31) | collective-permute-done | bytes 524320 | tf_op jit(solution)/shard_map/ppermute | solution.py:41
  332.3 8.6 %collective-permute-done.26 = bf16[256,1024]{1,0:T(8,128)(2,1)S(1)} collective-permute-done((bf16[256,1024]{1,0:T(8,128)(2,1)}, bf16[256,1024]{1,0:T(8,128)(2,1)S(1)}, u32[]{:S(2)}, u32[]{:S(2)}) %collective-permute-start.26) | collective-permute-done | bytes 524320 | tf_op jit(solution)/shard_map/ppermute | solution.py:41
  340.9 3.3 collective-permute-done.32
  346.7 10.6 %collective-permute-done.38.refs_4_ = bf16[256,1024]{1,0:T(8,128)(2,1)S(1)} collective-permute-done((bf16[256,1024]{1,0:T(8,128)(2,1)S(1)}, bf16[256,1024]{1,0:T(8,128)(2,1)S(1)}, u32[]{:S(2)}, u32[]{:S(2)}) %collective-permute-start.38) | collective-permute-done | bytes 524320 | tf_op jit(solution)/shard_map/ppermute | solution.py:41
  358.6 10.3 %collective-permute-done.45.refs_6_ = bf16[256,1024]{1,0:T(8,128)(2,1)S(1)} collective-permute-done((bf16[256,1024]{1,0:T(8,128)(2,1)S(1)}, bf16[256,1024]{1,0:T(8,128)(2,1)S(1)}, u32[]{:S(2)}, u32[]{:S(2)}) %collective-permute-start.45) | collective-permute-done | bytes 524320 | tf_op jit(solution)/shard_map/ppermute | solution.py:41
  378.7 21.6 %shard_map.240 = (bf16[2,272,1024]{2,1,0:T(8,128)(2,1)}, bf16[2,272,1024]{2,1,0:T(8,128)(2,1)}, bf16[4,384,1024]{2,1,0:T(8,128)(2,1)}, bf16[4,384,1024]{2,1,0:T(...) custom-call(s32[1]{0:T(128)} %bitcast.8.first_ref, ...), custom_call_target="tpu_custom_call" | custom-call | tf_op jit(solution)/shard_map/pallas_call | solution.py:80
  401.9 21.2 %shard_map.241 = (bf16[2,272,1024]{2,1,0:T(8,128)(2,1)}, bf16[2,272,1024]{2,1,0:T(8,128)(2,1)}, bf16[4,384,1024]{2,1,0:T(8,128)(2,1)}, bf16[4,384,1024]{2,1,0:T(...) custom-call(s32[1]{0:T(128)} %bitcast.8.first_ref, ...), custom_call_target="tpu_custom_call" | custom-call | tf_op jit(solution)/shard_map/pallas_call | solution.py:80
  429.1 19.1 %shard_map.242 = (bf16[4,192,1024]{2,1,0:T(8,128)(2,1)}, bf16[4,192,1024]{2,1,0:T(8,128)(2,1)}, bf16[4,192,1024]{2,1,0:T(8,128)(2,1)}, bf16[4,192,1024]{2,1,0:T(...) custom-call(s32[1]{0:T(128)} %bitcast.39.at_ref, ...), custom_call_target="tpu_custom_call" | custom-call | tf_op jit(solution)/shard_map/pallas_call | solution.py:684
  456.7 28.1 %collective-permute-done.35 = f32[8,128]{1,0:T(8,128)S(1)} collective-permute-done((f32[8,128]{1,0:T(8,128)S(1)}, f32[8,128]{1,0:T(8,128)S(1)}, u32[]{:S(2)}, u32[]{:S(2)}) %collective-permute-start.35) | collective-permute-done | bytes 4128 | tf_op jit(solution)/shard_map/ppermute | solution.py:41
  505.1 12.5 %shard_map.243.qkv_grad_ref = bf16[256,2048]{1,0:T(8,128)(2,1)} custom-call(s32[1]{0:T(128)} %copy.79.length_ref, bf16[256,2048]{1,0:T(8,128)(2,1)} %get-tuple-element.152.rot_ref, bf16[256,1024]{1,0:T(8,128)(2,1)} %convolution_convert_fusion.1.grad_ref, f32[256,128]{1,0:T(8,128)} %get-tuple-element.257.cos_ref, f32[256,128]{1,0:T(8,128)} %get-tuple-element.258.sin_ref), custom_call_target="tpu_custom_call" | custom-call | tf_op jit(solution)/shard_map/pallas_call | solution.py:60
  517.6 5.3 collective-permute-done.52
  527.9 8.9 %shard_map.244 = (bf16[2,256,2176]{2,1,0:T(8,128)(2,1)}, bf16[2,256,2176]{2,1,0:T(8,128)(2,1)}, f32[256,1024]{1,0:T(8,128)}) custom-call(s32[1]{0:T(128)} %bitcast.34.core_ref, bf16[256,2048]{1,0:T(8,128)(2,1)} %shard_map.243.qkv_grad_ref, bf16[256,1024]{1,0:T(8,128)(2,1)} %copy-done.22, bf16[1024,2176]{1,0:T(8,128)(2,1)} %bitcast.125, ...), custom_call_target="tpu_custom_call" | custom-call | tf_op jit(solution)/shard_map/pallas_call | solution.py:60
  550.9 67.7 %collective-permute-done.55 = bf16[1,1,4,1,32,1024]{5,4,3,2,1,0:T(8,128)(2,1)S(1)} collective-permute-done((bf16[1,1,4,1,32,1024]{5,4,3,2,1,0:T(8,128)(2,1)S(1)}, bf16[1,1,4,1,32,1024]{5,4,3,2,1,0:T(8,128)(2,1)S(1)}, u32[]{:S(2)}, u32[]{:S(2)}) %collective-permute-start.55) | collective-permute-done | bytes 262176 | tf_op jit(solution)/shard_map/ppermute | solution.py:41
  630.4 68.9 %collective-permute-done.58 = bf16[1,1,1,1,32,1024]{5,4,3,2,1,0:T(8,128)(2,1)S(1)} collective-permute-done((bf16[1,1,1,1,32,1024]{5,4,3,2,1,0:T(8,128)(2,1)S(1)}, bf16[1,1,1,1,32,1024]{5,4,3,2,1,0:T(8,128)(2,1)S(1)}, u32[]{:S(2)}, u32[]{:S(2)}) %collective-permute-start.58) | collective-permute-done | bytes 65568 | tf_op jit(solution)/shard_map/ppermute | solution.py:41
  701.8 32.5 %collective-permute-done.64 = bf16[4,192,1024]{2,1,0:T(8,128)(2,1)S(1)} collective-permute-done((bf16[4,192,1024]{2,1,0:T(8,128)(2,1)S(1)}, bf16[4,192,1024]{2,1,0:T(8,128)(2,1)S(1)}, u32[]{:S(2)}, u32[]{:S(2)}) %collective-permute-start.64) | collective-permute-done | bytes 1572896 | tf_op jit(solution)/shard_map/ppermute | solution.py:41
  734.4 32.3 %collective-permute-done.63 = bf16[4,192,1024]{2,1,0:T(8,128)(2,1)S(1)} collective-permute-done((bf16[4,192,1024]{2,1,0:T(8,128)(2,1)S(1)}, bf16[4,192,1024]{2,1,0:T(8,128)(2,1)S(1)}, u32[]{:S(2)}, u32[]{:S(2)}) %collective-permute-start.63) | collective-permute-done | bytes 1572896 | tf_op jit(solution)/shard_map/ppermute | solution.py:41
  774.5 35.7 %collective-permute-done.65 = bf16[1,1,1,1,32,2176]{5,4,3,2,1,0:T(8,128)(2,1)S(1)} collective-permute-done((bf16[1,1,1,1,32,2176]{5,4,3,2,1,0:T(8,128)(2,1)S(1)}, bf16[1,1,1,1,32,2176]{5,4,3,2,1,0:T(8,128)(2,1)S(1)}, u32[]{:S(2)}, u32[]{:S(2)}) %collective-permute-start.65) | collective-permute-done | bytes 139296 | tf_op jit(solution)/shard_map/ppermute | solution.py:41
  (327 shorter events, 193.8 us)
Async XLA Ops:
  19.8 35.9 %collective-permute-start.4 = (bf16[4,192,1024]{2,1,0:T(8,128)(2,1)}, bf16[4,192,1024]{2,1,0:T(8,128)(2,1)}, u32[]{:S(2)}, u32[]{:S(2)}) collective-permute-start(bf16[4,192,1024]{2,1,0:T(8,128)(2,1)} %get-tuple-element.130), channel_id=1, source_target_pairs={{0,1},{1,0},{2,3},{3,2},{4,5},{5,4},{6,7},{7,6},{8,9},{9,8},{10,11... | collective-permute-start | bytes 4718600 | tf_op jit(solution)/shard_map/ppermute | solution.py:41
  26.3 35.1 %collective-permute-start.6 = (bf16[4,192,1024]{2,1,0:T(8,128)(2,1)}, bf16[4,192,1024]{2,1,0:T(8,128)(2,1)S(1)}, u32[]{:S(2)}, u32[]{:S(2)}) collective-permute-start(bf16[4,192,1024]{2,1,0:T(8,128)(2,1)} %constant_dynamic-slice_fusion.7), channel_id=1, source_target_pairs={{0,2},{1,3},{2,0},{3,1},{4,6},{5,7},{6,4},{7,5},{8,10},{9,11},{10,... | collective-permute-start | bytes 4718600 | tf_op jit(solution)/shard_map/ppermute | solution.py:41
  86.3 76.7 %collective-permute-start.7 = (bf16[2,1,4,2,32,2176]{5,4,3,2,1,0:T(8,128)(2,1)S(1)}, bf16[2,1,4,2,32,2176]{5,4,3,2,1,0:T(8,128)(2,1)}, u32[]{:S(2)}, u32[]{:S(2)}) collective-permute-start(bf16[2,1,4,2,32,2176]{5,4,3,2,1,0:T(8,128)(2,1)S(1)} %maximum_select_fusion.1), channel_id=1, source_target_pairs={{0,8},{8,0},{16,24},{24,16},{1,9},{9,1},{17,25},{25,17},{2,10},{10... | collective-permute-start | bytes 6684680 | tf_op jit(solution)/shard_map/ppermute | solution.py:41
  86.6 89.2 %collective-permute-start.12 = (bf16[4,192,1024]{2,1,0:T(8,128)(2,1)}, bf16[4,192,1024]{2,1,0:T(8,128)(2,1)}, u32[]{:S(2)}, u32[]{:S(2)}) collective-permute-start(bf16[4,192,1024]{2,1,0:T(8,128)(2,1)} %get-tuple-element.130), channel_id=1, source_target_pairs={{0,4},{1,5},{2,6},{3,7},{4,0},{5,1},{6,2},{7,3},{8,12},{9,13},{10,... | collective-permute-start | bytes 4718600 | tf_op jit(solution)/shard_map/ppermute | solution.py:41
  88.9 36.6 %collective-permute-start.8 = (bf16[1,1,1,1,32,1024]{5,4,3,2,1,0:T(8,128)(2,1)}, bf16[1,1,1,1,32,1024]{5,4,3,2,1,0:T(8,128)(2,1)S(1)}, u32[]{:S(2)}, u32[]{:S(2)}) collective-permute-start(bf16[1,1,1,1,32,1024]{5,4,3,2,1,0:T(8,128)(2,1)} %bitcast.5), channel_id=1, source_target_pairs={{0,2},{1,3},{2,0},{3,1},{4,6},{5,7},{6,4},{7,5},{8,10},{9,11},{10,... | collective-permute-start | bytes 196616 | tf_op jit(solution)/shard_map/ppermute | solution.py:41
  90.4 72.6 %collective-permute-start.9 = (bf16[1,1,1,1,32,1024]{5,4,3,2,1,0:T(8,128)(2,1)}, bf16[1,1,1,1,32,1024]{5,4,3,2,1,0:T(8,128)(2,1)S(1)}, u32[]{:S(2)}, u32[]{:S(2)}) collective-permute-start(bf16[1,1,1,1,32,1024]{5,4,3,2,1,0:T(8,128)(2,1)} %bitcast.5), channel_id=1, source_target_pairs={{0,4},{1,5},{2,6},{3,7},{4,0},{5,1},{6,2},{7,3},{8,12},{9,13},{10,... | collective-permute-start | bytes 196616 | tf_op jit(solution)/shard_map/ppermute | solution.py:41
  91.0 72.0 %collective-permute-start.10 = (bf16[1,1,1,1,32,1024]{5,4,3,2,1,0:T(8,128)(2,1)}, bf16[1,1,1,1,32,1024]{5,4,3,2,1,0:T(8,128)(2,1)S(1)}, u32[]{:S(2)}, u32[]{:S(2)}) collective-permute-start(bf16[1,1,1,1,32,1024]{5,4,3,2,1,0:T(8,128)(2,1)} %bitcast.5), channel_id=1, source_target_pairs={{0,6},{1,7},{2,4},{3,5},{4,2},{5,3},{6,0},{7,1},{8,14},{9,15},{10,... | collective-permute-start | bytes 196616 | tf_op jit(solution)/shard_map/ppermute | solution.py:41
  125.5 63.1 %collective-permute-start.15 = (bf16[4,192,1024]{2,1,0:T(8,128)(2,1)S(1)}, bf16[4,192,1024]{2,1,0:T(8,128)(2,1)S(1)}, u32[]{:S(2)}, u32[]{:S(2)}) collective-permute-start(bf16[4,192,1024]{2,1,0:T(8,128)(2,1)S(1)} %copy-done.6), channel_id=1, source_target_pairs={{0,1},{1,0},{2,3},{3,2},{4,5},{5,4},{6,7},{7,6},{8,9},{9,8},{10,11... | collective-permute-start | bytes 4718600 | tf_op jit(solution)/shard_map/ppermute | solution.py:41
  165.3 37.6 %collective-permute-start.14 = (bf16[4,96,1024]{2,1,0:T(8,128)(2,1)S(1)}, bf16[4,96,1024]{2,1,0:T(8,128)(2,1)S(1)}, u32[]{:S(2)}, u32[]{:S(2)}) collective-permute-start(bf16[4,96,1024]{2,1,0:T(8,128)(2,1)S(1)} %get-tuple-element.136), channel_id=1, source_target_pairs={{0,4},{1,5},{2,6},{3,7},{4,0},{5,1},{6,2},{7,3},{8,12},{9,13},{10,... | collective-permute-start | bytes 2359304 | tf_op jit(solution)/shard_map/ppermute | solution.py:41
  208.8 39.1 %collective-permute-start.18 = (bf16[4,192,1024]{2,1,0:T(8,128)(2,1)}, bf16[4,192,1024]{2,1,0:T(8,128)(2,1)}, u32[]{:S(2)}, u32[]{:S(2)}) collective-permute-start(bf16[4,192,1024]{2,1,0:T(8,128)(2,1)} %collective-permute-done.12), channel_id=1, source_target_pairs={{0,1},{1,0},{2,3},{3,2},{4,5},{5,4},{6,7},{7,6},{8,9},{9,8},{10,11... | collective-permute-start | bytes 4718600 | tf_op jit(solution)/shard_map/ppermute | solution.py:41
  210.2 37.2 %collective-permute-start.20 = (bf16[4,96,1024]{2,1,0:T(8,128)(2,1)}, bf16[4,96,1024]{2,1,0:T(8,128)(2,1)}, u32[]{:S(2)}, u32[]{:S(2)}) collective-permute-start(bf16[4,96,1024]{2,1,0:T(8,128)(2,1)} %get-tuple-element.146), channel_id=1, source_target_pairs={{0,4},{1,5},{2,6},{3,7},{4,0},{5,1},{6,2},{7,3},{8,12},{9,13},{10,... | collective-permute-start | bytes 2359304 | tf_op jit(solution)/shard_map/ppermute | solution.py:41
  217.1 34.0 %collective-permute-start.17 = (bf16[272,1024]{1,0:T(8,128)(2,1)S(1)}, bf16[272,1024]{1,0:T(8,128)(2,1)S(1)}, u32[]{:S(2)}, u32[]{:S(2)}) collective-permute-start(bf16[272,1024]{1,0:T(8,128)(2,1)S(1)} %pad_maximum_fusion.2.refs_0_), channel_id=1, source_target_pairs={{0,2},{1,3},{2,0},{3,1},{4,6},{5,7},{6,4},{7,5},{8,10},{9,11},{10,... | collective-permute-start | bytes 1671176 | tf_op jit(solution)/shard_map/ppermute | solution.py:41
  222.6 40.5 %collective-permute-start.19 = (bf16[4,96,1024]{2,1,0:T(8,128)(2,1)S(1)}, bf16[4,96,1024]{2,1,0:T(8,128)(2,1)S(1)}, u32[]{:S(2)}, u32[]{:S(2)}) collective-permute-start(bf16[4,96,1024]{2,1,0:T(8,128)(2,1)S(1)} %copy-done.36), channel_id=1, source_target_pairs={{0,1},{1,0},{2,3},{3,2},{4,5},{5,4},{6,7},{7,6},{8,9},{9,8},{10,11... | collective-permute-start | bytes 2359304 | tf_op jit(solution)/shard_map/ppermute | solution.py:41
  357.9 42.4 %collective-permute-start.44 = (bf16[256,1024]{1,0:T(8,128)(2,1)S(1)}, bf16[256,1024]{1,0:T(8,128)(2,1)S(1)}, u32[]{:S(2)}, u32[]{:S(2)}) collective-permute-start(bf16[256,1024]{1,0:T(8,128)(2,1)S(1)} %collective-permute-done.38.refs_4_), channel_id=1, source_target_pairs={{0,8},{8,0},{16,24},{24,16},{1,9},{9,1},{17,25},{25,17},{2,10},{10... | collective-permute-start | bytes 1572872 | tf_op jit(solution)/shard_map/ppermute | solution.py:41
  448.2 44.2 %collective-permute-start.50 = (bf16[4,192,1024]{2,1,0:T(8,128)(2,1)}, bf16[4,192,1024]{2,1,0:T(8,128)(2,1)}, u32[]{:S(2)}, u32[]{:S(2)}) collective-permute-start(bf16[4,192,1024]{2,1,0:T(8,128)(2,1)} %get-tuple-element.170), channel_id=1, source_target_pairs={{0,1},{1,0},{2,3},{3,2},{4,5},{5,4},{6,7},{7,6},{8,9},{9,8},{10,11... | collective-permute-start | bytes 4718600 | tf_op jit(solution)/shard_map/ppermute | solution.py:41
  450.7 39.1 %collective-permute-start.43 = (bf16[272,1024]{1,0:T(8,128)(2,1)}, bf16[272,1024]{1,0:T(8,128)(2,1)}, u32[]{:S(2)}, u32[]{:S(2)}) collective-permute-start(bf16[272,1024]{1,0:T(8,128)(2,1)} %fusion.10), channel_id=1, source_target_pairs={{0,16},{8,24},{16,0},{24,8},{1,17},{9,25},{17,1},{25,9},{2,18},{10... | collective-permute-start | bytes 1671176 | tf_op jit(solution)/shard_map/ppermute | solution.py:41
  454.6 36.6 %collective-permute-start.49 = (bf16[272,1024]{1,0:T(8,128)(2,1)}, bf16[272,1024]{1,0:T(8,128)(2,1)}, u32[]{:S(2)}, u32[]{:S(2)}) collective-permute-start(bf16[272,1024]{1,0:T(8,128)(2,1)} %fusion.7), channel_id=1, source_target_pairs={{0,2},{1,3},{2,0},{3,1},{4,6},{5,7},{6,4},{7,5},{8,10},{9,11},{10,... | collective-permute-start | bytes 1671176 | tf_op jit(solution)/shard_map/ppermute | solution.py:41
  488.4 34.5 %collective-permute-start.52 = (bf16[4,192,1024]{2,1,0:T(8,128)(2,1)}, bf16[4,192,1024]{2,1,0:T(8,128)(2,1)}, u32[]{:S(2)}, u32[]{:S(2)}) collective-permute-start(bf16[4,192,1024]{2,1,0:T(8,128)(2,1)} %get-tuple-element.172), channel_id=1, source_target_pairs={{0,1},{1,0},{2,3},{3,2},{4,5},{5,4},{6,7},{7,6},{8,9},{9,8},{10,11... | collective-permute-start | bytes 4718600 | tf_op jit(solution)/shard_map/ppermute | solution.py:41
  537.6 81.0 %collective-permute-start.54 = (bf16[2,1,4,2,32,2176]{5,4,3,2,1,0:T(8,128)(2,1)}, bf16[2,1,4,2,32,2176]{5,4,3,2,1,0:T(8,128)(2,1)S(1)}, u32[]{:S(2)}, u32[]{:S(2)}) collective-permute-start(bf16[2,1,4,2,32,2176]{5,4,3,2,1,0:T(8,128)(2,1)} %bitcast.137), channel_id=1, source_target_pairs={{0,8},{8,0},{16,24},{24,16},{1,9},{9,1},{17,25},{25,17},{2,10},{10... | collective-permute-start | bytes 6684680 | tf_op jit(solution)/shard_map/ppermute | solution.py:41
  543.3 82.2 %collective-permute-start.60 = (bf16[4,192,1024]{2,1,0:T(8,128)(2,1)}, bf16[4,192,1024]{2,1,0:T(8,128)(2,1)S(1)}, u32[]{:S(2)}, u32[]{:S(2)}) collective-permute-start(bf16[4,192,1024]{2,1,0:T(8,128)(2,1)} %get-tuple-element.187), channel_id=1, source_target_pairs={{0,1},{1,0},{2,3},{3,2},{4,5},{5,4},{6,7},{7,6},{8,9},{9,8},{10,11... | collective-permute-start | bytes 4718600 | tf_op jit(solution)/shard_map/ppermute | solution.py:41
  544.8 82.6 %collective-permute-start.61 = (bf16[4,192,1024]{2,1,0:T(8,128)(2,1)}, bf16[4,192,1024]{2,1,0:T(8,128)(2,1)S(1)}, u32[]{:S(2)}, u32[]{:S(2)}) collective-permute-start(bf16[4,192,1024]{2,1,0:T(8,128)(2,1)} %get-tuple-element.188), channel_id=1, source_target_pairs={{0,1},{1,0},{2,3},{3,2},{4,5},{5,4},{6,7},{7,6},{8,9},{9,8},{10,11... | collective-permute-start | bytes 4718600 | tf_op jit(solution)/shard_map/ppermute | solution.py:41
  546.7 71.9 %collective-permute-start.55 = (bf16[1,1,4,1,32,1024]{5,4,3,2,1,0:T(8,128)(2,1)S(1)}, bf16[1,1,4,1,32,1024]{5,4,3,2,1,0:T(8,128)(2,1)S(1)}, u32[]{:S(2)}, u32[]{:S(2)}) collective-permute-start(bf16[1,1,4,1,32,1024]{5,4,3,2,1,0:T(8,128)(2,1)S(1)} %dynamic-slice_convert_fusion.4), channel_id=1, source_target_pairs={{0,1},{1,0},{2,3},{3,2},{4,5},{5,4},{6,7},{7,6},{8,9},{9,8},{10,11... | collective-permute-start | bytes 786440 | tf_op jit(solution)/shard_map/ppermute | solution.py:41
  619.2 80.0 %collective-permute-start.56 = (bf16[1,1,4,2,32,2176]{5,4,3,2,1,0:T(8,128)(2,1)S(1)}, bf16[1,1,4,2,32,2176]{5,4,3,2,1,0:T(8,128)(2,1)S(1)}, u32[]{:S(2)}, u32[]{:S(2)}) collective-permute-start(bf16[1,1,4,2,32,2176]{5,4,3,2,1,0:T(8,128)(2,1)S(1)} %dynamic-slice_convert_fusion), channel_id=1, source_target_pairs={{0,16},{8,24},{16,0},{24,8},{1,17},{9,25},{17,1},{25,9},{2,18},{10... | collective-permute-start | bytes 3342344 | tf_op jit(solution)/shard_map/ppermute | solution.py:41
  624.2 75.0 %collective-permute-start.58 = (bf16[1,1,1,1,32,1024]{5,4,3,2,1,0:T(8,128)(2,1)S(1)}, bf16[1,1,1,1,32,1024]{5,4,3,2,1,0:T(8,128)(2,1)S(1)}, u32[]{:S(2)}, u32[]{:S(2)}) collective-permute-start(bf16[1,1,1,1,32,1024]{5,4,3,2,1,0:T(8,128)(2,1)S(1)} %get-tuple-element.238), channel_id=1, source_target_pairs={{0,4},{1,5},{2,6},{3,7},{4,0},{5,1},{6,2},{7,3},{8,12},{9,13},{10,... | collective-permute-start | bytes 196616 | tf_op jit(solution)/shard_map/ppermute | solution.py:41
  625.5 73.7 %collective-permute-start.59 = (bf16[1,1,1,1,32,1024]{5,4,3,2,1,0:T(8,128)(2,1)S(1)}, bf16[1,1,1,1,32,1024]{5,4,3,2,1,0:T(8,128)(2,1)S(1)}, u32[]{:S(2)}, u32[]{:S(2)}) collective-permute-start(bf16[1,1,1,1,32,1024]{5,4,3,2,1,0:T(8,128)(2,1)S(1)} %get-tuple-element.237), channel_id=1, source_target_pairs={{0,6},{1,7},{2,4},{3,5},{4,2},{5,3},{6,0},{7,1},{8,14},{9,15},{10,... | collective-permute-start | bytes 196616 | tf_op jit(solution)/shard_map/ppermute | solution.py:41
  627.4 107.0 %collective-permute-start.64 = (bf16[4,192,1024]{2,1,0:T(8,128)(2,1)S(1)}, bf16[4,192,1024]{2,1,0:T(8,128)(2,1)S(1)}, u32[]{:S(2)}, u32[]{:S(2)}) collective-permute-start(bf16[4,192,1024]{2,1,0:T(8,128)(2,1)S(1)} %add_convert_fusion.1), channel_id=1, source_target_pairs={{0,4},{1,5},{2,6},{3,7},{4,0},{5,1},{6,2},{7,3},{8,12},{9,13},{10,... | collective-permute-start | bytes 4718600 | tf_op jit(solution)/shard_map/ppermute | solution.py:41
  628.6 138.0 %collective-permute-start.63 = (bf16[4,192,1024]{2,1,0:T(8,128)(2,1)S(1)}, bf16[4,192,1024]{2,1,0:T(8,128)(2,1)S(1)}, u32[]{:S(2)}, u32[]{:S(2)}) collective-permute-start(bf16[4,192,1024]{2,1,0:T(8,128)(2,1)S(1)} %add_convert_fusion.2), channel_id=1, source_target_pairs={{0,4},{1,5},{2,6},{3,7},{4,0},{5,1},{6,2},{7,3},{8,12},{9,13},{10,... | collective-permute-start | bytes 4718600 | tf_op jit(solution)/shard_map/ppermute | solution.py:41
  699.6 67.1 %collective-permute-start.62 = (bf16[1,1,4,1,32,2176]{5,4,3,2,1,0:T(8,128)(2,1)S(1)}, bf16[1,1,4,1,32,2176]{5,4,3,2,1,0:T(8,128)(2,1)S(1)}, u32[]{:S(2)}, u32[]{:S(2)}) collective-permute-start(bf16[1,1,4,1,32,2176]{5,4,3,2,1,0:T(8,128)(2,1)S(1)} %dynamic-slice_convert_fusion.1), channel_id=1, source_target_pairs={{0,1},{1,0},{2,3},{3,2},{4,5},{5,4},{6,7},{7,6},{8,9},{9,8},{10,11... | collective-permute-start | bytes 1671176 | tf_op jit(solution)/shard_map/ppermute | solution.py:41
  767.7 44.2 %collective-permute-start.68 = (bf16[4,192,1024]{2,1,0:T(8,128)(2,1)S(1)}, bf16[4,192,1024]{2,1,0:T(8,128)(2,1)S(1)}, u32[]{:S(2)}, u32[]{:S(2)}) collective-permute-start(bf16[4,192,1024]{2,1,0:T(8,128)(2,1)S(1)} %add_convert_fusion), channel_id=1, source_target_pairs={{0,2},{1,3},{2,0},{3,1},{4,6},{5,7},{6,4},{7,5},{8,10},{9,11},{10,... | collective-permute-start | bytes 4718600 | tf_op jit(solution)/shard_map/ppermute | solution.py:41
  768.0 42.2 %collective-permute-start.65 = (bf16[1,1,1,1,32,2176]{5,4,3,2,1,0:T(8,128)(2,1)S(1)}, bf16[1,1,1,1,32,2176]{5,4,3,2,1,0:T(8,128)(2,1)S(1)}, u32[]{:S(2)}, u32[]{:S(2)}) collective-permute-start(bf16[1,1,1,1,32,2176]{5,4,3,2,1,0:T(8,128)(2,1)S(1)} %get-tuple-element.230), channel_id=1, source_target_pairs={{0,2},{1,3},{2,0},{3,1},{4,6},{5,7},{6,4},{7,5},{8,10},{9,11},{10,... | collective-permute-start | bytes 417800 | tf_op jit(solution)/shard_map/ppermute | solution.py:41
  770.1 40.1 %collective-permute-start.66 = (bf16[1,1,1,1,32,2176]{5,4,3,2,1,0:T(8,128)(2,1)S(1)}, bf16[1,1,1,1,32,2176]{5,4,3,2,1,0:T(8,128)(2,1)S(1)}, u32[]{:S(2)}, u32[]{:S(2)}) collective-permute-start(bf16[1,1,1,1,32,2176]{5,4,3,2,1,0:T(8,128)(2,1)S(1)} %get-tuple-element.229), channel_id=1, source_target_pairs={{0,4},{1,5},{2,6},{3,7},{4,0},{5,1},{6,2},{7,3},{8,12},{9,13},{10,... | collective-permute-start | bytes 417800 | tf_op jit(solution)/shard_map/ppermute | solution.py:41
  770.6 41.3 %collective-permute-start.67 = (bf16[1,1,1,1,32,2176]{5,4,3,2,1,0:T(8,128)(2,1)S(1)}, bf16[1,1,1,1,32,2176]{5,4,3,2,1,0:T(8,128)(2,1)S(1)}, u32[]{:S(2)}, u32[]{:S(2)}) collective-permute-start(bf16[1,1,1,1,32,2176]{5,4,3,2,1,0:T(8,128)(2,1)S(1)} %get-tuple-element.228), channel_id=1, source_target_pairs={{0,6},{1,7},{2,4},{3,5},{4,2},{5,3},{6,0},{7,1},{8,14},{9,15},{10,... | collective-permute-start | bytes 417800 | tf_op jit(solution)/shard_map/ppermute | solution.py:41
  (86 other events, 1177.9 us)

commit v7 on v6

--- a/solution.py
+++ b/solution.py
@@ -541,26 +541,30 @@
 
     arrived = {(0, 0): owned_by(0)}
     pack = pack.reshape(1, 1, 1, 1, row_block, -1)
+    out_w = w_out.reshape(1, 1, 1, 1, row_block, -1)
+    others, out_others = send(pack, 0), send(out_w, 0)
     arrived[1, 0] = swap(arrived[0, 0], "fsdp", 1)
-    pack = merge(pack, send(pack, 0), 0)
-    others = send(pack, 1)
-    near = [swap(after(owned_by(1), pack), "fsdp", HOP_BIT)]
-    far_own = far_swaps(after(arrived[0, 0], pack))
-    pack, others, arrived[1, 0] = join((pack, others, arrived[1, 0]))
-    pack = merge(pack, others, 1)
-    others = send(pack, 2)
-    pack, others, near = join((pack, others, near))
-    pack = merge(pack, others, 2)
-    others = send(pack, 3)
-    out_w = after(w_out, pack).reshape(1, 1, 1, 1, row_block, -1)
-    arrived[HOP_BIT, 0] = near[0]
-    near_low = swap(after(near[0], pack), "fsdp", 1)
-    out_others = send(out_w, 0)
     pack, others, out_w, out_others = join((pack, others, out_w, out_others))
-    far_near = [far_swaps(after(near[0][:, :half], others))]
+    pack, out_w = merge(pack, others, 0), merge(out_w, out_others, 0)
+    others, out_others = send(pack, 1), send(out_w, 1)
+    near = swap(after(owned_by(1), pack), "fsdp", HOP_BIT)
+    far_own = [far_swaps(after(arrived[0, 0][:, :half], pack))]
+    pack, others, out_w, out_others, arrived[1, 0] = join(
+        (pack, others, out_w, out_others, arrived[1, 0])
+    )
+    pack, out_w = merge(pack, others, 1), merge(out_w, out_others, 1)
+    others, out_others = send(pack, 2), send(out_w, 2)
+    pack, others, out_w, out_others, near, far_own = join(
+        (pack, others, out_w, out_others, near, far_own)
+    )
+    far_own.append(far_swaps(after(arrived[0, 0][:, half:], others)))
+    pack, out_w = merge(pack, others, 2), merge(out_w, out_others, 2)
+    others, out_others = send(pack, 3), send(out_w, 3)
+    arrived[HOP_BIT, 0] = near
+    near_low = swap(after(near, pack), "fsdp", 1)
+    far_near = [far_swaps(after(near[:, :half], pack))]
+    pack, others = join((pack, others))
     packed = merge(pack, others, 3).reshape(model_width, -1)
-    out_w = merge(out_w, out_others, 0)
-    out_others = send(out_w, 1)
     qkv_width = model_width + 2 * kv_width
     qkv_w = packed[:, :qkv_width]
     router_float = packed[:, qkv_width : qkv_width + experts].astype(f32)
@@ -574,12 +578,12 @@
     cos_lanes, sin_lanes = rotary_lanes(seq_len)
     qkv = dot(normed, qkv_w)
     qkv, out_w, out_others, far_own = join((qkv, out_w, out_others, far_own))
-    far_near.append(far_swaps(after(near[0][:, half:], qkv)))
-    out_w = merge(out_w, out_others, 1)
-    out_others = send(out_w, 2)
-    for m, piece in far_own.items():
-        arrived[m, 0] = piece
-        arrived[m ^ 1, 0] = swap(piece, "fsdp", 1)
+    far_near.append(far_swaps(after(near[:, half:], qkv)))
+    out_w = merge(out_w, out_others, 3).reshape(model_width, -1)
+    for i, pieces in enumerate(far_own):
+        for m, piece in pieces.items():
+            arrived[m, i * half] = piece
+            arrived[m ^ 1, i * half] = swap(piece, "fsdp", 1)
     rotated, mixed_rows = kernel_call(
         attention_forward,
         (
@@ -589,19 +593,8 @@
         (lengths, qkv, cos_lanes, sin_lanes),
         first_smem=True,
     )
-    mixed_rows, out_w, out_others, far_near[0], near_low = join(
-        (mixed_rows, out_w, out_others, far_near[0], near_low)
-    )
+    mixed_rows, far_near[0], near_low = join((mixed_rows, far_near[0], near_low))
     arrived[HOP_BIT ^ 1, 0] = near_low
-    out_w = merge(out_w, out_others, 2)
-    out_w = merge(out_w, send(out_w, 3), 3).reshape(model_width, -1)
-    for i, pieces in enumerate(far_near):
-        for m, piece in pieces.items():
-            arrived[m ^ HOP_BIT, i * half] = piece
-            arrived[m ^ HOP_BIT ^ 1, i * half] = swap(piece, "fsdp", 1)
-    expert_w = jnp.zeros((held, shards, shard.shape[1], model_width), bf16)
-    for (m, row), piece in arrived.items():
-        expert_w = lax.dynamic_update_slice(expert_w, piece[:, None], (0, fsdp_at ^ m, row, 0))
     hidden = tok_float + residual_scale * dot(mixed_rows, out_w)
     inv_two = lax.rsqrt(jnp.mean(hidden * hidden, axis=1, keepdims=True) + epsilon)
     normed_ffn = hidden * inv_two * gain_second
@@ -621,6 +614,14 @@
     )
     count = rows_y * CORES
     rows = count * CAP
+    outgoing, far_near, arrived = join((outgoing, far_near, arrived))
+    for i, pieces in enumerate(far_near):
+        for m, piece in pieces.items():
+            arrived[m ^ HOP_BIT, i * half] = piece
+            arrived[m ^ HOP_BIT ^ 1, i * half] = swap(piece, "fsdp", 1)
+    expert_w = jnp.zeros((held, shards, shard.shape[1], model_width), bf16)
+    for (m, row), piece in arrived.items():
+        expert_w = lax.dynamic_update_slice(expert_w, piece[:, None], (0, fsdp_at ^ m, row, 0))
     set_shape = jax.ShapeDtypeStruct((rows_y, seq_len, model_width), bf16)
     token_sets = []
 
@@ -741,13 +742,7 @@
     order = (rows_y, CORES, units, 2, row_block, -1)
     mixed_grad = dot_nt(attended_grad, out_w).astype(bf16)
     low_sum(first_low)
-    far_got = {}
     last_bit = far_bits[-1]
-
-    def start_far(m):
-        far_got[m ^ last_bit] = far_send(last_bit, m)
-
-    start_far(first_low)
     out_sum = halve(dot_tn(mixed_rows, attended_grad).astype(bf16).reshape(order), 3)
     lane = jnp.arange(128, dtype=jnp.int32)[None, :]
     ones = jnp.ones((seq_len, 1), f32)
@@ -763,6 +758,26 @@
         ),
         preferred_element_type=f32,
     )
+    early = [m for m in order_of[1:] if m & last_bit]
+    chunks = [(m, i) for m in order_of if m & last_bit for i in range(2)]
+    far_got = {}
+
+    def far_slot(slot, earlier):
+        size = len(chunks) // 4
+        for m, i in chunks[slot * size : slot * size + size]:
+            piece = sums_of[m][:, i * half : i * half + half].astype(bf16)
+            far_got[m ^ last_bit, i] = swap(after(piece, earlier), "fsdp", last_bit)
+
+    def far_sum(m):
+        sums_of[m] = sums_of[m] + jnp.concatenate(
+            [far_got[m, i].astype(f32) for i in range(2)], axis=1
+        )
+
+    far_slot(0, attended_grad)
+    mixed_grad, got = join((mixed_grad, [low_got[m] for m in early]))
+    low_got |= dict(zip(early, got, strict=True))
+    for m in early:
+        low_sum(m)
     qkv_grad = kernel_call(
         attention_backward,
         jax.ShapeDtypeStruct((seq_len, qkv_width), bf16),
@@ -770,14 +785,8 @@
         first_smem=True,
         scratch=(pltpu.VMEM((seq_len, model_width + kv_width), f32),),
     )
-    steps_left = order_of[1:]
-    wait_for = steps_left[: len(steps_left) // 3]
-    qkv_grad, out_sum, got = join((qkv_grad, out_sum, [low_got[m] for m in wait_for]))
-    low_got |= dict(zip(wait_for, got, strict=True))
-    for m in wait_for:
-        low_sum(m)
-        if m & last_bit:
-            start_far(m)
+    qkv_grad, out_sum, far_got = join((qkv_grad, out_sum, far_got))
+    far_slot(1, qkv_grad)
     out_sum = halve(total(*out_sum), 1)
     share = jax.ShapeDtypeStruct((rows_y, shards * row_block, qkv_width + 128), bf16)
     *grads, token_grad = kernel_call(
@@ -797,29 +806,37 @@
         first_smem=True,
         scratch=(pltpu.VMEM((model_width, qkv_width + 128), bf16),),
     )
-    grads, out_sum = join((grads, out_sum))
+    later = [m for m in order_of[:-1] if not m & last_bit]
+    grads, out_sum, got = join((grads, out_sum, [low_got[m] for m in later]))
+    low_got |= dict(zip(later, got, strict=True))
+    for m in later:
+        low_sum(m)
     grads = [g.reshape(rows_y, 1, units, 2, row_block, -1) for g in grads]
     part_sum = (grads[0].astype(f32), [swap(g, "dp", m + 1) for m, g in enumerate(grads[1:])])
     out_sum = halve(total(*out_sum), 2)
-    part_sum, out_sum = join((part_sum, out_sum))
+    part_sum, out_sum, far_got = join((part_sum, out_sum, far_got))
+    far_slot(2, part_sum)
     part_sum = halve(total(*part_sum), 1)
     out_sum = halve(total(*out_sum), 0)
-    part_sum, out_sum, low_got = join((part_sum, out_sum, low_got))
-    for m in order_of:
-        if m not in sums_of:
-            low_sum(m)
-            if m & last_bit:
-                start_far(m)
+    part_sum, out_sum, low_got[0], far_got = join((part_sum, out_sum, low_got[0], far_got))
+    far_slot(3, part_sum)
+    low_sum(0)
+    if len(far_bits) == 1:
+        far_sum(HOP_BIT)
+        hop_got = far_send(HOP_BIT, HOP_BIT)
     out_grad_w = total(*out_sum).reshape(row_block, -1)
     part_sum = halve(total(*part_sum), 2)
     part_sum, far_got = join((part_sum, far_got))
-    for m, got in far_got.items():
-        sums_of[m] = sums_of[m] + got.astype(f32)
-    for bit in far_bits[-2::-1]:
-        far_got = {m ^ bit: far_send(bit, m) for m in sums_of if m & bit and m < 2 * bit}
-        for m, got in far_got.items():
-            sums_of[m] = sums_of[m] + got.astype(f32)
-    hop_got = far_send(HOP_BIT, HOP_BIT)
+    if len(far_bits) == 1:
+        far_sum(0)
+    else:
+        for m in {m for m, _ in far_got}:
+            far_sum(m)
+        for bit in far_bits[-2::-1]:
+            got = {m ^ bit: far_send(bit, m) for m in sums_of if m & bit and m < 2 * bit}
+            for m, piece in got.items():
+                sums_of[m] = sums_of[m] + piece.astype(f32)
+        hop_got = far_send(HOP_BIT, HOP_BIT)
     part_sum, hop_got = join((halve(total(*part_sum), 0), hop_got))
     small = total(*part_sum).reshape(row_block, -1)
     expert_out = jnp.zeros((owned, shard.shape[1], model_width), f32)

time: 825 us -> 713 us (0.86)
  waiting for transfers between devices: 504 us -> 382 us
  local copies, waits for them, and re-layouts: 52.1 us -> 61.9 us
    ppermute x69 -> x73, waiting for transfers between devices: 504 us -> 382 us  [swap(): lax.ppermute(values, axis, [(i, i ^ mask) for i in range(lax.axis_size(ax...]
    dynamic_update_slice x10 -> x12, local copies, waits for them, and re-layouts: 17.9 us -> 25.1 us  [on_device(): lax.dynamic_update_slice(expert_w, piece[:, None], (0, fsdp_at ^ m, row, 0))]
    ppermute x69 -> x73, starting transfers between devices: 70.1 us -> 69 us  [swap(): lax.ppermute(values, axis, [(i, i ^ mask) for i in range(lax.axis_size(ax...]
  transfers between devices with their start and end apart: 69 -> 73, of which waited for: 33 -> 30; matrix products, arithmetic and copies ran while one was open for 11% -> 15% of each run, Pallas kernels for 10% -> 12%
where the time goes in v7:
time: 713 us; the launch traced here: 707 us
  waiting for transfers between devices  382 us (54%)
  Pallas kernels  121 us (17%)
  starting transfers between devices  69 us (10%)
  local copies, waits for them, and re-layouts  61.9 us (9%)
  other arithmetic  56.1 us (8%)
  matrix products  11.5 us (2%)
    ppermute x73, waiting for transfers between devices, swap(): lax.ppermute(values, axis, [(i, i ^ mask) for i in range(lax.axis_size(ax...  382 us
    pallas_call x4, Pallas kernels, expert_call(): pl.pallas_call(body, grid=(held,), out_shape=out_shape, in_specs=[smem(),...  70.4 us
    ppermute x73, starting transfers between devices, swap(): lax.ppermute(values, axis, [(i, i ^ mask) for i in range(lax.axis_size(ax...  69 us
    pallas_call x3, Pallas kernels, kernel_call(): pl.pallas_call(body, out_shape=out_shape, in_specs=specs, out_specs=jax.t...  31 us
    dynamic_update_slice x12, local copies, waits for them, and re-layouts, on_device(): lax.dynamic_update_slice(expert_w, piece[:, None], (0, fsdp_at ^ m, row, 0))  25.1 us
    pallas_call x1, Pallas kernels, on_device(): pl.pallas_call(functools.partial(expert_weight_grads, HOPS), grid=(held,)...  19.4 us
  transfers between devices with their start and end apart: 73, of which 30 were waited for; matrix products, arithmetic and copies ran while one was open for 15% of the time, Pallas kernels for 12%

profile of v7, /device:TPU:0, one launch (start us, length us, event | category | flops | bytes accessed | tf_op | source)
XLA Modules:
  0.0 707.1 jit_solution(8087018617785523280)
XLA Ops:
  10.4 3.5 collective-permute-start.4
  22.9 4.1 collective-permute-done.4
  33.4 14.9 %collective-permute-done.7 = bf16[1,1,4,1,32,1024]{5,4,3,2,1,0:T(8,128)(2,1)} collective-permute-done((bf16[1,1,4,1,32,1024]{5,4,3,2,1,0:T(8,128)(2,1)S(1)}, bf16[1,1,4,1,32,1024]{5,4,3,2,1,0:T(8,128)(2,1)}, u32[]{:S(2)}, u32[]{:S(2)}) %collective-permute-start.7) | collective-permute-done | bytes 262176 | tf_op jit(solution)/shard_map/ppermute | solution.py:41
  48.3 13.0 %collective-permute-done.8 = bf16[4,192,1024]{2,1,0:T(8,128)(2,1)} collective-permute-done((bf16[4,192,1024]{2,1,0:T(8,128)(2,1)}, bf16[4,192,1024]{2,1,0:T(8,128)(2,1)}, u32[]{:S(2)}, u32[]{:S(2)}) %collective-permute-start.8) | collective-permute-done | bytes 1572896 | tf_op jit(solution)/shard_map/ppermute | solution.py:41
  68.7 32.4 %collective-permute-done.12 = bf16[4,96,1024]{2,1,0:T(8,128)(2,1)} collective-permute-done((bf16[4,96,1024]{2,1,0:T(8,128)(2,1)}, bf16[4,96,1024]{2,1,0:T(8,128)(2,1)}, u32[]{:S(2)}, u32[]{:S(2)}) %collective-permute-start.12) | collective-permute-done | bytes 786464 | tf_op jit(solution)/shard_map/ppermute | solution.py:41
  113.4 3.5 maximum_select_fusion
  121.8 42.6 %collective-permute-done.15 = bf16[4,96,1024]{2,1,0:T(8,128)(2,1)} collective-permute-done((bf16[4,96,1024]{2,1,0:T(8,128)(2,1)S(1)}, bf16[4,96,1024]{2,1,0:T(8,128)(2,1)}, u32[]{:S(2)}, u32[]{:S(2)}) %collective-permute-start.15) | collective-permute-done | bytes 786464 | tf_op jit(solution)/shard_map/ppermute | solution.py:41
  165.4 9.7 %shard_map.237 = (bf16[256,2048]{1,0:T(8,128)(2,1)}, bf16[256,1024]{1,0:T(8,128)(2,1)}) custom-call(s32[1]{0:T(128)} %copy.90.length_ref, f32[256,2048]{1,0:T(8,128)} %fusion.qkv_ref, f32[256,128]{1,0:T(8,128)} %get-tuple-element.324.cos_ref, f32[256,128]{1,0:T(8,128)} %get-tuple-element.325.sin_ref), custom_call_target="tpu_custom_call" | custom-call | tf_op jit(solution)/shard_map/pallas_call | solution.py:60
  175.1 6.1 collective-permute-done.16
  186.6 33.3 %collective-permute-done.18 = bf16[4,96,1024]{2,1,0:T(8,128)(2,1)} collective-permute-done((bf16[4,96,1024]{2,1,0:T(8,128)(2,1)}, bf16[4,96,1024]{2,1,0:T(8,128)(2,1)}, u32[]{:S(2)}, u32[]{:S(2)}) %collective-permute-start.18) | collective-permute-done | bytes 786464 | tf_op jit(solution)/shard_map/ppermute | solution.py:41
  225.5 6.1 broadcast_in_dim.119
  251.4 8.0 %collective-permute-done.30.refs_2_ = bf16[272,1024]{1,0:T(8,128)(2,1)S(1)} collective-permute-done((bf16[272,1024]{1,0:T(8,128)(2,1)S(1)}, bf16[272,1024]{1,0:T(8,128)(2,1)S(1)}, u32[]{:S(2)}, u32[]{:S(2)}) %collective-permute-start.30) | collective-permute-done | bytes 557088 | tf_op jit(solution)/shard_map/ppermute | solution.py:41
  266.6 14.0 %shard_map.238 = (bf16[2,256,1024]{2,1,0:T(8,128)(2,1)}, bf16[2,256,1024]{2,1,0:T(8,128)(2,1)}) custom-call(s32[1]{0:T(128)} %bitcast.8.first_ref, bf16[4,8,192,1024]{3,2,1,0:T(8,128)(2,1)} %bitcast_dynamic-update-slice_fusion.11.weights_ref, bf16[272,1024]{1,0:T(8,128)(2,1)} %copy-done.3, bf16[272,1024]{1,0:T(8,128)(2,1)} %copy-done.13, ...), custom_call_target="tpu_custom_call" | custom-call | tf_op jit(solution)/shard_map/pallas_call | solution.py:80
  282.3 13.8 %shard_map.239 = (bf16[2,256,1024]{2,1,0:T(8,128)(2,1)}, bf16[2,256,1024]{2,1,0:T(8,128)(2,1)}) custom-call(s32[1]{0:T(128)} %bitcast.8.first_ref, bf16[4,8,192,1024]{3,2,1,0:T(8,128)(2,1)} %bitcast_dynamic-update-slice_fusion.11.weights_ref, bf16[272,1024]{1,0:T(8,128)(2,1)} %copy-done.12, bf16[272,1024]{1,0:T(8,128)(2,1)} %copy-done.16, ...), custom_call_target="tpu_custom_call" | custom-call | tf_op jit(solution)/shard_map/pallas_call | solution.py:80
  303.4 11.6 %collective-permute-done.33 = bf16[256,1024]{1,0:T(8,128)(2,1)S(1)} collective-permute-done((bf16[256,1024]{1,0:T(8,128)(2,1)S(1)}, bf16[256,1024]{1,0:T(8,128)(2,1)S(1)}, u32[]{:S(2)}, u32[]{:S(2)}) %collective-permute-start.33) | collective-permute-done | bytes 524320 | tf_op jit(solution)/shard_map/ppermute | solution.py:41
  316.9 8.7 %collective-permute-done.28 = bf16[256,1024]{1,0:T(8,128)(2,1)S(1)} collective-permute-done((bf16[256,1024]{1,0:T(8,128)(2,1)}, bf16[256,1024]{1,0:T(8,128)(2,1)S(1)}, u32[]{:S(2)}, u32[]{:S(2)}) %collective-permute-start.28) | collective-permute-done | bytes 524320 | tf_op jit(solution)/shard_map/ppermute | solution.py:41
  331.8 11.0 %collective-permute-done.40.refs_4_ = bf16[256,1024]{1,0:T(8,128)(2,1)S(1)} collective-permute-done((bf16[256,1024]{1,0:T(8,128)(2,1)S(1)}, bf16[256,1024]{1,0:T(8,128)(2,1)S(1)}, u32[]{:S(2)}, u32[]{:S(2)}) %collective-permute-start.40) | collective-permute-done | bytes 524320 | tf_op jit(solution)/shard_map/ppermute | solution.py:41
  343.9 10.3 %collective-permute-done.47.refs_6_ = bf16[256,1024]{1,0:T(8,128)(2,1)S(1)} collective-permute-done((bf16[256,1024]{1,0:T(8,128)(2,1)S(1)}, bf16[256,1024]{1,0:T(8,128)(2,1)S(1)}, u32[]{:S(2)}, u32[]{:S(2)}) %collective-permute-start.47) | collective-permute-done | bytes 524320 | tf_op jit(solution)/shard_map/ppermute | solution.py:41
  363.1 21.5 %shard_map.240 = (bf16[2,272,1024]{2,1,0:T(8,128)(2,1)}, bf16[2,272,1024]{2,1,0:T(8,128)(2,1)}, bf16[4,384,1024]{2,1,0:T(8,128)(2,1)}, bf16[4,384,1024]{2,1,0:T(...) custom-call(s32[1]{0:T(128)} %bitcast.8.first_ref, ...), custom_call_target="tpu_custom_call" | custom-call | tf_op jit(solution)/shard_map/pallas_call | solution.py:80
  386.2 21.1 %shard_map.241 = (bf16[2,272,1024]{2,1,0:T(8,128)(2,1)}, bf16[2,272,1024]{2,1,0:T(8,128)(2,1)}, bf16[4,384,1024]{2,1,0:T(8,128)(2,1)}, bf16[4,384,1024]{2,1,0:T(...) custom-call(s32[1]{0:T(128)} %bitcast.8.first_ref, ...), custom_call_target="tpu_custom_call" | custom-call | tf_op jit(solution)/shard_map/pallas_call | solution.py:80
  413.3 19.4 %shard_map.242 = (bf16[4,192,1024]{2,1,0:T(8,128)(2,1)}, bf16[4,192,1024]{2,1,0:T(8,128)(2,1)}, bf16[4,192,1024]{2,1,0:T(8,128)(2,1)}, bf16[4,192,1024]{2,1,0:T(...) custom-call(s32[1]{0:T(128)} %bitcast.44.at_ref, ...), custom_call_target="tpu_custom_call" | custom-call | tf_op jit(solution)/shard_map/pallas_call | solution.py:685
  442.3 27.0 %collective-permute-done.37 = f32[8,128]{1,0:T(8,128)S(1)} collective-permute-done((f32[8,128]{1,0:T(8,128)S(1)}, f32[8,128]{1,0:T(8,128)S(1)}, u32[]{:S(2)}, u32[]{:S(2)}) %collective-permute-start.37) | collective-permute-done | bytes 4128 | tf_op jit(solution)/shard_map/ppermute | solution.py:41
  497.2 13.3 %collective-permute-done.53 = bf16[4,192,1024]{2,1,0:T(8,128)(2,1)} collective-permute-done((bf16[4,192,1024]{2,1,0:T(8,128)(2,1)}, bf16[4,192,1024]{2,1,0:T(8,128)(2,1)}, u32[]{:S(2)}, u32[]{:S(2)}) %collective-permute-start.53) | collective-permute-done | bytes 1572896 | tf_op jit(solution)/shard_map/ppermute | solution.py:41
  510.5 12.3 %shard_map.243.qkv_grad_ref = bf16[256,2048]{1,0:T(8,128)(2,1)} custom-call(s32[1]{0:T(128)} %copy.90.length_ref, bf16[256,2048]{1,0:T(8,128)(2,1)} %get-tuple-element.201.rot_ref, bf16[256,1024]{1,0:T(8,128)(2,1)} %convolution_convert_fusion.1.grad_ref, f32[256,128]{1,0:T(8,128)} %get-tuple-element.324.cos_ref, f32[256,128]{1,0:T(8,128)} %get-tuple-element.325.sin_ref), custom_call_target="tpu_custom_call" | custom-call | tf_op jit(solution)/shard_map/pallas_call | solution.py:60
  522.7 4.6 collective-permute-done.55
  532.3 9.0 %shard_map.244 = (bf16[2,256,2176]{2,1,0:T(8,128)(2,1)}, bf16[2,256,2176]{2,1,0:T(8,128)(2,1)}, f32[256,1024]{1,0:T(8,128)}) custom-call(s32[1]{0:T(128)} %bitcast.39.core_ref, bf16[256,2048]{1,0:T(8,128)(2,1)} %shard_map.243.qkv_grad_ref, bf16[256,1024]{1,0:T(8,128)(2,1)} %copy-done.19, bf16[1024,2176]{1,0:T(8,128)(2,1)} %bitcast.133, ...), custom_call_target="tpu_custom_call" | custom-call | tf_op jit(solution)/shard_map/pallas_call | solution.py:60
  555.9 34.8 %collective-permute-done.59 = bf16[1,1,4,1,32,1024]{5,4,3,2,1,0:T(8,128)(2,1)S(1)} collective-permute-done((bf16[1,1,4,1,32,1024]{5,4,3,2,1,0:T(8,128)(2,1)S(1)}, bf16[1,1,4,1,32,1024]{5,4,3,2,1,0:T(8,128)(2,1)S(1)}, u32[]{:S(2)}, u32[]{:S(2)}) %collective-permute-start.59) | collective-permute-done | bytes 262176 | tf_op jit(solution)/shard_map/ppermute | solution.py:41
  598.6 13.1 %collective-permute-done.62 = bf16[1,1,1,1,32,1024]{5,4,3,2,1,0:T(8,128)(2,1)S(1)} collective-permute-done((bf16[1,1,1,1,32,1024]{5,4,3,2,1,0:T(8,128)(2,1)S(1)}, bf16[1,1,1,1,32,1024]{5,4,3,2,1,0:T(8,128)(2,1)S(1)}, u32[]{:S(2)}, u32[]{:S(2)}) %collective-permute-start.62) | collective-permute-done | bytes 65568 | tf_op jit(solution)/shard_map/ppermute | solution.py:41
  611.7 20.6 %collective-permute-done.63 = bf16[1,1,1,1,32,1024]{5,4,3,2,1,0:T(8,128)(2,1)S(1)} collective-permute-done((bf16[1,1,1,1,32,1024]{5,4,3,2,1,0:T(8,128)(2,1)S(1)}, bf16[1,1,1,1,32,1024]{5,4,3,2,1,0:T(8,128)(2,1)S(1)}, u32[]{:S(2)}, u32[]{:S(2)}) %collective-permute-start.63) | collective-permute-done | bytes 65568 | tf_op jit(solution)/shard_map/ppermute | solution.py:41
  640.3 6.8 collective-permute-done.67
  647.2 23.1 %collective-permute-done.68 = bf16[4,96,1024]{2,1,0:T(8,128)(2,1)S(1)} collective-permute-done((bf16[4,96,1024]{2,1,0:T(8,128)(2,1)S(1)}, bf16[4,96,1024]{2,1,0:T(8,128)(2,1)S(1)}, u32[]{:S(2)}, u32[]{:S(2)}) %collective-permute-start.68) | collective-permute-done | bytes 786464 | tf_op jit(solution)/shard_map/ppermute | solution.py:41
  676.8 21.7 %collective-permute-done.69 = bf16[1,1,1,1,32,2176]{5,4,3,2,1,0:T(8,128)(2,1)S(1)} collective-permute-done((bf16[1,1,1,1,32,2176]{5,4,3,2,1,0:T(8,128)(2,1)S(1)}, bf16[1,1,1,1,32,2176]{5,4,3,2,1,0:T(8,128)(2,1)S(1)}, u32[]{:S(2)}, u32[]{:S(2)}) %collective-permute-start.69) | collective-permute-done | bytes 139296 | tf_op jit(solution)/shard_map/ppermute | solution.py:41
  (346 shorter events, 206.6 us)
Async XLA Ops:
  26.9 34.4 %collective-permute-start.8 = (bf16[4,192,1024]{2,1,0:T(8,128)(2,1)}, bf16[4,192,1024]{2,1,0:T(8,128)(2,1)}, u32[]{:S(2)}, u32[]{:S(2)}) collective-permute-start(bf16[4,192,1024]{2,1,0:T(8,128)(2,1)} %get-tuple-element.186), channel_id=1, source_target_pairs={{0,1},{1,0},{2,3},{3,2},{4,5},{5,4},{6,7},{7,6},{8,9},{9,8},{10,11... | collective-permute-start | bytes 4718600 | tf_op jit(solution)/shard_map/ppermute | solution.py:41
  33.4 67.7 %collective-permute-start.11 = (bf16[4,192,1024]{2,1,0:T(8,128)(2,1)}, bf16[4,192,1024]{2,1,0:T(8,128)(2,1)}, u32[]{:S(2)}, u32[]{:S(2)}) collective-permute-start(bf16[4,192,1024]{2,1,0:T(8,128)(2,1)} %get-tuple-element.160), channel_id=1, source_target_pairs={{0,2},{1,3},{2,0},{3,1},{4,6},{5,7},{6,4},{7,5},{8,10},{9,11},{10,... | collective-permute-start | bytes 4718600 | tf_op jit(solution)/shard_map/ppermute | solution.py:41
  64.2 37.8 %collective-permute-start.9 = (bf16[2,1,4,1,32,2176]{5,4,3,2,1,0:T(8,128)(2,1)}, bf16[2,1,4,1,32,2176]{5,4,3,2,1,0:T(8,128)(2,1)}, u32[]{:S(2)}, u32[]{:S(2)}) collective-permute-start(bf16[2,1,4,1,32,2176]{5,4,3,2,1,0:T(8,128)(2,1)} %maximum_select_fusion.3), channel_id=1, source_target_pairs={{0,1},{1,0},{2,3},{3,2},{4,5},{5,4},{6,7},{7,6},{8,9},{9,8},{10,11... | collective-permute-start | bytes 3342344 | tf_op jit(solution)/shard_map/ppermute | solution.py:41
  67.0 34.1 %collective-permute-start.12 = (bf16[4,96,1024]{2,1,0:T(8,128)(2,1)}, bf16[4,96,1024]{2,1,0:T(8,128)(2,1)}, u32[]{:S(2)}, u32[]{:S(2)}) collective-permute-start(bf16[4,96,1024]{2,1,0:T(8,128)(2,1)} %get-tuple-element.161), channel_id=1, source_target_pairs={{0,4},{1,5},{2,6},{3,7},{4,0},{5,1},{6,2},{7,3},{8,12},{9,13},{10,... | collective-permute-start | bytes 2359304 | tf_op jit(solution)/shard_map/ppermute | solution.py:41
  68.1 33.0 %collective-permute-start.10 = (bf16[2,1,4,1,32,1024]{5,4,3,2,1,0:T(8,128)(2,1)S(1)}, bf16[2,1,4,1,32,1024]{5,4,3,2,1,0:T(8,128)(2,1)S(1)}, u32[]{:S(2)}, u32[]{:S(2)}) collective-permute-start(bf16[2,1,4,1,32,1024]{5,4,3,2,1,0:T(8,128)(2,1)S(1)} %maximum_select_fusion.5), channel_id=1, source_target_pairs={{0,1},{1,0},{2,3},{3,2},{4,5},{5,4},{6,7},{7,6},{8,9},{9,8},{10,11... | collective-permute-start | bytes 1572872 | tf_op jit(solution)/shard_map/ppermute | solution.py:41
  106.9 74.4 %collective-permute-start.17 = (bf16[4,192,1024]{2,1,0:T(8,128)(2,1)}, bf16[4,192,1024]{2,1,0:T(8,128)(2,1)}, u32[]{:S(2)}, u32[]{:S(2)}) collective-permute-start(bf16[4,192,1024]{2,1,0:T(8,128)(2,1)} %collective-permute-done.11), channel_id=1, source_target_pairs={{0,1},{1,0},{2,3},{3,2},{4,5},{5,4},{6,7},{7,6},{8,9},{9,8},{10,11... | collective-permute-start | bytes 4718600 | tf_op jit(solution)/shard_map/ppermute | solution.py:41
  110.2 54.2 %collective-permute-start.14 = (bf16[2,1,4,2,32,1024]{5,4,3,2,1,0:T(8,128)(2,1)S(1)}, bf16[2,1,4,2,32,1024]{5,4,3,2,1,0:T(8,128)(2,1)S(1)}, u32[]{:S(2)}, u32[]{:S(2)}) collective-permute-start(bf16[2,1,4,2,32,1024]{5,4,3,2,1,0:T(8,128)(2,1)S(1)} %maximum_select_fusion.4), channel_id=1, source_target_pairs={{0,8},{8,0},{16,24},{24,16},{1,9},{9,1},{17,25},{25,17},{2,10},{10... | collective-permute-start | bytes 3145736 | tf_op jit(solution)/shard_map/ppermute | solution.py:41
  110.4 54.0 %collective-permute-start.15 = (bf16[4,96,1024]{2,1,0:T(8,128)(2,1)S(1)}, bf16[4,96,1024]{2,1,0:T(8,128)(2,1)}, u32[]{:S(2)}, u32[]{:S(2)}) collective-permute-start(bf16[4,96,1024]{2,1,0:T(8,128)(2,1)S(1)} %copy-done.37), channel_id=1, source_target_pairs={{0,4},{1,5},{2,6},{3,7},{4,0},{5,1},{6,2},{7,3},{8,12},{9,13},{10,... | collective-permute-start | bytes 2359304 | tf_op jit(solution)/shard_map/ppermute | solution.py:41
  110.5 70.8 %collective-permute-start.16 = (bf16[4,96,1024]{2,1,0:T(8,128)(2,1)}, bf16[4,96,1024]{2,1,0:T(8,128)(2,1)}, u32[]{:S(2)}, u32[]{:S(2)}) collective-permute-start(bf16[4,96,1024]{2,1,0:T(8,128)(2,1)} %get-tuple-element.173), channel_id=1, source_target_pairs={{0,4},{1,5},{2,6},{3,7},{4,0},{5,1},{6,2},{7,3},{8,12},{9,13},{10,... | collective-permute-start | bytes 2359304 | tf_op jit(solution)/shard_map/ppermute | solution.py:41
  183.1 36.8 %collective-permute-start.18 = (bf16[4,96,1024]{2,1,0:T(8,128)(2,1)}, bf16[4,96,1024]{2,1,0:T(8,128)(2,1)}, u32[]{:S(2)}, u32[]{:S(2)}) collective-permute-start(bf16[4,96,1024]{2,1,0:T(8,128)(2,1)} %get-tuple-element.179), channel_id=1, source_target_pairs={{0,4},{1,5},{2,6},{3,7},{4,0},{5,1},{6,2},{7,3},{8,12},{9,13},{10,... | collective-permute-start | bytes 2359304 | tf_op jit(solution)/shard_map/ppermute | solution.py:41
  183.2 36.7 %collective-permute-start.19 = (bf16[4,96,1024]{2,1,0:T(8,128)(2,1)}, bf16[4,96,1024]{2,1,0:T(8,128)(2,1)S(1)}, u32[]{:S(2)}, u32[]{:S(2)}) collective-permute-start(bf16[4,96,1024]{2,1,0:T(8,128)(2,1)} %collective-permute-done.12), channel_id=1, source_target_pairs={{0,1},{1,0},{2,3},{3,2},{4,5},{5,4},{6,7},{7,6},{8,9},{9,8},{10,11... | collective-permute-start | bytes 2359304 | tf_op jit(solution)/shard_map/ppermute | solution.py:41
  184.8 35.2 %collective-permute-start.20 = (bf16[4,96,1024]{2,1,0:T(8,128)(2,1)}, bf16[4,96,1024]{2,1,0:T(8,128)(2,1)}, u32[]{:S(2)}, u32[]{:S(2)}) collective-permute-start(bf16[4,96,1024]{2,1,0:T(8,128)(2,1)} %collective-permute-done.15), channel_id=1, source_target_pairs={{0,1},{1,0},{2,3},{3,2},{4,5},{5,4},{6,7},{7,6},{8,9},{9,8},{10,11... | collective-permute-start | bytes 2359304 | tf_op jit(solution)/shard_map/ppermute | solution.py:41
  221.9 43.9 %collective-permute-start.24 = (bf16[272,1024]{1,0:T(8,128)(2,1)S(1)}, bf16[272,1024]{1,0:T(8,128)(2,1)S(1)}, u32[]{:S(2)}, u32[]{:S(2)}) collective-permute-start(bf16[272,1024]{1,0:T(8,128)(2,1)S(1)} %pad_maximum_fusion.2.refs_0_), channel_id=1, source_target_pairs={{0,8},{8,0},{16,24},{24,16},{1,9},{9,1},{17,25},{25,17},{2,10},{10... | collective-permute-start | bytes 1671176 | tf_op jit(solution)/shard_map/ppermute | solution.py:41
  225.0 38.8 %collective-permute-start.23 = (bf16[4,96,1024]{2,1,0:T(8,128)(2,1)}, bf16[4,96,1024]{2,1,0:T(8,128)(2,1)}, u32[]{:S(2)}, u32[]{:S(2)}) collective-permute-start(bf16[4,96,1024]{2,1,0:T(8,128)(2,1)} %collective-permute-done.18), channel_id=1, source_target_pairs={{0,1},{1,0},{2,3},{3,2},{4,5},{5,4},{6,7},{7,6},{8,9},{9,8},{10,11... | collective-permute-start | bytes 2359304 | tf_op jit(solution)/shard_map/ppermute | solution.py:41
  343.3 41.3 %collective-permute-start.46 = (bf16[256,1024]{1,0:T(8,128)(2,1)S(1)}, bf16[256,1024]{1,0:T(8,128)(2,1)S(1)}, u32[]{:S(2)}, u32[]{:S(2)}) collective-permute-start(bf16[256,1024]{1,0:T(8,128)(2,1)S(1)} %collective-permute-done.40.refs_4_), channel_id=1, source_target_pairs={{0,8},{8,0},{16,24},{24,16},{1,9},{9,1},{17,25},{25,17},{2,10},{10... | collective-permute-start | bytes 1572872 | tf_op jit(solution)/shard_map/ppermute | solution.py:41
  432.7 44.5 %collective-permute-start.52 = (bf16[4,192,1024]{2,1,0:T(8,128)(2,1)}, bf16[4,192,1024]{2,1,0:T(8,128)(2,1)}, u32[]{:S(2)}, u32[]{:S(2)}) collective-permute-start(bf16[4,192,1024]{2,1,0:T(8,128)(2,1)} %get-tuple-element.219), channel_id=1, source_target_pairs={{0,1},{1,0},{2,3},{3,2},{4,5},{5,4},{6,7},{7,6},{8,9},{9,8},{10,11... | collective-permute-start | bytes 4718600 | tf_op jit(solution)/shard_map/ppermute | solution.py:41
  436.4 38.0 %collective-permute-start.45 = (bf16[272,1024]{1,0:T(8,128)(2,1)}, bf16[272,1024]{1,0:T(8,128)(2,1)}, u32[]{:S(2)}, u32[]{:S(2)}) collective-permute-start(bf16[272,1024]{1,0:T(8,128)(2,1)} %fusion.10), channel_id=1, source_target_pairs={{0,16},{8,24},{16,0},{24,8},{1,17},{9,25},{17,1},{25,9},{2,18},{10... | collective-permute-start | bytes 1671176 | tf_op jit(solution)/shard_map/ppermute | solution.py:41
  440.2 35.7 %collective-permute-start.51 = (bf16[272,1024]{1,0:T(8,128)(2,1)}, bf16[272,1024]{1,0:T(8,128)(2,1)}, u32[]{:S(2)}, u32[]{:S(2)}) collective-permute-start(bf16[272,1024]{1,0:T(8,128)(2,1)} %fusion.7), channel_id=1, source_target_pairs={{0,2},{1,3},{2,0},{3,1},{4,6},{5,7},{6,4},{7,5},{8,10},{9,11},{10,... | collective-permute-start | bytes 1671176 | tf_op jit(solution)/shard_map/ppermute | solution.py:41
  472.9 37.6 %collective-permute-start.53 = (bf16[4,192,1024]{2,1,0:T(8,128)(2,1)}, bf16[4,192,1024]{2,1,0:T(8,128)(2,1)}, u32[]{:S(2)}, u32[]{:S(2)}) collective-permute-start(bf16[4,192,1024]{2,1,0:T(8,128)(2,1)} %get-tuple-element.221), channel_id=1, source_target_pairs={{0,1},{1,0},{2,3},{3,2},{4,5},{5,4},{6,7},{7,6},{8,9},{9,8},{10,11... | collective-permute-start | bytes 4718600 | tf_op jit(solution)/shard_map/ppermute | solution.py:41
  485.9 41.4 %collective-permute-start.54 = (bf16[2,1,4,2,32,1024]{5,4,3,2,1,0:T(8,128)(2,1)}, bf16[2,1,4,2,32,1024]{5,4,3,2,1,0:T(8,128)(2,1)}, u32[]{:S(2)}, u32[]{:S(2)}) collective-permute-start(bf16[2,1,4,2,32,1024]{5,4,3,2,1,0:T(8,128)(2,1)} %get-tuple-element.288), channel_id=1, source_target_pairs={{0,8},{8,0},{16,24},{24,16},{1,9},{9,1},{17,25},{25,17},{2,10},{10... | collective-permute-start | bytes 3145736 | tf_op jit(solution)/shard_map/ppermute | solution.py:41
  489.3 38.0 %collective-permute-start.55 = (bf16[4,96,1024]{2,1,0:T(8,128)(2,1)}, bf16[4,96,1024]{2,1,0:T(8,128)(2,1)}, u32[]{:S(2)}, u32[]{:S(2)}) collective-permute-start(bf16[4,96,1024]{2,1,0:T(8,128)(2,1)} %get-tuple-element.225), channel_id=1, source_target_pairs={{0,4},{1,5},{2,6},{3,7},{4,0},{5,1},{6,2},{7,3},{8,12},{9,13},{10,... | collective-permute-start | bytes 2359304 | tf_op jit(solution)/shard_map/ppermute | solution.py:41
  491.4 49.9 %collective-permute-start.57 = (bf16[4,192,1024]{2,1,0:T(8,128)(2,1)}, bf16[4,192,1024]{2,1,0:T(8,128)(2,1)}, u32[]{:S(2)}, u32[]{:S(2)}) collective-permute-start(bf16[4,192,1024]{2,1,0:T(8,128)(2,1)} %get-tuple-element.232), channel_id=1, source_target_pairs={{0,1},{1,0},{2,3},{3,2},{4,5},{5,4},{6,7},{7,6},{8,9},{9,8},{10,11... | collective-permute-start | bytes 4718600 | tf_op jit(solution)/shard_map/ppermute | solution.py:41
  543.5 47.3 %collective-permute-start.58 = (bf16[2,1,4,2,32,2176]{5,4,3,2,1,0:T(8,128)(2,1)}, bf16[2,1,4,2,32,2176]{5,4,3,2,1,0:T(8,128)(2,1)S(1)}, u32[]{:S(2)}, u32[]{:S(2)}) collective-permute-start(bf16[2,1,4,2,32,2176]{5,4,3,2,1,0:T(8,128)(2,1)} %bitcast.150), channel_id=1, source_target_pairs={{0,8},{8,0},{16,24},{24,16},{1,9},{9,1},{17,25},{25,17},{2,10},{10... | collective-permute-start | bytes 6684680 | tf_op jit(solution)/shard_map/ppermute | solution.py:41
  549.2 47.3 %collective-permute-start.65 = (bf16[4,192,1024]{2,1,0:T(8,128)(2,1)}, bf16[4,192,1024]{2,1,0:T(8,128)(2,1)S(1)}, u32[]{:S(2)}, u32[]{:S(2)}) collective-permute-start(bf16[4,192,1024]{2,1,0:T(8,128)(2,1)} %get-tuple-element.243), channel_id=1, source_target_pairs={{0,1},{1,0},{2,3},{3,2},{4,5},{5,4},{6,7},{7,6},{8,9},{9,8},{10,11... | collective-permute-start | bytes 4718600 | tf_op jit(solution)/shard_map/ppermute | solution.py:41
  549.7 41.0 %collective-permute-start.60 = (bf16[4,96,1024]{2,1,0:T(8,128)(2,1)}, bf16[4,96,1024]{2,1,0:T(8,128)(2,1)S(1)}, u32[]{:S(2)}, u32[]{:S(2)}) collective-permute-start(bf16[4,96,1024]{2,1,0:T(8,128)(2,1)} %get-tuple-element.238), channel_id=1, source_target_pairs={{0,4},{1,5},{2,6},{3,7},{4,0},{5,1},{6,2},{7,3},{8,12},{9,13},{10,... | collective-permute-start | bytes 2359304 | tf_op jit(solution)/shard_map/ppermute | solution.py:41
  552.5 38.2 %collective-permute-start.59 = (bf16[1,1,4,1,32,1024]{5,4,3,2,1,0:T(8,128)(2,1)S(1)}, bf16[1,1,4,1,32,1024]{5,4,3,2,1,0:T(8,128)(2,1)S(1)}, u32[]{:S(2)}, u32[]{:S(2)}) collective-permute-start(bf16[1,1,4,1,32,1024]{5,4,3,2,1,0:T(8,128)(2,1)S(1)} %dynamic-slice_convert_fusion.4), channel_id=1, source_target_pairs={{0,1},{1,0},{2,3},{3,2},{4,5},{5,4},{6,7},{7,6},{8,9},{9,8},{10,11... | collective-permute-start | bytes 786440 | tf_op jit(solution)/shard_map/ppermute | solution.py:41
  591.3 40.9 %collective-permute-start.61 = (bf16[1,1,4,2,32,2176]{5,4,3,2,1,0:T(8,128)(2,1)S(1)}, bf16[1,1,4,2,32,2176]{5,4,3,2,1,0:T(8,128)(2,1)S(1)}, u32[]{:S(2)}, u32[]{:S(2)}) collective-permute-start(bf16[1,1,4,2,32,2176]{5,4,3,2,1,0:T(8,128)(2,1)S(1)} %dynamic-slice_convert_fusion), channel_id=1, source_target_pairs={{0,16},{8,24},{16,0},{24,8},{1,17},{9,25},{17,1},{25,9},{2,18},{10... | collective-permute-start | bytes 3342344 | tf_op jit(solution)/shard_map/ppermute | solution.py:41
  593.1 39.2 %collective-permute-start.66 = (bf16[4,96,1024]{2,1,0:T(8,128)(2,1)S(1)}, bf16[4,96,1024]{2,1,0:T(8,128)(2,1)S(1)}, u32[]{:S(2)}, u32[]{:S(2)}) collective-permute-start(bf16[4,96,1024]{2,1,0:T(8,128)(2,1)S(1)} %get-tuple-element.246), channel_id=1, source_target_pairs={{0,4},{1,5},{2,6},{3,7},{4,0},{5,1},{6,2},{7,3},{8,12},{9,13},{10,... | collective-permute-start | bytes 2359304 | tf_op jit(solution)/shard_map/ppermute | solution.py:41
  595.9 36.4 %collective-permute-start.63 = (bf16[1,1,1,1,32,1024]{5,4,3,2,1,0:T(8,128)(2,1)S(1)}, bf16[1,1,1,1,32,1024]{5,4,3,2,1,0:T(8,128)(2,1)S(1)}, u32[]{:S(2)}, u32[]{:S(2)}) collective-permute-start(bf16[1,1,1,1,32,1024]{5,4,3,2,1,0:T(8,128)(2,1)S(1)} %get-tuple-element.305), channel_id=1, source_target_pairs={{0,4},{1,5},{2,6},{3,7},{4,0},{5,1},{6,2},{7,3},{8,12},{9,13},{10,... | collective-permute-start | bytes 196616 | tf_op jit(solution)/shard_map/ppermute | solution.py:41
  596.5 35.8 %collective-permute-start.64 = (bf16[1,1,1,1,32,1024]{5,4,3,2,1,0:T(8,128)(2,1)S(1)}, bf16[1,1,1,1,32,1024]{5,4,3,2,1,0:T(8,128)(2,1)S(1)}, u32[]{:S(2)}, u32[]{:S(2)}) collective-permute-start(bf16[1,1,1,1,32,1024]{5,4,3,2,1,0:T(8,128)(2,1)S(1)} %get-tuple-element.304), channel_id=1, source_target_pairs={{0,6},{1,7},{2,4},{3,5},{4,2},{5,3},{6,0},{7,1},{8,14},{9,15},{10,... | collective-permute-start | bytes 196616 | tf_op jit(solution)/shard_map/ppermute | solution.py:41
  634.2 36.0 %collective-permute-start.68 = (bf16[4,96,1024]{2,1,0:T(8,128)(2,1)S(1)}, bf16[4,96,1024]{2,1,0:T(8,128)(2,1)S(1)}, u32[]{:S(2)}, u32[]{:S(2)}) collective-permute-start(bf16[4,96,1024]{2,1,0:T(8,128)(2,1)S(1)} %get-tuple-element.252), channel_id=1, source_target_pairs={{0,4},{1,5},{2,6},{3,7},{4,0},{5,1},{6,2},{7,3},{8,12},{9,13},{10,... | collective-permute-start | bytes 2359304 | tf_op jit(solution)/shard_map/ppermute | solution.py:41
  638.9 59.7 %collective-permute-start.72 = (bf16[4,192,1024]{2,1,0:T(8,128)(2,1)S(1)}, bf16[4,192,1024]{2,1,0:T(8,128)(2,1)S(1)}, u32[]{:S(2)}, u32[]{:S(2)}) collective-permute-start(bf16[4,192,1024]{2,1,0:T(8,128)(2,1)S(1)} %add_convert_fusion), channel_id=1, source_target_pairs={{0,2},{1,3},{2,0},{3,1},{4,6},{5,7},{6,4},{7,5},{8,10},{9,11},{10,... | collective-permute-start | bytes 4718600 | tf_op jit(solution)/shard_map/ppermute | solution.py:41
  (93 other events, 1469.0 us)

commit v8 on v7

--- a/solution.py
+++ b/solution.py
@@ -549,15 +549,15 @@
     others, out_others = send(pack, 1), send(out_w, 1)
     near = swap(after(owned_by(1), pack), "fsdp", HOP_BIT)
     far_own = [far_swaps(after(arrived[0, 0][:, :half], pack))]
-    pack, others, out_w, out_others, arrived[1, 0] = join(
-        (pack, others, out_w, out_others, arrived[1, 0])
-    )
+    pack, others, out_w, out_others, arrived[1, 0], far_own = join(
+        (pack, others, out_w, out_others, arrived[1, 0], far_own)
+    )
+    far_own.append(far_swaps(after(arrived[0, 0][:, half:], others)))
     pack, out_w = merge(pack, others, 1), merge(out_w, out_others, 1)
     others, out_others = send(pack, 2), send(out_w, 2)
     pack, others, out_w, out_others, near, far_own = join(
         (pack, others, out_w, out_others, near, far_own)
     )
-    far_own.append(far_swaps(after(arrived[0, 0][:, half:], others)))
     pack, out_w = merge(pack, others, 2), merge(out_w, out_others, 2)
     others, out_others = send(pack, 3), send(out_w, 3)
     arrived[HOP_BIT, 0] = near
@@ -807,23 +807,26 @@
         scratch=(pltpu.VMEM((model_width, qkv_width + 128), bf16),),
     )
     later = [m for m in order_of[:-1] if not m & last_bit]
-    grads, out_sum, got = join((grads, out_sum, [low_got[m] for m in later]))
+    grads, out_sum, got, far_got = join((grads, out_sum, [low_got[m] for m in later], far_got))
     low_got |= dict(zip(later, got, strict=True))
     for m in later:
         low_sum(m)
     grads = [g.reshape(rows_y, 1, units, 2, row_block, -1) for g in grads]
     part_sum = (grads[0].astype(f32), [swap(g, "dp", m + 1) for m, g in enumerate(grads[1:])])
     out_sum = halve(total(*out_sum), 2)
-    part_sum, out_sum, far_got = join((part_sum, out_sum, far_got))
-    far_slot(2, part_sum)
+    far_slot(2, grads)
+    part_sum, out_sum = join((part_sum, out_sum))
+    hop_got = None
+    if len(far_bits) == 1:
+        far_sum(HOP_BIT)
+        hop_got = swap(after(sums_of[HOP_BIT].astype(bf16), part_sum), "fsdp", HOP_BIT)
     part_sum = halve(total(*part_sum), 1)
     out_sum = halve(total(*out_sum), 0)
-    part_sum, out_sum, low_got[0], far_got = join((part_sum, out_sum, low_got[0], far_got))
+    part_sum, out_sum, low_got[0], far_got, hop_got = join(
+        (part_sum, out_sum, low_got[0], far_got, hop_got)
+    )
     far_slot(3, part_sum)
     low_sum(0)
-    if len(far_bits) == 1:
-        far_sum(HOP_BIT)
-        hop_got = far_send(HOP_BIT, HOP_BIT)
     out_grad_w = total(*out_sum).reshape(row_block, -1)
     part_sum = halve(total(*part_sum), 2)
     part_sum, far_got = join((part_sum, far_got))

time: 713 us -> 694 us (0.973)
  waiting for transfers between devices: 382 us -> 362 us
  starting transfers between devices: 69 us -> 77.7 us
    ppermute x73, waiting for transfers between devices: 382 us -> 362 us  [swap(): lax.ppermute(values, axis, [(i, i ^ mask) for i in range(lax.axis_size(ax...]
    ppermute x73, starting transfers between devices: 69 us -> 77.7 us  [swap(): lax.ppermute(values, axis, [(i, i ^ mask) for i in range(lax.axis_size(ax...]
  transfers between devices with their start and end apart: 73 -> 73, of which waited for: 30 -> 33; matrix products, arithmetic and copies ran while one was open for 15% -> 14% of each run, Pallas kernels for 12% -> 12%
where the time goes in v8:
time: 694 us; the launch traced here: 689 us
  waiting for transfers between devices  362 us (52%)
  Pallas kernels  121 us (17%)
  starting transfers between devices  77.7 us (11%)
  local copies, waits for them, and re-layouts  59.3 us (9%)
  other arithmetic  52.5 us (8%)
  matrix products  11.5 us (2%)
    ppermute x73, waiting for transfers between devices, swap(): lax.ppermute(values, axis, [(i, i ^ mask) for i in range(lax.axis_size(ax...  362 us
    ppermute x73, starting transfers between devices, swap(): lax.ppermute(values, axis, [(i, i ^ mask) for i in range(lax.axis_size(ax...  77.7 us
    pallas_call x4, Pallas kernels, expert_call(): pl.pallas_call(body, grid=(held,), out_shape=out_shape, in_specs=[smem(),...  70.4 us
    pallas_call x3, Pallas kernels, kernel_call(): pl.pallas_call(body, out_shape=out_shape, in_specs=specs, out_specs=jax.t...  30.9 us
    dynamic_update_slice x12, local copies, waits for them, and re-layouts, on_device(): lax.dynamic_update_slice(expert_w, piece[:, None], (0, fsdp_at ^ m, row, 0))  23.9 us
    pallas_call x1, Pallas kernels, on_device(): pl.pallas_call(functools.partial(expert_weight_grads, HOPS), grid=(held,)...  19.4 us
  transfers between devices with their start and end apart: 73, of which 33 were waited for; matrix products, arithmetic and copies ran while one was open for 14% of the time, Pallas kernels for 12%

profile of v8, /device:TPU:0, one launch (start us, length us, event | category | flops | bytes accessed | tf_op | source)
XLA Modules:
  0.0 689.0 jit_solution(5716123288472145044)
XLA Ops:
  22.1 4.8 collective-permute-done.4
  35.8 13.2 %collective-permute-done.7 = bf16[1,1,4,1,32,1024]{5,4,3,2,1,0:T(8,128)(2,1)S(1)} collective-permute-done((bf16[1,1,4,1,32,1024]{5,4,3,2,1,0:T(8,128)(2,1)S(1)}, bf16[1,1,4,1,32,1024]{5,4,3,2,1,0:T(8,128)(2,1)S(1)}, u32[]{:S(2)}, u32[]{:S(2)}) %collective-permute-start.7) | collective-permute-done | bytes 262176 | tf_op jit(solution)/shard_map/ppermute | solution.py:41
  49.0 15.5 %collective-permute-done.9 = bf16[4,96,1024]{2,1,0:T(8,128)(2,1)} collective-permute-done((bf16[4,96,1024]{2,1,0:T(8,128)(2,1)S(1)}, bf16[4,96,1024]{2,1,0:T(8,128)(2,1)}, u32[]{:S(2)}, u32[]{:S(2)}) %collective-permute-start.9) | collective-permute-done | bytes 786464 | tf_op jit(solution)/shard_map/ppermute | solution.py:41
  69.2 26.6 %collective-permute-done.12 = bf16[4,192,1024]{2,1,0:T(8,128)(2,1)S(1)} collective-permute-done((bf16[4,192,1024]{2,1,0:T(8,128)(2,1)}, bf16[4,192,1024]{2,1,0:T(8,128)(2,1)S(1)}, u32[]{:S(2)}, u32[]{:S(2)}) %collective-permute-start.12) | collective-permute-done | bytes 1572896 | tf_op jit(solution)/shard_map/ppermute | solution.py:41
  95.7 8.7 %collective-permute-done.11 = bf16[2,1,4,1,32,1024]{5,4,3,2,1,0:T(8,128)(2,1)S(1)} collective-permute-done((bf16[2,1,4,1,32,1024]{5,4,3,2,1,0:T(8,128)(2,1)S(1)}, bf16[2,1,4,1,32,1024]{5,4,3,2,1,0:T(8,128)(2,1)S(1)}, u32[]{:S(2)}, u32[]{:S(2)}) %collective-permute-start.11) | collective-permute-done | bytes 524320 | tf_op jit(solution)/shard_map/ppermute | solution.py:41
  122.5 9.8 %shard_map.237 = (bf16[256,2048]{1,0:T(8,128)(2,1)}, bf16[256,1024]{1,0:T(8,128)(2,1)}) custom-call(s32[1]{0:T(128)} %copy.90.length_ref, f32[256,2048]{1,0:T(8,128)} %fusion.qkv_ref, f32[256,128]{1,0:T(8,128)} %get-tuple-element.328.cos_ref, f32[256,128]{1,0:T(8,128)} %get-tuple-element.329.sin_ref), custom_call_target="tpu_custom_call" | custom-call | tf_op jit(solution)/shard_map/pallas_call | solution.py:60
  132.3 18.5 %collective-permute-done.16 = bf16[4,96,1024]{2,1,0:T(8,128)(2,1)S(1)} collective-permute-done((bf16[4,96,1024]{2,1,0:T(8,128)(2,1)}, bf16[4,96,1024]{2,1,0:T(8,128)(2,1)S(1)}, u32[]{:S(2)}, u32[]{:S(2)}) %collective-permute-start.16) | collective-permute-done | bytes 786464 | tf_op jit(solution)/shard_map/ppermute | solution.py:41
  156.5 32.7 %collective-permute-done.18 = bf16[4,96,1024]{2,1,0:T(8,128)(2,1)} collective-permute-done((bf16[4,96,1024]{2,1,0:T(8,128)(2,1)}, bf16[4,96,1024]{2,1,0:T(8,128)(2,1)}, u32[]{:S(2)}, u32[]{:S(2)}) %collective-permute-start.18) | collective-permute-done | bytes 786464 | tf_op jit(solution)/shard_map/ppermute | solution.py:41
  194.7 6.1 broadcast_in_dim.119
  219.3 8.0 %collective-permute-done.30.refs_2_ = bf16[272,1024]{1,0:T(8,128)(2,1)S(1)} collective-permute-done((bf16[272,1024]{1,0:T(8,128)(2,1)S(1)}, bf16[272,1024]{1,0:T(8,128)(2,1)S(1)}, u32[]{:S(2)}, u32[]{:S(2)}) %collective-permute-start.30) | collective-permute-done | bytes 557088 | tf_op jit(solution)/shard_map/ppermute | solution.py:41
  234.6 14.0 %shard_map.238 = (bf16[2,256,1024]{2,1,0:T(8,128)(2,1)}, bf16[2,256,1024]{2,1,0:T(8,128)(2,1)}) custom-call(s32[1]{0:T(128)} %bitcast.8.first_ref, bf16[4,8,192,1024]{3,2,1,0:T(8,128)(2,1)} %bitcast_dynamic-update-slice_fusion.11.weights_ref, bf16[272,1024]{1,0:T(8,128)(2,1)} %copy-done.6, bf16[272,1024]{1,0:T(8,128)(2,1)} %copy-done.16, ...), custom_call_target="tpu_custom_call" | custom-call | tf_op jit(solution)/shard_map/pallas_call | solution.py:80
  249.5 13.9 %shard_map.239 = (bf16[2,256,1024]{2,1,0:T(8,128)(2,1)}, bf16[2,256,1024]{2,1,0:T(8,128)(2,1)}) custom-call(s32[1]{0:T(128)} %bitcast.8.first_ref, bf16[4,8,192,1024]{3,2,1,0:T(8,128)(2,1)} %bitcast_dynamic-update-slice_fusion.11.weights_ref, bf16[272,1024]{1,0:T(8,128)(2,1)} %copy-done.15, bf16[272,1024]{1,0:T(8,128)(2,1)} %copy-done.19, ...), custom_call_target="tpu_custom_call" | custom-call | tf_op jit(solution)/shard_map/pallas_call | solution.py:80
  270.7 11.6 %collective-permute-done.33 = bf16[256,1024]{1,0:T(8,128)(2,1)S(1)} collective-permute-done((bf16[256,1024]{1,0:T(8,128)(2,1)S(1)}, bf16[256,1024]{1,0:T(8,128)(2,1)S(1)}, u32[]{:S(2)}, u32[]{:S(2)}) %collective-permute-start.33) | collective-permute-done | bytes 524320 | tf_op jit(solution)/shard_map/ppermute | solution.py:41
  283.6 9.3 %collective-permute-done.28 = bf16[256,1024]{1,0:T(8,128)(2,1)S(1)} collective-permute-done((bf16[256,1024]{1,0:T(8,128)(2,1)}, bf16[256,1024]{1,0:T(8,128)(2,1)S(1)}, u32[]{:S(2)}, u32[]{:S(2)}) %collective-permute-start.28) | collective-permute-done | bytes 524320 | tf_op jit(solution)/shard_map/ppermute | solution.py:41
  298.1 11.0 %collective-permute-done.40.refs_4_ = bf16[256,1024]{1,0:T(8,128)(2,1)S(1)} collective-permute-done((bf16[256,1024]{1,0:T(8,128)(2,1)S(1)}, bf16[256,1024]{1,0:T(8,128)(2,1)S(1)}, u32[]{:S(2)}, u32[]{:S(2)}) %collective-permute-start.40) | collective-permute-done | bytes 524320 | tf_op jit(solution)/shard_map/ppermute | solution.py:41
  310.2 10.2 %collective-permute-done.47.refs_6_ = bf16[256,1024]{1,0:T(8,128)(2,1)S(1)} collective-permute-done((bf16[256,1024]{1,0:T(8,128)(2,1)S(1)}, bf16[256,1024]{1,0:T(8,128)(2,1)S(1)}, u32[]{:S(2)}, u32[]{:S(2)}) %collective-permute-start.47) | collective-permute-done | bytes 524320 | tf_op jit(solution)/shard_map/ppermute | solution.py:41
  329.3 21.4 %shard_map.240 = (bf16[2,272,1024]{2,1,0:T(8,128)(2,1)}, bf16[2,272,1024]{2,1,0:T(8,128)(2,1)}, bf16[4,384,1024]{2,1,0:T(8,128)(2,1)}, bf16[4,384,1024]{2,1,0:T(...) custom-call(s32[1]{0:T(128)} %bitcast.8.first_ref, ...), custom_call_target="tpu_custom_call" | custom-call | tf_op jit(solution)/shard_map/pallas_call | solution.py:80
  352.3 21.1 %shard_map.241 = (bf16[2,272,1024]{2,1,0:T(8,128)(2,1)}, bf16[2,272,1024]{2,1,0:T(8,128)(2,1)}, bf16[4,384,1024]{2,1,0:T(8,128)(2,1)}, bf16[4,384,1024]{2,1,0:T(...) custom-call(s32[1]{0:T(128)} %bitcast.8.first_ref, ...), custom_call_target="tpu_custom_call" | custom-call | tf_op jit(solution)/shard_map/pallas_call | solution.py:80
  379.4 19.4 %shard_map.242 = (bf16[4,192,1024]{2,1,0:T(8,128)(2,1)}, bf16[4,192,1024]{2,1,0:T(8,128)(2,1)}, bf16[4,192,1024]{2,1,0:T(8,128)(2,1)}, bf16[4,192,1024]{2,1,0:T(...) custom-call(s32[1]{0:T(128)} %bitcast.44.at_ref, ...), custom_call_target="tpu_custom_call" | custom-call | tf_op jit(solution)/shard_map/pallas_call | solution.py:685
  408.5 26.9 %collective-permute-done.37 = f32[8,128]{1,0:T(8,128)S(1)} collective-permute-done((f32[8,128]{1,0:T(8,128)S(1)}, f32[8,128]{1,0:T(8,128)S(1)}, u32[]{:S(2)}, u32[]{:S(2)}) %collective-permute-start.37) | collective-permute-done | bytes 4128 | tf_op jit(solution)/shard_map/ppermute | solution.py:41
  463.4 13.2 %collective-permute-done.53 = bf16[4,192,1024]{2,1,0:T(8,128)(2,1)} collective-permute-done((bf16[4,192,1024]{2,1,0:T(8,128)(2,1)}, bf16[4,192,1024]{2,1,0:T(8,128)(2,1)}, u32[]{:S(2)}, u32[]{:S(2)}) %collective-permute-start.53) | collective-permute-done | bytes 1572896 | tf_op jit(solution)/shard_map/ppermute | solution.py:41
  476.6 12.3 %shard_map.243.qkv_grad_ref = bf16[256,2048]{1,0:T(8,128)(2,1)} custom-call(s32[1]{0:T(128)} %copy.90.length_ref, bf16[256,2048]{1,0:T(8,128)(2,1)} %get-tuple-element.205.rot_ref, bf16[256,1024]{1,0:T(8,128)(2,1)} %convolution_convert_fusion.1.grad_ref, f32[256,128]{1,0:T(8,128)} %get-tuple-element.328.cos_ref, f32[256,128]{1,0:T(8,128)} %get-tuple-element.329.sin_ref), custom_call_target="tpu_custom_call" | custom-call | tf_op jit(solution)/shard_map/pallas_call | solution.py:60
  488.9 4.5 collective-permute-done.55
  498.2 8.9 %shard_map.244 = (bf16[2,256,2176]{2,1,0:T(8,128)(2,1)}, bf16[2,256,2176]{2,1,0:T(8,128)(2,1)}, f32[256,1024]{1,0:T(8,128)}) custom-call(s32[1]{0:T(128)} %bitcast.39.core_ref, bf16[256,2048]{1,0:T(8,128)(2,1)} %shard_map.243.qkv_grad_ref, bf16[256,1024]{1,0:T(8,128)(2,1)} %copy-done.21, bf16[1024,2176]{1,0:T(8,128)(2,1)} %bitcast.133, ...), custom_call_target="tpu_custom_call" | custom-call | tf_op jit(solution)/shard_map/pallas_call | solution.py:60
  508.6 21.6 %collective-permute-done.58 = bf16[4,96,1024]{2,1,0:T(8,128)(2,1)} collective-permute-done((bf16[4,96,1024]{2,1,0:T(8,128)(2,1)}, bf16[4,96,1024]{2,1,0:T(8,128)(2,1)}, u32[]{:S(2)}, u32[]{:S(2)}) %collective-permute-start.58) | collective-permute-done | bytes 786464 | tf_op jit(solution)/shard_map/ppermute | solution.py:41
  530.9 3.8 collective-permute-done.39
  545.1 32.4 %collective-permute-done.60 = bf16[1,1,4,1,32,1024]{5,4,3,2,1,0:T(8,128)(2,1)S(1)} collective-permute-done((bf16[1,1,4,1,32,1024]{5,4,3,2,1,0:T(8,128)(2,1)S(1)}, bf16[1,1,4,1,32,1024]{5,4,3,2,1,0:T(8,128)(2,1)S(1)}, u32[]{:S(2)}, u32[]{:S(2)}) %collective-permute-start.60) | collective-permute-done | bytes 262176 | tf_op jit(solution)/shard_map/ppermute | solution.py:41
  585.3 43.8 %collective-permute-done.66 = bf16[4,96,1024]{2,1,0:T(8,128)(2,1)S(1)} collective-permute-done((bf16[4,96,1024]{2,1,0:T(8,128)(2,1)S(1)}, bf16[4,96,1024]{2,1,0:T(8,128)(2,1)S(1)}, u32[]{:S(2)}, u32[]{:S(2)}) %collective-permute-start.66) | collective-permute-done | bytes 786464 | tf_op jit(solution)/shard_map/ppermute | solution.py:41
  635.4 10.8 %collective-permute-start.69 = (bf16[4,96,1024]{2,1,0:T(8,128)(2,1)S(1)}, bf16[4,96,1024]{2,1,0:T(8,128)(2,1)S(1)}, u32[]{:S(2)}, u32[]{:S(2)}) collective-permute-start(bf16[4,96,1024]{2,1,0:T(8,128)(2,1)S(1)} %get-tuple-element.259), channel_id=1, source_target_pairs={{0,4},{1,5},{2,6},{3,7},{4,0},{5,1},{6,2},{7,3},{8,12},{9,13},{10,... | collective-permute-start | bytes 2359304 | tf_op jit(solution)/shard_map/ppermute | solution.py:41
  647.7 8.1 %collective-permute-done.68 = bf16[1,1,4,1,32,2176]{5,4,3,2,1,0:T(8,128)(2,1)S(1)} collective-permute-done((bf16[1,1,4,1,32,2176]{5,4,3,2,1,0:T(8,128)(2,1)S(1)}, bf16[1,1,4,1,32,2176]{5,4,3,2,1,0:T(8,128)(2,1)S(1)}, u32[]{:S(2)}, u32[]{:S(2)}) %collective-permute-start.68) | collective-permute-done | bytes 557088 | tf_op jit(solution)/shard_map/ppermute | solution.py:41
  655.9 13.7 %collective-permute-done.69 = bf16[4,96,1024]{2,1,0:T(8,128)(2,1)S(1)} collective-permute-done((bf16[4,96,1024]{2,1,0:T(8,128)(2,1)S(1)}, bf16[4,96,1024]{2,1,0:T(8,128)(2,1)S(1)}, u32[]{:S(2)}, u32[]{:S(2)}) %collective-permute-start.69) | collective-permute-done | bytes 786464 | tf_op jit(solution)/shard_map/ppermute | solution.py:41
  676.5 3.9 collective-permute-done.71
  (358 shorter events, 203.8 us)
Async XLA Ops:
  26.9 37.6 %collective-permute-start.8 = (bf16[4,192,1024]{2,1,0:T(8,128)(2,1)}, bf16[4,192,1024]{2,1,0:T(8,128)(2,1)}, u32[]{:S(2)}, u32[]{:S(2)}) collective-permute-start(bf16[4,192,1024]{2,1,0:T(8,128)(2,1)} %get-tuple-element.190), channel_id=1, source_target_pairs={{0,1},{1,0},{2,3},{3,2},{4,5},{5,4},{6,7},{7,6},{8,9},{9,8},{10,11... | collective-permute-start | bytes 4718600 | tf_op jit(solution)/shard_map/ppermute | solution.py:41
  29.6 34.9 %collective-permute-start.9 = (bf16[4,96,1024]{2,1,0:T(8,128)(2,1)S(1)}, bf16[4,96,1024]{2,1,0:T(8,128)(2,1)}, u32[]{:S(2)}, u32[]{:S(2)}) collective-permute-start(bf16[4,96,1024]{2,1,0:T(8,128)(2,1)S(1)} %copy-done.38), channel_id=1, source_target_pairs={{0,4},{1,5},{2,6},{3,7},{4,0},{5,1},{6,2},{7,3},{8,12},{9,13},{10,... | collective-permute-start | bytes 2359304 | tf_op jit(solution)/shard_map/ppermute | solution.py:41
  33.6 62.1 %collective-permute-start.12 = (bf16[4,192,1024]{2,1,0:T(8,128)(2,1)}, bf16[4,192,1024]{2,1,0:T(8,128)(2,1)S(1)}, u32[]{:S(2)}, u32[]{:S(2)}) collective-permute-start(bf16[4,192,1024]{2,1,0:T(8,128)(2,1)} %get-tuple-element.163), channel_id=1, source_target_pairs={{0,2},{1,3},{2,0},{3,1},{4,6},{5,7},{6,4},{7,5},{8,10},{9,11},{10,... | collective-permute-start | bytes 4718600 | tf_op jit(solution)/shard_map/ppermute | solution.py:41
  67.0 38.3 %collective-permute-start.10 = (bf16[2,1,4,1,32,2176]{5,4,3,2,1,0:T(8,128)(2,1)}, bf16[2,1,4,1,32,2176]{5,4,3,2,1,0:T(8,128)(2,1)}, u32[]{:S(2)}, u32[]{:S(2)}) collective-permute-start(bf16[2,1,4,1,32,2176]{5,4,3,2,1,0:T(8,128)(2,1)} %maximum_select_fusion.3), channel_id=1, source_target_pairs={{0,1},{1,0},{2,3},{3,2},{4,5},{5,4},{6,7},{7,6},{8,9},{9,8},{10,11... | collective-permute-start | bytes 3342344 | tf_op jit(solution)/shard_map/ppermute | solution.py:41
  67.8 36.6 %collective-permute-start.13 = (bf16[4,96,1024]{2,1,0:T(8,128)(2,1)}, bf16[4,96,1024]{2,1,0:T(8,128)(2,1)}, u32[]{:S(2)}, u32[]{:S(2)}) collective-permute-start(bf16[4,96,1024]{2,1,0:T(8,128)(2,1)} %get-tuple-element.165), channel_id=1, source_target_pairs={{0,4},{1,5},{2,6},{3,7},{4,0},{5,1},{6,2},{7,3},{8,12},{9,13},{10,... | collective-permute-start | bytes 2359304 | tf_op jit(solution)/shard_map/ppermute | solution.py:41
  67.9 36.5 %collective-permute-start.11 = (bf16[2,1,4,1,32,1024]{5,4,3,2,1,0:T(8,128)(2,1)S(1)}, bf16[2,1,4,1,32,1024]{5,4,3,2,1,0:T(8,128)(2,1)S(1)}, u32[]{:S(2)}, u32[]{:S(2)}) collective-permute-start(bf16[2,1,4,1,32,1024]{5,4,3,2,1,0:T(8,128)(2,1)S(1)} %maximum_select_fusion.5), channel_id=1, source_target_pairs={{0,1},{1,0},{2,3},{3,2},{4,5},{5,4},{6,7},{7,6},{8,9},{9,8},{10,11... | collective-permute-start | bytes 1572872 | tf_op jit(solution)/shard_map/ppermute | solution.py:41
  110.6 40.1 %collective-permute-start.17 = (bf16[4,192,1024]{2,1,0:T(8,128)(2,1)}, bf16[4,192,1024]{2,1,0:T(8,128)(2,1)}, u32[]{:S(2)}, u32[]{:S(2)}) collective-permute-start(bf16[4,192,1024]{2,1,0:T(8,128)(2,1)} %copy-done.2), channel_id=1, source_target_pairs={{0,1},{1,0},{2,3},{3,2},{4,5},{5,4},{6,7},{7,6},{8,9},{9,8},{10,11... | collective-permute-start | bytes 4718600 | tf_op jit(solution)/shard_map/ppermute | solution.py:41
  113.0 37.8 %collective-permute-start.16 = (bf16[4,96,1024]{2,1,0:T(8,128)(2,1)}, bf16[4,96,1024]{2,1,0:T(8,128)(2,1)S(1)}, u32[]{:S(2)}, u32[]{:S(2)}) collective-permute-start(bf16[4,96,1024]{2,1,0:T(8,128)(2,1)} %get-tuple-element.177), channel_id=1, source_target_pairs={{0,4},{1,5},{2,6},{3,7},{4,0},{5,1},{6,2},{7,3},{8,12},{9,13},{10,... | collective-permute-start | bytes 2359304 | tf_op jit(solution)/shard_map/ppermute | solution.py:41
  153.0 36.2 %collective-permute-start.18 = (bf16[4,96,1024]{2,1,0:T(8,128)(2,1)}, bf16[4,96,1024]{2,1,0:T(8,128)(2,1)}, u32[]{:S(2)}, u32[]{:S(2)}) collective-permute-start(bf16[4,96,1024]{2,1,0:T(8,128)(2,1)} %get-tuple-element.183), channel_id=1, source_target_pairs={{0,4},{1,5},{2,6},{3,7},{4,0},{5,1},{6,2},{7,3},{8,12},{9,13},{10,... | collective-permute-start | bytes 2359304 | tf_op jit(solution)/shard_map/ppermute | solution.py:41
  153.0 36.1 %collective-permute-start.19 = (bf16[4,96,1024]{2,1,0:T(8,128)(2,1)}, bf16[4,96,1024]{2,1,0:T(8,128)(2,1)}, u32[]{:S(2)}, u32[]{:S(2)}) collective-permute-start(bf16[4,96,1024]{2,1,0:T(8,128)(2,1)} %collective-permute-done.9), channel_id=1, source_target_pairs={{0,1},{1,0},{2,3},{3,2},{4,5},{5,4},{6,7},{7,6},{8,9},{9,8},{10,11... | collective-permute-start | bytes 2359304 | tf_op jit(solution)/shard_map/ppermute | solution.py:41
  154.5 34.9 %collective-permute-start.20 = (bf16[4,96,1024]{2,1,0:T(8,128)(2,1)}, bf16[4,96,1024]{2,1,0:T(8,128)(2,1)}, u32[]{:S(2)}, u32[]{:S(2)}) collective-permute-start(bf16[4,96,1024]{2,1,0:T(8,128)(2,1)} %collective-permute-done.13), channel_id=1, source_target_pairs={{0,1},{1,0},{2,3},{3,2},{4,5},{5,4},{6,7},{7,6},{8,9},{9,8},{10,11... | collective-permute-start | bytes 2359304 | tf_op jit(solution)/shard_map/ppermute | solution.py:41
  191.2 42.7 %collective-permute-start.24 = (bf16[272,1024]{1,0:T(8,128)(2,1)S(1)}, bf16[272,1024]{1,0:T(8,128)(2,1)S(1)}, u32[]{:S(2)}, u32[]{:S(2)}) collective-permute-start(bf16[272,1024]{1,0:T(8,128)(2,1)S(1)} %pad_maximum_fusion.2.refs_0_), channel_id=1, source_target_pairs={{0,8},{8,0},{16,24},{24,16},{1,9},{9,1},{17,25},{25,17},{2,10},{10... | collective-permute-start | bytes 1671176 | tf_op jit(solution)/shard_map/ppermute | solution.py:41
  194.1 37.6 %collective-permute-start.23 = (bf16[4,96,1024]{2,1,0:T(8,128)(2,1)}, bf16[4,96,1024]{2,1,0:T(8,128)(2,1)}, u32[]{:S(2)}, u32[]{:S(2)}) collective-permute-start(bf16[4,96,1024]{2,1,0:T(8,128)(2,1)} %collective-permute-done.18), channel_id=1, source_target_pairs={{0,1},{1,0},{2,3},{3,2},{4,5},{5,4},{6,7},{7,6},{8,9},{9,8},{10,11... | collective-permute-start | bytes 2359304 | tf_op jit(solution)/shard_map/ppermute | solution.py:41
  309.6 41.1 %collective-permute-start.46 = (bf16[256,1024]{1,0:T(8,128)(2,1)S(1)}, bf16[256,1024]{1,0:T(8,128)(2,1)S(1)}, u32[]{:S(2)}, u32[]{:S(2)}) collective-permute-start(bf16[256,1024]{1,0:T(8,128)(2,1)S(1)} %collective-permute-done.40.refs_4_), channel_id=1, source_target_pairs={{0,8},{8,0},{16,24},{24,16},{1,9},{9,1},{17,25},{25,17},{2,10},{10... | collective-permute-start | bytes 1572872 | tf_op jit(solution)/shard_map/ppermute | solution.py:41
  320.4 30.3 %collective-permute-start.48 = (bf16[256,1024]{1,0:T(8,128)(2,1)S(1)}, bf16[256,1024]{1,0:T(8,128)(2,1)S(1)}, u32[]{:S(2)}, u32[]{:S(2)}) collective-permute-start(bf16[256,1024]{1,0:T(8,128)(2,1)S(1)} %collective-permute-done.47.refs_6_), channel_id=1, source_target_pairs={{0,8},{8,0},{16,24},{24,16},{1,9},{9,1},{17,25},{25,17},{2,10},{10... | collective-permute-start | bytes 1572872 | tf_op jit(solution)/shard_map/ppermute | solution.py:41
  398.8 44.3 %collective-permute-start.52 = (bf16[4,192,1024]{2,1,0:T(8,128)(2,1)}, bf16[4,192,1024]{2,1,0:T(8,128)(2,1)}, u32[]{:S(2)}, u32[]{:S(2)}) collective-permute-start(bf16[4,192,1024]{2,1,0:T(8,128)(2,1)} %get-tuple-element.223), channel_id=1, source_target_pairs={{0,1},{1,0},{2,3},{3,2},{4,5},{5,4},{6,7},{7,6},{8,9},{9,8},{10,11... | collective-permute-start | bytes 4718600 | tf_op jit(solution)/shard_map/ppermute | solution.py:41
  402.3 38.0 %collective-permute-start.45 = (bf16[272,1024]{1,0:T(8,128)(2,1)}, bf16[272,1024]{1,0:T(8,128)(2,1)}, u32[]{:S(2)}, u32[]{:S(2)}) collective-permute-start(bf16[272,1024]{1,0:T(8,128)(2,1)} %fusion.10), channel_id=1, source_target_pairs={{0,16},{8,24},{16,0},{24,8},{1,17},{9,25},{17,1},{25,9},{2,18},{10... | collective-permute-start | bytes 1671176 | tf_op jit(solution)/shard_map/ppermute | solution.py:41
  406.1 35.8 %collective-permute-start.51 = (bf16[272,1024]{1,0:T(8,128)(2,1)}, bf16[272,1024]{1,0:T(8,128)(2,1)}, u32[]{:S(2)}, u32[]{:S(2)}) collective-permute-start(bf16[272,1024]{1,0:T(8,128)(2,1)} %fusion.7), channel_id=1, source_target_pairs={{0,2},{1,3},{2,0},{3,1},{4,6},{5,7},{6,4},{7,5},{8,10},{9,11},{10,... | collective-permute-start | bytes 1671176 | tf_op jit(solution)/shard_map/ppermute | solution.py:41
  439.0 37.6 %collective-permute-start.53 = (bf16[4,192,1024]{2,1,0:T(8,128)(2,1)}, bf16[4,192,1024]{2,1,0:T(8,128)(2,1)}, u32[]{:S(2)}, u32[]{:S(2)}) collective-permute-start(bf16[4,192,1024]{2,1,0:T(8,128)(2,1)} %get-tuple-element.225), channel_id=1, source_target_pairs={{0,1},{1,0},{2,3},{3,2},{4,5},{5,4},{6,7},{7,6},{8,9},{9,8},{10,11... | collective-permute-start | bytes 4718600 | tf_op jit(solution)/shard_map/ppermute | solution.py:41
  451.8 41.5 %collective-permute-start.54 = (bf16[2,1,4,2,32,1024]{5,4,3,2,1,0:T(8,128)(2,1)}, bf16[2,1,4,2,32,1024]{5,4,3,2,1,0:T(8,128)(2,1)}, u32[]{:S(2)}, u32[]{:S(2)}) collective-permute-start(bf16[2,1,4,2,32,1024]{5,4,3,2,1,0:T(8,128)(2,1)} %get-tuple-element.292), channel_id=1, source_target_pairs={{0,8},{8,0},{16,24},{24,16},{1,9},{9,1},{17,25},{25,17},{2,10},{10... | collective-permute-start | bytes 3145736 | tf_op jit(solution)/shard_map/ppermute | solution.py:41
  455.3 38.0 %collective-permute-start.55 = (bf16[4,96,1024]{2,1,0:T(8,128)(2,1)}, bf16[4,96,1024]{2,1,0:T(8,128)(2,1)}, u32[]{:S(2)}, u32[]{:S(2)}) collective-permute-start(bf16[4,96,1024]{2,1,0:T(8,128)(2,1)} %get-tuple-element.229), channel_id=1, source_target_pairs={{0,4},{1,5},{2,6},{3,7},{4,0},{5,1},{6,2},{7,3},{8,12},{9,13},{10,... | collective-permute-start | bytes 2359304 | tf_op jit(solution)/shard_map/ppermute | solution.py:41
  457.7 49.5 %collective-permute-start.57 = (bf16[4,192,1024]{2,1,0:T(8,128)(2,1)}, bf16[4,192,1024]{2,1,0:T(8,128)(2,1)}, u32[]{:S(2)}, u32[]{:S(2)}) collective-permute-start(bf16[4,192,1024]{2,1,0:T(8,128)(2,1)} %get-tuple-element.236), channel_id=1, source_target_pairs={{0,1},{1,0},{2,3},{3,2},{4,5},{5,4},{6,7},{7,6},{8,9},{9,8},{10,11... | collective-permute-start | bytes 4718600 | tf_op jit(solution)/shard_map/ppermute | solution.py:41
  493.3 36.9 %collective-permute-start.58 = (bf16[4,96,1024]{2,1,0:T(8,128)(2,1)}, bf16[4,96,1024]{2,1,0:T(8,128)(2,1)}, u32[]{:S(2)}, u32[]{:S(2)}) collective-permute-start(bf16[4,96,1024]{2,1,0:T(8,128)(2,1)} %get-tuple-element.238), channel_id=1, source_target_pairs={{0,4},{1,5},{2,6},{3,7},{4,0},{5,1},{6,2},{7,3},{8,12},{9,13},{10,... | collective-permute-start | bytes 2359304 | tf_op jit(solution)/shard_map/ppermute | solution.py:41
  530.2 47.2 %collective-permute-start.59 = (bf16[2,1,4,2,32,2176]{5,4,3,2,1,0:T(8,128)(2,1)}, bf16[2,1,4,2,32,2176]{5,4,3,2,1,0:T(8,128)(2,1)S(1)}, u32[]{:S(2)}, u32[]{:S(2)}) collective-permute-start(bf16[2,1,4,2,32,2176]{5,4,3,2,1,0:T(8,128)(2,1)} %bitcast.150), channel_id=1, source_target_pairs={{0,8},{8,0},{16,24},{24,16},{1,9},{9,1},{17,25},{25,17},{2,10},{10... | collective-permute-start | bytes 6684680 | tf_op jit(solution)/shard_map/ppermute | solution.py:41
  536.0 46.6 %collective-permute-start.65 = (bf16[4,192,1024]{2,1,0:T(8,128)(2,1)}, bf16[4,192,1024]{2,1,0:T(8,128)(2,1)S(1)}, u32[]{:S(2)}, u32[]{:S(2)}) collective-permute-start(bf16[4,192,1024]{2,1,0:T(8,128)(2,1)} %get-tuple-element.247), channel_id=1, source_target_pairs={{0,1},{1,0},{2,3},{3,2},{4,5},{5,4},{6,7},{7,6},{8,9},{9,8},{10,11... | collective-permute-start | bytes 4718600 | tf_op jit(solution)/shard_map/ppermute | solution.py:41
  540.7 36.8 %collective-permute-start.60 = (bf16[1,1,4,1,32,1024]{5,4,3,2,1,0:T(8,128)(2,1)S(1)}, bf16[1,1,4,1,32,1024]{5,4,3,2,1,0:T(8,128)(2,1)S(1)}, u32[]{:S(2)}, u32[]{:S(2)}) collective-permute-start(bf16[1,1,4,1,32,1024]{5,4,3,2,1,0:T(8,128)(2,1)S(1)} %dynamic-slice_convert_fusion.4), channel_id=1, source_target_pairs={{0,1},{1,0},{2,3},{3,2},{4,5},{5,4},{6,7},{7,6},{8,9},{9,8},{10,11... | collective-permute-start | bytes 786440 | tf_op jit(solution)/shard_map/ppermute | solution.py:41
  577.5 57.7 %collective-permute-start.67 = (bf16[4,192,1024]{2,1,0:T(8,128)(2,1)S(1)}, bf16[4,192,1024]{2,1,0:T(8,128)(2,1)S(1)}, u32[]{:S(2)}, u32[]{:S(2)}) collective-permute-start(bf16[4,192,1024]{2,1,0:T(8,128)(2,1)S(1)} %add_convert_fusion), channel_id=1, source_target_pairs={{0,2},{1,3},{2,0},{3,1},{4,6},{5,7},{6,4},{7,5},{8,10},{9,11},{10,... | collective-permute-start | bytes 4718600 | tf_op jit(solution)/shard_map/ppermute | solution.py:41
  578.1 57.0 %collective-permute-start.61 = (bf16[1,1,4,2,32,2176]{5,4,3,2,1,0:T(8,128)(2,1)S(1)}, bf16[1,1,4,2,32,2176]{5,4,3,2,1,0:T(8,128)(2,1)S(1)}, u32[]{:S(2)}, u32[]{:S(2)}) collective-permute-start(bf16[1,1,4,2,32,2176]{5,4,3,2,1,0:T(8,128)(2,1)S(1)} %dynamic-slice_convert_fusion), channel_id=1, source_target_pairs={{0,16},{8,24},{16,0},{24,8},{1,17},{9,25},{17,1},{25,9},{2,18},{10... | collective-permute-start | bytes 3342344 | tf_op jit(solution)/shard_map/ppermute | solution.py:41
  579.9 49.2 %collective-permute-start.66 = (bf16[4,96,1024]{2,1,0:T(8,128)(2,1)S(1)}, bf16[4,96,1024]{2,1,0:T(8,128)(2,1)S(1)}, u32[]{:S(2)}, u32[]{:S(2)}) collective-permute-start(bf16[4,96,1024]{2,1,0:T(8,128)(2,1)S(1)} %get-tuple-element.250), channel_id=1, source_target_pairs={{0,4},{1,5},{2,6},{3,7},{4,0},{5,1},{6,2},{7,3},{8,12},{9,13},{10,... | collective-permute-start | bytes 2359304 | tf_op jit(solution)/shard_map/ppermute | solution.py:41
  581.9 50.7 %collective-permute-start.62 = (bf16[1,1,1,1,32,1024]{5,4,3,2,1,0:T(8,128)(2,1)S(1)}, bf16[1,1,1,1,32,1024]{5,4,3,2,1,0:T(8,128)(2,1)S(1)}, u32[]{:S(2)}, u32[]{:S(2)}) collective-permute-start(bf16[1,1,1,1,32,1024]{5,4,3,2,1,0:T(8,128)(2,1)S(1)} %get-tuple-element.310), channel_id=1, source_target_pairs={{0,2},{1,3},{2,0},{3,1},{4,6},{5,7},{6,4},{7,5},{8,10},{9,11},{10,... | collective-permute-start | bytes 196616 | tf_op jit(solution)/shard_map/ppermute | solution.py:41
  582.6 50.1 %collective-permute-start.63 = (bf16[1,1,1,1,32,1024]{5,4,3,2,1,0:T(8,128)(2,1)S(1)}, bf16[1,1,1,1,32,1024]{5,4,3,2,1,0:T(8,128)(2,1)S(1)}, u32[]{:S(2)}, u32[]{:S(2)}) collective-permute-start(bf16[1,1,1,1,32,1024]{5,4,3,2,1,0:T(8,128)(2,1)S(1)} %get-tuple-element.309), channel_id=1, source_target_pairs={{0,4},{1,5},{2,6},{3,7},{4,0},{5,1},{6,2},{7,3},{8,12},{9,13},{10,... | collective-permute-start | bytes 196616 | tf_op jit(solution)/shard_map/ppermute | solution.py:41
  635.4 34.2 %collective-permute-start.69 = (bf16[4,96,1024]{2,1,0:T(8,128)(2,1)S(1)}, bf16[4,96,1024]{2,1,0:T(8,128)(2,1)S(1)}, u32[]{:S(2)}, u32[]{:S(2)}) collective-permute-start(bf16[4,96,1024]{2,1,0:T(8,128)(2,1)S(1)} %get-tuple-element.259), channel_id=1, source_target_pairs={{0,4},{1,5},{2,6},{3,7},{4,0},{5,1},{6,2},{7,3},{8,12},{9,13},{10,... | collective-permute-start | bytes 2359304 | tf_op jit(solution)/shard_map/ppermute | solution.py:41
  (99 other events, 1290.3 us)

commit v9 on v8

--- a/solution.py
+++ b/solution.py
@@ -614,7 +614,6 @@
     )
     count = rows_y * CORES
     rows = count * CAP
-    outgoing, far_near, arrived = join((outgoing, far_near, arrived))
     for i, pieces in enumerate(far_near):
         for m, piece in pieces.items():
             arrived[m ^ HOP_BIT, i * half] = piece
@@ -700,7 +699,7 @@
         *[saved[k][i] for i in range(4) for k in range(HOPS)],
     )
     order_of = sorted(range(0, shards, 2), key=lambda m: -m)
-    low_got = {m: swap(expert_grad[m ^ 1], "fsdp", 1) for m in order_of}
+    low_got = {m: swap(expert_grad[m ^ 1], "fsdp", 1) for m in order_of[:-1]}
     first_low = order_of[0]
     returned, low_got[first_low] = join((finish((expert_grad[0], loss_steps[3])), low_got[first_low]))
     sums_of = {}
@@ -766,18 +765,21 @@
         size = len(chunks) // 4
         for m, i in chunks[slot * size : slot * size + size]:
             piece = sums_of[m][:, i * half : i * half + half].astype(bf16)
-            far_got[m ^ last_bit, i] = swap(after(piece, earlier), "fsdp", last_bit)
+            if earlier is not None:
+                piece = after(piece, earlier)
+            far_got[m ^ last_bit, i] = swap(piece, "fsdp", last_bit)
 
     def far_sum(m):
         sums_of[m] = sums_of[m] + jnp.concatenate(
             [far_got[m, i].astype(f32) for i in range(2)], axis=1
         )
 
-    far_slot(0, attended_grad)
-    mixed_grad, got = join((mixed_grad, [low_got[m] for m in early]))
+    far_slot(0, None)
+    mixed_grad, got, far_got = join((mixed_grad, [low_got[m] for m in early], far_got))
     low_got |= dict(zip(early, got, strict=True))
     for m in early:
         low_sum(m)
+    far_slot(1, mixed_grad)
     qkv_grad = kernel_call(
         attention_backward,
         jax.ShapeDtypeStruct((seq_len, qkv_width), bf16),
@@ -786,7 +788,7 @@
         scratch=(pltpu.VMEM((seq_len, model_width + kv_width), f32),),
     )
     qkv_grad, out_sum, far_got = join((qkv_grad, out_sum, far_got))
-    far_slot(1, qkv_grad)
+    far_slot(2, qkv_grad)
     out_sum = halve(total(*out_sum), 1)
     share = jax.ShapeDtypeStruct((rows_y, shards * row_block, qkv_width + 128), bf16)
     *grads, token_grad = kernel_call(
@@ -814,8 +816,9 @@
     grads = [g.reshape(rows_y, 1, units, 2, row_block, -1) for g in grads]
     part_sum = (grads[0].astype(f32), [swap(g, "dp", m + 1) for m, g in enumerate(grads[1:])])
     out_sum = halve(total(*out_sum), 2)
-    far_slot(2, grads)
+    far_slot(3, grads)
     part_sum, out_sum = join((part_sum, out_sum))
+    low_got[0] = swap(after(expert_grad[1], part_sum), "fsdp", 1)
     hop_got = None
     if len(far_bits) == 1:
         far_sum(HOP_BIT)
@@ -825,7 +828,6 @@
     part_sum, out_sum, low_got[0], far_got, hop_got = join(
         (part_sum, out_sum, low_got[0], far_got, hop_got)
     )
-    far_slot(3, part_sum)
     low_sum(0)
     out_grad_w = total(*out_sum).reshape(row_block, -1)
     part_sum = halve(total(*part_sum), 2)

time: 694 us -> 689 us (level)
  waiting for transfers between devices: 362 us -> 353 us
  starting transfers between devices: 77.7 us -> 69.4 us
  local copies, waits for them, and re-layouts: 59.3 us -> 66.8 us
    ppermute x73, starting transfers between devices: 77.7 us -> 69.4 us  [swap(): lax.ppermute(values, axis, [(i, i ^ mask) for i in range(lax.axis_size(ax...]
    unnamed x116 -> x128, local copies, waits for them, and re-layouts: 9.59 us -> 17.8 us
    ppermute x73, waiting for transfers between devices: 362 us -> 353 us  [swap(): lax.ppermute(values, axis, [(i, i ^ mask) for i in range(lax.axis_size(ax...]
  transfers between devices with their start and end apart: 73 -> 73, of which waited for: 33 -> 33; matrix products, arithmetic and copies ran while one was open for 14% -> 14% of each run, Pallas kernels for 12% -> 13%
where the time goes in v9:
time: 689 us; the launch traced here: 683 us
  waiting for transfers between devices  353 us (51%)
  Pallas kernels  121 us (18%)
  starting transfers between devices  69.4 us (10%)
  local copies, waits for them, and re-layouts  66.8 us (10%)
  other arithmetic  57.3 us (8%)
  matrix products  9.63 us (1%)
    ppermute x73, waiting for transfers between devices, swap(): lax.ppermute(values, axis, [(i, i ^ mask) for i in range(lax.axis_size(ax...  353 us
    pallas_call x4, Pallas kernels, expert_call(): pl.pallas_call(body, grid=(held,), out_shape=out_shape, in_specs=[smem(),...  70.5 us
    ppermute x73, starting transfers between devices, swap(): lax.ppermute(values, axis, [(i, i ^ mask) for i in range(lax.axis_size(ax...  69.4 us
    pallas_call x3, Pallas kernels, kernel_call(): pl.pallas_call(body, out_shape=out_shape, in_specs=specs, out_specs=jax.t...  30.9 us
    dynamic_update_slice x12, local copies, waits for them, and re-layouts, on_device(): lax.dynamic_update_slice(expert_w, piece[:, None], (0, fsdp_at ^ m, row, 0))  20.2 us
    pallas_call x1, Pallas kernels, on_device(): pl.pallas_call(functools.partial(expert_weight_grads, HOPS), grid=(held,)...  19.3 us
    unnamed x128, local copies, waits for them, and re-layouts  17.8 us
  transfers between devices with their start and end apart: 73, of which 33 were waited for; matrix products, arithmetic and copies ran while one was open for 14% of the time, Pallas kernels for 13%

profile of v9, /device:TPU:0, one launch (start us, length us, event | category | flops | bytes accessed | tf_op | source)
XLA Modules:
  0.0 682.8 jit_solution(5308560941023540016)
XLA Ops:
  20.7 6.1 broadcast_in_dim.119
  38.4 13.1 %collective-permute-done.7 = bf16[1,1,4,1,32,1024]{5,4,3,2,1,0:T(8,128)(2,1)} collective-permute-done((bf16[1,1,4,1,32,1024]{5,4,3,2,1,0:T(8,128)(2,1)S(1)}, bf16[1,1,4,1,32,1024]{5,4,3,2,1,0:T(8,128)(2,1)}, u32[]{:S(2)}, u32[]{:S(2)}) %collective-permute-start.7) | collective-permute-done | bytes 262176 | tf_op jit(solution)/shard_map/ppermute | solution.py:41
  51.6 16.0 %collective-permute-done.9 = bf16[4,96,1024]{2,1,0:T(8,128)(2,1)} collective-permute-done((bf16[4,96,1024]{2,1,0:T(8,128)(2,1)}, bf16[4,96,1024]{2,1,0:T(8,128)(2,1)}, u32[]{:S(2)}, u32[]{:S(2)}) %collective-permute-start.9) | collective-permute-done | bytes 786464 | tf_op jit(solution)/shard_map/ppermute | solution.py:41
  73.5 25.5 %collective-permute-done.12 = bf16[4,192,1024]{2,1,0:T(8,128)(2,1)} collective-permute-done((bf16[4,192,1024]{2,1,0:T(8,128)(2,1)}, bf16[4,192,1024]{2,1,0:T(8,128)(2,1)}, u32[]{:S(2)}, u32[]{:S(2)}) %collective-permute-start.12) | collective-permute-done | bytes 1572896 | tf_op jit(solution)/shard_map/ppermute | solution.py:41
  99.0 8.6 %collective-permute-done.11 = bf16[2,1,4,1,32,1024]{5,4,3,2,1,0:T(8,128)(2,1)S(1)} collective-permute-done((bf16[2,1,4,1,32,1024]{5,4,3,2,1,0:T(8,128)(2,1)S(1)}, bf16[2,1,4,1,32,1024]{5,4,3,2,1,0:T(8,128)(2,1)S(1)}, u32[]{:S(2)}, u32[]{:S(2)}) %collective-permute-start.11) | collective-permute-done | bytes 524320 | tf_op jit(solution)/shard_map/ppermute | solution.py:41
  130.6 9.7 %shard_map.237 = (bf16[256,2048]{1,0:T(8,128)(2,1)}, bf16[256,1024]{1,0:T(8,128)(2,1)}) custom-call(s32[1]{0:T(128)} %copy.87.length_ref, f32[256,2048]{1,0:T(8,128)} %fusion.qkv_ref, f32[256,128]{1,0:T(8,128)} %get-tuple-element.313.cos_ref, f32[256,128]{1,0:T(8,128)} %get-tuple-element.314.sin_ref), custom_call_target="tpu_custom_call" | custom-call | tf_op jit(solution)/shard_map/pallas_call | solution.py:60
  140.4 17.5 %collective-permute-done.16 = bf16[4,96,1024]{2,1,0:T(8,128)(2,1)S(1)} collective-permute-done((bf16[4,96,1024]{2,1,0:T(8,128)(2,1)}, bf16[4,96,1024]{2,1,0:T(8,128)(2,1)S(1)}, u32[]{:S(2)}, u32[]{:S(2)}) %collective-permute-start.16) | collective-permute-done | bytes 786464 | tf_op jit(solution)/shard_map/ppermute | solution.py:41
  171.1 13.8 %collective-permute-done.18.refs_0_ = bf16[272,1024]{1,0:T(8,128)(2,1)S(1)} collective-permute-done((bf16[272,1024]{1,0:T(8,128)(2,1)S(1)}, bf16[272,1024]{1,0:T(8,128)(2,1)S(1)}, u32[]{:S(2)}, u32[]{:S(2)}) %collective-permute-start.18) | collective-permute-done | bytes 557088 | tf_op jit(solution)/shard_map/ppermute | solution.py:41
  189.5 9.3 %collective-permute-done.20 = bf16[4,96,1024]{2,1,0:T(8,128)(2,1)S(1)} collective-permute-done((bf16[4,96,1024]{2,1,0:T(8,128)(2,1)S(1)}, bf16[4,96,1024]{2,1,0:T(8,128)(2,1)S(1)}, u32[]{:S(2)}, u32[]{:S(2)}) %collective-permute-start.20) | collective-permute-done | bytes 786464 | tf_op jit(solution)/shard_map/ppermute | solution.py:41
  210.1 5.5 collective-permute-done.21
  218.0 13.6 %collective-permute-done.23 = bf16[4,96,1024]{2,1,0:T(8,128)(2,1)S(1)} collective-permute-done((bf16[4,96,1024]{2,1,0:T(8,128)(2,1)S(1)}, bf16[4,96,1024]{2,1,0:T(8,128)(2,1)S(1)}, u32[]{:S(2)}, u32[]{:S(2)}) %collective-permute-start.23) | collective-permute-done | bytes 786464 | tf_op jit(solution)/shard_map/ppermute | solution.py:41
  234.2 14.1 %shard_map.238 = (bf16[2,256,1024]{2,1,0:T(8,128)(2,1)}, bf16[2,256,1024]{2,1,0:T(8,128)(2,1)}) custom-call(s32[1]{0:T(128)} %bitcast.8.first_ref, bf16[4,8,192,1024]{3,2,1,0:T(8,128)(2,1)} %bitcast_dynamic-update-slice_fusion.11.weights_ref, bf16[272,1024]{1,0:T(8,128)(2,1)} %copy-done.6, bf16[272,1024]{1,0:T(8,128)(2,1)} %copy-done.18, ...), custom_call_target="tpu_custom_call" | custom-call | tf_op jit(solution)/shard_map/pallas_call | solution.py:80
  249.9 13.8 %shard_map.239 = (bf16[2,256,1024]{2,1,0:T(8,128)(2,1)}, bf16[2,256,1024]{2,1,0:T(8,128)(2,1)}) custom-call(s32[1]{0:T(128)} %bitcast.8.first_ref, bf16[4,8,192,1024]{3,2,1,0:T(8,128)(2,1)} %bitcast_dynamic-update-slice_fusion.11.weights_ref, bf16[272,1024]{1,0:T(8,128)(2,1)} %copy-done.17, bf16[272,1024]{1,0:T(8,128)(2,1)} %copy-done.21, ...), custom_call_target="tpu_custom_call" | custom-call | tf_op jit(solution)/shard_map/pallas_call | solution.py:80
  270.9 11.8 %collective-permute-done.33 = bf16[256,1024]{1,0:T(8,128)(2,1)S(1)} collective-permute-done((bf16[256,1024]{1,0:T(8,128)(2,1)S(1)}, bf16[256,1024]{1,0:T(8,128)(2,1)S(1)}, u32[]{:S(2)}, u32[]{:S(2)}) %collective-permute-start.33) | collective-permute-done | bytes 524320 | tf_op jit(solution)/shard_map/ppermute | solution.py:41
  283.7 9.4 %collective-permute-done.28 = bf16[256,1024]{1,0:T(8,128)(2,1)S(1)} collective-permute-done((bf16[256,1024]{1,0:T(8,128)(2,1)S(1)}, bf16[256,1024]{1,0:T(8,128)(2,1)S(1)}, u32[]{:S(2)}, u32[]{:S(2)}) %collective-permute-start.28) | collective-permute-done | bytes 524320 | tf_op jit(solution)/shard_map/ppermute | solution.py:41
  299.4 9.9 %collective-permute-done.40.refs_4_ = bf16[256,1024]{1,0:T(8,128)(2,1)S(1)} collective-permute-done((bf16[256,1024]{1,0:T(8,128)(2,1)S(1)}, bf16[256,1024]{1,0:T(8,128)(2,1)S(1)}, u32[]{:S(2)}, u32[]{:S(2)}) %collective-permute-start.40) | collective-permute-done | bytes 524320 | tf_op jit(solution)/shard_map/ppermute | solution.py:41
  311.3 9.2 %collective-permute-done.47.refs_6_ = bf16[256,1024]{1,0:T(8,128)(2,1)S(1)} collective-permute-done((bf16[256,1024]{1,0:T(8,128)(2,1)S(1)}, bf16[256,1024]{1,0:T(8,128)(2,1)S(1)}, u32[]{:S(2)}, u32[]{:S(2)}) %collective-permute-start.47) | collective-permute-done | bytes 524320 | tf_op jit(solution)/shard_map/ppermute | solution.py:41
  329.5 21.5 %shard_map.240 = (bf16[2,272,1024]{2,1,0:T(8,128)(2,1)}, bf16[2,272,1024]{2,1,0:T(8,128)(2,1)}, bf16[4,384,1024]{2,1,0:T(8,128)(2,1)}, bf16[4,384,1024]{2,1,0:T(...) custom-call(s32[1]{0:T(128)} %bitcast.8.first_ref, ...), custom_call_target="tpu_custom_call" | custom-call | tf_op jit(solution)/shard_map/pallas_call | solution.py:80
  352.6 21.1 %shard_map.241 = (bf16[2,272,1024]{2,1,0:T(8,128)(2,1)}, bf16[2,272,1024]{2,1,0:T(8,128)(2,1)}, bf16[4,384,1024]{2,1,0:T(8,128)(2,1)}, bf16[4,384,1024]{2,1,0:T(...) custom-call(s32[1]{0:T(128)} %bitcast.8.first_ref, ...), custom_call_target="tpu_custom_call" | custom-call | tf_op jit(solution)/shard_map/pallas_call | solution.py:80
  381.3 19.3 %shard_map.242 = (bf16[4,192,1024]{2,1,0:T(8,128)(2,1)}, bf16[4,192,1024]{2,1,0:T(8,128)(2,1)}, bf16[4,192,1024]{2,1,0:T(8,128)(2,1)}, bf16[4,192,1024]{2,1,0:T(...) custom-call(s32[1]{0:T(128)} %bitcast.43.at_ref, ...), custom_call_target="tpu_custom_call" | custom-call | tf_op jit(solution)/shard_map/pallas_call | solution.py:684
  409.4 27.8 %collective-permute-done.37 = f32[8,128]{1,0:T(8,128)S(1)} collective-permute-done((f32[8,128]{1,0:T(8,128)S(1)}, f32[8,128]{1,0:T(8,128)S(1)}, u32[]{:S(2)}, u32[]{:S(2)}) %collective-permute-start.37) | collective-permute-done | bytes 4128 | tf_op jit(solution)/shard_map/ppermute | solution.py:41
  459.8 15.5 %collective-permute-done.53 = bf16[4,192,1024]{2,1,0:T(8,128)(2,1)} collective-permute-done((bf16[4,192,1024]{2,1,0:T(8,128)(2,1)}, bf16[4,192,1024]{2,1,0:T(8,128)(2,1)}, u32[]{:S(2)}, u32[]{:S(2)}) %collective-permute-start.53) | collective-permute-done | bytes 1572896 | tf_op jit(solution)/shard_map/ppermute | solution.py:41
  475.3 9.3 %collective-permute-done.54 = bf16[4,96,1024]{2,1,0:T(8,128)(2,1)} collective-permute-done((bf16[4,96,1024]{2,1,0:T(8,128)(2,1)S(1)}, bf16[4,96,1024]{2,1,0:T(8,128)(2,1)}, u32[]{:S(2)}, u32[]{:S(2)}) %collective-permute-start.54) | collective-permute-done | bytes 786464 | tf_op jit(solution)/shard_map/ppermute | solution.py:41
  487.0 12.3 %shard_map.243.qkv_grad_ref = bf16[256,2048]{1,0:T(8,128)(2,1)} custom-call(s32[1]{0:T(128)} %copy.87.length_ref, bf16[256,2048]{1,0:T(8,128)(2,1)} %get-tuple-element.187.rot_ref, bf16[256,1024]{1,0:T(8,128)(2,1)} %convolution_convert_fusion.1.grad_ref, f32[256,128]{1,0:T(8,128)} %get-tuple-element.313.cos_ref, f32[256,128]{1,0:T(8,128)} %get-tuple-element.314.sin_ref), custom_call_target="tpu_custom_call" | custom-call | tf_op jit(solution)/shard_map/pallas_call | solution.py:60
  502.7 17.8 %collective-permute-done.56 = bf16[4,96,1024]{2,1,0:T(8,128)(2,1)} collective-permute-done((bf16[4,96,1024]{2,1,0:T(8,128)(2,1)}, bf16[4,96,1024]{2,1,0:T(8,128)(2,1)}, u32[]{:S(2)}, u32[]{:S(2)}) %collective-permute-start.56) | collective-permute-done | bytes 786464 | tf_op jit(solution)/shard_map/ppermute | solution.py:41
  523.4 8.9 %shard_map.244 = (bf16[2,256,2176]{2,1,0:T(8,128)(2,1)}, bf16[2,256,2176]{2,1,0:T(8,128)(2,1)}, f32[256,1024]{1,0:T(8,128)}) custom-call(s32[1]{0:T(128)} %bitcast.38.core_ref, bf16[256,2048]{1,0:T(8,128)(2,1)} %shard_map.243.qkv_grad_ref, bf16[256,1024]{1,0:T(8,128)(2,1)} %copy-done.24, bf16[1024,2176]{1,0:T(8,128)(2,1)} %bitcast.129, ...), custom_call_target="tpu_custom_call" | custom-call | tf_op jit(solution)/shard_map/pallas_call | solution.py:60
  534.9 22.2 %collective-permute-done.59 = bf16[4,96,1024]{2,1,0:T(8,128)(2,1)} collective-permute-done((bf16[4,96,1024]{2,1,0:T(8,128)(2,1)}, bf16[4,96,1024]{2,1,0:T(8,128)(2,1)}, u32[]{:S(2)}, u32[]{:S(2)}) %collective-permute-start.59) | collective-permute-done | bytes 786464 | tf_op jit(solution)/shard_map/ppermute | solution.py:41
  575.6 27.1 %collective-permute-done.39 = f32[8,128]{1,0:T(8,128)S(1)} collective-permute-done((f32[8,128]{1,0:T(8,128)S(1)}, f32[8,128]{1,0:T(8,128)S(1)}, u32[]{:S(2)}, u32[]{:S(2)}) %collective-permute-start.39) | collective-permute-done | bytes 4128 | tf_op jit(solution)/shard_map/ppermute | solution.py:41
  610.2 30.1 %collective-permute-done.67 = bf16[4,96,1024]{2,1,0:T(8,128)(2,1)S(1)} collective-permute-done((bf16[4,96,1024]{2,1,0:T(8,128)(2,1)S(1)}, bf16[4,96,1024]{2,1,0:T(8,128)(2,1)S(1)}, u32[]{:S(2)}, u32[]{:S(2)}) %collective-permute-start.67) | collective-permute-done | bytes 786464 | tf_op jit(solution)/shard_map/ppermute | solution.py:41
  642.6 4.2 collective-permute-done.64
  649.5 9.7 %collective-permute-done.69 = bf16[1,1,4,1,32,2176]{5,4,3,2,1,0:T(8,128)(2,1)S(1)} collective-permute-done((bf16[1,1,4,1,32,2176]{5,4,3,2,1,0:T(8,128)(2,1)S(1)}, bf16[1,1,4,1,32,2176]{5,4,3,2,1,0:T(8,128)(2,1)S(1)}, u32[]{:S(2)}, u32[]{:S(2)}) %collective-permute-start.69) | collective-permute-done | bytes 557088 | tf_op jit(solution)/shard_map/ppermute | solution.py:41
  668.2 4.7 collective-permute-done.71
  (370 shorter events, 218.8 us)
Async XLA Ops:
  28.9 38.6 %collective-permute-start.8 = (bf16[4,192,1024]{2,1,0:T(8,128)(2,1)}, bf16[4,192,1024]{2,1,0:T(8,128)(2,1)}, u32[]{:S(2)}, u32[]{:S(2)}) collective-permute-start(bf16[4,192,1024]{2,1,0:T(8,128)(2,1)} %get-tuple-element.269), channel_id=1, source_target_pairs={{0,1},{1,0},{2,3},{3,2},{4,5},{5,4},{6,7},{7,6},{8,9},{9,8},{10,11... | collective-permute-start | bytes 4718600 | tf_op jit(solution)/shard_map/ppermute | solution.py:41
  32.4 35.2 %collective-permute-start.9 = (bf16[4,96,1024]{2,1,0:T(8,128)(2,1)}, bf16[4,96,1024]{2,1,0:T(8,128)(2,1)}, u32[]{:S(2)}, u32[]{:S(2)}) collective-permute-start(bf16[4,96,1024]{2,1,0:T(8,128)(2,1)} %get-tuple-element.151), channel_id=1, source_target_pairs={{0,4},{1,5},{2,6},{3,7},{4,0},{5,1},{6,2},{7,3},{8,12},{9,13},{10,... | collective-permute-start | bytes 2359304 | tf_op jit(solution)/shard_map/ppermute | solution.py:41
  37.8 61.2 %collective-permute-start.12 = (bf16[4,192,1024]{2,1,0:T(8,128)(2,1)}, bf16[4,192,1024]{2,1,0:T(8,128)(2,1)}, u32[]{:S(2)}, u32[]{:S(2)}) collective-permute-start(bf16[4,192,1024]{2,1,0:T(8,128)(2,1)} %constant_dynamic-slice_fusion.9), channel_id=1, source_target_pairs={{0,2},{1,3},{2,0},{3,1},{4,6},{5,7},{6,4},{7,5},{8,10},{9,11},{10,... | collective-permute-start | bytes 4718600 | tf_op jit(solution)/shard_map/ppermute | solution.py:41
  70.3 39.0 %collective-permute-start.10 = (bf16[2,1,4,1,32,2176]{5,4,3,2,1,0:T(8,128)(2,1)}, bf16[2,1,4,1,32,2176]{5,4,3,2,1,0:T(8,128)(2,1)}, u32[]{:S(2)}, u32[]{:S(2)}) collective-permute-start(bf16[2,1,4,1,32,2176]{5,4,3,2,1,0:T(8,128)(2,1)} %maximum_select_fusion.3), channel_id=1, source_target_pairs={{0,1},{1,0},{2,3},{3,2},{4,5},{5,4},{6,7},{7,6},{8,9},{9,8},{10,11... | collective-permute-start | bytes 3342344 | tf_op jit(solution)/shard_map/ppermute | solution.py:41
  70.9 36.7 %collective-permute-start.13 = (bf16[4,96,1024]{2,1,0:T(8,128)(2,1)S(1)}, bf16[4,96,1024]{2,1,0:T(8,128)(2,1)S(1)}, u32[]{:S(2)}, u32[]{:S(2)}) collective-permute-start(bf16[4,96,1024]{2,1,0:T(8,128)(2,1)S(1)} %copy-done.41), channel_id=1, source_target_pairs={{0,4},{1,5},{2,6},{3,7},{4,0},{5,1},{6,2},{7,3},{8,12},{9,13},{10,... | collective-permute-start | bytes 2359304 | tf_op jit(solution)/shard_map/ppermute | solution.py:41
  72.0 35.6 %collective-permute-start.11 = (bf16[2,1,4,1,32,1024]{5,4,3,2,1,0:T(8,128)(2,1)S(1)}, bf16[2,1,4,1,32,1024]{5,4,3,2,1,0:T(8,128)(2,1)S(1)}, u32[]{:S(2)}, u32[]{:S(2)}) collective-permute-start(bf16[2,1,4,1,32,1024]{5,4,3,2,1,0:T(8,128)(2,1)S(1)} %maximum_select_fusion.5), channel_id=1, source_target_pairs={{0,1},{1,0},{2,3},{3,2},{4,5},{5,4},{6,7},{7,6},{8,9},{9,8},{10,11... | collective-permute-start | bytes 1572872 | tf_op jit(solution)/shard_map/ppermute | solution.py:41
  117.6 40.3 %collective-permute-start.17 = (bf16[4,192,1024]{2,1,0:T(8,128)(2,1)}, bf16[4,192,1024]{2,1,0:T(8,128)(2,1)}, u32[]{:S(2)}, u32[]{:S(2)}) collective-permute-start(bf16[4,192,1024]{2,1,0:T(8,128)(2,1)} %collective-permute-done.12), channel_id=1, source_target_pairs={{0,1},{1,0},{2,3},{3,2},{4,5},{5,4},{6,7},{7,6},{8,9},{9,8},{10,11... | collective-permute-start | bytes 4718600 | tf_op jit(solution)/shard_map/ppermute | solution.py:41
  121.2 36.7 %collective-permute-start.16 = (bf16[4,96,1024]{2,1,0:T(8,128)(2,1)}, bf16[4,96,1024]{2,1,0:T(8,128)(2,1)S(1)}, u32[]{:S(2)}, u32[]{:S(2)}) collective-permute-start(bf16[4,96,1024]{2,1,0:T(8,128)(2,1)} %get-tuple-element.170), channel_id=1, source_target_pairs={{0,4},{1,5},{2,6},{3,7},{4,0},{5,1},{6,2},{7,3},{8,12},{9,13},{10,... | collective-permute-start | bytes 2359304 | tf_op jit(solution)/shard_map/ppermute | solution.py:41
  166.0 66.5 %collective-permute-start.24 = (bf16[272,1024]{1,0:T(8,128)(2,1)S(1)}, bf16[272,1024]{1,0:T(8,128)(2,1)S(1)}, u32[]{:S(2)}, u32[]{:S(2)}) collective-permute-start(bf16[272,1024]{1,0:T(8,128)(2,1)S(1)} %pad_maximum_fusion.2.refs_0_), channel_id=1, source_target_pairs={{0,8},{8,0},{16,24},{24,16},{1,9},{9,1},{17,25},{25,17},{2,10},{10... | collective-permute-start | bytes 1671176 | tf_op jit(solution)/shard_map/ppermute | solution.py:41
  166.0 32.7 %collective-permute-start.20 = (bf16[4,96,1024]{2,1,0:T(8,128)(2,1)S(1)}, bf16[4,96,1024]{2,1,0:T(8,128)(2,1)S(1)}, u32[]{:S(2)}, u32[]{:S(2)}) collective-permute-start(bf16[4,96,1024]{2,1,0:T(8,128)(2,1)S(1)} %copy-done.38), channel_id=1, source_target_pairs={{0,1},{1,0},{2,3},{3,2},{4,5},{5,4},{6,7},{7,6},{8,9},{9,8},{10,11... | collective-permute-start | bytes 2359304 | tf_op jit(solution)/shard_map/ppermute | solution.py:41
  166.5 37.5 %collective-permute-start.22 = (bf16[4,96,1024]{2,1,0:T(8,128)(2,1)S(1)}, bf16[4,96,1024]{2,1,0:T(8,128)(2,1)S(1)}, u32[]{:S(2)}, u32[]{:S(2)}) collective-permute-start(bf16[4,96,1024]{2,1,0:T(8,128)(2,1)S(1)} %copy-done.43), channel_id=1, source_target_pairs={{0,4},{1,5},{2,6},{3,7},{4,0},{5,1},{6,2},{7,3},{8,12},{9,13},{10,... | collective-permute-start | bytes 2359304 | tf_op jit(solution)/shard_map/ppermute | solution.py:41
  186.5 29.1 %collective-permute-start.21 = (bf16[4,96,1024]{2,1,0:T(8,128)(2,1)S(1)}, bf16[4,96,1024]{2,1,0:T(8,128)(2,1)S(1)}, u32[]{:S(2)}, u32[]{:S(2)}) collective-permute-start(bf16[4,96,1024]{2,1,0:T(8,128)(2,1)S(1)} %copy-done.40), channel_id=1, source_target_pairs={{0,1},{1,0},{2,3},{3,2},{4,5},{5,4},{6,7},{7,6},{8,9},{9,8},{10,11... | collective-permute-start | bytes 2359304 | tf_op jit(solution)/shard_map/ppermute | solution.py:41
  210.1 38.2 %collective-permute-start.29 = (bf16[272,1024]{1,0:T(8,128)(2,1)S(1)}, bf16[272,1024]{1,0:T(8,128)(2,1)S(1)}, u32[]{:S(2)}, u32[]{:S(2)}) collective-permute-start(bf16[272,1024]{1,0:T(8,128)(2,1)S(1)} %collective-permute-done.18.refs_0_), channel_id=1, source_target_pairs={{0,8},{8,0},{16,24},{24,16},{1,9},{9,1},{17,25},{25,17},{2,10},{10... | collective-permute-start | bytes 1671176 | tf_op jit(solution)/shard_map/ppermute | solution.py:41
  215.6 32.7 %collective-permute-start.31 = (bf16[272,1024]{1,0:T(8,128)(2,1)S(1)}, bf16[272,1024]{1,0:T(8,128)(2,1)S(1)}, u32[]{:S(2)}, u32[]{:S(2)}) collective-permute-start(bf16[272,1024]{1,0:T(8,128)(2,1)S(1)} %collective-permute-done.30.refs_2_), channel_id=1, source_target_pairs={{0,8},{8,0},{16,24},{24,16},{1,9},{9,1},{17,25},{25,17},{2,10},{10... | collective-permute-start | bytes 1671176 | tf_op jit(solution)/shard_map/ppermute | solution.py:41
  310.8 40.2 %collective-permute-start.46 = (bf16[256,1024]{1,0:T(8,128)(2,1)S(1)}, bf16[256,1024]{1,0:T(8,128)(2,1)S(1)}, u32[]{:S(2)}, u32[]{:S(2)}) collective-permute-start(bf16[256,1024]{1,0:T(8,128)(2,1)S(1)} %collective-permute-done.40.refs_4_), channel_id=1, source_target_pairs={{0,8},{8,0},{16,24},{24,16},{1,9},{9,1},{17,25},{25,17},{2,10},{10... | collective-permute-start | bytes 1572872 | tf_op jit(solution)/shard_map/ppermute | solution.py:41
  320.6 30.5 %collective-permute-start.48 = (bf16[256,1024]{1,0:T(8,128)(2,1)S(1)}, bf16[256,1024]{1,0:T(8,128)(2,1)S(1)}, u32[]{:S(2)}, u32[]{:S(2)}) collective-permute-start(bf16[256,1024]{1,0:T(8,128)(2,1)S(1)} %collective-permute-done.47.refs_6_), channel_id=1, source_target_pairs={{0,8},{8,0},{16,24},{24,16},{1,9},{9,1},{17,25},{25,17},{2,10},{10... | collective-permute-start | bytes 1572872 | tf_op jit(solution)/shard_map/ppermute | solution.py:41
  373.8 28.4 %collective-permute-start.44 = (bf16[2,272,1024]{2,1,0:T(8,128)(2,1)}, bf16[2,272,1024]{2,1,0:T(8,128)(2,1)}, u32[]{:S(2)}, u32[]{:S(2)}) collective-permute-start(bf16[2,272,1024]{2,1,0:T(8,128)(2,1)} %get-tuple-element.190), channel_id=1, source_target_pairs={{0,8},{8,0},{16,24},{24,16},{1,9},{9,1},{17,25},{25,17},{2,10},{10... | collective-permute-start | bytes 3342344 | tf_op jit(solution)/shard_map/ppermute | solution.py:41
  400.6 44.5 %collective-permute-start.52 = (bf16[4,192,1024]{2,1,0:T(8,128)(2,1)}, bf16[4,192,1024]{2,1,0:T(8,128)(2,1)}, u32[]{:S(2)}, u32[]{:S(2)}) collective-permute-start(bf16[4,192,1024]{2,1,0:T(8,128)(2,1)} %get-tuple-element.205), channel_id=1, source_target_pairs={{0,1},{1,0},{2,3},{3,2},{4,5},{5,4},{6,7},{7,6},{8,9},{9,8},{10,11... | collective-permute-start | bytes 4718600 | tf_op jit(solution)/shard_map/ppermute | solution.py:41
  404.4 37.9 %collective-permute-start.45 = (bf16[272,1024]{1,0:T(8,128)(2,1)}, bf16[272,1024]{1,0:T(8,128)(2,1)S(1)}, u32[]{:S(2)}, u32[]{:S(2)}) collective-permute-start(bf16[272,1024]{1,0:T(8,128)(2,1)} %fusion.10), channel_id=1, source_target_pairs={{0,16},{8,24},{16,0},{24,8},{1,17},{9,25},{17,1},{25,9},{2,18},{10... | collective-permute-start | bytes 1671176 | tf_op jit(solution)/shard_map/ppermute | solution.py:41
  407.2 36.6 %collective-permute-start.51 = (bf16[272,1024]{1,0:T(8,128)(2,1)}, bf16[272,1024]{1,0:T(8,128)(2,1)}, u32[]{:S(2)}, u32[]{:S(2)}) collective-permute-start(bf16[272,1024]{1,0:T(8,128)(2,1)} %fusion.7), channel_id=1, source_target_pairs={{0,2},{1,3},{2,0},{3,1},{4,6},{5,7},{6,4},{7,5},{8,10},{9,11},{10,... | collective-permute-start | bytes 1671176 | tf_op jit(solution)/shard_map/ppermute | solution.py:41
  440.8 34.5 %collective-permute-start.53 = (bf16[4,192,1024]{2,1,0:T(8,128)(2,1)}, bf16[4,192,1024]{2,1,0:T(8,128)(2,1)}, u32[]{:S(2)}, u32[]{:S(2)}) collective-permute-start(bf16[4,192,1024]{2,1,0:T(8,128)(2,1)} %get-tuple-element.207), channel_id=1, source_target_pairs={{0,1},{1,0},{2,3},{3,2},{4,5},{5,4},{6,7},{7,6},{8,9},{9,8},{10,11... | collective-permute-start | bytes 4718600 | tf_op jit(solution)/shard_map/ppermute | solution.py:41
  449.7 34.9 %collective-permute-start.54 = (bf16[4,96,1024]{2,1,0:T(8,128)(2,1)S(1)}, bf16[4,96,1024]{2,1,0:T(8,128)(2,1)}, u32[]{:S(2)}, u32[]{:S(2)}) collective-permute-start(bf16[4,96,1024]{2,1,0:T(8,128)(2,1)S(1)} %get-tuple-element.281), channel_id=1, source_target_pairs={{0,4},{1,5},{2,6},{3,7},{4,0},{5,1},{6,2},{7,3},{8,12},{9,13},{10,... | collective-permute-start | bytes 2359304 | tf_op jit(solution)/shard_map/ppermute | solution.py:41
  457.9 44.8 %collective-permute-start.55 = (bf16[2,1,4,2,32,1024]{5,4,3,2,1,0:T(8,128)(2,1)}, bf16[2,1,4,2,32,1024]{5,4,3,2,1,0:T(8,128)(2,1)S(1)}, u32[]{:S(2)}, u32[]{:S(2)}) collective-permute-start(bf16[2,1,4,2,32,1024]{5,4,3,2,1,0:T(8,128)(2,1)} %get-tuple-element.276), channel_id=1, source_target_pairs={{0,8},{8,0},{16,24},{24,16},{1,9},{9,1},{17,25},{25,17},{2,10},{10... | collective-permute-start | bytes 3145736 | tf_op jit(solution)/shard_map/ppermute | solution.py:41
  484.6 35.9 %collective-permute-start.56 = (bf16[4,96,1024]{2,1,0:T(8,128)(2,1)}, bf16[4,96,1024]{2,1,0:T(8,128)(2,1)}, u32[]{:S(2)}, u32[]{:S(2)}) collective-permute-start(bf16[4,96,1024]{2,1,0:T(8,128)(2,1)} %get-tuple-element.212), channel_id=1, source_target_pairs={{0,4},{1,5},{2,6},{3,7},{4,0},{5,1},{6,2},{7,3},{8,12},{9,13},{10,... | collective-permute-start | bytes 2359304 | tf_op jit(solution)/shard_map/ppermute | solution.py:41
  486.5 45.9 %collective-permute-start.58 = (bf16[4,192,1024]{2,1,0:T(8,128)(2,1)}, bf16[4,192,1024]{2,1,0:T(8,128)(2,1)S(1)}, u32[]{:S(2)}, u32[]{:S(2)}) collective-permute-start(bf16[4,192,1024]{2,1,0:T(8,128)(2,1)} %get-tuple-element.219), channel_id=1, source_target_pairs={{0,1},{1,0},{2,3},{3,2},{4,5},{5,4},{6,7},{7,6},{8,9},{9,8},{10,11... | collective-permute-start | bytes 4718600 | tf_op jit(solution)/shard_map/ppermute | solution.py:41
  520.5 36.6 %collective-permute-start.59 = (bf16[4,96,1024]{2,1,0:T(8,128)(2,1)}, bf16[4,96,1024]{2,1,0:T(8,128)(2,1)}, u32[]{:S(2)}, u32[]{:S(2)}) collective-permute-start(bf16[4,96,1024]{2,1,0:T(8,128)(2,1)} %get-tuple-element.222), channel_id=1, source_target_pairs={{0,4},{1,5},{2,6},{3,7},{4,0},{5,1},{6,2},{7,3},{8,12},{9,13},{10,... | collective-permute-start | bytes 2359304 | tf_op jit(solution)/shard_map/ppermute | solution.py:41
  568.3 78.4 %collective-permute-start.66 = (bf16[4,192,1024]{2,1,0:T(8,128)(2,1)}, bf16[4,192,1024]{2,1,0:T(8,128)(2,1)}, u32[]{:S(2)}, u32[]{:S(2)}) collective-permute-start(bf16[4,192,1024]{2,1,0:T(8,128)(2,1)} %get-tuple-element.234), channel_id=1, source_target_pairs={{0,1},{1,0},{2,3},{3,2},{4,5},{5,4},{6,7},{7,6},{8,9},{9,8},{10,11... | collective-permute-start | bytes 4718600 | tf_op jit(solution)/shard_map/ppermute | solution.py:41
  568.9 77.9 %collective-permute-start.68 = (bf16[4,192,1024]{2,1,0:T(8,128)(2,1)}, bf16[4,192,1024]{2,1,0:T(8,128)(2,1)}, u32[]{:S(2)}, u32[]{:S(2)}) collective-permute-start(bf16[4,192,1024]{2,1,0:T(8,128)(2,1)} %add_convert_fusion), channel_id=1, source_target_pairs={{0,2},{1,3},{2,0},{3,1},{4,6},{5,7},{6,4},{7,5},{8,10},{9,11},{10,... | collective-permute-start | bytes 4718600 | tf_op jit(solution)/shard_map/ppermute | solution.py:41
  571.8 75.0 %collective-permute-start.62 = (bf16[1,1,4,2,32,2176]{5,4,3,2,1,0:T(8,128)(2,1)S(1)}, bf16[1,1,4,2,32,2176]{5,4,3,2,1,0:T(8,128)(2,1)S(1)}, u32[]{:S(2)}, u32[]{:S(2)}) collective-permute-start(bf16[1,1,4,2,32,2176]{5,4,3,2,1,0:T(8,128)(2,1)S(1)} %dynamic-slice_convert_fusion), channel_id=1, source_target_pairs={{0,16},{8,24},{16,0},{24,8},{1,17},{9,25},{17,1},{25,9},{2,18},{10... | collective-permute-start | bytes 3342344 | tf_op jit(solution)/shard_map/ppermute | solution.py:41
  572.4 30.3 %collective-permute-start.39 = (f32[8,128]{1,0:T(8,128)S(1)}, f32[8,128]{1,0:T(8,128)S(1)}, u32[]{:S(2)}, u32[]{:S(2)}) collective-permute-start(f32[8,128]{1,0:T(8,128)S(1)} %add.291), channel_id=1, source_target_pairs={{0,4},{1,5},{2,6},{3,7},{4,0},{5,1},{6,2},{7,3},{8,12},{9,13},{10,... | collective-permute-start | bytes 12296 | tf_op jit(solution)/shard_map/ppermute | solution.py:41
  603.9 36.4 %collective-permute-start.67 = (bf16[4,96,1024]{2,1,0:T(8,128)(2,1)S(1)}, bf16[4,96,1024]{2,1,0:T(8,128)(2,1)S(1)}, u32[]{:S(2)}, u32[]{:S(2)}) collective-permute-start(bf16[4,96,1024]{2,1,0:T(8,128)(2,1)S(1)} %copy-done.42), channel_id=1, source_target_pairs={{0,4},{1,5},{2,6},{3,7},{4,0},{5,1},{6,2},{7,3},{8,12},{9,13},{10,... | collective-permute-start | bytes 2359304 | tf_op jit(solution)/shard_map/ppermute | solution.py:41
  608.3 32.0 %collective-permute-start.63 = (bf16[1,1,1,1,32,1024]{5,4,3,2,1,0:T(8,128)(2,1)S(1)}, bf16[1,1,1,1,32,1024]{5,4,3,2,1,0:T(8,128)(2,1)S(1)}, u32[]{:S(2)}, u32[]{:S(2)}) collective-permute-start(bf16[1,1,1,1,32,1024]{5,4,3,2,1,0:T(8,128)(2,1)S(1)} %get-tuple-element.295), channel_id=1, source_target_pairs={{0,2},{1,3},{2,0},{3,1},{4,6},{5,7},{6,4},{7,5},{8,10},{9,11},{10,... | collective-permute-start | bytes 196616 | tf_op jit(solution)/shard_map/ppermute | solution.py:41
  (105 other events, 1355.6 us)

commit v10 on v9

--- a/solution.py
+++ b/solution.py
@@ -701,7 +701,7 @@
     order_of = sorted(range(0, shards, 2), key=lambda m: -m)
     low_got = {m: swap(expert_grad[m ^ 1], "fsdp", 1) for m in order_of[:-1]}
     first_low = order_of[0]
-    returned, low_got[first_low] = join((finish((expert_grad[0], loss_steps[3])), low_got[first_low]))
+    returned, low_got[first_low] = join((finish((expert_grad[0], loss_steps[-1])), low_got[first_low]))
     sums_of = {}
 
     def low_sum(m):

time: 689 us -> 671 us (0.974)
  waiting for transfers between devices: 353 us -> 334 us
    ppermute x73, waiting for transfers between devices: 353 us -> 334 us  [swap(): lax.ppermute(values, axis, [(i, i ^ mask) for i in range(lax.axis_size(ax...]
  transfers between devices with their start and end apart: 73 -> 73, of which waited for: 33 -> 35; matrix products, arithmetic and copies ran while one was open for 14% -> 15% of each run, Pallas kernels for 13% -> 13%
where the time goes in v10:
time: 671 us; the launch traced here: 665 us
  waiting for transfers between devices  334 us (50%)
  Pallas kernels  121 us (18%)
  starting transfers between devices  71.2 us (11%)
  local copies, waits for them, and re-layouts  66.7 us (10%)
  other arithmetic  57.3 us (9%)
  matrix products  9.62 us (1%)
    ppermute x73, waiting for transfers between devices, swap(): lax.ppermute(values, axis, [(i, i ^ mask) for i in range(lax.axis_size(ax...  334 us
    ppermute x73, starting transfers between devices, swap(): lax.ppermute(values, axis, [(i, i ^ mask) for i in range(lax.axis_size(ax...  71.2 us
    pallas_call x4, Pallas kernels, expert_call(): pl.pallas_call(body, grid=(held,), out_shape=out_shape, in_specs=[smem(),...  70.5 us
    pallas_call x3, Pallas kernels, kernel_call(): pl.pallas_call(body, out_shape=out_shape, in_specs=specs, out_specs=jax.t...  30.9 us
    dynamic_update_slice x12, local copies, waits for them, and re-layouts, on_device(): lax.dynamic_update_slice(expert_w, piece[:, None], (0, fsdp_at ^ m, row, 0))  20.2 us
    pallas_call x1, Pallas kernels, on_device(): pl.pallas_call(functools.partial(expert_weight_grads, HOPS), grid=(held,)...  19.3 us
    unnamed x128, local copies, waits for them, and re-layouts  17.8 us
  transfers between devices with their start and end apart: 73, of which 35 were waited for; matrix products, arithmetic and copies ran while one was open for 15% of the time, Pallas kernels for 13%

profile of v10, /device:TPU:0, one launch (start us, length us, event | category | flops | bytes accessed | tf_op | source)
XLA Modules:
  0.0 665.2 jit_solution(14289665677033837771)
XLA Ops:
  20.7 6.1 broadcast_in_dim.119
  38.4 13.1 %collective-permute-done.7 = bf16[1,1,4,1,32,1024]{5,4,3,2,1,0:T(8,128)(2,1)} collective-permute-done((bf16[1,1,4,1,32,1024]{5,4,3,2,1,0:T(8,128)(2,1)S(1)}, bf16[1,1,4,1,32,1024]{5,4,3,2,1,0:T(8,128)(2,1)}, u32[]{:S(2)}, u32[]{:S(2)}) %collective-permute-start.7) | collective-permute-done | bytes 262176 | tf_op jit(solution)/shard_map/ppermute | solution.py:41
  51.6 16.0 %collective-permute-done.9 = bf16[4,96,1024]{2,1,0:T(8,128)(2,1)} collective-permute-done((bf16[4,96,1024]{2,1,0:T(8,128)(2,1)}, bf16[4,96,1024]{2,1,0:T(8,128)(2,1)}, u32[]{:S(2)}, u32[]{:S(2)}) %collective-permute-start.9) | collective-permute-done | bytes 786464 | tf_op jit(solution)/shard_map/ppermute | solution.py:41
  73.5 25.5 %collective-permute-done.12 = bf16[4,192,1024]{2,1,0:T(8,128)(2,1)} collective-permute-done((bf16[4,192,1024]{2,1,0:T(8,128)(2,1)}, bf16[4,192,1024]{2,1,0:T(8,128)(2,1)}, u32[]{:S(2)}, u32[]{:S(2)}) %collective-permute-start.12) | collective-permute-done | bytes 1572896 | tf_op jit(solution)/shard_map/ppermute | solution.py:41
  99.0 8.6 %collective-permute-done.11 = bf16[2,1,4,1,32,1024]{5,4,3,2,1,0:T(8,128)(2,1)S(1)} collective-permute-done((bf16[2,1,4,1,32,1024]{5,4,3,2,1,0:T(8,128)(2,1)S(1)}, bf16[2,1,4,1,32,1024]{5,4,3,2,1,0:T(8,128)(2,1)S(1)}, u32[]{:S(2)}, u32[]{:S(2)}) %collective-permute-start.11) | collective-permute-done | bytes 524320 | tf_op jit(solution)/shard_map/ppermute | solution.py:41
  130.6 9.7 %shard_map.237 = (bf16[256,2048]{1,0:T(8,128)(2,1)}, bf16[256,1024]{1,0:T(8,128)(2,1)}) custom-call(s32[1]{0:T(128)} %copy.87.length_ref, f32[256,2048]{1,0:T(8,128)} %fusion.qkv_ref, f32[256,128]{1,0:T(8,128)} %get-tuple-element.313.cos_ref, f32[256,128]{1,0:T(8,128)} %get-tuple-element.314.sin_ref), custom_call_target="tpu_custom_call" | custom-call | tf_op jit(solution)/shard_map/pallas_call | solution.py:60
  140.4 17.5 %collective-permute-done.16 = bf16[4,96,1024]{2,1,0:T(8,128)(2,1)S(1)} collective-permute-done((bf16[4,96,1024]{2,1,0:T(8,128)(2,1)}, bf16[4,96,1024]{2,1,0:T(8,128)(2,1)S(1)}, u32[]{:S(2)}, u32[]{:S(2)}) %collective-permute-start.16) | collective-permute-done | bytes 786464 | tf_op jit(solution)/shard_map/ppermute | solution.py:41
  171.1 13.8 %collective-permute-done.18.refs_0_ = bf16[272,1024]{1,0:T(8,128)(2,1)S(1)} collective-permute-done((bf16[272,1024]{1,0:T(8,128)(2,1)S(1)}, bf16[272,1024]{1,0:T(8,128)(2,1)S(1)}, u32[]{:S(2)}, u32[]{:S(2)}) %collective-permute-start.18) | collective-permute-done | bytes 557088 | tf_op jit(solution)/shard_map/ppermute | solution.py:41
  189.5 9.3 %collective-permute-done.20 = bf16[4,96,1024]{2,1,0:T(8,128)(2,1)S(1)} collective-permute-done((bf16[4,96,1024]{2,1,0:T(8,128)(2,1)S(1)}, bf16[4,96,1024]{2,1,0:T(8,128)(2,1)S(1)}, u32[]{:S(2)}, u32[]{:S(2)}) %collective-permute-start.20) | collective-permute-done | bytes 786464 | tf_op jit(solution)/shard_map/ppermute | solution.py:41
  200.3 3.7 collective-permute-done.22
  210.1 5.5 collective-permute-done.21
  218.0 13.6 %collective-permute-done.23 = bf16[4,96,1024]{2,1,0:T(8,128)(2,1)S(1)} collective-permute-done((bf16[4,96,1024]{2,1,0:T(8,128)(2,1)S(1)}, bf16[4,96,1024]{2,1,0:T(8,128)(2,1)S(1)}, u32[]{:S(2)}, u32[]{:S(2)}) %collective-permute-start.23) | collective-permute-done | bytes 786464 | tf_op jit(solution)/shard_map/ppermute | solution.py:41
  234.2 14.1 %shard_map.238 = (bf16[2,256,1024]{2,1,0:T(8,128)(2,1)}, bf16[2,256,1024]{2,1,0:T(8,128)(2,1)}) custom-call(s32[1]{0:T(128)} %bitcast.8.first_ref, bf16[4,8,192,1024]{3,2,1,0:T(8,128)(2,1)} %bitcast_dynamic-update-slice_fusion.11.weights_ref, bf16[272,1024]{1,0:T(8,128)(2,1)} %copy-done.6, bf16[272,1024]{1,0:T(8,128)(2,1)} %copy-done.18, ...), custom_call_target="tpu_custom_call" | custom-call | tf_op jit(solution)/shard_map/pallas_call | solution.py:80
  249.9 13.8 %shard_map.239 = (bf16[2,256,1024]{2,1,0:T(8,128)(2,1)}, bf16[2,256,1024]{2,1,0:T(8,128)(2,1)}) custom-call(s32[1]{0:T(128)} %bitcast.8.first_ref, bf16[4,8,192,1024]{3,2,1,0:T(8,128)(2,1)} %bitcast_dynamic-update-slice_fusion.11.weights_ref, bf16[272,1024]{1,0:T(8,128)(2,1)} %copy-done.17, bf16[272,1024]{1,0:T(8,128)(2,1)} %copy-done.21, ...), custom_call_target="tpu_custom_call" | custom-call | tf_op jit(solution)/shard_map/pallas_call | solution.py:80
  270.9 11.8 %collective-permute-done.33 = bf16[256,1024]{1,0:T(8,128)(2,1)S(1)} collective-permute-done((bf16[256,1024]{1,0:T(8,128)(2,1)S(1)}, bf16[256,1024]{1,0:T(8,128)(2,1)S(1)}, u32[]{:S(2)}, u32[]{:S(2)}) %collective-permute-start.33) | collective-permute-done | bytes 524320 | tf_op jit(solution)/shard_map/ppermute | solution.py:41
  283.7 9.4 %collective-permute-done.28 = bf16[256,1024]{1,0:T(8,128)(2,1)S(1)} collective-permute-done((bf16[256,1024]{1,0:T(8,128)(2,1)S(1)}, bf16[256,1024]{1,0:T(8,128)(2,1)S(1)}, u32[]{:S(2)}, u32[]{:S(2)}) %collective-permute-start.28) | collective-permute-done | bytes 524320 | tf_op jit(solution)/shard_map/ppermute | solution.py:41
  299.4 9.9 %collective-permute-done.40.refs_4_ = bf16[256,1024]{1,0:T(8,128)(2,1)S(1)} collective-permute-done((bf16[256,1024]{1,0:T(8,128)(2,1)S(1)}, bf16[256,1024]{1,0:T(8,128)(2,1)S(1)}, u32[]{:S(2)}, u32[]{:S(2)}) %collective-permute-start.40) | collective-permute-done | bytes 524320 | tf_op jit(solution)/shard_map/ppermute | solution.py:41
  311.3 9.2 %collective-permute-done.47.refs_6_ = bf16[256,1024]{1,0:T(8,128)(2,1)S(1)} collective-permute-done((bf16[256,1024]{1,0:T(8,128)(2,1)S(1)}, bf16[256,1024]{1,0:T(8,128)(2,1)S(1)}, u32[]{:S(2)}, u32[]{:S(2)}) %collective-permute-start.47) | collective-permute-done | bytes 524320 | tf_op jit(solution)/shard_map/ppermute | solution.py:41
  329.5 21.5 %shard_map.240 = (bf16[2,272,1024]{2,1,0:T(8,128)(2,1)}, bf16[2,272,1024]{2,1,0:T(8,128)(2,1)}, bf16[4,384,1024]{2,1,0:T(8,128)(2,1)}, bf16[4,384,1024]{2,1,0:T(...) custom-call(s32[1]{0:T(128)} %bitcast.8.first_ref, ...), custom_call_target="tpu_custom_call" | custom-call | tf_op jit(solution)/shard_map/pallas_call | solution.py:80
  352.6 21.1 %shard_map.241 = (bf16[2,272,1024]{2,1,0:T(8,128)(2,1)}, bf16[2,272,1024]{2,1,0:T(8,128)(2,1)}, bf16[4,384,1024]{2,1,0:T(8,128)(2,1)}, bf16[4,384,1024]{2,1,0:T(...) custom-call(s32[1]{0:T(128)} %bitcast.8.first_ref, ...), custom_call_target="tpu_custom_call" | custom-call | tf_op jit(solution)/shard_map/pallas_call | solution.py:80
  381.3 19.3 %shard_map.242 = (bf16[4,192,1024]{2,1,0:T(8,128)(2,1)}, bf16[4,192,1024]{2,1,0:T(8,128)(2,1)}, bf16[4,192,1024]{2,1,0:T(8,128)(2,1)}, bf16[4,192,1024]{2,1,0:T(...) custom-call(s32[1]{0:T(128)} %bitcast.43.at_ref, ...), custom_call_target="tpu_custom_call" | custom-call | tf_op jit(solution)/shard_map/pallas_call | solution.py:684
  409.4 27.8 %collective-permute-done.37 = f32[8,128]{1,0:T(8,128)S(1)} collective-permute-done((f32[8,128]{1,0:T(8,128)S(1)}, f32[8,128]{1,0:T(8,128)S(1)}, u32[]{:S(2)}, u32[]{:S(2)}) %collective-permute-start.37) | collective-permute-done | bytes 4128 | tf_op jit(solution)/shard_map/ppermute | solution.py:41
  464.3 14.4 %collective-permute-done.53 = bf16[4,192,1024]{2,1,0:T(8,128)(2,1)} collective-permute-done((bf16[4,192,1024]{2,1,0:T(8,128)(2,1)}, bf16[4,192,1024]{2,1,0:T(8,128)(2,1)}, u32[]{:S(2)}, u32[]{:S(2)}) %collective-permute-start.53) | collective-permute-done | bytes 1572896 | tf_op jit(solution)/shard_map/ppermute | solution.py:41
  478.7 9.3 %collective-permute-done.54 = bf16[4,96,1024]{2,1,0:T(8,128)(2,1)} collective-permute-done((bf16[4,96,1024]{2,1,0:T(8,128)(2,1)S(1)}, bf16[4,96,1024]{2,1,0:T(8,128)(2,1)}, u32[]{:S(2)}, u32[]{:S(2)}) %collective-permute-start.54) | collective-permute-done | bytes 786464 | tf_op jit(solution)/shard_map/ppermute | solution.py:41
  490.4 12.3 %shard_map.243.qkv_grad_ref = bf16[256,2048]{1,0:T(8,128)(2,1)} custom-call(s32[1]{0:T(128)} %copy.87.length_ref, bf16[256,2048]{1,0:T(8,128)(2,1)} %get-tuple-element.187.rot_ref, bf16[256,1024]{1,0:T(8,128)(2,1)} %convolution_convert_fusion.1.grad_ref, f32[256,128]{1,0:T(8,128)} %get-tuple-element.313.cos_ref, f32[256,128]{1,0:T(8,128)} %get-tuple-element.314.sin_ref), custom_call_target="tpu_custom_call" | custom-call | tf_op jit(solution)/shard_map/pallas_call | solution.py:60
  506.0 17.8 %collective-permute-done.56 = bf16[4,96,1024]{2,1,0:T(8,128)(2,1)} collective-permute-done((bf16[4,96,1024]{2,1,0:T(8,128)(2,1)}, bf16[4,96,1024]{2,1,0:T(8,128)(2,1)}, u32[]{:S(2)}, u32[]{:S(2)}) %collective-permute-start.56) | collective-permute-done | bytes 786464 | tf_op jit(solution)/shard_map/ppermute | solution.py:41
  526.8 8.9 %shard_map.244 = (bf16[2,256,2176]{2,1,0:T(8,128)(2,1)}, bf16[2,256,2176]{2,1,0:T(8,128)(2,1)}, f32[256,1024]{1,0:T(8,128)}) custom-call(s32[1]{0:T(128)} %bitcast.38.core_ref, bf16[256,2048]{1,0:T(8,128)(2,1)} %shard_map.243.qkv_grad_ref, bf16[256,1024]{1,0:T(8,128)(2,1)} %copy-done.24, bf16[1024,2176]{1,0:T(8,128)(2,1)} %bitcast.129, ...), custom_call_target="tpu_custom_call" | custom-call | tf_op jit(solution)/shard_map/pallas_call | solution.py:60
  538.2 22.2 %collective-permute-done.59 = bf16[4,96,1024]{2,1,0:T(8,128)(2,1)} collective-permute-done((bf16[4,96,1024]{2,1,0:T(8,128)(2,1)}, bf16[4,96,1024]{2,1,0:T(8,128)(2,1)}, u32[]{:S(2)}, u32[]{:S(2)}) %collective-permute-start.59) | collective-permute-done | bytes 786464 | tf_op jit(solution)/shard_map/ppermute | solution.py:41
  564.6 3.6 add_convert_fusion
  568.2 3.5 collective-permute-done.61
  583.2 40.3 %collective-permute-done.67 = bf16[4,96,1024]{2,1,0:T(8,128)(2,1)S(1)} collective-permute-done((bf16[4,96,1024]{2,1,0:T(8,128)(2,1)S(1)}, bf16[4,96,1024]{2,1,0:T(8,128)(2,1)S(1)}, u32[]{:S(2)}, u32[]{:S(2)}) %collective-permute-start.67) | collective-permute-done | bytes 786464 | tf_op jit(solution)/shard_map/ppermute | solution.py:41
  635.8 9.1 %collective-permute-done.69 = bf16[1,1,4,1,32,2176]{5,4,3,2,1,0:T(8,128)(2,1)S(1)} collective-permute-done((bf16[1,1,4,1,32,2176]{5,4,3,2,1,0:T(8,128)(2,1)S(1)}, bf16[1,1,4,1,32,2176]{5,4,3,2,1,0:T(8,128)(2,1)S(1)}, u32[]{:S(2)}, u32[]{:S(2)}) %collective-permute-start.69) | collective-permute-done | bytes 557088 | tf_op jit(solution)/shard_map/ppermute | solution.py:41
  (370 shorter events, 217.9 us)
Async XLA Ops:
  28.9 38.6 %collective-permute-start.8 = (bf16[4,192,1024]{2,1,0:T(8,128)(2,1)}, bf16[4,192,1024]{2,1,0:T(8,128)(2,1)}, u32[]{:S(2)}, u32[]{:S(2)}) collective-permute-start(bf16[4,192,1024]{2,1,0:T(8,128)(2,1)} %get-tuple-element.269), channel_id=1, source_target_pairs={{0,1},{1,0},{2,3},{3,2},{4,5},{5,4},{6,7},{7,6},{8,9},{9,8},{10,11... | collective-permute-start | bytes 4718600 | tf_op jit(solution)/shard_map/ppermute | solution.py:41
  32.4 35.2 %collective-permute-start.9 = (bf16[4,96,1024]{2,1,0:T(8,128)(2,1)}, bf16[4,96,1024]{2,1,0:T(8,128)(2,1)}, u32[]{:S(2)}, u32[]{:S(2)}) collective-permute-start(bf16[4,96,1024]{2,1,0:T(8,128)(2,1)} %get-tuple-element.151), channel_id=1, source_target_pairs={{0,4},{1,5},{2,6},{3,7},{4,0},{5,1},{6,2},{7,3},{8,12},{9,13},{10,... | collective-permute-start | bytes 2359304 | tf_op jit(solution)/shard_map/ppermute | solution.py:41
  37.8 61.2 %collective-permute-start.12 = (bf16[4,192,1024]{2,1,0:T(8,128)(2,1)}, bf16[4,192,1024]{2,1,0:T(8,128)(2,1)}, u32[]{:S(2)}, u32[]{:S(2)}) collective-permute-start(bf16[4,192,1024]{2,1,0:T(8,128)(2,1)} %constant_dynamic-slice_fusion.9), channel_id=1, source_target_pairs={{0,2},{1,3},{2,0},{3,1},{4,6},{5,7},{6,4},{7,5},{8,10},{9,11},{10,... | collective-permute-start | bytes 4718600 | tf_op jit(solution)/shard_map/ppermute | solution.py:41
  70.3 39.0 %collective-permute-start.10 = (bf16[2,1,4,1,32,2176]{5,4,3,2,1,0:T(8,128)(2,1)}, bf16[2,1,4,1,32,2176]{5,4,3,2,1,0:T(8,128)(2,1)}, u32[]{:S(2)}, u32[]{:S(2)}) collective-permute-start(bf16[2,1,4,1,32,2176]{5,4,3,2,1,0:T(8,128)(2,1)} %maximum_select_fusion.3), channel_id=1, source_target_pairs={{0,1},{1,0},{2,3},{3,2},{4,5},{5,4},{6,7},{7,6},{8,9},{9,8},{10,11... | collective-permute-start | bytes 3342344 | tf_op jit(solution)/shard_map/ppermute | solution.py:41
  70.9 36.7 %collective-permute-start.13 = (bf16[4,96,1024]{2,1,0:T(8,128)(2,1)S(1)}, bf16[4,96,1024]{2,1,0:T(8,128)(2,1)S(1)}, u32[]{:S(2)}, u32[]{:S(2)}) collective-permute-start(bf16[4,96,1024]{2,1,0:T(8,128)(2,1)S(1)} %copy-done.41), channel_id=1, source_target_pairs={{0,4},{1,5},{2,6},{3,7},{4,0},{5,1},{6,2},{7,3},{8,12},{9,13},{10,... | collective-permute-start | bytes 2359304 | tf_op jit(solution)/shard_map/ppermute | solution.py:41
  72.0 35.6 %collective-permute-start.11 = (bf16[2,1,4,1,32,1024]{5,4,3,2,1,0:T(8,128)(2,1)S(1)}, bf16[2,1,4,1,32,1024]{5,4,3,2,1,0:T(8,128)(2,1)S(1)}, u32[]{:S(2)}, u32[]{:S(2)}) collective-permute-start(bf16[2,1,4,1,32,1024]{5,4,3,2,1,0:T(8,128)(2,1)S(1)} %maximum_select_fusion.5), channel_id=1, source_target_pairs={{0,1},{1,0},{2,3},{3,2},{4,5},{5,4},{6,7},{7,6},{8,9},{9,8},{10,11... | collective-permute-start | bytes 1572872 | tf_op jit(solution)/shard_map/ppermute | solution.py:41
  117.6 40.3 %collective-permute-start.17 = (bf16[4,192,1024]{2,1,0:T(8,128)(2,1)}, bf16[4,192,1024]{2,1,0:T(8,128)(2,1)}, u32[]{:S(2)}, u32[]{:S(2)}) collective-permute-start(bf16[4,192,1024]{2,1,0:T(8,128)(2,1)} %collective-permute-done.12), channel_id=1, source_target_pairs={{0,1},{1,0},{2,3},{3,2},{4,5},{5,4},{6,7},{7,6},{8,9},{9,8},{10,11... | collective-permute-start | bytes 4718600 | tf_op jit(solution)/shard_map/ppermute | solution.py:41
  121.2 36.7 %collective-permute-start.16 = (bf16[4,96,1024]{2,1,0:T(8,128)(2,1)}, bf16[4,96,1024]{2,1,0:T(8,128)(2,1)S(1)}, u32[]{:S(2)}, u32[]{:S(2)}) collective-permute-start(bf16[4,96,1024]{2,1,0:T(8,128)(2,1)} %get-tuple-element.170), channel_id=1, source_target_pairs={{0,4},{1,5},{2,6},{3,7},{4,0},{5,1},{6,2},{7,3},{8,12},{9,13},{10,... | collective-permute-start | bytes 2359304 | tf_op jit(solution)/shard_map/ppermute | solution.py:41
  166.0 66.5 %collective-permute-start.24 = (bf16[272,1024]{1,0:T(8,128)(2,1)S(1)}, bf16[272,1024]{1,0:T(8,128)(2,1)S(1)}, u32[]{:S(2)}, u32[]{:S(2)}) collective-permute-start(bf16[272,1024]{1,0:T(8,128)(2,1)S(1)} %pad_maximum_fusion.2.refs_0_), channel_id=1, source_target_pairs={{0,8},{8,0},{16,24},{24,16},{1,9},{9,1},{17,25},{25,17},{2,10},{10... | collective-permute-start | bytes 1671176 | tf_op jit(solution)/shard_map/ppermute | solution.py:41
  166.0 32.7 %collective-permute-start.20 = (bf16[4,96,1024]{2,1,0:T(8,128)(2,1)S(1)}, bf16[4,96,1024]{2,1,0:T(8,128)(2,1)S(1)}, u32[]{:S(2)}, u32[]{:S(2)}) collective-permute-start(bf16[4,96,1024]{2,1,0:T(8,128)(2,1)S(1)} %copy-done.38), channel_id=1, source_target_pairs={{0,1},{1,0},{2,3},{3,2},{4,5},{5,4},{6,7},{7,6},{8,9},{9,8},{10,11... | collective-permute-start | bytes 2359304 | tf_op jit(solution)/shard_map/ppermute | solution.py:41
  166.5 37.5 %collective-permute-start.22 = (bf16[4,96,1024]{2,1,0:T(8,128)(2,1)S(1)}, bf16[4,96,1024]{2,1,0:T(8,128)(2,1)S(1)}, u32[]{:S(2)}, u32[]{:S(2)}) collective-permute-start(bf16[4,96,1024]{2,1,0:T(8,128)(2,1)S(1)} %copy-done.43), channel_id=1, source_target_pairs={{0,4},{1,5},{2,6},{3,7},{4,0},{5,1},{6,2},{7,3},{8,12},{9,13},{10,... | collective-permute-start | bytes 2359304 | tf_op jit(solution)/shard_map/ppermute | solution.py:41
  186.5 29.1 %collective-permute-start.21 = (bf16[4,96,1024]{2,1,0:T(8,128)(2,1)S(1)}, bf16[4,96,1024]{2,1,0:T(8,128)(2,1)S(1)}, u32[]{:S(2)}, u32[]{:S(2)}) collective-permute-start(bf16[4,96,1024]{2,1,0:T(8,128)(2,1)S(1)} %copy-done.40), channel_id=1, source_target_pairs={{0,1},{1,0},{2,3},{3,2},{4,5},{5,4},{6,7},{7,6},{8,9},{9,8},{10,11... | collective-permute-start | bytes 2359304 | tf_op jit(solution)/shard_map/ppermute | solution.py:41
  210.1 38.2 %collective-permute-start.29 = (bf16[272,1024]{1,0:T(8,128)(2,1)S(1)}, bf16[272,1024]{1,0:T(8,128)(2,1)S(1)}, u32[]{:S(2)}, u32[]{:S(2)}) collective-permute-start(bf16[272,1024]{1,0:T(8,128)(2,1)S(1)} %collective-permute-done.18.refs_0_), channel_id=1, source_target_pairs={{0,8},{8,0},{16,24},{24,16},{1,9},{9,1},{17,25},{25,17},{2,10},{10... | collective-permute-start | bytes 1671176 | tf_op jit(solution)/shard_map/ppermute | solution.py:41
  215.6 32.7 %collective-permute-start.31 = (bf16[272,1024]{1,0:T(8,128)(2,1)S(1)}, bf16[272,1024]{1,0:T(8,128)(2,1)S(1)}, u32[]{:S(2)}, u32[]{:S(2)}) collective-permute-start(bf16[272,1024]{1,0:T(8,128)(2,1)S(1)} %collective-permute-done.30.refs_2_), channel_id=1, source_target_pairs={{0,8},{8,0},{16,24},{24,16},{1,9},{9,1},{17,25},{25,17},{2,10},{10... | collective-permute-start | bytes 1671176 | tf_op jit(solution)/shard_map/ppermute | solution.py:41
  310.8 40.2 %collective-permute-start.46 = (bf16[256,1024]{1,0:T(8,128)(2,1)S(1)}, bf16[256,1024]{1,0:T(8,128)(2,1)S(1)}, u32[]{:S(2)}, u32[]{:S(2)}) collective-permute-start(bf16[256,1024]{1,0:T(8,128)(2,1)S(1)} %collective-permute-done.40.refs_4_), channel_id=1, source_target_pairs={{0,8},{8,0},{16,24},{24,16},{1,9},{9,1},{17,25},{25,17},{2,10},{10... | collective-permute-start | bytes 1572872 | tf_op jit(solution)/shard_map/ppermute | solution.py:41
  320.6 30.5 %collective-permute-start.48 = (bf16[256,1024]{1,0:T(8,128)(2,1)S(1)}, bf16[256,1024]{1,0:T(8,128)(2,1)S(1)}, u32[]{:S(2)}, u32[]{:S(2)}) collective-permute-start(bf16[256,1024]{1,0:T(8,128)(2,1)S(1)} %collective-permute-done.47.refs_6_), channel_id=1, source_target_pairs={{0,8},{8,0},{16,24},{24,16},{1,9},{9,1},{17,25},{25,17},{2,10},{10... | collective-permute-start | bytes 1572872 | tf_op jit(solution)/shard_map/ppermute | solution.py:41
  373.8 28.4 %collective-permute-start.44 = (bf16[2,272,1024]{2,1,0:T(8,128)(2,1)}, bf16[2,272,1024]{2,1,0:T(8,128)(2,1)}, u32[]{:S(2)}, u32[]{:S(2)}) collective-permute-start(bf16[2,272,1024]{2,1,0:T(8,128)(2,1)} %get-tuple-element.190), channel_id=1, source_target_pairs={{0,8},{8,0},{16,24},{24,16},{1,9},{9,1},{17,25},{25,17},{2,10},{10... | collective-permute-start | bytes 3342344 | tf_op jit(solution)/shard_map/ppermute | solution.py:41
  400.6 49.0 %collective-permute-start.52 = (bf16[4,192,1024]{2,1,0:T(8,128)(2,1)}, bf16[4,192,1024]{2,1,0:T(8,128)(2,1)}, u32[]{:S(2)}, u32[]{:S(2)}) collective-permute-start(bf16[4,192,1024]{2,1,0:T(8,128)(2,1)} %get-tuple-element.205), channel_id=1, source_target_pairs={{0,1},{1,0},{2,3},{3,2},{4,5},{5,4},{6,7},{7,6},{8,9},{9,8},{10,11... | collective-permute-start | bytes 4718600 | tf_op jit(solution)/shard_map/ppermute | solution.py:41
  404.4 42.4 %collective-permute-start.45 = (bf16[272,1024]{1,0:T(8,128)(2,1)}, bf16[272,1024]{1,0:T(8,128)(2,1)S(1)}, u32[]{:S(2)}, u32[]{:S(2)}) collective-permute-start(bf16[272,1024]{1,0:T(8,128)(2,1)} %fusion.10), channel_id=1, source_target_pairs={{0,16},{8,24},{16,0},{24,8},{1,17},{9,25},{17,1},{25,9},{2,18},{10... | collective-permute-start | bytes 1671176 | tf_op jit(solution)/shard_map/ppermute | solution.py:41
  407.2 41.1 %collective-permute-start.51 = (bf16[272,1024]{1,0:T(8,128)(2,1)}, bf16[272,1024]{1,0:T(8,128)(2,1)}, u32[]{:S(2)}, u32[]{:S(2)}) collective-permute-start(bf16[272,1024]{1,0:T(8,128)(2,1)} %fusion.7), channel_id=1, source_target_pairs={{0,2},{1,3},{2,0},{3,1},{4,6},{5,7},{6,4},{7,5},{8,10},{9,11},{10,... | collective-permute-start | bytes 1671176 | tf_op jit(solution)/shard_map/ppermute | solution.py:41
  408.9 28.3 %collective-permute-start.37 = (f32[8,128]{1,0:T(8,128)S(1)}, f32[8,128]{1,0:T(8,128)S(1)}, u32[]{:S(2)}, u32[]{:S(2)}) collective-permute-start(f32[8,128]{1,0:T(8,128)S(1)} %fusion.56), channel_id=1, source_target_pairs={{0,1},{1,0},{2,3},{3,2},{4,5},{5,4},{6,7},{7,6},{8,9},{9,8},{10,11... | collective-permute-start | bytes 12296 | tf_op jit(solution)/shard_map/ppermute | solution.py:41
  445.3 33.4 %collective-permute-start.53 = (bf16[4,192,1024]{2,1,0:T(8,128)(2,1)}, bf16[4,192,1024]{2,1,0:T(8,128)(2,1)}, u32[]{:S(2)}, u32[]{:S(2)}) collective-permute-start(bf16[4,192,1024]{2,1,0:T(8,128)(2,1)} %get-tuple-element.207), channel_id=1, source_target_pairs={{0,1},{1,0},{2,3},{3,2},{4,5},{5,4},{6,7},{7,6},{8,9},{9,8},{10,11... | collective-permute-start | bytes 4718600 | tf_op jit(solution)/shard_map/ppermute | solution.py:41
  454.2 33.8 %collective-permute-start.54 = (bf16[4,96,1024]{2,1,0:T(8,128)(2,1)S(1)}, bf16[4,96,1024]{2,1,0:T(8,128)(2,1)}, u32[]{:S(2)}, u32[]{:S(2)}) collective-permute-start(bf16[4,96,1024]{2,1,0:T(8,128)(2,1)S(1)} %get-tuple-element.281), channel_id=1, source_target_pairs={{0,4},{1,5},{2,6},{3,7},{4,0},{5,1},{6,2},{7,3},{8,12},{9,13},{10,... | collective-permute-start | bytes 2359304 | tf_op jit(solution)/shard_map/ppermute | solution.py:41
  462.4 43.6 %collective-permute-start.55 = (bf16[2,1,4,2,32,1024]{5,4,3,2,1,0:T(8,128)(2,1)}, bf16[2,1,4,2,32,1024]{5,4,3,2,1,0:T(8,128)(2,1)S(1)}, u32[]{:S(2)}, u32[]{:S(2)}) collective-permute-start(bf16[2,1,4,2,32,1024]{5,4,3,2,1,0:T(8,128)(2,1)} %get-tuple-element.276), channel_id=1, source_target_pairs={{0,8},{8,0},{16,24},{24,16},{1,9},{9,1},{17,25},{25,17},{2,10},{10... | collective-permute-start | bytes 3145736 | tf_op jit(solution)/shard_map/ppermute | solution.py:41
  488.0 35.9 %collective-permute-start.56 = (bf16[4,96,1024]{2,1,0:T(8,128)(2,1)}, bf16[4,96,1024]{2,1,0:T(8,128)(2,1)}, u32[]{:S(2)}, u32[]{:S(2)}) collective-permute-start(bf16[4,96,1024]{2,1,0:T(8,128)(2,1)} %get-tuple-element.212), channel_id=1, source_target_pairs={{0,4},{1,5},{2,6},{3,7},{4,0},{5,1},{6,2},{7,3},{8,12},{9,13},{10,... | collective-permute-start | bytes 2359304 | tf_op jit(solution)/shard_map/ppermute | solution.py:41
  489.9 45.9 %collective-permute-start.58 = (bf16[4,192,1024]{2,1,0:T(8,128)(2,1)}, bf16[4,192,1024]{2,1,0:T(8,128)(2,1)S(1)}, u32[]{:S(2)}, u32[]{:S(2)}) collective-permute-start(bf16[4,192,1024]{2,1,0:T(8,128)(2,1)} %get-tuple-element.219), channel_id=1, source_target_pairs={{0,1},{1,0},{2,3},{3,2},{4,5},{5,4},{6,7},{7,6},{8,9},{9,8},{10,11... | collective-permute-start | bytes 4718600 | tf_op jit(solution)/shard_map/ppermute | solution.py:41
  523.9 36.6 %collective-permute-start.59 = (bf16[4,96,1024]{2,1,0:T(8,128)(2,1)}, bf16[4,96,1024]{2,1,0:T(8,128)(2,1)}, u32[]{:S(2)}, u32[]{:S(2)}) collective-permute-start(bf16[4,96,1024]{2,1,0:T(8,128)(2,1)} %get-tuple-element.222), channel_id=1, source_target_pairs={{0,4},{1,5},{2,6},{3,7},{4,0},{5,1},{6,2},{7,3},{8,12},{9,13},{10,... | collective-permute-start | bytes 2359304 | tf_op jit(solution)/shard_map/ppermute | solution.py:41
  571.7 61.4 %collective-permute-start.66 = (bf16[4,192,1024]{2,1,0:T(8,128)(2,1)}, bf16[4,192,1024]{2,1,0:T(8,128)(2,1)}, u32[]{:S(2)}, u32[]{:S(2)}) collective-permute-start(bf16[4,192,1024]{2,1,0:T(8,128)(2,1)} %get-tuple-element.234), channel_id=1, source_target_pairs={{0,1},{1,0},{2,3},{3,2},{4,5},{5,4},{6,7},{7,6},{8,9},{9,8},{10,11... | collective-permute-start | bytes 4718600 | tf_op jit(solution)/shard_map/ppermute | solution.py:41
  572.2 60.9 %collective-permute-start.68 = (bf16[4,192,1024]{2,1,0:T(8,128)(2,1)}, bf16[4,192,1024]{2,1,0:T(8,128)(2,1)}, u32[]{:S(2)}, u32[]{:S(2)}) collective-permute-start(bf16[4,192,1024]{2,1,0:T(8,128)(2,1)} %add_convert_fusion), channel_id=1, source_target_pairs={{0,2},{1,3},{2,0},{3,1},{4,6},{5,7},{6,4},{7,5},{8,10},{9,11},{10,... | collective-permute-start | bytes 4718600 | tf_op jit(solution)/shard_map/ppermute | solution.py:41
  575.1 58.0 %collective-permute-start.62 = (bf16[1,1,4,2,32,2176]{5,4,3,2,1,0:T(8,128)(2,1)S(1)}, bf16[1,1,4,2,32,2176]{5,4,3,2,1,0:T(8,128)(2,1)S(1)}, u32[]{:S(2)}, u32[]{:S(2)}) collective-permute-start(bf16[1,1,4,2,32,2176]{5,4,3,2,1,0:T(8,128)(2,1)S(1)} %dynamic-slice_convert_fusion), channel_id=1, source_target_pairs={{0,16},{8,24},{16,0},{24,8},{1,17},{9,25},{17,1},{25,9},{2,18},{10... | collective-permute-start | bytes 3342344 | tf_op jit(solution)/shard_map/ppermute | solution.py:41
  577.5 46.0 %collective-permute-start.67 = (bf16[4,96,1024]{2,1,0:T(8,128)(2,1)S(1)}, bf16[4,96,1024]{2,1,0:T(8,128)(2,1)S(1)}, u32[]{:S(2)}, u32[]{:S(2)}) collective-permute-start(bf16[4,96,1024]{2,1,0:T(8,128)(2,1)S(1)} %copy-done.42), channel_id=1, source_target_pairs={{0,4},{1,5},{2,6},{3,7},{4,0},{5,1},{6,2},{7,3},{8,12},{9,13},{10,... | collective-permute-start | bytes 2359304 | tf_op jit(solution)/shard_map/ppermute | solution.py:41
  581.3 45.8 %collective-permute-start.63 = (bf16[1,1,1,1,32,1024]{5,4,3,2,1,0:T(8,128)(2,1)S(1)}, bf16[1,1,1,1,32,1024]{5,4,3,2,1,0:T(8,128)(2,1)S(1)}, u32[]{:S(2)}, u32[]{:S(2)}) collective-permute-start(bf16[1,1,1,1,32,1024]{5,4,3,2,1,0:T(8,128)(2,1)S(1)} %get-tuple-element.295), channel_id=1, source_target_pairs={{0,2},{1,3},{2,0},{3,1},{4,6},{5,7},{6,4},{7,5},{8,10},{9,11},{10,... | collective-permute-start | bytes 196616 | tf_op jit(solution)/shard_map/ppermute | solution.py:41
  (105 other events, 1294.4 us)

commit v11 on v10

--- a/solution.py
+++ b/solution.py
@@ -816,18 +816,23 @@
     grads = [g.reshape(rows_y, 1, units, 2, row_block, -1) for g in grads]
     part_sum = (grads[0].astype(f32), [swap(g, "dp", m + 1) for m, g in enumerate(grads[1:])])
     out_sum = halve(total(*out_sum), 2)
-    far_slot(3, grads)
-    part_sum, out_sum = join((part_sum, out_sum))
-    low_got[0] = swap(after(expert_grad[1], part_sum), "fsdp", 1)
-    hop_got = None
+    hop_parts = None
     if len(far_bits) == 1:
         far_sum(HOP_BIT)
-        hop_got = swap(after(sums_of[HOP_BIT].astype(bf16), part_sum), "fsdp", HOP_BIT)
+        hop_rows = sums_of[HOP_BIT].astype(bf16)
+        hop_parts = [swap(hop_rows[:, :half], "fsdp", HOP_BIT)]
+    far_slot(3, grads)
+    part_sum, out_sum, hop_parts = join((part_sum, out_sum, hop_parts))
+    if hop_parts is not None:
+        hop_parts.append(swap(after(hop_rows[:, half:], part_sum), "fsdp", HOP_BIT))
+    low_got[0] = swap(after(expert_grad[1], part_sum), "fsdp", 1)
     part_sum = halve(total(*part_sum), 1)
     out_sum = halve(total(*out_sum), 0)
-    part_sum, out_sum, low_got[0], far_got, hop_got = join(
-        (part_sum, out_sum, low_got[0], far_got, hop_got)
-    )
+    part_sum, out_sum, low_got[0], far_got, hop_parts = join(
+        (part_sum, out_sum, low_got[0], far_got, hop_parts)
+    )
+    if hop_parts is not None:
+        hop_got = jnp.concatenate(hop_parts, axis=1)
     low_sum(0)
     out_grad_w = total(*out_sum).reshape(row_block, -1)
     part_sum = halve(total(*part_sum), 2)

time: 671 us -> 681 us (1.015)
  waiting for transfers between devices: 334 us -> 348 us
    ppermute x73 -> x74, waiting for transfers between devices: 334 us -> 348 us  [swap(): lax.ppermute(values, axis, [(i, i ^ mask) for i in range(lax.axis_size(ax...]
    ppermute x73 -> x74, starting transfers between devices: 71.2 us -> 67.5 us  [swap(): lax.ppermute(values, axis, [(i, i ^ mask) for i in range(lax.axis_size(ax...]
    unnamed x128 -> x120, local copies, waits for them, and re-layouts: 17.8 us -> 16.8 us
  transfers between devices with their start and end apart: 73 -> 74, of which waited for: 35 -> 36; matrix products, arithmetic and copies ran while one was open for 15% -> 15% of each run, Pallas kernels for 13% -> 13%
where the time goes in v11:
time: 681 us; the launch traced here: 675 us
  waiting for transfers between devices  348 us (51%)
  Pallas kernels  121 us (18%)
  starting transfers between devices  67.5 us (10%)
  local copies, waits for them, and re-layouts  67.2 us (10%)
  other arithmetic  56.5 us (8%)
  matrix products  9.64 us (1%)
    ppermute x74, waiting for transfers between devices, swap(): lax.ppermute(values, axis, [(i, i ^ mask) for i in range(lax.axis_size(ax...  348 us
    pallas_call x4, Pallas kernels, expert_call(): pl.pallas_call(body, grid=(held,), out_shape=out_shape, in_specs=[smem(),...  70.8 us
    ppermute x74, starting transfers between devices, swap(): lax.ppermute(values, axis, [(i, i ^ mask) for i in range(lax.axis_size(ax...  67.5 us
    pallas_call x3, Pallas kernels, kernel_call(): pl.pallas_call(body, out_shape=out_shape, in_specs=specs, out_specs=jax.t...  31.2 us
    dynamic_update_slice x12, local copies, waits for them, and re-layouts, on_device(): lax.dynamic_update_slice(expert_w, piece[:, None], (0, fsdp_at ^ m, row, 0))  20.4 us
    pallas_call x1, Pallas kernels, on_device(): pl.pallas_call(functools.partial(expert_weight_grads, HOPS), grid=(held,)...  19 us
    unnamed x120, local copies, waits for them, and re-layouts  16.8 us
  transfers between devices with their start and end apart: 74, of which 36 were waited for; matrix products, arithmetic and copies ran while one was open for 15% of the time, Pallas kernels for 13%

profile of v11, /device:TPU:0, one launch (start us, length us, event | category | flops | bytes accessed | tf_op | source)
XLA Modules:
  0.0 675.3 jit_solution(4713570773376226141)
XLA Ops:
  20.7 6.1 broadcast_in_dim.119
  38.4 13.2 %collective-permute-done.7 = bf16[1,1,4,1,32,1024]{5,4,3,2,1,0:T(8,128)(2,1)} collective-permute-done((bf16[1,1,4,1,32,1024]{5,4,3,2,1,0:T(8,128)(2,1)S(1)}, bf16[1,1,4,1,32,1024]{5,4,3,2,1,0:T(8,128)(2,1)}, u32[]{:S(2)}, u32[]{:S(2)}) %collective-permute-start.7) | collective-permute-done | bytes 262176 | tf_op jit(solution)/shard_map/ppermute | solution.py:41
  51.6 16.0 %collective-permute-done.9 = bf16[4,96,1024]{2,1,0:T(8,128)(2,1)} collective-permute-done((bf16[4,96,1024]{2,1,0:T(8,128)(2,1)}, bf16[4,96,1024]{2,1,0:T(8,128)(2,1)}, u32[]{:S(2)}, u32[]{:S(2)}) %collective-permute-start.9) | collective-permute-done | bytes 786464 | tf_op jit(solution)/shard_map/ppermute | solution.py:41
  73.5 25.5 %collective-permute-done.12 = bf16[4,192,1024]{2,1,0:T(8,128)(2,1)} collective-permute-done((bf16[4,192,1024]{2,1,0:T(8,128)(2,1)}, bf16[4,192,1024]{2,1,0:T(8,128)(2,1)}, u32[]{:S(2)}, u32[]{:S(2)}) %collective-permute-start.12) | collective-permute-done | bytes 1572896 | tf_op jit(solution)/shard_map/ppermute | solution.py:41
  99.1 8.5 %collective-permute-done.11 = bf16[2,1,4,1,32,1024]{5,4,3,2,1,0:T(8,128)(2,1)S(1)} collective-permute-done((bf16[2,1,4,1,32,1024]{5,4,3,2,1,0:T(8,128)(2,1)S(1)}, bf16[2,1,4,1,32,1024]{5,4,3,2,1,0:T(8,128)(2,1)S(1)}, u32[]{:S(2)}, u32[]{:S(2)}) %collective-permute-start.11) | collective-permute-done | bytes 524320 | tf_op jit(solution)/shard_map/ppermute | solution.py:41
  130.4 9.7 %shard_map.237 = (bf16[256,2048]{1,0:T(8,128)(2,1)}, bf16[256,1024]{1,0:T(8,128)(2,1)}) custom-call(s32[1]{0:T(128)} %copy.87.length_ref, f32[256,2048]{1,0:T(8,128)} %fusion.qkv_ref, f32[256,128]{1,0:T(8,128)} %get-tuple-element.319.cos_ref, f32[256,128]{1,0:T(8,128)} %get-tuple-element.320.sin_ref), custom_call_target="tpu_custom_call" | custom-call | tf_op jit(solution)/shard_map/pallas_call | solution.py:60
  140.1 17.8 %collective-permute-done.16 = bf16[4,96,1024]{2,1,0:T(8,128)(2,1)S(1)} collective-permute-done((bf16[4,96,1024]{2,1,0:T(8,128)(2,1)}, bf16[4,96,1024]{2,1,0:T(8,128)(2,1)S(1)}, u32[]{:S(2)}, u32[]{:S(2)}) %collective-permute-start.16) | collective-permute-done | bytes 786464 | tf_op jit(solution)/shard_map/ppermute | solution.py:41
  171.0 13.8 %collective-permute-done.18.refs_0_ = bf16[272,1024]{1,0:T(8,128)(2,1)S(1)} collective-permute-done((bf16[272,1024]{1,0:T(8,128)(2,1)S(1)}, bf16[272,1024]{1,0:T(8,128)(2,1)S(1)}, u32[]{:S(2)}, u32[]{:S(2)}) %collective-permute-start.18) | collective-permute-done | bytes 557088 | tf_op jit(solution)/shard_map/ppermute | solution.py:41
  189.3 9.4 %collective-permute-done.20 = bf16[4,96,1024]{2,1,0:T(8,128)(2,1)S(1)} collective-permute-done((bf16[4,96,1024]{2,1,0:T(8,128)(2,1)S(1)}, bf16[4,96,1024]{2,1,0:T(8,128)(2,1)S(1)}, u32[]{:S(2)}, u32[]{:S(2)}) %collective-permute-start.20) | collective-permute-done | bytes 786464 | tf_op jit(solution)/shard_map/ppermute | solution.py:41
  210.1 5.5 collective-permute-done.21
  218.0 13.5 %collective-permute-done.23 = bf16[4,96,1024]{2,1,0:T(8,128)(2,1)S(1)} collective-permute-done((bf16[4,96,1024]{2,1,0:T(8,128)(2,1)S(1)}, bf16[4,96,1024]{2,1,0:T(8,128)(2,1)S(1)}, u32[]{:S(2)}, u32[]{:S(2)}) %collective-permute-start.23) | collective-permute-done | bytes 786464 | tf_op jit(solution)/shard_map/ppermute | solution.py:41
  234.1 14.4 %shard_map.238 = (bf16[2,256,1024]{2,1,0:T(8,128)(2,1)}, bf16[2,256,1024]{2,1,0:T(8,128)(2,1)}) custom-call(s32[1]{0:T(128)} %bitcast.8.first_ref, bf16[4,8,192,1024]{3,2,1,0:T(8,128)(2,1)} %bitcast_dynamic-update-slice_fusion.11.weights_ref, bf16[272,1024]{1,0:T(8,128)(2,1)} %copy-done.6, bf16[272,1024]{1,0:T(8,128)(2,1)} %copy-done.18, ...), custom_call_target="tpu_custom_call" | custom-call | tf_op jit(solution)/shard_map/pallas_call | solution.py:80
  250.2 13.8 %shard_map.239 = (bf16[2,256,1024]{2,1,0:T(8,128)(2,1)}, bf16[2,256,1024]{2,1,0:T(8,128)(2,1)}) custom-call(s32[1]{0:T(128)} %bitcast.8.first_ref, bf16[4,8,192,1024]{3,2,1,0:T(8,128)(2,1)} %bitcast_dynamic-update-slice_fusion.11.weights_ref, bf16[272,1024]{1,0:T(8,128)(2,1)} %copy-done.17, bf16[272,1024]{1,0:T(8,128)(2,1)} %copy-done.21, ...), custom_call_target="tpu_custom_call" | custom-call | tf_op jit(solution)/shard_map/pallas_call | solution.py:80
  271.2 11.8 %collective-permute-done.33 = bf16[256,1024]{1,0:T(8,128)(2,1)S(1)} collective-permute-done((bf16[256,1024]{1,0:T(8,128)(2,1)S(1)}, bf16[256,1024]{1,0:T(8,128)(2,1)S(1)}, u32[]{:S(2)}, u32[]{:S(2)}) %collective-permute-start.33) | collective-permute-done | bytes 524320 | tf_op jit(solution)/shard_map/ppermute | solution.py:41
  283.9 9.4 %collective-permute-done.28 = bf16[256,1024]{1,0:T(8,128)(2,1)S(1)} collective-permute-done((bf16[256,1024]{1,0:T(8,128)(2,1)S(1)}, bf16[256,1024]{1,0:T(8,128)(2,1)S(1)}, u32[]{:S(2)}, u32[]{:S(2)}) %collective-permute-start.28) | collective-permute-done | bytes 524320 | tf_op jit(solution)/shard_map/ppermute | solution.py:41
  299.6 9.9 %collective-permute-done.40.refs_4_ = bf16[256,1024]{1,0:T(8,128)(2,1)S(1)} collective-permute-done((bf16[256,1024]{1,0:T(8,128)(2,1)S(1)}, bf16[256,1024]{1,0:T(8,128)(2,1)S(1)}, u32[]{:S(2)}, u32[]{:S(2)}) %collective-permute-start.40) | collective-permute-done | bytes 524320 | tf_op jit(solution)/shard_map/ppermute | solution.py:41
  311.6 9.2 %collective-permute-done.47.refs_6_ = bf16[256,1024]{1,0:T(8,128)(2,1)S(1)} collective-permute-done((bf16[256,1024]{1,0:T(8,128)(2,1)S(1)}, bf16[256,1024]{1,0:T(8,128)(2,1)S(1)}, u32[]{:S(2)}, u32[]{:S(2)}) %collective-permute-start.47) | collective-permute-done | bytes 524320 | tf_op jit(solution)/shard_map/ppermute | solution.py:41
  329.8 21.4 %shard_map.240 = (bf16[2,272,1024]{2,1,0:T(8,128)(2,1)}, bf16[2,272,1024]{2,1,0:T(8,128)(2,1)}, bf16[4,384,1024]{2,1,0:T(8,128)(2,1)}, bf16[4,384,1024]{2,1,0:T(...) custom-call(s32[1]{0:T(128)} %bitcast.8.first_ref, ...), custom_call_target="tpu_custom_call" | custom-call | tf_op jit(solution)/shard_map/pallas_call | solution.py:80
  352.8 21.1 %shard_map.241 = (bf16[2,272,1024]{2,1,0:T(8,128)(2,1)}, bf16[2,272,1024]{2,1,0:T(8,128)(2,1)}, bf16[4,384,1024]{2,1,0:T(8,128)(2,1)}, bf16[4,384,1024]{2,1,0:T(...) custom-call(s32[1]{0:T(128)} %bitcast.8.first_ref, ...), custom_call_target="tpu_custom_call" | custom-call | tf_op jit(solution)/shard_map/pallas_call | solution.py:80
  381.5 19.0 %shard_map.242 = (bf16[4,192,1024]{2,1,0:T(8,128)(2,1)}, bf16[4,192,1024]{2,1,0:T(8,128)(2,1)}, bf16[4,192,1024]{2,1,0:T(8,128)(2,1)}, bf16[4,192,1024]{2,1,0:T(...) custom-call(s32[1]{0:T(128)} %bitcast.43.at_ref, ...), custom_call_target="tpu_custom_call" | custom-call | tf_op jit(solution)/shard_map/pallas_call | solution.py:684
  409.4 27.8 %collective-permute-done.37 = f32[8,128]{1,0:T(8,128)S(1)} collective-permute-done((f32[8,128]{1,0:T(8,128)S(1)}, f32[8,128]{1,0:T(8,128)S(1)}, u32[]{:S(2)}, u32[]{:S(2)}) %collective-permute-start.37) | collective-permute-done | bytes 4128 | tf_op jit(solution)/shard_map/ppermute | solution.py:41
  464.3 14.4 %collective-permute-done.53 = bf16[4,192,1024]{2,1,0:T(8,128)(2,1)} collective-permute-done((bf16[4,192,1024]{2,1,0:T(8,128)(2,1)}, bf16[4,192,1024]{2,1,0:T(8,128)(2,1)}, u32[]{:S(2)}, u32[]{:S(2)}) %collective-permute-start.53) | collective-permute-done | bytes 1572896 | tf_op jit(solution)/shard_map/ppermute | solution.py:41
  478.7 9.2 %collective-permute-done.54 = bf16[4,96,1024]{2,1,0:T(8,128)(2,1)} collective-permute-done((bf16[4,96,1024]{2,1,0:T(8,128)(2,1)S(1)}, bf16[4,96,1024]{2,1,0:T(8,128)(2,1)}, u32[]{:S(2)}, u32[]{:S(2)}) %collective-permute-start.54) | collective-permute-done | bytes 786464 | tf_op jit(solution)/shard_map/ppermute | solution.py:41
  490.4 12.5 %shard_map.243.qkv_grad_ref = bf16[256,2048]{1,0:T(8,128)(2,1)} custom-call(s32[1]{0:T(128)} %copy.87.length_ref, bf16[256,2048]{1,0:T(8,128)(2,1)} %get-tuple-element.189.rot_ref, bf16[256,1024]{1,0:T(8,128)(2,1)} %convolution_convert_fusion.1.grad_ref, f32[256,128]{1,0:T(8,128)} %get-tuple-element.319.cos_ref, f32[256,128]{1,0:T(8,128)} %get-tuple-element.320.sin_ref), custom_call_target="tpu_custom_call" | custom-call | tf_op jit(solution)/shard_map/pallas_call | solution.py:60
  506.1 17.8 %collective-permute-done.56 = bf16[4,96,1024]{2,1,0:T(8,128)(2,1)} collective-permute-done((bf16[4,96,1024]{2,1,0:T(8,128)(2,1)}, bf16[4,96,1024]{2,1,0:T(8,128)(2,1)}, u32[]{:S(2)}, u32[]{:S(2)}) %collective-permute-start.56) | collective-permute-done | bytes 786464 | tf_op jit(solution)/shard_map/ppermute | solution.py:41
  526.7 8.9 %shard_map.244 = (bf16[2,256,2176]{2,1,0:T(8,128)(2,1)}, bf16[2,256,2176]{2,1,0:T(8,128)(2,1)}, f32[256,1024]{1,0:T(8,128)}) custom-call(s32[1]{0:T(128)} %bitcast.38.core_ref, bf16[256,2048]{1,0:T(8,128)(2,1)} %shard_map.243.qkv_grad_ref, bf16[256,1024]{1,0:T(8,128)(2,1)} %copy-done.24, bf16[1024,2176]{1,0:T(8,128)(2,1)} %bitcast.129, ...), custom_call_target="tpu_custom_call" | custom-call | tf_op jit(solution)/shard_map/pallas_call | solution.py:60
  538.2 21.9 %collective-permute-done.59 = bf16[4,96,1024]{2,1,0:T(8,128)(2,1)} collective-permute-done((bf16[4,96,1024]{2,1,0:T(8,128)(2,1)S(1)}, bf16[4,96,1024]{2,1,0:T(8,128)(2,1)}, u32[]{:S(2)}, u32[]{:S(2)}) %collective-permute-start.59) | collective-permute-done | bytes 786464 | tf_op jit(solution)/shard_map/ppermute | solution.py:41
  567.6 5.9 collective-permute-done.61
  573.5 11.1 %collective-permute-done.62 = bf16[4,96,1024]{2,1,0:T(8,128)(2,1)S(1)} collective-permute-done((bf16[4,96,1024]{2,1,0:T(8,128)(2,1)}, bf16[4,96,1024]{2,1,0:T(8,128)(2,1)S(1)}, u32[]{:S(2)}, u32[]{:S(2)}) %collective-permute-start.62) | collective-permute-done | bytes 786464 | tf_op jit(solution)/shard_map/ppermute | solution.py:41
  597.2 31.8 %collective-permute-done.68 = bf16[4,96,1024]{2,1,0:T(8,128)(2,1)S(1)} collective-permute-done((bf16[4,96,1024]{2,1,0:T(8,128)(2,1)}, bf16[4,96,1024]{2,1,0:T(8,128)(2,1)S(1)}, u32[]{:S(2)}, u32[]{:S(2)}) %collective-permute-start.68) | collective-permute-done | bytes 786464 | tf_op jit(solution)/shard_map/ppermute | solution.py:41
  640.1 11.7 %collective-permute-done.70 = bf16[1,1,4,1,32,2176]{5,4,3,2,1,0:T(8,128)(2,1)S(1)} collective-permute-done((bf16[1,1,4,1,32,2176]{5,4,3,2,1,0:T(8,128)(2,1)S(1)}, bf16[1,1,4,1,32,2176]{5,4,3,2,1,0:T(8,128)(2,1)S(1)}, u32[]{:S(2)}, u32[]{:S(2)}) %collective-permute-start.70) | collective-permute-done | bytes 557088 | tf_op jit(solution)/shard_map/ppermute | solution.py:41
  660.5 6.3 collective-permute-done.72
  (366 shorter events, 221.2 us)
Async XLA Ops:
  28.9 38.6 %collective-permute-start.8 = (bf16[4,192,1024]{2,1,0:T(8,128)(2,1)}, bf16[4,192,1024]{2,1,0:T(8,128)(2,1)}, u32[]{:S(2)}, u32[]{:S(2)}) collective-permute-start(bf16[4,192,1024]{2,1,0:T(8,128)(2,1)} %get-tuple-element.273), channel_id=1, source_target_pairs={{0,1},{1,0},{2,3},{3,2},{4,5},{5,4},{6,7},{7,6},{8,9},{9,8},{10,11... | collective-permute-start | bytes 4718600 | tf_op jit(solution)/shard_map/ppermute | solution.py:41
  32.4 35.2 %collective-permute-start.9 = (bf16[4,96,1024]{2,1,0:T(8,128)(2,1)}, bf16[4,96,1024]{2,1,0:T(8,128)(2,1)}, u32[]{:S(2)}, u32[]{:S(2)}) collective-permute-start(bf16[4,96,1024]{2,1,0:T(8,128)(2,1)} %get-tuple-element.153), channel_id=1, source_target_pairs={{0,4},{1,5},{2,6},{3,7},{4,0},{5,1},{6,2},{7,3},{8,12},{9,13},{10,... | collective-permute-start | bytes 2359304 | tf_op jit(solution)/shard_map/ppermute | solution.py:41
  37.9 61.2 %collective-permute-start.12 = (bf16[4,192,1024]{2,1,0:T(8,128)(2,1)}, bf16[4,192,1024]{2,1,0:T(8,128)(2,1)}, u32[]{:S(2)}, u32[]{:S(2)}) collective-permute-start(bf16[4,192,1024]{2,1,0:T(8,128)(2,1)} %constant_dynamic-slice_fusion.9), channel_id=1, source_target_pairs={{0,2},{1,3},{2,0},{3,1},{4,6},{5,7},{6,4},{7,5},{8,10},{9,11},{10,... | collective-permute-start | bytes 4718600 | tf_op jit(solution)/shard_map/ppermute | solution.py:41
  70.3 39.0 %collective-permute-start.10 = (bf16[2,1,4,1,32,2176]{5,4,3,2,1,0:T(8,128)(2,1)}, bf16[2,1,4,1,32,2176]{5,4,3,2,1,0:T(8,128)(2,1)}, u32[]{:S(2)}, u32[]{:S(2)}) collective-permute-start(bf16[2,1,4,1,32,2176]{5,4,3,2,1,0:T(8,128)(2,1)} %maximum_select_fusion.3), channel_id=1, source_target_pairs={{0,1},{1,0},{2,3},{3,2},{4,5},{5,4},{6,7},{7,6},{8,9},{9,8},{10,11... | collective-permute-start | bytes 3342344 | tf_op jit(solution)/shard_map/ppermute | solution.py:41
  70.9 36.8 %collective-permute-start.13 = (bf16[4,96,1024]{2,1,0:T(8,128)(2,1)S(1)}, bf16[4,96,1024]{2,1,0:T(8,128)(2,1)S(1)}, u32[]{:S(2)}, u32[]{:S(2)}) collective-permute-start(bf16[4,96,1024]{2,1,0:T(8,128)(2,1)S(1)} %copy-done.39), channel_id=1, source_target_pairs={{0,4},{1,5},{2,6},{3,7},{4,0},{5,1},{6,2},{7,3},{8,12},{9,13},{10,... | collective-permute-start | bytes 2359304 | tf_op jit(solution)/shard_map/ppermute | solution.py:41
  72.0 35.6 %collective-permute-start.11 = (bf16[2,1,4,1,32,1024]{5,4,3,2,1,0:T(8,128)(2,1)S(1)}, bf16[2,1,4,1,32,1024]{5,4,3,2,1,0:T(8,128)(2,1)S(1)}, u32[]{:S(2)}, u32[]{:S(2)}) collective-permute-start(bf16[2,1,4,1,32,1024]{5,4,3,2,1,0:T(8,128)(2,1)S(1)} %maximum_select_fusion.5), channel_id=1, source_target_pairs={{0,1},{1,0},{2,3},{3,2},{4,5},{5,4},{6,7},{7,6},{8,9},{9,8},{10,11... | collective-permute-start | bytes 1572872 | tf_op jit(solution)/shard_map/ppermute | solution.py:41
  117.6 40.3 %collective-permute-start.17 = (bf16[4,192,1024]{2,1,0:T(8,128)(2,1)}, bf16[4,192,1024]{2,1,0:T(8,128)(2,1)}, u32[]{:S(2)}, u32[]{:S(2)}) collective-permute-start(bf16[4,192,1024]{2,1,0:T(8,128)(2,1)} %collective-permute-done.12), channel_id=1, source_target_pairs={{0,1},{1,0},{2,3},{3,2},{4,5},{5,4},{6,7},{7,6},{8,9},{9,8},{10,11... | collective-permute-start | bytes 4718600 | tf_op jit(solution)/shard_map/ppermute | solution.py:41
  121.1 36.8 %collective-permute-start.16 = (bf16[4,96,1024]{2,1,0:T(8,128)(2,1)}, bf16[4,96,1024]{2,1,0:T(8,128)(2,1)S(1)}, u32[]{:S(2)}, u32[]{:S(2)}) collective-permute-start(bf16[4,96,1024]{2,1,0:T(8,128)(2,1)} %get-tuple-element.172), channel_id=1, source_target_pairs={{0,4},{1,5},{2,6},{3,7},{4,0},{5,1},{6,2},{7,3},{8,12},{9,13},{10,... | collective-permute-start | bytes 2359304 | tf_op jit(solution)/shard_map/ppermute | solution.py:41
  165.9 66.6 %collective-permute-start.24 = (bf16[272,1024]{1,0:T(8,128)(2,1)S(1)}, bf16[272,1024]{1,0:T(8,128)(2,1)S(1)}, u32[]{:S(2)}, u32[]{:S(2)}) collective-permute-start(bf16[272,1024]{1,0:T(8,128)(2,1)S(1)} %pad_maximum_fusion.3.refs_0_), channel_id=1, source_target_pairs={{0,8},{8,0},{16,24},{24,16},{1,9},{9,1},{17,25},{25,17},{2,10},{10... | collective-permute-start | bytes 1671176 | tf_op jit(solution)/shard_map/ppermute | solution.py:41
  165.9 32.9 %collective-permute-start.20 = (bf16[4,96,1024]{2,1,0:T(8,128)(2,1)S(1)}, bf16[4,96,1024]{2,1,0:T(8,128)(2,1)S(1)}, u32[]{:S(2)}, u32[]{:S(2)}) collective-permute-start(bf16[4,96,1024]{2,1,0:T(8,128)(2,1)S(1)} %copy-done.36), channel_id=1, source_target_pairs={{0,1},{1,0},{2,3},{3,2},{4,5},{5,4},{6,7},{7,6},{8,9},{9,8},{10,11... | collective-permute-start | bytes 2359304 | tf_op jit(solution)/shard_map/ppermute | solution.py:41
  166.5 37.5 %collective-permute-start.22 = (bf16[4,96,1024]{2,1,0:T(8,128)(2,1)S(1)}, bf16[4,96,1024]{2,1,0:T(8,128)(2,1)S(1)}, u32[]{:S(2)}, u32[]{:S(2)}) collective-permute-start(bf16[4,96,1024]{2,1,0:T(8,128)(2,1)S(1)} %copy-done.42), channel_id=1, source_target_pairs={{0,4},{1,5},{2,6},{3,7},{4,0},{5,1},{6,2},{7,3},{8,12},{9,13},{10,... | collective-permute-start | bytes 2359304 | tf_op jit(solution)/shard_map/ppermute | solution.py:41
  186.3 29.3 %collective-permute-start.21 = (bf16[4,96,1024]{2,1,0:T(8,128)(2,1)S(1)}, bf16[4,96,1024]{2,1,0:T(8,128)(2,1)S(1)}, u32[]{:S(2)}, u32[]{:S(2)}) collective-permute-start(bf16[4,96,1024]{2,1,0:T(8,128)(2,1)S(1)} %copy-done.38), channel_id=1, source_target_pairs={{0,1},{1,0},{2,3},{3,2},{4,5},{5,4},{6,7},{7,6},{8,9},{9,8},{10,11... | collective-permute-start | bytes 2359304 | tf_op jit(solution)/shard_map/ppermute | solution.py:41
  210.0 38.5 %collective-permute-start.29 = (bf16[272,1024]{1,0:T(8,128)(2,1)S(1)}, bf16[272,1024]{1,0:T(8,128)(2,1)S(1)}, u32[]{:S(2)}, u32[]{:S(2)}) collective-permute-start(bf16[272,1024]{1,0:T(8,128)(2,1)S(1)} %collective-permute-done.18.refs_0_), channel_id=1, source_target_pairs={{0,8},{8,0},{16,24},{24,16},{1,9},{9,1},{17,25},{25,17},{2,10},{10... | collective-permute-start | bytes 1671176 | tf_op jit(solution)/shard_map/ppermute | solution.py:41
  215.6 32.9 %collective-permute-start.31 = (bf16[272,1024]{1,0:T(8,128)(2,1)S(1)}, bf16[272,1024]{1,0:T(8,128)(2,1)S(1)}, u32[]{:S(2)}, u32[]{:S(2)}) collective-permute-start(bf16[272,1024]{1,0:T(8,128)(2,1)S(1)} %collective-permute-done.30.refs_2_), channel_id=1, source_target_pairs={{0,8},{8,0},{16,24},{24,16},{1,9},{9,1},{17,25},{25,17},{2,10},{10... | collective-permute-start | bytes 1671176 | tf_op jit(solution)/shard_map/ppermute | solution.py:41
  311.0 40.2 %collective-permute-start.46 = (bf16[256,1024]{1,0:T(8,128)(2,1)S(1)}, bf16[256,1024]{1,0:T(8,128)(2,1)S(1)}, u32[]{:S(2)}, u32[]{:S(2)}) collective-permute-start(bf16[256,1024]{1,0:T(8,128)(2,1)S(1)} %collective-permute-done.40.refs_4_), channel_id=1, source_target_pairs={{0,8},{8,0},{16,24},{24,16},{1,9},{9,1},{17,25},{25,17},{2,10},{10... | collective-permute-start | bytes 1572872 | tf_op jit(solution)/shard_map/ppermute | solution.py:41
  320.8 30.4 %collective-permute-start.48 = (bf16[256,1024]{1,0:T(8,128)(2,1)S(1)}, bf16[256,1024]{1,0:T(8,128)(2,1)S(1)}, u32[]{:S(2)}, u32[]{:S(2)}) collective-permute-start(bf16[256,1024]{1,0:T(8,128)(2,1)S(1)} %collective-permute-done.47.refs_6_), channel_id=1, source_target_pairs={{0,8},{8,0},{16,24},{24,16},{1,9},{9,1},{17,25},{25,17},{2,10},{10... | collective-permute-start | bytes 1572872 | tf_op jit(solution)/shard_map/ppermute | solution.py:41
  374.0 28.0 %collective-permute-start.44 = (bf16[2,272,1024]{2,1,0:T(8,128)(2,1)}, bf16[2,272,1024]{2,1,0:T(8,128)(2,1)}, u32[]{:S(2)}, u32[]{:S(2)}) collective-permute-start(bf16[2,272,1024]{2,1,0:T(8,128)(2,1)} %get-tuple-element.192), channel_id=1, source_target_pairs={{0,8},{8,0},{16,24},{24,16},{1,9},{9,1},{17,25},{25,17},{2,10},{10... | collective-permute-start | bytes 3342344 | tf_op jit(solution)/shard_map/ppermute | solution.py:41
  400.6 48.9 %collective-permute-start.52 = (bf16[4,192,1024]{2,1,0:T(8,128)(2,1)}, bf16[4,192,1024]{2,1,0:T(8,128)(2,1)}, u32[]{:S(2)}, u32[]{:S(2)}) collective-permute-start(bf16[4,192,1024]{2,1,0:T(8,128)(2,1)} %get-tuple-element.207), channel_id=1, source_target_pairs={{0,1},{1,0},{2,3},{3,2},{4,5},{5,4},{6,7},{7,6},{8,9},{9,8},{10,11... | collective-permute-start | bytes 4718600 | tf_op jit(solution)/shard_map/ppermute | solution.py:41
  404.3 42.4 %collective-permute-start.45 = (bf16[272,1024]{1,0:T(8,128)(2,1)}, bf16[272,1024]{1,0:T(8,128)(2,1)S(1)}, u32[]{:S(2)}, u32[]{:S(2)}) collective-permute-start(bf16[272,1024]{1,0:T(8,128)(2,1)} %fusion.10), channel_id=1, source_target_pairs={{0,16},{8,24},{16,0},{24,8},{1,17},{9,25},{17,1},{25,9},{2,18},{10... | collective-permute-start | bytes 1671176 | tf_op jit(solution)/shard_map/ppermute | solution.py:41
  407.1 41.1 %collective-permute-start.51 = (bf16[272,1024]{1,0:T(8,128)(2,1)}, bf16[272,1024]{1,0:T(8,128)(2,1)}, u32[]{:S(2)}, u32[]{:S(2)}) collective-permute-start(bf16[272,1024]{1,0:T(8,128)(2,1)} %fusion.7), channel_id=1, source_target_pairs={{0,2},{1,3},{2,0},{3,1},{4,6},{5,7},{6,4},{7,5},{8,10},{9,11},{10,... | collective-permute-start | bytes 1671176 | tf_op jit(solution)/shard_map/ppermute | solution.py:41
  408.7 28.4 %collective-permute-start.37 = (f32[8,128]{1,0:T(8,128)S(1)}, f32[8,128]{1,0:T(8,128)S(1)}, u32[]{:S(2)}, u32[]{:S(2)}) collective-permute-start(f32[8,128]{1,0:T(8,128)S(1)} %fusion.57), channel_id=1, source_target_pairs={{0,1},{1,0},{2,3},{3,2},{4,5},{5,4},{6,7},{7,6},{8,9},{9,8},{10,11... | collective-permute-start | bytes 12296 | tf_op jit(solution)/shard_map/ppermute | solution.py:41
  445.3 33.4 %collective-permute-start.53 = (bf16[4,192,1024]{2,1,0:T(8,128)(2,1)}, bf16[4,192,1024]{2,1,0:T(8,128)(2,1)}, u32[]{:S(2)}, u32[]{:S(2)}) collective-permute-start(bf16[4,192,1024]{2,1,0:T(8,128)(2,1)} %get-tuple-element.209), channel_id=1, source_target_pairs={{0,1},{1,0},{2,3},{3,2},{4,5},{5,4},{6,7},{7,6},{8,9},{9,8},{10,11... | collective-permute-start | bytes 4718600 | tf_op jit(solution)/shard_map/ppermute | solution.py:41
  454.1 33.8 %collective-permute-start.54 = (bf16[4,96,1024]{2,1,0:T(8,128)(2,1)S(1)}, bf16[4,96,1024]{2,1,0:T(8,128)(2,1)}, u32[]{:S(2)}, u32[]{:S(2)}) collective-permute-start(bf16[4,96,1024]{2,1,0:T(8,128)(2,1)S(1)} %get-tuple-element.287), channel_id=1, source_target_pairs={{0,4},{1,5},{2,6},{3,7},{4,0},{5,1},{6,2},{7,3},{8,12},{9,13},{10,... | collective-permute-start | bytes 2359304 | tf_op jit(solution)/shard_map/ppermute | solution.py:41
  462.4 43.7 %collective-permute-start.55 = (bf16[2,1,4,2,32,1024]{5,4,3,2,1,0:T(8,128)(2,1)}, bf16[2,1,4,2,32,1024]{5,4,3,2,1,0:T(8,128)(2,1)S(1)}, u32[]{:S(2)}, u32[]{:S(2)}) collective-permute-start(bf16[2,1,4,2,32,1024]{5,4,3,2,1,0:T(8,128)(2,1)} %get-tuple-element.280), channel_id=1, source_target_pairs={{0,8},{8,0},{16,24},{24,16},{1,9},{9,1},{17,25},{25,17},{2,10},{10... | collective-permute-start | bytes 3145736 | tf_op jit(solution)/shard_map/ppermute | solution.py:41
  487.9 36.0 %collective-permute-start.56 = (bf16[4,96,1024]{2,1,0:T(8,128)(2,1)}, bf16[4,96,1024]{2,1,0:T(8,128)(2,1)}, u32[]{:S(2)}, u32[]{:S(2)}) collective-permute-start(bf16[4,96,1024]{2,1,0:T(8,128)(2,1)} %get-tuple-element.214), channel_id=1, source_target_pairs={{0,4},{1,5},{2,6},{3,7},{4,0},{5,1},{6,2},{7,3},{8,12},{9,13},{10,... | collective-permute-start | bytes 2359304 | tf_op jit(solution)/shard_map/ppermute | solution.py:41
  489.7 46.0 %collective-permute-start.58 = (bf16[4,192,1024]{2,1,0:T(8,128)(2,1)}, bf16[4,192,1024]{2,1,0:T(8,128)(2,1)}, u32[]{:S(2)}, u32[]{:S(2)}) collective-permute-start(bf16[4,192,1024]{2,1,0:T(8,128)(2,1)} %get-tuple-element.221), channel_id=1, source_target_pairs={{0,1},{1,0},{2,3},{3,2},{4,5},{5,4},{6,7},{7,6},{8,9},{9,8},{10,11... | collective-permute-start | bytes 4718600 | tf_op jit(solution)/shard_map/ppermute | solution.py:41
  523.9 36.3 %collective-permute-start.59 = (bf16[4,96,1024]{2,1,0:T(8,128)(2,1)S(1)}, bf16[4,96,1024]{2,1,0:T(8,128)(2,1)}, u32[]{:S(2)}, u32[]{:S(2)}) collective-permute-start(bf16[4,96,1024]{2,1,0:T(8,128)(2,1)S(1)} %get-tuple-element.224), channel_id=1, source_target_pairs={{0,4},{1,5},{2,6},{3,7},{4,0},{5,1},{6,2},{7,3},{8,12},{9,13},{10,... | collective-permute-start | bytes 2359304 | tf_op jit(solution)/shard_map/ppermute | solution.py:41
  584.6 52.1 %collective-permute-start.67 = (bf16[4,192,1024]{2,1,0:T(8,128)(2,1)}, bf16[4,192,1024]{2,1,0:T(8,128)(2,1)S(1)}, u32[]{:S(2)}, u32[]{:S(2)}) collective-permute-start(bf16[4,192,1024]{2,1,0:T(8,128)(2,1)} %get-tuple-element.240), channel_id=1, source_target_pairs={{0,1},{1,0},{2,3},{3,2},{4,5},{5,4},{6,7},{7,6},{8,9},{9,8},{10,11... | collective-permute-start | bytes 4718600 | tf_op jit(solution)/shard_map/ppermute | solution.py:41
  589.8 46.9 %collective-permute-start.63 = (bf16[1,1,4,2,32,2176]{5,4,3,2,1,0:T(8,128)(2,1)S(1)}, bf16[1,1,4,2,32,2176]{5,4,3,2,1,0:T(8,128)(2,1)}, u32[]{:S(2)}, u32[]{:S(2)}) collective-permute-start(bf16[1,1,4,2,32,2176]{5,4,3,2,1,0:T(8,128)(2,1)S(1)} %dynamic-slice_convert_fusion), channel_id=1, source_target_pairs={{0,16},{8,24},{16,0},{24,8},{1,17},{9,25},{17,1},{25,9},{2,18},{10... | collective-permute-start | bytes 3342344 | tf_op jit(solution)/shard_map/ppermute | solution.py:41
  592.2 36.9 %collective-permute-start.68 = (bf16[4,96,1024]{2,1,0:T(8,128)(2,1)}, bf16[4,96,1024]{2,1,0:T(8,128)(2,1)S(1)}, u32[]{:S(2)}, u32[]{:S(2)}) collective-permute-start(bf16[4,96,1024]{2,1,0:T(8,128)(2,1)} %get-tuple-element.242), channel_id=1, source_target_pairs={{0,4},{1,5},{2,6},{3,7},{4,0},{5,1},{6,2},{7,3},{8,12},{9,13},{10,... | collective-permute-start | bytes 2359304 | tf_op jit(solution)/shard_map/ppermute | solution.py:41
  593.3 43.4 %collective-permute-start.69 = (bf16[4,96,1024]{2,1,0:T(8,128)(2,1)}, bf16[4,96,1024]{2,1,0:T(8,128)(2,1)S(1)}, u32[]{:S(2)}, u32[]{:S(2)}) collective-permute-start(bf16[4,96,1024]{2,1,0:T(8,128)(2,1)} %get-tuple-element.244), channel_id=1, source_target_pairs={{0,2},{1,3},{2,0},{3,1},{4,6},{5,7},{6,4},{7,5},{8,10},{9,11},{10,... | collective-permute-start | bytes 2359304 | tf_op jit(solution)/shard_map/ppermute | solution.py:41
  595.1 35.4 %collective-permute-start.64 = (bf16[1,1,1,1,32,1024]{5,4,3,2,1,0:T(8,128)(2,1)S(1)}, bf16[1,1,1,1,32,1024]{5,4,3,2,1,0:T(8,128)(2,1)S(1)}, u32[]{:S(2)}, u32[]{:S(2)}) collective-permute-start(bf16[1,1,1,1,32,1024]{5,4,3,2,1,0:T(8,128)(2,1)S(1)} %get-tuple-element.301), channel_id=1, source_target_pairs={{0,2},{1,3},{2,0},{3,1},{4,6},{5,7},{6,4},{7,5},{8,10},{9,11},{10,... | collective-permute-start | bytes 196616 | tf_op jit(solution)/shard_map/ppermute | solution.py:41
  (102 other events, 1309.5 us)
